TPU v7x, 32 devices: a whole 2x2x4 slice. The times are simulated.
32 devices in a mesh: shard: 16 (over z, y, x), rep: 2 (over core).
Axes of the slice: x: 2, y: 2, z: 4, core: 2. Of those that a mesh axis runs over, the one named last changes fastest.
Arguments:
- user_emb: bfloat16 [256, 1024, 256], P('shard', 'rep'), may hold values from -6 to 6
- elig_owner: int32 [256, 4], P('shard'), may hold values from 0 to 15, all different within a row; in each aligned block of 16 rows (0 to 15, 16 to 31, ...) at most 8 rows name the same one
- elig_local: int32 [256, 4], P('shard'), may hold values from 0 to 127
- cluster_size: int32 [256], P('shard'), may hold values from 1 to 1024, 163840 in all
- camp_emb: bfloat16 [2048, 128, 256], P('shard'), may hold values from -6 to 6
- camp_count: int32 [2048], P('shard'), may hold values from 1 to 128, 196608 in all
- dual_init: float32 [2048, 128], P('shard'), may hold values from 0 to 2
- spend_limit: float32 [2048, 128], P('shard'), may hold values from 0.1 to 10
Outputs:
- user_dual: float32 [256, 1024], P('shard', 'rep')
- campaign_dual: float32 [2048, 128], P('shard')
Inputs may be any that keep to these rules, and one draw needn't show every extreme that they name: `elig_owner`: each row names 4 different owners; among the 16 rows of one shard index no owner is named more than 8 times.
All inputs are finite; a program needn't handle non-finite values. No bound on the sum of `cluster_size` or of `camp_count` on one device may be relied on, other than what follows from the above.
Results may differ from a plain program's by a relative error of at most 0.0015.
Values may be sent and summed in bfloat16 or wider, within the bound.
No kernel may reach another device: no remote copies, remote signals or barrier semaphores. Data moves between devices by JAX's collectives and lax.ppermute only.
A program may use at most 128 MiB of HBM per device.

v0:
```python
import functools
import math

import jax
import jax.numpy as jnp
from jax import lax
from jax.experimental import pallas as pl
from jax.experimental.pallas import tpu as pltpu
from jax.sharding import PartitionSpec as P


epsilon = 1e-06
temper = 0.25
sharpness = 16.0
gain = 1.0 / (temper * math.log(2.0))
masked = 1e30


VMEM = pl.BlockSpec(memory_space=pltpu.VMEM)
SMEM = pl.BlockSpec(memory_space=pltpu.SMEM)
ANY = pl.BlockSpec(memory_space=pl.ANY)
HBM = pl.BlockSpec(memory_space=pltpu.HBM)


def in_hbm(x):
    return pltpu.with_memory_space_constraint(x, pltpu.HBM)


def in_vmem(x):
    return pltpu.with_memory_space_constraint(x, pltpu.VMEM)


def send_order(shards):
    top = shards // 2
    far = [top + n for n in range(top)]
    first = far[: top // 2]
    return first + list(range(1, top)) + far[top // 2 :]


def gather_kernel(half, where_ref, asked_ref, camp_ref, *rest):
    outs, sem = rest[:-1], rest[-1]
    me, rep = where_ref[0], where_ref[1]
    copies = []
    for n, out in enumerate(outs):
        for j in range(half):
            block = asked_ref[me ^ (n + 1), rep * half + j]
            copies.append(pltpu.make_async_copy(camp_ref.at[block], out.at[j], sem.at[n * half + j]))
    for copy in copies:
        copy.start()
    for copy in copies:
        copy.wait()


def user_kernel(user_ref, scale_ref):
    rows = user_ref[0].astype(jnp.float32)
    scale = lax.rsqrt(jnp.sum(rows * rows, axis=1, keepdims=True) * (1.0 / rows.shape[1]) + epsilon)
    scale_ref[0] = jnp.broadcast_to(scale * (sharpness / rows.shape[1] * gain), scale_ref.shape[1:])


def updated(duals, spend, limit):
    return jnp.maximum(0.0, duals + temper * jnp.log((spend + limit) / (2.0 * limit)))


def totals(match_ref, mine_ref, other_ref):
    return jnp.dot(
        match_ref[0], mine_ref[...], preferred_element_type=jnp.float32
    ) + jnp.dot(match_ref[1], other_ref[...], preferred_element_type=jnp.float32)


def start_rows(user_hbm, scale_hbm, user_ref, scale_ref, sem):
    def start(k, carry):
        pltpu.make_async_copy(user_hbm.at[k], user_ref.at[k], sem.at[0, k]).start()
        pltpu.make_async_copy(scale_hbm.at[k], scale_ref.at[k], sem.at[1, k]).start()
        return carry

    lax.fori_loop(0, user_ref.shape[0], start, 0)


def start_items(item_hbm, item_ref, sem):
    def start(k, carry):
        pltpu.make_async_copy(item_hbm.at[k], item_ref.at[k], sem.at[k]).start()
        return carry

    lax.fori_loop(0, item_ref.shape[0], start, 0)


def sweep_users(
    user_hbm, scale_hbm, user_ref, scale_ref, item_ref, row_sem, item_sem, item_scale_ref, dual_scr,
    dots_a, dots_b, finish, fanout
):
    clusters, users, _ = user_ref.shape
    camps = item_ref.shape[1]
    width = item_ref.shape[2]
    rows = 64

    def landed(k):
        pltpu.make_async_copy(user_hbm.at[k], user_ref.at[k], row_sem.at[0, k]).wait()
        pltpu.make_async_copy(scale_hbm.at[k], scale_ref.at[k], row_sem.at[1, k]).wait()
        for e in range(fanout):
            item = k * fanout + e
            pltpu.make_async_copy(item_ref.at[item], item_ref.at[item], item_sem.at[item]).wait()

    def multiply(k, dots):
        blocks = item_ref[pl.ds(pl.multiple_of(k * fanout, fanout), fanout)].reshape(fanout * camps, width)
        dots[...] = lax.dot_general(
            user_ref[k], blocks, (((1,), (1,)), ((), ())), preferred_element_type=jnp.float32
        )

    def cluster(k, dots):
        first = pl.multiple_of(k * fanout, fanout)
        item_scale = item_scale_ref[pl.ds(first, fanout), :]
        shift = dual_scr[pl.ds(first, fanout), :]
        scales = [jnp.broadcast_to(item_scale[e : e + 1], (rows, camps)) for e in range(fanout)]
        shifts = [jnp.broadcast_to(shift[e : e + 1], (rows, camps)) for e in range(fanout)]
        sums = [jnp.zeros((8, camps), jnp.float32) for _ in range(fanout)]
        for start in range(0, users, rows):
            user_scale = scale_ref[k, start : start + rows, :]
            weights = []
            for e in range(fanout):
                raw = dots[start : start + rows, e * camps : (e + 1) * camps]
                weights.append(jnp.exp2(raw * user_scale * scales[e] - shifts[e]))
            den = 1.0 + jnp.sum(functools.reduce(jnp.add, weights), axis=1, keepdims=True)
            sums = finish(k, start, rows, weights, den, sums)
        finish(k, None, rows, None, None, sums)

    landed(0)
    multiply(0, dots_a)

    def two(n, carry):
        k = 2 * n
        landed(k + 1)

        @pl.when(k + 2 < clusters)
        def _():
            landed(k + 2)

        multiply(k + 1, dots_b)
        cluster(k, dots_a)
        multiply(jnp.minimum(k + 2, clusters - 1), dots_a)
        cluster(k + 1, dots_b)
        return carry

    lax.fori_loop(0, clusters // 2, two, 0)


def spend_finish(where_ref, size_ref, users, fanout, spend_scr):
    def finish(k, start, rows, weights, den, sums):
        if start is None:
            for e in range(fanout):
                spend_scr[pl.ds(k * fanout + e, 1), :] = jnp.sum(sums[e], axis=0, keepdims=True)
            return 0
        place = where_ref[1] * users + start + lax.broadcasted_iota(jnp.int32, (rows, 1), 0)
        share = jnp.where(place < size_ref[k], 1.0 / den, 0.0)
        out = []
        for e in range(fanout):
            part = weights[e] * share
            total = sums[e]
            for r in range(0, rows, 8):
                total = total + part[r : r + 8]
            out.append(total)
        return out

    return finish


def halves(where_ref, spend_scr, mine_ref, theirs_ref):
    count = mine_ref.shape[0]
    rep = where_ref[1]
    mine_ref[...] = spend_scr[pl.ds(pl.multiple_of(rep * count, count), count), :]
    theirs_ref[...] = spend_scr[pl.ds(pl.multiple_of((1 - rep) * count, count), count), :]


def first_kernel(
    shards, half, fanout, where_ref, size_ref, item_at_ref, own_ref, duals_ref, live_ref, item_scale_ref, user_hbm,
    scale_hbm, camp_ref, *rest
):
    received, (mine_ref, theirs_ref, item_out) = rest[: 2 * (shards - 1)], rest[2 * (shards - 1) :][:3]
    user_ref, scale_ref, item_ref, row_sem, item_sem, dots_a, dots_b, dual_scr, spend_scr, out_sem = rest[-10:]
    cap = 2 * half
    rep = where_ref[1]
    users = user_ref.shape[1]

    def fetch(slot, source):
        item = item_at_ref[slot]

        @pl.when(item >= 0)
        def _():
            pltpu.make_async_copy(source, item_ref.at[item], item_sem.at[item]).start()

    for j in range(cap):
        fetch(j, camp_ref.at[own_ref[j]])
    for n in range(shards - 1):
        for j in range(half):
            fetch((n + 1) * cap + rep * half + j, received[2 * n].at[j])
            fetch((n + 1) * cap + (1 - rep) * half + j, received[2 * n + 1].at[j])
    start_rows(user_hbm, scale_hbm, user_ref, scale_ref, row_sem)
    dual_scr[...] = jnp.where(live_ref[...] > 0.5, duals_ref[...] * gain, masked)
    finish = spend_finish(where_ref, size_ref, users, fanout, spend_scr)
    sweep_users(
        user_hbm, scale_hbm, user_ref, scale_ref, item_ref, row_sem, item_sem, item_scale_ref,
        dual_scr, dots_a, dots_b, finish, fanout
    )
    keep = pltpu.make_async_copy(item_ref, item_out, out_sem)
    keep.start()
    halves(where_ref, spend_scr, mine_ref, theirs_ref)
    keep.wait()


def second_kernel(
    fanout, where_ref, size_ref, duals_ref, live_ref, item_scale_ref, limit_ref, match_ref, got_ref, other_ref,
    user_hbm, scale_hbm, item_hbm, mine_ref, theirs_ref, next_ref, user_ref, scale_ref, item_ref, row_sem, item_sem,
    dots_a, dots_b, dual_scr, spend_scr
):
    start_items(item_hbm, item_ref, item_sem)
    start_rows(user_hbm, scale_hbm, user_ref, scale_ref, row_sem)
    duals = updated(duals_ref[...], totals(match_ref, got_ref, other_ref), limit_ref[...])
    next_ref[...] = duals
    dual_scr[...] = jnp.where(live_ref[...] > 0.5, duals * gain, masked)
    finish = spend_finish(where_ref, size_ref, user_ref.shape[1], fanout, spend_scr)
    sweep_users(
        user_hbm, scale_hbm, user_ref, scale_ref, item_ref, row_sem, item_sem, item_scale_ref,
        dual_scr, dots_a, dots_b, finish, fanout
    )
    halves(where_ref, spend_scr, mine_ref, theirs_ref)


def third_kernel(
    fanout, where_ref, size_ref, duals_ref, live_ref, item_scale_ref, limit_ref, match_ref, got_ref, other_ref,
    own_match_ref, got_one_ref, other_one_ref, own_dual_ref, own_limit_ref, user_hbm, scale_hbm, item_hbm,
    user_dual_ref, own_out_ref, user_ref, scale_ref, item_ref, row_sem, item_sem, dots_a, dots_b, dual_scr, row_scr
):
    start_items(item_hbm, item_ref, item_sem)
    start_rows(user_hbm, scale_hbm, user_ref, scale_ref, row_sem)
    duals = updated(duals_ref[...], totals(match_ref, got_ref, other_ref), limit_ref[...])
    dual_scr[...] = jnp.where(live_ref[...] > 0.5, duals * gain, masked)
    own = updated(own_dual_ref[...], totals(own_match_ref, got_one_ref, other_one_ref), own_limit_ref[...])
    own_out_ref[...] = updated(own, totals(own_match_ref, got_ref, other_ref), own_limit_ref[...])
    users = user_ref.shape[1]
    partial = []

    def finish(k, start, rows, weights, den, sums):
        if start is None:
            return 0
        lanes = 128
        offset = start % lanes
        wide = jnp.broadcast_to(den, (rows, lanes))
        eye = offset + lax.broadcasted_iota(jnp.int32, (rows, lanes), 0) == lax.broadcasted_iota(
            jnp.int32, (rows, lanes), 1
        )
        row = jnp.sum(jnp.where(eye, wide, 0.0), axis=0, keepdims=True)
        if offset:
            row = row + partial.pop()
        if offset + rows < lanes:
            partial.append(row)
            return sums
        base = start - offset
        place = where_ref[1] * users + base + lax.broadcasted_iota(jnp.int32, (1, lanes), 1)
        row_scr[k, base // lanes : base // lanes + 1, :] = jnp.where(
            place < size_ref[k], temper * jnp.log(row), 0.0
        )
        return sums

    sweep_users(
        user_hbm, scale_hbm, user_ref, scale_ref, item_ref, row_sem, item_sem, item_scale_ref,
        dual_scr, dots_a, dots_b, finish, fanout
    )
    for n in range(row_scr.shape[1]):
        user_dual_ref[:, n * 128 : (n + 1) * 128] = row_scr[:, n, :]


def program(
    user_emb, elig_owner, elig_local, cluster_size, camp_emb, camp_count, dual_init, spend_limit
):
    shards = lax.axis_size("shard")
    reps = lax.axis_size("rep")
    me = lax.axis_index("shard").astype(jnp.int32)
    rep = lax.axis_index("rep").astype(jnp.int32)
    clusters, users, width = user_emb.shape
    blocks, camps, _ = camp_emb.shape
    fanout = elig_owner.shape[1]
    items = clusters * fanout
    cap = 2 * items // shards
    half = cap // reps
    part = items // reps
    swap = [(0, 1), (1, 0)]
    f32 = jnp.float32

    owners = elig_owner.reshape(-1)
    locals_ = elig_local.reshape(-1)
    shard_ids = jnp.arange(shards, dtype=jnp.int32)
    hot = (owners[:, None] == shard_ids[None, :]).astype(jnp.int32)
    rank = jnp.sum((jnp.cumsum(hot, axis=0) - hot) * hot, axis=1)
    slot = owners * cap + rank
    hit = slot[:, None] == jnp.arange(shards * cap, dtype=jnp.int32)[None, :]
    wanted = jnp.sum(jnp.where(hit, locals_[:, None], 0), axis=0).reshape(shards, cap)
    names = owners * blocks + locals_
    ask = jnp.concatenate([wanted, jnp.broadcast_to(names[None, :], (shards, items))], axis=1)
    heard = lax.all_to_all(ask, "shard", split_axis=0, concat_axis=0, tiled=True)
    where = jnp.stack([me, rep])

    sent = pl.pallas_call(
        functools.partial(gather_kernel, half),
        out_shape=[pltpu.VMEM((half, camps, width), camp_emb.dtype)] * (shards - 1),
        in_specs=[SMEM, SMEM, HBM],
        out_specs=[VMEM] * (shards - 1),
        scratch_shapes=[pltpu.SemaphoreType.DMA(((shards - 1) * half,))],
        compiler_params=pltpu.CompilerParams(vmem_limit_bytes=8 * 2**20),
        cost_estimate=pl.CostEstimate(flops=0, bytes_accessed=8 * 2**20, transcendentals=0),
    )(where, heard, in_hbm(camp_emb))

    got_blocks = []
    for n in range(shards - 1):
        got_blocks.append(lax.ppermute(sent[n], "shard", [(i, i ^ (n + 1)) for i in range(shards)]))

    heard, camp_late, user_late, _ = lax.optimization_barrier((heard, camp_emb, user_emb, got_blocks[0]))
    incoming = lax.dynamic_slice_in_dim(heard[:, :cap], rep * half, half, 1)
    all_names = heard[:, cap:]
    item_of_slot = (
        jnp.sum(
            jnp.where(
                ((owners ^ me) * cap + rank)[:, None] == jnp.arange(shards * cap, dtype=jnp.int32)[None, :],
                jnp.arange(1, items + 1, dtype=jnp.int32)[:, None],
                0,
            ),
            axis=0,
        )
        - 1
    )
    own_wanted = lax.dynamic_slice_in_dim(wanted, me, 1, 0).reshape(cap)
    camp_scale = lax.rsqrt(jnp.mean(jnp.square(camp_late.astype(f32)), axis=-1) + epsilon)
    live = (jnp.arange(camps, dtype=jnp.int32)[None, :] < camp_count[:, None]).astype(f32)
    table = jnp.concatenate([dual_init, spend_limit, camp_scale, live], axis=1)
    facts = jnp.take(table, incoming.reshape(-1), axis=0, mode="clip").reshape(shards, half, 4 * camps)
    facts = lax.all_to_all(facts, "shard", split_axis=0, concat_axis=0, tiled=True)
    other_facts = lax.ppermute(facts, "rep", swap)
    pair = jnp.stack([facts, other_facts]).reshape(reps * shards * half, 4 * camps)
    spot = (rank // half ^ rep) * (shards * half) + owners * half + rank % half
    item_facts = jnp.take(pair, spot, axis=0, mode="clip")
    item_dual, item_limit, item_scale, item_live = (
        item_facts[:, n * camps : (n + 1) * camps] for n in range(4)
    )
    user_scale = pl.pallas_call(
        user_kernel,
        out_shape=jax.ShapeDtypeStruct((clusters, users, camps), f32),
        grid=(clusters,),
        in_specs=[pl.BlockSpec((1, users, width), lambda k: (k, 0, 0))],
        out_specs=pl.BlockSpec((1, users, camps), lambda k: (k, 0, 0)),
        compiler_params=pltpu.CompilerParams(vmem_limit_bytes=16 * 2**20),
        cost_estimate=pl.CostEstimate(flops=8 * 2**20, bytes_accessed=8 * 2**20, transcendentals=0),
    )(user_late)

    def columns(which):
        return lax.dynamic_slice_in_dim(all_names, which * part, part, 1).reshape(1, -1)

    sides = (columns(rep), columns(1 - rep))
    own_names = me * blocks + jnp.arange(blocks, dtype=jnp.int32)
    match = jnp.stack([(names[:, None] == side).astype(jnp.bfloat16) for side in sides])
    own_match = jnp.stack([(own_names[:, None] == side).astype(jnp.bfloat16) for side in sides])

    last = send_order(shards)[-1] - 1
    (got_blocks[last], item_dual, item_limit, item_scale, item_live, user_scale, match, own_match) = (
        lax.optimization_barrier(
            (got_blocks[last], item_dual, item_limit, item_scale, item_live, user_scale, match, own_match)
        )
    )
    received = []
    for got in got_blocks:
        received += [got, lax.ppermute(got, "rep", swap)]
    user_rows, user_scale = in_hbm(user_emb), in_hbm(user_scale)

    def exchange(mine, theirs):
        total = mine + lax.ppermute(theirs, "rep", swap)
        spread = jnp.broadcast_to(total.astype(jnp.bfloat16)[None], (shards, part, camps))
        got = lax.all_to_all(spread, "shard", split_axis=0, concat_axis=0, tiled=True)
        got = got.reshape(shards * part, camps)
        return in_vmem(got), in_vmem(lax.ppermute(got, "rep", swap))

    spend_out = [jax.ShapeDtypeStruct((part, camps), f32)] * 2
    work = [
        pltpu.VMEM((clusters, users, width), user_emb.dtype),
        pltpu.VMEM((clusters, users, camps), f32),
        pltpu.VMEM((items, camps, width), camp_emb.dtype),
        pltpu.SemaphoreType.DMA((2, clusters)),
        pltpu.SemaphoreType.DMA((items,)),
        pltpu.VMEM((users, fanout * camps), f32),
        pltpu.VMEM((users, fanout * camps), f32),
        pltpu.VMEM((items, camps), f32),
    ]
    spend_work = [pltpu.VMEM((items, camps), f32)]
    limits = pltpu.CompilerParams(vmem_limit_bytes=24 * 2**20)

    mine, theirs, item_emb = pl.pallas_call(
        functools.partial(first_kernel, shards, half, fanout),
        out_shape=spend_out + [pltpu.HBM((items, camps, width), camp_emb.dtype)],
        in_specs=[SMEM] * 4 + [VMEM] * 3 + [HBM] * 3 + [ANY] * len(received),
        out_specs=[VMEM] * 2 + [HBM],
        scratch_shapes=work + spend_work + [pltpu.SemaphoreType.DMA],
        compiler_params=limits,
    )(where, cluster_size, item_of_slot, own_wanted, item_dual, item_live, item_scale, user_rows, user_scale,
      in_hbm(camp_emb), *received)
    item_emb = in_hbm(item_emb)
    got_one, other_one = exchange(mine, theirs)

    mine, theirs, next_dual = pl.pallas_call(
        functools.partial(second_kernel, fanout),
        out_shape=spend_out + [jax.ShapeDtypeStruct((items, camps), f32)],
        in_specs=[SMEM] * 2 + [VMEM] * 7 + [HBM] * 3,
        out_specs=[VMEM] * 3,
        scratch_shapes=work + spend_work,
        compiler_params=limits,
    )(where, cluster_size, item_dual, item_live, item_scale, item_limit, match, got_one, other_one, user_rows,
      user_scale, item_emb)
    got_two, other_two = exchange(mine, theirs)

    user_dual, own_dual = pl.pallas_call(
        functools.partial(third_kernel, fanout),
        out_shape=[
            jax.ShapeDtypeStruct((clusters, users), f32),
            jax.ShapeDtypeStruct((blocks, camps), f32),
        ],
        in_specs=[SMEM] * 2 + [VMEM] * 12 + [HBM] * 3,
        out_specs=[VMEM] * 2,
        scratch_shapes=work + [pltpu.VMEM((clusters, users // 128, 128), f32)],
        compiler_params=limits,
    )(where, cluster_size, next_dual, item_live, item_scale, item_limit, match, got_two, other_two, own_match,
      got_one, other_one, dual_init, spend_limit, user_rows, user_scale, item_emb)
    return (user_dual, own_dual)


def solution(mesh):
    return jax.shard_map(
        program,
        mesh=mesh,
        in_specs=(
            P("shard", "rep", None),
            P("shard", None),
            P("shard", None),
            P("shard"),
            P("shard", None, None),
            P("shard"),
            P("shard", None),
            P("shard", None),
        ),
        out_specs=(P("shard", "rep"), P("shard", None)),
        check_vma=False,
    )
```

profile of v0, /device:TPU:0, one launch (start us, length us, event | category | flops | bytes accessed | tf_op | source)
XLA Modules:
  0.0 220.5 jit_solution(3945477251434579495)
XLA Ops:
  3.6 8.3 %all-to-all-start = ((s32[16,1,72]{2,1,0:T(1,128)}), s32[16,1,72]{2,1,0:T(1,128)S(1)}, u32[]{:S(2)}, u32[]{:S(2)}) async-start(s32[16,1,72]{2,1,0:T(1,128)} %bitcast.2), calls=%async_computation | async-start | bytes 16384 | tf_op jit(solution)/shard_map/all_to_all | solution.py:298
  14.2 5.0 %all-to-all-done = s32[16,1,72]{2,1,0:T(1,128)S(1)} async-done(((s32[16,1,72]{2,1,0:T(1,128)}), s32[16,1,72]{2,1,0:T(1,128)S(1)}, u32[]{:S(2)}, u32[]{:S(2)}) %all-to-all-start) | async-done | bytes 4640 | tf_op jit(solution)/shard_map/all_to_all | solution.py:298
  19.2 5.2 %shard_map.95 = (bf16[4,128,256]{2,1,0:T(8,128)(2,1)S(1)}, bf16[4,128,256]{2,1,0:T(8,128)(2,1)S(1)}, bf16[4,128,256]{2,1,0:T(8,128)(2,1)S(1)}, bf16[4,128,256]{2...) custom-call(s32[2]{0:T(128)S(1)} %pad_add_fusion.1.where_ref, ...), custom_call_target="tpu_custom_call" | custom-call | bytes 8388608 | tf_op jit(solution)/shard_map/pallas_call | solution.py:301
  28.6 2.7 %collective-permute-start.4 = (bf16[4,128,256]{2,1,0:T(8,128)(2,1)S(1)}, bf16[4,128,256]{2,1,0:T(8,128)(2,1)S(1)}, u32[]{:S(2)}, u32[]{:S(2)}) collective-permute-start(bf16[4,128,256]{2,1,0:T(8,128)(2,1)S(1)} %get-tuple-element.45), channel_id=1, source_target_pairs={{0,4},{2,6},{4,0},{6,2},{8,12},{10,14},{12,8},{14,10},{16,20},{18,... | collective-permute-start | bytes 786440 | tf_op jit(solution)/shard_map/ppermute | solution.py:313
  32.4 9.0 %collective-permute-done.1.rest_0_ = bf16[4,128,256]{2,1,0:T(8,128)(2,1)S(1)} collective-permute-done((bf16[4,128,256]{2,1,0:T(8,128)(2,1)S(1)}, bf16[4,128,256]{2,1,0:T(8,128)(2,1)S(1)}, u32[]{:S(2)}, u32[]{:S(2)}) %collective-permute-start.1) | collective-permute-done | bytes 262176 | tf_op jit(solution)/shard_map/ppermute | solution.py:313
  41.3 5.6 %multiply_reduce_fusion = f32[128,128]{1,0:T(8,128)S(1)} fusion(bf16[128,128,256]{2,1,0:T(8,128)(2,1)} %camp_ref.3), kind=kLoop, calls=%fused_computation.2 | loop fusion | flops 12566528 | bytes 8454144 | tf_op jit(solution)/shard_map/reduce_sum | solution.py:330
  47.1 2.4 %collective-permute-start.12 = (bf16[4,128,256]{2,1,0:T(8,128)(2,1)}, bf16[4,128,256]{2,1,0:T(8,128)(2,1)S(1)}, u32[]{:S(2)}, u32[]{:S(2)}) collective-permute-start(bf16[4,128,256]{2,1,0:T(8,128)(2,1)} %get-tuple-element.49), channel_id=1, source_target_pairs={{0,12},{2,14},{4,8},{6,10},{8,4},{10,6},{12,0},{14,2},{16,28},{18,... | collective-permute-start | bytes 786440 | tf_op jit(solution)/shard_map/ppermute | solution.py:313
  50.8 5.8 %collective-permute-start.16 = (bf16[4,128,256]{2,1,0:T(8,128)(2,1)}, bf16[4,128,256]{2,1,0:T(8,128)(2,1)S(1)}, u32[]{:S(2)}, u32[]{:S(2)}) collective-permute-start(bf16[4,128,256]{2,1,0:T(8,128)(2,1)} %get-tuple-element.51), channel_id=1, source_target_pairs={{0,16},{2,18},{4,20},{6,22},{8,24},{10,26},{12,28},{14,30},{16,0},... | collective-permute-start | bytes 786440 | tf_op jit(solution)/shard_map/ppermute | solution.py:313
  57.2 2.1 collective-permute-start.20
  60.8 3.7 %collective-permute-start.22 = (bf16[4,128,256]{2,1,0:T(8,128)(2,1)}, bf16[4,128,256]{2,1,0:T(8,128)(2,1)S(1)}, u32[]{:S(2)}, u32[]{:S(2)}) collective-permute-start(bf16[4,128,256]{2,1,0:T(8,128)(2,1)} %get-tuple-element.54), channel_id=1, source_target_pairs={{0,22},{2,20},{4,18},{6,16},{8,30},{10,28},{12,26},{14,24},{16,6},... | collective-permute-start | bytes 786440 | tf_op jit(solution)/shard_map/ppermute | solution.py:313
  64.5 4.3 %collective-permute-done.14.rest_12_ = bf16[4,128,256]{2,1,0:T(8,128)(2,1)S(1)} collective-permute-done((bf16[4,128,256]{2,1,0:T(8,128)(2,1)S(1)}, bf16[4,128,256]{2,1,0:T(8,128)(2,1)S(1)}, u32[]{:S(2)}, u32[]{:S(2)}) %collective-permute-start.14) | collective-permute-done | bytes 262176 | tf_op jit(solution)/shard_map/ppermute | solution.py:313
  68.8 3.5 %collective-permute-start.24 = (bf16[4,128,256]{2,1,0:T(8,128)(2,1)}, bf16[4,128,256]{2,1,0:T(8,128)(2,1)S(1)}, u32[]{:S(2)}, u32[]{:S(2)}) collective-permute-start(bf16[4,128,256]{2,1,0:T(8,128)(2,1)} %copy-done.11), channel_id=1, source_target_pairs={{0,24},{2,26},{4,28},{6,30},{8,16},{10,18},{12,20},{14,22},{16,8},... | collective-permute-start | bytes 786440 | tf_op jit(solution)/shard_map/ppermute | solution.py:313
  72.3 24.9 %collective-permute-done.16.rest_14_ = bf16[4,128,256]{2,1,0:T(8,128)(2,1)S(1)} collective-permute-done((bf16[4,128,256]{2,1,0:T(8,128)(2,1)}, bf16[4,128,256]{2,1,0:T(8,128)(2,1)S(1)}, u32[]{:S(2)}, u32[]{:S(2)}) %collective-permute-start.16) | collective-permute-done | bytes 262176 | tf_op jit(solution)/shard_map/ppermute | solution.py:313
  97.2 9.0 %collective-permute-start.26 = (bf16[4,128,256]{2,1,0:T(8,128)(2,1)}, bf16[4,128,256]{2,1,0:T(8,128)(2,1)}, u32[]{:S(2)}, u32[]{:S(2)}) collective-permute-start(bf16[4,128,256]{2,1,0:T(8,128)(2,1)} %copy-done.10), channel_id=1, source_target_pairs={{0,26},{2,24},{4,30},{6,28},{8,18},{10,16},{12,22},{14,20},{16,10}... | collective-permute-start | bytes 786440 | tf_op jit(solution)/shard_map/ppermute | solution.py:313
  107.4 1.4 eq.128
  108.7 1.4 eq.131
  110.1 1.8 gather_fusion
  112.6 10.1 %all-to-all-start.1 = ((f32[16,4,512]{2,1,0:T(4,128)}), f32[16,4,512]{2,1,0:T(4,128)}, u32[]{:S(2)}, u32[]{:S(2)}) async-start(f32[16,4,512]{2,1,0:T(4,128)} %reshape.374), calls=%async_computation.1 | async-start | bytes 262144 | tf_op jit(solution)/shard_map/all_to_all | solution.py:334
  122.8 1.5 broadcast_compare_fusion.1
  126.1 12.9 %all-to-all-done.1 = f32[16,4,512]{2,1,0:T(4,128)} async-done(((f32[16,4,512]{2,1,0:T(4,128)}), f32[16,4,512]{2,1,0:T(4,128)}, u32[]{:S(2)}, u32[]{:S(2)}) %all-to-all-start.1) | async-done | bytes 131104 | tf_op jit(solution)/shard_map/all_to_all | solution.py:334
  139.1 2.2 copy-done
  141.3 2.6 %shard_map.96.scale_hbm = f32[16,512,128]{2,1,0:T(8,128)S(1)} custom-call(bf16[16,512,256]{2,1,0:T(8,128)(2,1)S(1)} %copy-done), custom_call_target="tpu_custom_call" | custom-call | flops 8388608 | bytes 8388608 | tf_op jit(solution)/shard_map/pallas_call | solution.py:342
  143.9 2.0 copy-done.1
  147.5 1.7 pad_maximum_fusion.1
  149.2 1.8 reshape.375
  151.0 2.5 %gather_fusion.1 = f32[64,512]{1,0:T(8,128)} fusion(f32[128,512]{1,0:T(8,128)} %reshape.375, s32[1024]{0:T(1024)} %pad_clamp_fusion), kind=kCustom, calls=%fused_computation.1 | custom fusion | bytes 262400 | tf_op jit(solution)/shard_map/jit(_take)/gather | solution.py:338
  158.3 15.0 %shard_map.97 = (f32[32,128]{1,0:T(8,128)S(1)}, f32[32,128]{1,0:T(8,128)S(1)}, bf16[64,128,256]{2,1,0:T(8,128)(2,1)}) custom-call(s32[2]{0:T(128)S(1)} %pad_add_fusion.1.where_ref, s32[16]{0:T(128)S(1)} %copy-done.8, s32[128]{0:T(128)S(1)} %broadcast_add_fusion.item_at_ref, s32[8]{0:T(128)S(1)} %fusion.3.own_ref, f32[64,128]{1,0:T(8,128)S(1)} %get-tuple-element.39.duals_ref, ...), custom_call_target="tpu_custom_call" | custom-call | tf_op jit(solution)/shard_map/pallas_call | solution.py:392
  174.6 11.1 %all_to_all.26 = bf16[16,32,128]{2,1,0:T(8,128)(2,1)S(1)} all-to-all(bf16[16,32,128]{2,1,0:T(8,128)(2,1)S(1)} %broadcast_in_dim.61), channel_id=1, replica_groups=mesh['shard'=16,'rep'=2] {'shard'}, dimensions={0} | all-to-all | bytes 262144 | tf_op jit(solution)/shard_map/all_to_all | solution.py:374
  185.7 1.3 collective-permute-done.32.other_ref.other_one_ref
  187.1 10.2 %shard_map.98 = (f32[32,128]{1,0:T(8,128)S(1)}, f32[32,128]{1,0:T(8,128)S(1)}, f32[64,128]{1,0:T(8,128)S(1)}) custom-call(s32[2]{0:T(128)S(1)} %pad_add_fusion.1.where_ref, s32[16]{0:T(128)S(1)} %copy-done.8, f32[64,128]{1,0:T(8,128)S(1)} %get-tuple-element.39.duals_ref, f32[64,128]{1,0:T(8,128)S(1)} %get-tuple-element.40.live_ref, ...), custom_call_target="tpu_custom_call" | custom-call | tf_op jit(solution)/shard_map/pallas_call | solution.py:404
  198.5 10.7 %all_to_all.27 = bf16[16,32,128]{2,1,0:T(8,128)(2,1)S(1)} all-to-all(bf16[16,32,128]{2,1,0:T(8,128)(2,1)S(1)} %broadcast_in_dim.62), channel_id=1, replica_groups=mesh['shard'=16,'rep'=2] {'shard'}, dimensions={0} | all-to-all | bytes 262144 | tf_op jit(solution)/shard_map/all_to_all | solution.py:374
  210.6 9.9 %shard_map.99 = (f32[16,512]{1,0:T(8,128)}, f32[128,128]{1,0:T(8,128)}) custom-call(s32[2]{0:T(128)S(1)} %pad_add_fusion.1.where_ref, s32[16]{0:T(128)S(1)} %copy-done.8, f32[64,128]{1,0:T(8,128)S(1)} %get-tuple-element.62.duals_ref, f32[64,128]{1,0:T(8,128)S(1)} %get-tuple-element.40.live_ref, f32[64,128]{1,0:T(8,128)S(1)} %get-tuple-element.41.item_scale_ref, ...), custom_call_target="tpu_custom_call" | custom-call | tf_op jit(solution)/shard_map/pallas_call | solution.py:415
  (128 shorter events, 28.2 us)
Async XLA Ops:
  3.6 15.6 %all-to-all-start = ((s32[16,1,72]{2,1,0:T(1,128)}), s32[16,1,72]{2,1,0:T(1,128)S(1)}, u32[]{:S(2)}, u32[]{:S(2)}) async-start(s32[16,1,72]{2,1,0:T(1,128)} %bitcast.2), calls=%async_computation | async-start | bytes 16384 | tf_op jit(solution)/shard_map/all_to_all | solution.py:298
  26.5 14.8 %collective-permute-start.1 = (bf16[4,128,256]{2,1,0:T(8,128)(2,1)S(1)}, bf16[4,128,256]{2,1,0:T(8,128)(2,1)S(1)}, u32[]{:S(2)}, u32[]{:S(2)}) collective-permute-start(bf16[4,128,256]{2,1,0:T(8,128)(2,1)S(1)} %get-tuple-element.35), channel_id=1, source_target_pairs={{0,2},{2,0},{4,6},{6,4},{8,10},{10,8},{12,14},{14,12},{16,18},{18,... | collective-permute-start | bytes 786440 | tf_op jit(solution)/shard_map/ppermute | solution.py:313
  28.2 18.9 %collective-permute-start = (bf16[4,128,256]{2,1,0:T(8,128)(2,1)S(1)}, bf16[4,128,256]{2,1,0:T(8,128)(2,1)S(1)}, u32[]{:S(2)}, u32[]{:S(2)}) collective-permute-start(bf16[4,128,256]{2,1,0:T(8,128)(2,1)S(1)} %get-tuple-element.34), channel_id=1, source_target_pairs={{0,30},{2,28},{4,26},{6,24},{8,22},{10,20},{12,18},{14,16},{16,14}... | collective-permute-start | bytes 786440 | tf_op jit(solution)/shard_map/ppermute | solution.py:313
  28.6 20.9 %collective-permute-start.4 = (bf16[4,128,256]{2,1,0:T(8,128)(2,1)S(1)}, bf16[4,128,256]{2,1,0:T(8,128)(2,1)S(1)}, u32[]{:S(2)}, u32[]{:S(2)}) collective-permute-start(bf16[4,128,256]{2,1,0:T(8,128)(2,1)S(1)} %get-tuple-element.45), channel_id=1, source_target_pairs={{0,4},{2,6},{4,0},{6,2},{8,12},{10,14},{12,8},{14,10},{16,20},{18,... | collective-permute-start | bytes 786440 | tf_op jit(solution)/shard_map/ppermute | solution.py:313
  31.2 19.6 %collective-permute-start.6 = (bf16[4,128,256]{2,1,0:T(8,128)(2,1)S(1)}, bf16[4,128,256]{2,1,0:T(8,128)(2,1)S(1)}, u32[]{:S(2)}, u32[]{:S(2)}) collective-permute-start(bf16[4,128,256]{2,1,0:T(8,128)(2,1)S(1)} %get-tuple-element.46), channel_id=1, source_target_pairs={{0,6},{2,4},{4,2},{6,0},{8,14},{10,12},{12,10},{14,8},{16,22},{18,... | collective-permute-start | bytes 786440 | tf_op jit(solution)/shard_map/ppermute | solution.py:313
  31.2 25.3 %collective-permute-start.8 = (bf16[4,128,256]{2,1,0:T(8,128)(2,1)S(1)}, bf16[4,128,256]{2,1,0:T(8,128)(2,1)S(1)}, u32[]{:S(2)}, u32[]{:S(2)}) collective-permute-start(bf16[4,128,256]{2,1,0:T(8,128)(2,1)S(1)} %get-tuple-element.47), channel_id=1, source_target_pairs={{0,8},{2,10},{4,12},{6,14},{8,0},{10,2},{12,4},{14,6},{16,24},{18,... | collective-permute-start | bytes 786440 | tf_op jit(solution)/shard_map/ppermute | solution.py:313
  41.3 15.9 %collective-permute-start.10 = (bf16[4,128,256]{2,1,0:T(8,128)(2,1)S(1)}, bf16[4,128,256]{2,1,0:T(8,128)(2,1)S(1)}, u32[]{:S(2)}, u32[]{:S(2)}) collective-permute-start(bf16[4,128,256]{2,1,0:T(8,128)(2,1)S(1)} %get-tuple-element.48), channel_id=1, source_target_pairs={{0,10},{2,8},{4,14},{6,12},{8,2},{10,0},{12,6},{14,4},{16,26},{18,... | collective-permute-start | bytes 786440 | tf_op jit(solution)/shard_map/ppermute | solution.py:313
  47.1 13.7 %collective-permute-start.12 = (bf16[4,128,256]{2,1,0:T(8,128)(2,1)}, bf16[4,128,256]{2,1,0:T(8,128)(2,1)S(1)}, u32[]{:S(2)}, u32[]{:S(2)}) collective-permute-start(bf16[4,128,256]{2,1,0:T(8,128)(2,1)} %get-tuple-element.49), channel_id=1, source_target_pairs={{0,12},{2,14},{4,8},{6,10},{8,4},{10,6},{12,0},{14,2},{16,28},{18,... | collective-permute-start | bytes 786440 | tf_op jit(solution)/shard_map/ppermute | solution.py:313
  49.4 19.4 %collective-permute-start.14 = (bf16[4,128,256]{2,1,0:T(8,128)(2,1)S(1)}, bf16[4,128,256]{2,1,0:T(8,128)(2,1)S(1)}, u32[]{:S(2)}, u32[]{:S(2)}) collective-permute-start(bf16[4,128,256]{2,1,0:T(8,128)(2,1)S(1)} %get-tuple-element.50), channel_id=1, source_target_pairs={{0,14},{2,12},{4,10},{6,8},{8,6},{10,4},{12,2},{14,0},{16,30},{18,... | collective-permute-start | bytes 786440 | tf_op jit(solution)/shard_map/ppermute | solution.py:313
  50.8 46.5 %collective-permute-start.16 = (bf16[4,128,256]{2,1,0:T(8,128)(2,1)}, bf16[4,128,256]{2,1,0:T(8,128)(2,1)S(1)}, u32[]{:S(2)}, u32[]{:S(2)}) collective-permute-start(bf16[4,128,256]{2,1,0:T(8,128)(2,1)} %get-tuple-element.51), channel_id=1, source_target_pairs={{0,16},{2,18},{4,20},{6,22},{8,24},{10,26},{12,28},{14,30},{16,0},... | collective-permute-start | bytes 786440 | tf_op jit(solution)/shard_map/ppermute | solution.py:313
  56.5 49.7 %collective-permute-start.18 = (bf16[4,128,256]{2,1,0:T(8,128)(2,1)}, bf16[4,128,256]{2,1,0:T(8,128)(2,1)S(1)}, u32[]{:S(2)}, u32[]{:S(2)}) collective-permute-start(bf16[4,128,256]{2,1,0:T(8,128)(2,1)} %get-tuple-element.52), channel_id=1, source_target_pairs={{0,18},{2,16},{4,22},{6,20},{8,26},{10,24},{12,30},{14,28},{16,2},... | collective-permute-start | bytes 786440 | tf_op jit(solution)/shard_map/ppermute | solution.py:313
  57.2 65.5 %collective-permute-start.20 = (bf16[4,128,256]{2,1,0:T(8,128)(2,1)}, bf16[4,128,256]{2,1,0:T(8,128)(2,1)S(1)}, u32[]{:S(2)}, u32[]{:S(2)}) collective-permute-start(bf16[4,128,256]{2,1,0:T(8,128)(2,1)} %get-tuple-element.53), channel_id=1, source_target_pairs={{0,20},{2,22},{4,16},{6,18},{8,28},{10,30},{12,24},{14,26},{16,4},... | collective-permute-start | bytes 786440 | tf_op jit(solution)/shard_map/ppermute | solution.py:313
  60.8 63.5 %collective-permute-start.22 = (bf16[4,128,256]{2,1,0:T(8,128)(2,1)}, bf16[4,128,256]{2,1,0:T(8,128)(2,1)S(1)}, u32[]{:S(2)}, u32[]{:S(2)}) collective-permute-start(bf16[4,128,256]{2,1,0:T(8,128)(2,1)} %get-tuple-element.54), channel_id=1, source_target_pairs={{0,22},{2,20},{4,18},{6,16},{8,30},{10,28},{12,26},{14,24},{16,6},... | collective-permute-start | bytes 786440 | tf_op jit(solution)/shard_map/ppermute | solution.py:313
  68.8 55.9 %collective-permute-start.24 = (bf16[4,128,256]{2,1,0:T(8,128)(2,1)}, bf16[4,128,256]{2,1,0:T(8,128)(2,1)S(1)}, u32[]{:S(2)}, u32[]{:S(2)}) collective-permute-start(bf16[4,128,256]{2,1,0:T(8,128)(2,1)} %copy-done.11), channel_id=1, source_target_pairs={{0,24},{2,26},{4,28},{6,30},{8,16},{10,18},{12,20},{14,22},{16,8},... | collective-permute-start | bytes 786440 | tf_op jit(solution)/shard_map/ppermute | solution.py:313
  97.2 27.6 %collective-permute-start.26 = (bf16[4,128,256]{2,1,0:T(8,128)(2,1)}, bf16[4,128,256]{2,1,0:T(8,128)(2,1)}, u32[]{:S(2)}, u32[]{:S(2)}) collective-permute-start(bf16[4,128,256]{2,1,0:T(8,128)(2,1)} %copy-done.10), channel_id=1, source_target_pairs={{0,26},{2,24},{4,30},{6,28},{8,18},{10,16},{12,22},{14,20},{16,10}... | collective-permute-start | bytes 786440 | tf_op jit(solution)/shard_map/ppermute | solution.py:313
  106.2 19.0 %collective-permute-start.28 = (bf16[4,128,256]{2,1,0:T(8,128)(2,1)}, bf16[4,128,256]{2,1,0:T(8,128)(2,1)}, u32[]{:S(2)}, u32[]{:S(2)}) collective-permute-start(bf16[4,128,256]{2,1,0:T(8,128)(2,1)} %copy-done.9), channel_id=1, source_target_pairs={{0,28},{2,30},{4,24},{6,26},{8,20},{10,22},{12,16},{14,18},{16,12}... | collective-permute-start | bytes 786440 | tf_op jit(solution)/shard_map/ppermute | solution.py:313
  112.6 26.4 %all-to-all-start.1 = ((f32[16,4,512]{2,1,0:T(4,128)}), f32[16,4,512]{2,1,0:T(4,128)}, u32[]{:S(2)}, u32[]{:S(2)}) async-start(f32[16,4,512]{2,1,0:T(4,128)} %reshape.374), calls=%async_computation.1 | async-start | bytes 262144 | tf_op jit(solution)/shard_map/all_to_all | solution.py:334
  122.7 16.3 %collective-permute-start.3 = (bf16[4,128,256]{2,1,0:T(8,128)(2,1)S(1)}, bf16[4,128,256]{2,1,0:T(8,128)(2,1)}, u32[]{:S(2)}, u32[]{:S(2)}) collective-permute-start(bf16[4,128,256]{2,1,0:T(8,128)(2,1)S(1)} %collective-permute-done.1.rest_0_), channel_id=1, source_target_pairs={{0,1},{1,0},{2,3},{3,2},{4,5},{5,4},{6,7},{7,6},{8,9},{9,8},{10,11... | collective-permute-start | bytes 786440 | tf_op jit(solution)/shard_map/ppermute | solution.py:368
  124.2 21.7 %collective-permute-start.5 = (bf16[4,128,256]{2,1,0:T(8,128)(2,1)S(1)}, bf16[4,128,256]{2,1,0:T(8,128)(2,1)}, u32[]{:S(2)}, u32[]{:S(2)}) collective-permute-start(bf16[4,128,256]{2,1,0:T(8,128)(2,1)S(1)} %collective-permute-done.4.rest_2_), channel_id=1, source_target_pairs={{0,1},{1,0},{2,3},{3,2},{4,5},{5,4},{6,7},{7,6},{8,9},{9,8},{10,11... | collective-permute-start | bytes 786440 | tf_op jit(solution)/shard_map/ppermute | solution.py:368
  124.7 21.7 %collective-permute-start.7 = (bf16[4,128,256]{2,1,0:T(8,128)(2,1)S(1)}, bf16[4,128,256]{2,1,0:T(8,128)(2,1)}, u32[]{:S(2)}, u32[]{:S(2)}) collective-permute-start(bf16[4,128,256]{2,1,0:T(8,128)(2,1)S(1)} %collective-permute-done.6.rest_4_), channel_id=1, source_target_pairs={{0,1},{1,0},{2,3},{3,2},{4,5},{5,4},{6,7},{7,6},{8,9},{9,8},{10,11... | collective-permute-start | bytes 786440 | tf_op jit(solution)/shard_map/ppermute | solution.py:368
  124.8 21.7 %collective-permute-start.9 = (bf16[4,128,256]{2,1,0:T(8,128)(2,1)S(1)}, bf16[4,128,256]{2,1,0:T(8,128)(2,1)}, u32[]{:S(2)}, u32[]{:S(2)}) collective-permute-start(bf16[4,128,256]{2,1,0:T(8,128)(2,1)S(1)} %collective-permute-done.8.rest_6_), channel_id=1, source_target_pairs={{0,1},{1,0},{2,3},{3,2},{4,5},{5,4},{6,7},{7,6},{8,9},{9,8},{10,11... | collective-permute-start | bytes 786440 | tf_op jit(solution)/shard_map/ppermute | solution.py:368
  125.3 21.7 %collective-permute-start.11 = (bf16[4,128,256]{2,1,0:T(8,128)(2,1)S(1)}, bf16[4,128,256]{2,1,0:T(8,128)(2,1)}, u32[]{:S(2)}, u32[]{:S(2)}) collective-permute-start(bf16[4,128,256]{2,1,0:T(8,128)(2,1)S(1)} %collective-permute-done.10.rest_8_), channel_id=1, source_target_pairs={{0,1},{1,0},{2,3},{3,2},{4,5},{5,4},{6,7},{7,6},{8,9},{9,8},{10,11... | collective-permute-start | bytes 786440 | tf_op jit(solution)/shard_map/ppermute | solution.py:368
  139.0 8.0 %collective-permute-start.2 = (f32[16,4,512]{2,1,0:T(4,128)}, f32[16,4,512]{2,1,0:T(4,128)S(1)}, u32[]{:S(2)}, u32[]{:S(2)}) collective-permute-start(f32[16,4,512]{2,1,0:T(4,128)} %all-to-all-done.1), channel_id=1, source_target_pairs={{0,1},{1,0},{2,3},{3,2},{4,5},{5,4},{6,7},{7,6},{8,9},{9,8},{10,11... | collective-permute-start | bytes 393224 | tf_op jit(solution)/shard_map/ppermute | solution.py:335
  145.9 8.3 %collective-permute-start.13 = (bf16[4,128,256]{2,1,0:T(8,128)(2,1)S(1)}, bf16[4,128,256]{2,1,0:T(8,128)(2,1)}, u32[]{:S(2)}, u32[]{:S(2)}) collective-permute-start(bf16[4,128,256]{2,1,0:T(8,128)(2,1)S(1)} %collective-permute-done.12.rest_10_), channel_id=1, source_target_pairs={{0,1},{1,0},{2,3},{3,2},{4,5},{5,4},{6,7},{7,6},{8,9},{9,8},{10,11... | collective-permute-start | bytes 786440 | tf_op jit(solution)/shard_map/ppermute | solution.py:368
  146.5 7.9 %collective-permute-start.15 = (bf16[4,128,256]{2,1,0:T(8,128)(2,1)S(1)}, bf16[4,128,256]{2,1,0:T(8,128)(2,1)}, u32[]{:S(2)}, u32[]{:S(2)}) collective-permute-start(bf16[4,128,256]{2,1,0:T(8,128)(2,1)S(1)} %collective-permute-done.14.rest_12_), channel_id=1, source_target_pairs={{0,1},{1,0},{2,3},{3,2},{4,5},{5,4},{6,7},{7,6},{8,9},{9,8},{10,11... | collective-permute-start | bytes 786440 | tf_op jit(solution)/shard_map/ppermute | solution.py:368
  146.5 8.3 %collective-permute-start.17 = (bf16[4,128,256]{2,1,0:T(8,128)(2,1)S(1)}, bf16[4,128,256]{2,1,0:T(8,128)(2,1)}, u32[]{:S(2)}, u32[]{:S(2)}) collective-permute-start(bf16[4,128,256]{2,1,0:T(8,128)(2,1)S(1)} %collective-permute-done.16.rest_14_), channel_id=1, source_target_pairs={{0,1},{1,0},{2,3},{3,2},{4,5},{5,4},{6,7},{7,6},{8,9},{9,8},{10,11... | collective-permute-start | bytes 786440 | tf_op jit(solution)/shard_map/ppermute | solution.py:368
  147.0 7.9 %collective-permute-start.19 = (bf16[4,128,256]{2,1,0:T(8,128)(2,1)S(1)}, bf16[4,128,256]{2,1,0:T(8,128)(2,1)}, u32[]{:S(2)}, u32[]{:S(2)}) collective-permute-start(bf16[4,128,256]{2,1,0:T(8,128)(2,1)S(1)} %collective-permute-done.18.rest_16_), channel_id=1, source_target_pairs={{0,1},{1,0},{2,3},{3,2},{4,5},{5,4},{6,7},{7,6},{8,9},{9,8},{10,11... | collective-permute-start | bytes 786440 | tf_op jit(solution)/shard_map/ppermute | solution.py:368
  147.1 8.3 %collective-permute-start.21 = (bf16[4,128,256]{2,1,0:T(8,128)(2,1)S(1)}, bf16[4,128,256]{2,1,0:T(8,128)(2,1)}, u32[]{:S(2)}, u32[]{:S(2)}) collective-permute-start(bf16[4,128,256]{2,1,0:T(8,128)(2,1)S(1)} %collective-permute-done.20.rest_18_), channel_id=1, source_target_pairs={{0,1},{1,0},{2,3},{3,2},{4,5},{5,4},{6,7},{7,6},{8,9},{9,8},{10,11... | collective-permute-start | bytes 786440 | tf_op jit(solution)/shard_map/ppermute | solution.py:368
  154.2 1.9 collective-permute-start.23
  154.4 1.8 collective-permute-start.25
  154.9 2.1 collective-permute-start.29
  155.3 2.0 collective-permute-start.30
  (21 other events, 358.0 us)
where the time goes:
time: 221 us
  waiting for transfers between devices  62.5 us (28%)
  starting transfers between devices  55.4 us (25%)
  Pallas kernels  42.9 us (19%)
  blocking collectives  21.8 us (10%)
  local copies, waits for them, and re-layouts  20.9 us (9%)
  other arithmetic  16 us (7%)
    ppermute x15, waiting for transfers between devices, program(): lax.ppermute(sent[n], 'shard', [(i, i ^ n + 1) for i in range(shards)])  38.5 us
    ppermute x15, starting transfers between devices, program(): lax.ppermute(sent[n], 'shard', [(i, i ^ n + 1) for i in range(shards)])  32.8 us
    all_to_all x2, blocking collectives, exchange(): lax.all_to_all(spread, 'shard', split_axis=0, concat_axis=0, tiled=True)  21.8 us
    pallas_call x1, Pallas kernels, program(): pl.pallas_call(functools.partial(first_kernel, shards, half, fanout), out...  15 us
    all_to_all x1, waiting for transfers between devices, program(): lax.all_to_all(facts, 'shard', split_axis=0, concat_axis=0, tiled=True)  12.9 us
    pallas_call x1, Pallas kernels, program(): pl.pallas_call(functools.partial(second_kernel, fanout), out_shape=spend_...  10.2 us
    all_to_all x1, starting transfers between devices, program(): lax.all_to_all(facts, 'shard', split_axis=0, concat_axis=0, tiled=True)  10.1 us
    pallas_call x1, Pallas kernels, program(): pl.pallas_call(functools.partial(third_kernel, fanout), out_shape=[jax.Sh...  9.91 us
  transfers between devices with their start and end apart: 37, of which 14 were waited for; matrix products, arithmetic and copies ran while one was open for 12% of the time, Pallas kernels for 1%

commit v1 on v0

--- a/solution.py
+++ b/solution.py
@@ -37,17 +37,28 @@
     return first + list(range(1, top)) + far[top // 2 :]
 
 
-def gather_kernel(half, where_ref, asked_ref, camp_ref, *rest):
-    outs, sem = rest[:-1], rest[-1]
+def gather_kernel(half, shifts, where_ref, asked_ref, camp_ref, fact_ref, *rest):
+    outs, (stage, sem) = rest[:-2], rest[-2:]
     me, rep = where_ref[0], where_ref[1]
-    copies = []
-    for n, out in enumerate(outs):
+    camps = camp_ref.shape[1]
+    arriving, leaving = [], []
+    for n, (shift, out) in enumerate(zip(shifts, outs)):
         for j in range(half):
-            block = asked_ref[me ^ (n + 1), rep * half + j]
-            copies.append(pltpu.make_async_copy(camp_ref.at[block], out.at[j], sem.at[n * half + j]))
-    for copy in copies:
+            at = n * half + j
+            block = asked_ref[me ^ shift, rep * half + j]
+            for part, source, rows in (
+                (0, camp_ref, pl.ds(0, camps)),
+                (1, fact_ref, pl.ds(camps, fact_ref.shape[1])),
+            ):
+                copy = pltpu.make_async_copy(source.at[block], stage.at[at, rows], sem.at[part, at])
+                copy.start()
+                arriving.append(copy)
+            leaving.append(pltpu.make_async_copy(stage.at[at], out.at[j], sem.at[2, at]))
+    for at, copy in enumerate(leaving):
+        arriving[2 * at].wait()
+        arriving[2 * at + 1].wait()
         copy.start()
-    for copy in copies:
+    for copy in leaving:
         copy.wait()
 
 
@@ -84,24 +95,28 @@
     lax.fori_loop(0, item_ref.shape[0], start, 0)
 
 
+def item_landed(item, item_ref, item_sem):
+    pltpu.make_async_copy(item_ref.at[item], item_ref.at[item], item_sem.at[item]).wait()
+
+
 def sweep_users(
     user_hbm, scale_hbm, user_ref, scale_ref, item_ref, row_sem, item_sem, item_scale_ref, dual_scr,
     dots_a, dots_b, finish, fanout
 ):
     clusters, users, _ = user_ref.shape
-    camps = item_ref.shape[1]
+    camps = item_scale_ref.shape[1]
     width = item_ref.shape[2]
     rows = 64
 
     def landed(k):
         pltpu.make_async_copy(user_hbm.at[k], user_ref.at[k], row_sem.at[0, k]).wait()
         pltpu.make_async_copy(scale_hbm.at[k], scale_ref.at[k], row_sem.at[1, k]).wait()
-        for e in range(fanout):
-            item = k * fanout + e
-            pltpu.make_async_copy(item_ref.at[item], item_ref.at[item], item_sem.at[item]).wait()
+        if item_sem is not None:
+            for e in range(fanout):
+                item_landed(k * fanout + e, item_ref, item_sem)
 
     def multiply(k, dots):
-        blocks = item_ref[pl.ds(pl.multiple_of(k * fanout, fanout), fanout)].reshape(fanout * camps, width)
+        blocks = item_ref[pl.ds(pl.multiple_of(k * fanout, fanout), fanout), :camps].reshape(fanout * camps, width)
         dots[...] = lax.dot_general(
             user_ref[k], blocks, (((1,), (1,)), ((), ())), preferred_element_type=jnp.float32
         )
@@ -170,38 +185,68 @@
     theirs_ref[...] = spend_scr[pl.ds(pl.multiple_of((1 - rep) * count, count), count), :]
 
 
+def item_facts(item_ref, item_sem, dual_ref, limit_ref, live_ref, item_scale_ref):
+    items, camps = dual_ref.shape
+    width = item_ref.shape[2]
+    eye = lax.broadcasted_iota(jnp.int32, (camps, camps), 0) == lax.broadcasted_iota(jnp.int32, (camps, camps), 1)
+
+    def one(item, carry):
+        item_landed(item, item_ref, item_sem)
+        facts = item_ref[item, camps:, :camps].astype(jnp.float32)
+        dual_ref[pl.ds(item, 1), :] = facts[0:1] + facts[1:2] + facts[2:3]
+        limit_ref[pl.ds(item, 1), :] = facts[3:4] + facts[4:5] + facts[5:6]
+        live_ref[pl.ds(item, 1), :] = facts[6:7]
+        rows = item_ref[item, :camps].astype(jnp.float32)
+        total = jnp.broadcast_to(jnp.sum(rows * rows, axis=1, keepdims=True), (camps, camps))
+        total = jnp.sum(jnp.where(eye, total, 0.0), axis=0, keepdims=True)
+        item_scale_ref[pl.ds(item, 1), :] = lax.rsqrt(total * (1.0 / width) + epsilon)
+        return carry
+
+    lax.fori_loop(0, items, one, 0, unroll=4)
+
+
 def first_kernel(
-    shards, half, fanout, where_ref, size_ref, item_at_ref, own_ref, duals_ref, live_ref, item_scale_ref, user_hbm,
-    scale_hbm, camp_ref, *rest
+    shards, half, fanout, where_ref, size_ref, item_at_ref, own_ref, user_hbm, scale_hbm, camp_ref, fact_ref, *rest
 ):
-    received, (mine_ref, theirs_ref, item_out) = rest[: 2 * (shards - 1)], rest[2 * (shards - 1) :][:3]
+    received, outs = rest[: 2 * (shards - 1)], rest[2 * (shards - 1) :][:7]
+    mine_ref, theirs_ref, duals_ref, limit_ref, live_ref, item_scale_ref, item_out = outs
     user_ref, scale_ref, item_ref, row_sem, item_sem, dots_a, dots_b, dual_scr, spend_scr, out_sem = rest[-10:]
     cap = 2 * half
     rep = where_ref[1]
     users = user_ref.shape[1]
-
-    def fetch(slot, source):
+    camps = camp_ref.shape[1]
+
+    def fetch(slot, pairs):
         item = item_at_ref[slot]
 
         @pl.when(item >= 0)
         def _():
-            pltpu.make_async_copy(source, item_ref.at[item], item_sem.at[item]).start()
-
+            for source, rows in pairs:
+                pltpu.make_async_copy(source, item_ref.at[item, rows], item_sem.at[item]).start()
+
+    everything = pl.ds(0, item_ref.shape[1])
     for j in range(cap):
-        fetch(j, camp_ref.at[own_ref[j]])
+        fetch(
+            j,
+            [
+                (camp_ref.at[own_ref[j]], pl.ds(0, camps)),
+                (fact_ref.at[own_ref[j]], pl.ds(camps, fact_ref.shape[1])),
+            ],
+        )
     for n in range(shards - 1):
         for j in range(half):
-            fetch((n + 1) * cap + rep * half + j, received[2 * n].at[j])
-            fetch((n + 1) * cap + (1 - rep) * half + j, received[2 * n + 1].at[j])
+            fetch((n + 1) * cap + rep * half + j, [(received[2 * n].at[j], everything)])
+            fetch((n + 1) * cap + (1 - rep) * half + j, [(received[2 * n + 1].at[j], everything)])
     start_rows(user_hbm, scale_hbm, user_ref, scale_ref, row_sem)
+    item_facts(item_ref, item_sem, duals_ref, limit_ref, live_ref, item_scale_ref)
+    keep = pltpu.make_async_copy(item_ref, item_out, out_sem)
+    keep.start()
     dual_scr[...] = jnp.where(live_ref[...] > 0.5, duals_ref[...] * gain, masked)
     finish = spend_finish(where_ref, size_ref, users, fanout, spend_scr)
     sweep_users(
-        user_hbm, scale_hbm, user_ref, scale_ref, item_ref, row_sem, item_sem, item_scale_ref,
+        user_hbm, scale_hbm, user_ref, scale_ref, item_ref, row_sem, None, item_scale_ref,
         dual_scr, dots_a, dots_b, finish, fanout
     )
-    keep = pltpu.make_async_copy(item_ref, item_out, out_sem)
-    keep.start()
     halves(where_ref, spend_scr, mine_ref, theirs_ref)
     keep.wait()
 
@@ -298,22 +343,43 @@
     heard = lax.all_to_all(ask, "shard", split_axis=0, concat_axis=0, tiled=True)
     where = jnp.stack([me, rep])
 
-    sent = pl.pallas_call(
-        functools.partial(gather_kernel, half),
-        out_shape=[pltpu.VMEM((half, camps, width), camp_emb.dtype)] * (shards - 1),
-        in_specs=[SMEM, SMEM, HBM],
-        out_specs=[VMEM] * (shards - 1),
-        scratch_shapes=[pltpu.SemaphoreType.DMA(((shards - 1) * half,))],
-        compiler_params=pltpu.CompilerParams(vmem_limit_bytes=8 * 2**20),
-        cost_estimate=pl.CostEstimate(flops=0, bytes_accessed=8 * 2**20, transcendentals=0),
-    )(where, heard, in_hbm(camp_emb))
-
-    got_blocks = []
-    for n in range(shards - 1):
-        got_blocks.append(lax.ppermute(sent[n], "shard", [(i, i ^ (n + 1)) for i in range(shards)]))
-
-    heard, camp_late, user_late, _ = lax.optimization_barrier((heard, camp_emb, user_emb, got_blocks[0]))
-    incoming = lax.dynamic_slice_in_dim(heard[:, :cap], rep * half, half, 1)
+    def pieces(x):
+        out = []
+        for _ in range(3):
+            piece = lax.reduce_precision(x, exponent_bits=8, mantissa_bits=7)
+            out.append(piece)
+            x = x - piece
+        return out
+
+    live = (jnp.arange(camps, dtype=jnp.int32)[None, :] < camp_count[:, None]).astype(f32)
+    rows = pieces(dual_init) + pieces(spend_limit) + [live, jnp.zeros_like(live)]
+    facts = jnp.stack(rows, axis=1).astype(camp_emb.dtype)
+    facts = jnp.concatenate([facts, jnp.zeros_like(facts)], axis=2)
+    fact_rows = len(rows)
+    camp_rows, facts = in_hbm(camp_emb), in_hbm(facts)
+
+    order = send_order(shards)
+    sent = {}
+    for shifts in (order[:4], order[4:]):
+        outs = pl.pallas_call(
+            functools.partial(gather_kernel, half, shifts),
+            out_shape=[pltpu.HBM((half, camps + fact_rows, width), camp_emb.dtype)] * len(shifts),
+            in_specs=[SMEM, SMEM, HBM, HBM],
+            out_specs=[HBM] * len(shifts),
+            scratch_shapes=[
+                pltpu.VMEM((len(shifts) * half, camps + fact_rows, width), camp_emb.dtype),
+                pltpu.SemaphoreType.DMA((3, len(shifts) * half)),
+            ],
+            compiler_params=pltpu.CompilerParams(vmem_limit_bytes=8 * 2**20),
+            cost_estimate=pl.CostEstimate(flops=0, bytes_accessed=len(shifts) * 2**19, transcendentals=0),
+        )(where, heard, camp_rows, facts)
+        sent.update(zip(shifts, outs))
+
+    got_blocks = {}
+    for shift in order:
+        got_blocks[shift] = lax.ppermute(sent[shift], "shard", [(i, i ^ shift) for i in range(shards)])
+
+    heard, user_late, _ = lax.optimization_barrier((heard, user_emb, got_blocks[1]))
     all_names = heard[:, cap:]
     item_of_slot = (
         jnp.sum(
@@ -327,18 +393,6 @@
         - 1
     )
     own_wanted = lax.dynamic_slice_in_dim(wanted, me, 1, 0).reshape(cap)
-    camp_scale = lax.rsqrt(jnp.mean(jnp.square(camp_late.astype(f32)), axis=-1) + epsilon)
-    live = (jnp.arange(camps, dtype=jnp.int32)[None, :] < camp_count[:, None]).astype(f32)
-    table = jnp.concatenate([dual_init, spend_limit, camp_scale, live], axis=1)
-    facts = jnp.take(table, incoming.reshape(-1), axis=0, mode="clip").reshape(shards, half, 4 * camps)
-    facts = lax.all_to_all(facts, "shard", split_axis=0, concat_axis=0, tiled=True)
-    other_facts = lax.ppermute(facts, "rep", swap)
-    pair = jnp.stack([facts, other_facts]).reshape(reps * shards * half, 4 * camps)
-    spot = (rank // half ^ rep) * (shards * half) + owners * half + rank % half
-    item_facts = jnp.take(pair, spot, axis=0, mode="clip")
-    item_dual, item_limit, item_scale, item_live = (
-        item_facts[:, n * camps : (n + 1) * camps] for n in range(4)
-    )
     user_scale = pl.pallas_call(
         user_kernel,
         out_shape=jax.ShapeDtypeStruct((clusters, users, camps), f32),
@@ -347,7 +401,7 @@
         out_specs=pl.BlockSpec((1, users, camps), lambda k: (k, 0, 0)),
         compiler_params=pltpu.CompilerParams(vmem_limit_bytes=16 * 2**20),
         cost_estimate=pl.CostEstimate(flops=8 * 2**20, bytes_accessed=8 * 2**20, transcendentals=0),
-    )(user_late)
+    )(in_hbm(user_late))
 
     def columns(which):
         return lax.dynamic_slice_in_dim(all_names, which * part, part, 1).reshape(1, -1)
@@ -357,15 +411,13 @@
     match = jnp.stack([(names[:, None] == side).astype(jnp.bfloat16) for side in sides])
     own_match = jnp.stack([(own_names[:, None] == side).astype(jnp.bfloat16) for side in sides])
 
-    last = send_order(shards)[-1] - 1
-    (got_blocks[last], item_dual, item_limit, item_scale, item_live, user_scale, match, own_match) = (
-        lax.optimization_barrier(
-            (got_blocks[last], item_dual, item_limit, item_scale, item_live, user_scale, match, own_match)
-        )
+    last = order[-1]
+    got_blocks[last], item_of_slot, own_wanted, user_scale, match, own_match = lax.optimization_barrier(
+        (got_blocks[last], item_of_slot, own_wanted, user_scale, match, own_match)
     )
     received = []
-    for got in got_blocks:
-        received += [got, lax.ppermute(got, "rep", swap)]
+    for shift in range(1, shards):
+        received += [got_blocks[shift], lax.ppermute(got_blocks[shift], "rep", swap)]
     user_rows, user_scale = in_hbm(user_emb), in_hbm(user_scale)
 
     def exchange(mine, theirs):
@@ -379,7 +431,7 @@
     work = [
         pltpu.VMEM((clusters, users, width), user_emb.dtype),
         pltpu.VMEM((clusters, users, camps), f32),
-        pltpu.VMEM((items, camps, width), camp_emb.dtype),
+        pltpu.VMEM((items, camps + fact_rows, width), camp_emb.dtype),
         pltpu.SemaphoreType.DMA((2, clusters)),
         pltpu.SemaphoreType.DMA((items,)),
         pltpu.VMEM((users, fanout * camps), f32),
@@ -389,15 +441,16 @@
     spend_work = [pltpu.VMEM((items, camps), f32)]
     limits = pltpu.CompilerParams(vmem_limit_bytes=24 * 2**20)
 
-    mine, theirs, item_emb = pl.pallas_call(
+    mine, theirs, item_dual, item_limit, item_live, item_scale, item_emb = pl.pallas_call(
         functools.partial(first_kernel, shards, half, fanout),
-        out_shape=spend_out + [pltpu.HBM((items, camps, width), camp_emb.dtype)],
-        in_specs=[SMEM] * 4 + [VMEM] * 3 + [HBM] * 3 + [ANY] * len(received),
-        out_specs=[VMEM] * 2 + [HBM],
+        out_shape=spend_out
+        + [jax.ShapeDtypeStruct((items, camps), f32)] * 4
+        + [pltpu.HBM((items, camps + fact_rows, width), camp_emb.dtype)],
+        in_specs=[SMEM] * 4 + [HBM] * 4 + [ANY] * len(received),
+        out_specs=[VMEM] * 6 + [HBM],
         scratch_shapes=work + spend_work + [pltpu.SemaphoreType.DMA],
         compiler_params=limits,
-    )(where, cluster_size, item_of_slot, own_wanted, item_dual, item_live, item_scale, user_rows, user_scale,
-      in_hbm(camp_emb), *received)
+    )(where, cluster_size, item_of_slot, own_wanted, user_rows, user_scale, camp_rows, facts, *received)
     item_emb = in_hbm(item_emb)
     got_one, other_one = exchange(mine, theirs)
 

time: 221 us -> 221 us (level)
  waiting for transfers between devices: 62.5 us -> 82 us
  Pallas kernels: 42.9 us -> 59.7 us
  starting transfers between devices: 55.4 us -> 39.2 us
  local copies, waits for them, and re-layouts: 20.9 us -> 6.98 us
  other arithmetic: 16 us -> 3.34 us
  blocking collectives: 21.8 us -> 28.1 us
    ppermute x31 -> x30, waiting for transfers between devices: 39.8 us -> 74.6 us  [the longest x15 72.4 us: program(): lax.ppermute(sent[shift], 'shard', [(i, i ^ shift) for i in range(shards)])]
    all_to_all x1 -> x0, waiting for transfers between devices: 12.9 us -> none  [program(): lax.all_to_all(facts, 'shard', split_axis=0, concat_axis=0, tiled=True)]
    all_to_all x1 -> x0, starting transfers between devices: 10.1 us -> none  [program(): lax.all_to_all(facts, 'shard', split_axis=0, concat_axis=0, tiled=True)]
    pallas_call x1, Pallas kernels: 2.57 us -> 9.19 us  [program(): pl.pallas_call(user_kernel, out_shape=jax.ShapeDtypeStruct((clusters, use...]
    all_to_all x2, blocking collectives: 21.8 us -> 28.1 us  [exchange(): lax.all_to_all(spread, 'shard', split_axis=0, concat_axis=0, tiled=True)]
    ppermute x31 -> x30, starting transfers between devices: 36.7 us -> 30.6 us  [the longest x15 27.7 us: program(): lax.ppermute(sent[shift], 'shard', [(i, i ^ shift) for i in range(shards)])]
    pallas_call x1, Pallas kernels: 15 us -> 20.9 us  [program(): pl.pallas_call(functools.partial(first_kernel, shards, half, fanout), out...]
    reduce_sum x1 -> x0, other arithmetic: 5.62 us -> none  [program(): jnp.mean(jnp.square(camp_late.astype(f32)), axis=-1) + epsilon]
  transfers between devices with their start and end apart: 37 -> 35, of which waited for: 14 -> 21; matrix products, arithmetic and copies ran while one was open for 12% -> 2% of each run, Pallas kernels for 1% -> 7%
where the time goes in v1:
time: 221 us; the launch traced here: 220 us
  waiting for transfers between devices  82 us (37%)
  Pallas kernels  59.7 us (27%)
  starting transfers between devices  39.2 us (18%)
  blocking collectives  28.1 us (13%)
  local copies, waits for them, and re-layouts  6.98 us (3%)
  other arithmetic  3.34 us (2%)
    ppermute x15, waiting for transfers between devices, program(): lax.ppermute(sent[shift], 'shard', [(i, i ^ shift) for i in range(shards)])  72.4 us
    all_to_all x2, blocking collectives, exchange(): lax.all_to_all(spread, 'shard', split_axis=0, concat_axis=0, tiled=True)  28.1 us
    ppermute x15, starting transfers between devices, program(): lax.ppermute(sent[shift], 'shard', [(i, i ^ shift) for i in range(shards)])  27.7 us
    pallas_call x1, Pallas kernels, program(): pl.pallas_call(functools.partial(first_kernel, shards, half, fanout), out...  20.9 us
    pallas_call x1, Pallas kernels, program(): pl.pallas_call(functools.partial(second_kernel, fanout), out_shape=spend_...  10.3 us
    pallas_call x1, Pallas kernels, program(): pl.pallas_call(functools.partial(third_kernel, fanout), out_shape=[jax.Sh...  10 us
    pallas_call x2, Pallas kernels, program(): pl.pallas_call(functools.partial(gather_kernel, half, shifts), out_shape=...  9.29 us
    pallas_call x1, Pallas kernels, program(): pl.pallas_call(user_kernel, out_shape=jax.ShapeDtypeStruct((clusters, use...  9.19 us
  transfers between devices with their start and end apart: 35, of which 21 were waited for; matrix products, arithmetic and copies ran while one was open for 2% of the time, Pallas kernels for 7%

profile of v1, /device:TPU:0, one launch (start us, length us, event | category | flops | bytes accessed | tf_op | source)
XLA Modules:
  0.0 220.2 jit_solution(1378017322957828485)
XLA Ops:
  3.6 8.3 %all-to-all-start = ((s32[16,1,72]{2,1,0:T(1,128)}), s32[16,1,72]{2,1,0:T(1,128)S(1)}, u32[]{:S(2)}, u32[]{:S(2)}) async-start(s32[16,1,72]{2,1,0:T(1,128)} %bitcast.2), calls=%async_computation | async-start | bytes 16384 | tf_op jit(solution)/shard_map/all_to_all | solution.py:343
  16.6 2.5 %all-to-all-done = s32[16,1,72]{2,1,0:T(1,128)S(1)} async-done(((s32[16,1,72]{2,1,0:T(1,128)}), s32[16,1,72]{2,1,0:T(1,128)S(1)}, u32[]{:S(2)}, u32[]{:S(2)}) %all-to-all-start) | async-done | bytes 4640 | tf_op jit(solution)/shard_map/all_to_all | solution.py:343
  19.2 3.3 %shard_map.97 = (bf16[4,136,256]{2,1,0:T(8,128)(2,1)}, bf16[4,136,256]{2,1,0:T(8,128)(2,1)}, bf16[4,136,256]{2,1,0:T(8,128)(2,1)}, bf16[4,136,256]{2,1,0:T(8,128)(2,1)}) custom-call(s32[2]{0:T(128)S(1)} %pad_add_fusion.1.where_ref, s32[16,72]{1,0:T(8,128)S(1)} %bitcast.26, bf16[128,128,256]{2,1,0:T(8,128)(2,1)} %camp_ref.5, ...), custom_call_target="tpu_custom_call" | custom-call | bytes 2097152 | tf_op jit(solution)/shard_map/pallas_call | solution.py:364
  22.9 3.0 %collective-permute-start.17 = (bf16[4,136,256]{2,1,0:T(8,128)(2,1)}, bf16[4,136,256]{2,1,0:T(8,128)(2,1)S(1)}, u32[]{:S(2)}, u32[]{:S(2)}) collective-permute-start(bf16[4,136,256]{2,1,0:T(8,128)(2,1)} %get-tuple-element.49), channel_id=1, source_target_pairs={{0,18},{2,16},{4,22},{6,20},{8,26},{10,24},{12,30},{14,28},{16,2},... | collective-permute-start | bytes 835592 | tf_op jit(solution)/shard_map/ppermute | solution.py:380
  25.9 2.0 collective-permute-start.19
  27.9 2.3 %collective-permute-start.21 = (bf16[4,136,256]{2,1,0:T(8,128)(2,1)}, bf16[4,136,256]{2,1,0:T(8,128)(2,1)S(1)}, u32[]{:S(2)}, u32[]{:S(2)}) collective-permute-start(bf16[4,136,256]{2,1,0:T(8,128)(2,1)} %get-tuple-element.51), channel_id=1, source_target_pairs={{0,22},{2,20},{4,18},{6,16},{8,30},{10,28},{12,26},{14,24},{16,6},... | collective-permute-start | bytes 835592 | tf_op jit(solution)/shard_map/ppermute | solution.py:380
  30.2 6.0 %shard_map.95 = (bf16[4,136,256]{2,1,0:T(8,128)(2,1)}, bf16[4,136,256]{2,1,0:T(8,128)(2,1)}, bf16[4,136,256]{2,1,0:T(8,128)(2,1)}, bf16[4,136,256]{2,1,0:T(8,128...) custom-call(s32[2]{0:T(128)S(1)} %pad_add_fusion.1.where_ref, ...), custom_call_target="tpu_custom_call" | custom-call | bytes 5767168 | tf_op jit(solution)/shard_map/pallas_call | solution.py:364
  36.2 2.2 collective-permute-start
  38.3 23.3 %collective-permute-done.15.rest_14_ = bf16[4,136,256]{2,1,0:T(8,128)(2,1)S(1)} collective-permute-done((bf16[4,136,256]{2,1,0:T(8,128)(2,1)}, bf16[4,136,256]{2,1,0:T(8,128)(2,1)S(1)}, u32[]{:S(2)}, u32[]{:S(2)}) %collective-permute-start.15) | collective-permute-done | bytes 278560 | tf_op jit(solution)/shard_map/ppermute | solution.py:380
  62.3 5.4 %collective-permute-done.17.rest_16_ = bf16[4,136,256]{2,1,0:T(8,128)(2,1)S(1)} collective-permute-done((bf16[4,136,256]{2,1,0:T(8,128)(2,1)}, bf16[4,136,256]{2,1,0:T(8,128)(2,1)S(1)}, u32[]{:S(2)}, u32[]{:S(2)}) %collective-permute-start.17) | collective-permute-done | bytes 278560 | tf_op jit(solution)/shard_map/ppermute | solution.py:380
  67.7 1.7 collective-permute-start.3
  69.5 4.7 %collective-permute-done.19.rest_18_ = bf16[4,136,256]{2,1,0:T(8,128)(2,1)S(1)} collective-permute-done((bf16[4,136,256]{2,1,0:T(8,128)(2,1)}, bf16[4,136,256]{2,1,0:T(8,128)(2,1)S(1)}, u32[]{:S(2)}, u32[]{:S(2)}) %collective-permute-start.19) | collective-permute-done | bytes 278560 | tf_op jit(solution)/shard_map/ppermute | solution.py:380
  75.2 5.6 %collective-permute-done.21.rest_20_ = bf16[4,136,256]{2,1,0:T(8,128)(2,1)S(1)} collective-permute-done((bf16[4,136,256]{2,1,0:T(8,128)(2,1)}, bf16[4,136,256]{2,1,0:T(8,128)(2,1)S(1)}, u32[]{:S(2)}, u32[]{:S(2)}) %collective-permute-start.21) | collective-permute-done | bytes 278560 | tf_op jit(solution)/shard_map/ppermute | solution.py:380
  80.9 5.8 %collective-permute-start.9 = (bf16[4,136,256]{2,1,0:T(8,128)(2,1)}, bf16[4,136,256]{2,1,0:T(8,128)(2,1)S(1)}, u32[]{:S(2)}, u32[]{:S(2)}) collective-permute-start(bf16[4,136,256]{2,1,0:T(8,128)(2,1)} %get-tuple-element.45), channel_id=1, source_target_pairs={{0,10},{2,8},{4,14},{6,12},{8,2},{10,0},{12,6},{14,4},{16,26},{18,... | collective-permute-start | bytes 835592 | tf_op jit(solution)/shard_map/ppermute | solution.py:380
  87.2 3.6 %collective-permute-done.3.rest_2_ = bf16[4,136,256]{2,1,0:T(8,128)(2,1)S(1)} collective-permute-done((bf16[4,136,256]{2,1,0:T(8,128)(2,1)}, bf16[4,136,256]{2,1,0:T(8,128)(2,1)S(1)}, u32[]{:S(2)}, u32[]{:S(2)}) %collective-permute-start.3) | collective-permute-done | bytes 278560 | tf_op jit(solution)/shard_map/ppermute | solution.py:380
  90.9 3.6 %collective-permute-start.23 = (bf16[4,136,256]{2,1,0:T(8,128)(2,1)}, bf16[4,136,256]{2,1,0:T(8,128)(2,1)}, u32[]{:S(2)}, u32[]{:S(2)}) collective-permute-start(bf16[4,136,256]{2,1,0:T(8,128)(2,1)} %get-tuple-element.52), channel_id=1, source_target_pairs={{0,24},{2,26},{4,28},{6,30},{8,16},{10,18},{12,20},{14,22},{16,8},... | collective-permute-start | bytes 835592 | tf_op jit(solution)/shard_map/ppermute | solution.py:380
  94.4 1.4 collective-permute-start.25
  95.9 3.2 %collective-permute-start.27 = (bf16[4,136,256]{2,1,0:T(8,128)(2,1)}, bf16[4,136,256]{2,1,0:T(8,128)(2,1)}, u32[]{:S(2)}, u32[]{:S(2)}) collective-permute-start(bf16[4,136,256]{2,1,0:T(8,128)(2,1)} %get-tuple-element.54), channel_id=1, source_target_pairs={{0,28},{2,30},{4,24},{6,26},{8,20},{10,22},{12,16},{14,18},{16,12}... | collective-permute-start | bytes 835592 | tf_op jit(solution)/shard_map/ppermute | solution.py:380
  99.1 3.1 %collective-permute-done.11.rest_10_ = bf16[4,136,256]{2,1,0:T(8,128)(2,1)S(1)} collective-permute-done((bf16[4,136,256]{2,1,0:T(8,128)(2,1)}, bf16[4,136,256]{2,1,0:T(8,128)(2,1)S(1)}, u32[]{:S(2)}, u32[]{:S(2)}) %collective-permute-start.11) | collective-permute-done | bytes 278560 | tf_op jit(solution)/shard_map/ppermute | solution.py:380
  102.2 5.8 %collective-permute-done.13.rest_12_ = bf16[4,136,256]{2,1,0:T(8,128)(2,1)S(1)} collective-permute-done((bf16[4,136,256]{2,1,0:T(8,128)(2,1)}, bf16[4,136,256]{2,1,0:T(8,128)(2,1)S(1)}, u32[]{:S(2)}, u32[]{:S(2)}) %collective-permute-start.13) | collective-permute-done | bytes 278560 | tf_op jit(solution)/shard_map/ppermute | solution.py:380
  108.0 10.7 %collective-permute-done.23.rest_22_ = bf16[4,136,256]{2,1,0:T(8,128)(2,1)} collective-permute-done((bf16[4,136,256]{2,1,0:T(8,128)(2,1)}, bf16[4,136,256]{2,1,0:T(8,128)(2,1)}, u32[]{:S(2)}, u32[]{:S(2)}) %collective-permute-start.23) | collective-permute-done | bytes 278560 | tf_op jit(solution)/shard_map/ppermute | solution.py:380
  118.8 7.6 %collective-permute-done.25.rest_24_ = bf16[4,136,256]{2,1,0:T(8,128)(2,1)} collective-permute-done((bf16[4,136,256]{2,1,0:T(8,128)(2,1)}, bf16[4,136,256]{2,1,0:T(8,128)(2,1)}, u32[]{:S(2)}, u32[]{:S(2)}) %collective-permute-start.25) | collective-permute-done | bytes 278560 | tf_op jit(solution)/shard_map/ppermute | solution.py:380
  126.4 2.4 %collective-permute-done.27.rest_26_ = bf16[4,136,256]{2,1,0:T(8,128)(2,1)} collective-permute-done((bf16[4,136,256]{2,1,0:T(8,128)(2,1)}, bf16[4,136,256]{2,1,0:T(8,128)(2,1)}, u32[]{:S(2)}, u32[]{:S(2)}) %collective-permute-start.27) | collective-permute-done | bytes 278560 | tf_op jit(solution)/shard_map/ppermute | solution.py:380
  131.1 9.2 %shard_map.96.scale_hbm = f32[16,512,128]{2,1,0:T(8,128)S(1)} custom-call(bf16[16,512,256]{2,1,0:T(8,128)(2,1)} %user_hbm.5), custom_call_target="tpu_custom_call" | custom-call | flops 8388608 | bytes 8388608 | tf_op jit(solution)/shard_map/pallas_call | solution.py:396
  140.3 2.0 copy-done
  145.6 20.9 %shard_map.98 = (f32[32,128]{1,0:T(8,128)S(1)}, f32[32,128]{1,0:T(8,128)S(1)}, f32[64,128]{1,0:T(8,128)S(1)}, f32[64,128]{1,0:T(8,128)S(1)}, f32[64,128]{1,0:T(8...) custom-call(s32[2]{0:T(128)S(1)} %pad_add_fusion.1.where_ref, s32[16]{0:T(128)S(1)} %copy-done.3, ...), custom_call_target="tpu_custom_call" | custom-call | tf_op jit(solution)/shard_map/pallas_call | solution.py:444
  167.8 17.4 %all_to_all.21 = bf16[16,32,128]{2,1,0:T(8,128)(2,1)S(1)} all-to-all(bf16[16,32,128]{2,1,0:T(8,128)(2,1)S(1)} %broadcast_in_dim.31), channel_id=1, replica_groups=mesh['shard'=16,'rep'=2] {'shard'}, dimensions={0} | all-to-all | bytes 262144 | tf_op jit(solution)/shard_map/all_to_all | solution.py:426
  185.2 1.3 collective-permute-done.31.other_ref.other_one_ref
  186.6 10.3 %shard_map.99 = (f32[32,128]{1,0:T(8,128)S(1)}, f32[32,128]{1,0:T(8,128)S(1)}, f32[64,128]{1,0:T(8,128)S(1)}) custom-call(s32[2]{0:T(128)S(1)} %pad_add_fusion.1.where_ref, s32[16]{0:T(128)S(1)} %copy-done.3, f32[64,128]{1,0:T(8,128)S(1)} %get-tuple-element.56.duals_ref, f32[64,128]{1,0:T(8,128)S(1)} %get-tuple-element.57.live_ref, ...), custom_call_target="tpu_custom_call" | custom-call | tf_op jit(solution)/shard_map/pallas_call | solution.py:457
  198.1 10.7 %all_to_all.22 = bf16[16,32,128]{2,1,0:T(8,128)(2,1)S(1)} all-to-all(bf16[16,32,128]{2,1,0:T(8,128)(2,1)S(1)} %broadcast_in_dim.32), channel_id=1, replica_groups=mesh['shard'=16,'rep'=2] {'shard'}, dimensions={0} | all-to-all | bytes 262144 | tf_op jit(solution)/shard_map/all_to_all | solution.py:426
  208.9 1.3 collective-permute-done.33.other_ref
  210.2 10.0 %shard_map.100 = (f32[16,512]{1,0:T(8,128)}, f32[128,128]{1,0:T(8,128)}) custom-call(s32[2]{0:T(128)S(1)} %pad_add_fusion.1.where_ref, s32[16]{0:T(128)S(1)} %copy-done.3, f32[64,128]{1,0:T(8,128)S(1)} %get-tuple-element.64.duals_ref, f32[64,128]{1,0:T(8,128)S(1)} %get-tuple-element.57.live_ref, f32[64,128]{1,0:T(8,128)S(1)} %get-tuple-element.58.item_scale_ref, ...), custom_call_target="tpu_custom_call" | custom-call | tf_op jit(solution)/shard_map/pallas_call | solution.py:468
  (96 shorter events, 18.5 us)
Async XLA Ops:
  3.6 15.6 %all-to-all-start = ((s32[16,1,72]{2,1,0:T(1,128)}), s32[16,1,72]{2,1,0:T(1,128)S(1)}, u32[]{:S(2)}, u32[]{:S(2)}) async-start(s32[16,1,72]{2,1,0:T(1,128)} %bitcast.2), calls=%async_computation | async-start | bytes 16384 | tf_op jit(solution)/shard_map/all_to_all | solution.py:343
  22.5 39.2 %collective-permute-start.15 = (bf16[4,136,256]{2,1,0:T(8,128)(2,1)}, bf16[4,136,256]{2,1,0:T(8,128)(2,1)S(1)}, u32[]{:S(2)}, u32[]{:S(2)}) collective-permute-start(bf16[4,136,256]{2,1,0:T(8,128)(2,1)} %get-tuple-element.48), channel_id=1, source_target_pairs={{0,16},{2,18},{4,20},{6,22},{8,24},{10,26},{12,28},{14,30},{16,0},... | collective-permute-start | bytes 835592 | tf_op jit(solution)/shard_map/ppermute | solution.py:380
  22.9 44.8 %collective-permute-start.17 = (bf16[4,136,256]{2,1,0:T(8,128)(2,1)}, bf16[4,136,256]{2,1,0:T(8,128)(2,1)S(1)}, u32[]{:S(2)}, u32[]{:S(2)}) collective-permute-start(bf16[4,136,256]{2,1,0:T(8,128)(2,1)} %get-tuple-element.49), channel_id=1, source_target_pairs={{0,18},{2,16},{4,22},{6,20},{8,26},{10,24},{12,30},{14,28},{16,2},... | collective-permute-start | bytes 835592 | tf_op jit(solution)/shard_map/ppermute | solution.py:380
  25.9 48.2 %collective-permute-start.19 = (bf16[4,136,256]{2,1,0:T(8,128)(2,1)}, bf16[4,136,256]{2,1,0:T(8,128)(2,1)S(1)}, u32[]{:S(2)}, u32[]{:S(2)}) collective-permute-start(bf16[4,136,256]{2,1,0:T(8,128)(2,1)} %get-tuple-element.50), channel_id=1, source_target_pairs={{0,20},{2,22},{4,16},{6,18},{8,28},{10,30},{12,24},{14,26},{16,4},... | collective-permute-start | bytes 835592 | tf_op jit(solution)/shard_map/ppermute | solution.py:380
  27.9 53.0 %collective-permute-start.21 = (bf16[4,136,256]{2,1,0:T(8,128)(2,1)}, bf16[4,136,256]{2,1,0:T(8,128)(2,1)S(1)}, u32[]{:S(2)}, u32[]{:S(2)}) collective-permute-start(bf16[4,136,256]{2,1,0:T(8,128)(2,1)} %get-tuple-element.51), channel_id=1, source_target_pairs={{0,22},{2,20},{4,18},{6,16},{8,30},{10,28},{12,26},{14,24},{16,6},... | collective-permute-start | bytes 835592 | tf_op jit(solution)/shard_map/ppermute | solution.py:380
  36.2 44.7 %collective-permute-start = (bf16[4,136,256]{2,1,0:T(8,128)(2,1)}, bf16[4,136,256]{2,1,0:T(8,128)(2,1)S(1)}, u32[]{:S(2)}, u32[]{:S(2)}) collective-permute-start(bf16[4,136,256]{2,1,0:T(8,128)(2,1)} %get-tuple-element.35), channel_id=1, source_target_pairs={{0,30},{2,28},{4,26},{6,24},{8,22},{10,20},{12,18},{14,16},{16,14}... | collective-permute-start | bytes 835592 | tf_op jit(solution)/shard_map/ppermute | solution.py:380
  61.7 25.1 %collective-permute-start.1 = (bf16[4,136,256]{2,1,0:T(8,128)(2,1)}, bf16[4,136,256]{2,1,0:T(8,128)(2,1)S(1)}, u32[]{:S(2)}, u32[]{:S(2)}) collective-permute-start(bf16[4,136,256]{2,1,0:T(8,128)(2,1)} %get-tuple-element.36), channel_id=1, source_target_pairs={{0,2},{2,0},{4,6},{6,4},{8,10},{10,8},{12,14},{14,12},{16,18},{18,... | collective-permute-start | bytes 835592 | tf_op jit(solution)/shard_map/ppermute | solution.py:380
  67.7 23.1 %collective-permute-start.3 = (bf16[4,136,256]{2,1,0:T(8,128)(2,1)}, bf16[4,136,256]{2,1,0:T(8,128)(2,1)S(1)}, u32[]{:S(2)}, u32[]{:S(2)}) collective-permute-start(bf16[4,136,256]{2,1,0:T(8,128)(2,1)} %get-tuple-element.42), channel_id=1, source_target_pairs={{0,4},{2,6},{4,0},{6,2},{8,12},{10,14},{12,8},{14,10},{16,20},{18,... | collective-permute-start | bytes 835592 | tf_op jit(solution)/shard_map/ppermute | solution.py:380
  74.1 16.7 %collective-permute-start.5 = (bf16[4,136,256]{2,1,0:T(8,128)(2,1)}, bf16[4,136,256]{2,1,0:T(8,128)(2,1)S(1)}, u32[]{:S(2)}, u32[]{:S(2)}) collective-permute-start(bf16[4,136,256]{2,1,0:T(8,128)(2,1)} %get-tuple-element.43), channel_id=1, source_target_pairs={{0,6},{2,4},{4,2},{6,0},{8,14},{10,12},{12,10},{14,8},{16,22},{18,... | collective-permute-start | bytes 835592 | tf_op jit(solution)/shard_map/ppermute | solution.py:380
  80.9 13.6 %collective-permute-start.7 = (bf16[4,136,256]{2,1,0:T(8,128)(2,1)}, bf16[4,136,256]{2,1,0:T(8,128)(2,1)S(1)}, u32[]{:S(2)}, u32[]{:S(2)}) collective-permute-start(bf16[4,136,256]{2,1,0:T(8,128)(2,1)} %get-tuple-element.44), channel_id=1, source_target_pairs={{0,8},{2,10},{4,12},{6,14},{8,0},{10,2},{12,4},{14,6},{16,24},{18,... | collective-permute-start | bytes 835592 | tf_op jit(solution)/shard_map/ppermute | solution.py:380
  80.9 15.0 %collective-permute-start.9 = (bf16[4,136,256]{2,1,0:T(8,128)(2,1)}, bf16[4,136,256]{2,1,0:T(8,128)(2,1)S(1)}, u32[]{:S(2)}, u32[]{:S(2)}) collective-permute-start(bf16[4,136,256]{2,1,0:T(8,128)(2,1)} %get-tuple-element.45), channel_id=1, source_target_pairs={{0,10},{2,8},{4,14},{6,12},{8,2},{10,0},{12,6},{14,4},{16,26},{18,... | collective-permute-start | bytes 835592 | tf_op jit(solution)/shard_map/ppermute | solution.py:380
  86.8 15.4 %collective-permute-start.11 = (bf16[4,136,256]{2,1,0:T(8,128)(2,1)}, bf16[4,136,256]{2,1,0:T(8,128)(2,1)S(1)}, u32[]{:S(2)}, u32[]{:S(2)}) collective-permute-start(bf16[4,136,256]{2,1,0:T(8,128)(2,1)} %get-tuple-element.46), channel_id=1, source_target_pairs={{0,12},{2,14},{4,8},{6,10},{8,4},{10,6},{12,0},{14,2},{16,28},{18,... | collective-permute-start | bytes 835592 | tf_op jit(solution)/shard_map/ppermute | solution.py:380
  90.9 17.2 %collective-permute-start.13 = (bf16[4,136,256]{2,1,0:T(8,128)(2,1)}, bf16[4,136,256]{2,1,0:T(8,128)(2,1)S(1)}, u32[]{:S(2)}, u32[]{:S(2)}) collective-permute-start(bf16[4,136,256]{2,1,0:T(8,128)(2,1)} %get-tuple-element.47), channel_id=1, source_target_pairs={{0,14},{2,12},{4,10},{6,8},{8,6},{10,4},{12,2},{14,0},{16,30},{18,... | collective-permute-start | bytes 835592 | tf_op jit(solution)/shard_map/ppermute | solution.py:380
  90.9 27.9 %collective-permute-start.23 = (bf16[4,136,256]{2,1,0:T(8,128)(2,1)}, bf16[4,136,256]{2,1,0:T(8,128)(2,1)}, u32[]{:S(2)}, u32[]{:S(2)}) collective-permute-start(bf16[4,136,256]{2,1,0:T(8,128)(2,1)} %get-tuple-element.52), channel_id=1, source_target_pairs={{0,24},{2,26},{4,28},{6,30},{8,16},{10,18},{12,20},{14,22},{16,8},... | collective-permute-start | bytes 835592 | tf_op jit(solution)/shard_map/ppermute | solution.py:380
  94.4 31.9 %collective-permute-start.25 = (bf16[4,136,256]{2,1,0:T(8,128)(2,1)}, bf16[4,136,256]{2,1,0:T(8,128)(2,1)}, u32[]{:S(2)}, u32[]{:S(2)}) collective-permute-start(bf16[4,136,256]{2,1,0:T(8,128)(2,1)} %get-tuple-element.53), channel_id=1, source_target_pairs={{0,26},{2,24},{4,30},{6,28},{8,18},{10,16},{12,22},{14,20},{16,10}... | collective-permute-start | bytes 835592 | tf_op jit(solution)/shard_map/ppermute | solution.py:380
  95.9 32.9 %collective-permute-start.27 = (bf16[4,136,256]{2,1,0:T(8,128)(2,1)}, bf16[4,136,256]{2,1,0:T(8,128)(2,1)}, u32[]{:S(2)}, u32[]{:S(2)}) collective-permute-start(bf16[4,136,256]{2,1,0:T(8,128)(2,1)} %get-tuple-element.54), channel_id=1, source_target_pairs={{0,28},{2,30},{4,24},{6,26},{8,20},{10,22},{12,16},{14,18},{16,12}... | collective-permute-start | bytes 835592 | tf_op jit(solution)/shard_map/ppermute | solution.py:380
  102.2 28.4 %collective-permute-start.2 = (bf16[4,136,256]{2,1,0:T(8,128)(2,1)S(1)}, bf16[4,136,256]{2,1,0:T(8,128)(2,1)}, u32[]{:S(2)}, u32[]{:S(2)}) collective-permute-start(bf16[4,136,256]{2,1,0:T(8,128)(2,1)S(1)} %collective-permute-done.1.rest_0_), channel_id=1, source_target_pairs={{0,1},{1,0},{2,3},{3,2},{4,5},{5,4},{6,7},{7,6},{8,9},{9,8},{10,11... | collective-permute-start | bytes 835592 | tf_op jit(solution)/shard_map/ppermute | solution.py:420
  108.0 21.1 %collective-permute-start.16 = (bf16[4,136,256]{2,1,0:T(8,128)(2,1)S(1)}, bf16[4,136,256]{2,1,0:T(8,128)(2,1)}, u32[]{:S(2)}, u32[]{:S(2)}) collective-permute-start(bf16[4,136,256]{2,1,0:T(8,128)(2,1)S(1)} %collective-permute-done.15.rest_14_), channel_id=1, source_target_pairs={{0,1},{1,0},{2,3},{3,2},{4,5},{5,4},{6,7},{7,6},{8,9},{9,8},{10,11... | collective-permute-start | bytes 835592 | tf_op jit(solution)/shard_map/ppermute | solution.py:420
  118.8 11.0 %collective-permute-start.18 = (bf16[4,136,256]{2,1,0:T(8,128)(2,1)S(1)}, bf16[4,136,256]{2,1,0:T(8,128)(2,1)}, u32[]{:S(2)}, u32[]{:S(2)}) collective-permute-start(bf16[4,136,256]{2,1,0:T(8,128)(2,1)S(1)} %collective-permute-done.17.rest_16_), channel_id=1, source_target_pairs={{0,1},{1,0},{2,3},{3,2},{4,5},{5,4},{6,7},{7,6},{8,9},{9,8},{10,11... | collective-permute-start | bytes 835592 | tf_op jit(solution)/shard_map/ppermute | solution.py:420
  126.4 3.5 %collective-permute-start.20 = (bf16[4,136,256]{2,1,0:T(8,128)(2,1)S(1)}, bf16[4,136,256]{2,1,0:T(8,128)(2,1)}, u32[]{:S(2)}, u32[]{:S(2)}) collective-permute-start(bf16[4,136,256]{2,1,0:T(8,128)(2,1)S(1)} %collective-permute-done.19.rest_18_), channel_id=1, source_target_pairs={{0,1},{1,0},{2,3},{3,2},{4,5},{5,4},{6,7},{7,6},{8,9},{9,8},{10,11... | collective-permute-start | bytes 835592 | tf_op jit(solution)/shard_map/ppermute | solution.py:420
  128.8 1.7 collective-permute-start.22
  129.2 13.2 %collective-permute-start.4 = (bf16[4,136,256]{2,1,0:T(8,128)(2,1)S(1)}, bf16[4,136,256]{2,1,0:T(8,128)(2,1)S(1)}, u32[]{:S(2)}, u32[]{:S(2)}) collective-permute-start(bf16[4,136,256]{2,1,0:T(8,128)(2,1)S(1)} %collective-permute-done.3.rest_2_), channel_id=1, source_target_pairs={{0,1},{1,0},{2,3},{3,2},{4,5},{5,4},{6,7},{7,6},{8,9},{9,8},{10,11... | collective-permute-start | bytes 835592 | tf_op jit(solution)/shard_map/ppermute | solution.py:420
  129.8 12.8 %collective-permute-start.6 = (bf16[4,136,256]{2,1,0:T(8,128)(2,1)S(1)}, bf16[4,136,256]{2,1,0:T(8,128)(2,1)S(1)}, u32[]{:S(2)}, u32[]{:S(2)}) collective-permute-start(bf16[4,136,256]{2,1,0:T(8,128)(2,1)S(1)} %collective-permute-done.5.rest_4_), channel_id=1, source_target_pairs={{0,1},{1,0},{2,3},{3,2},{4,5},{5,4},{6,7},{7,6},{8,9},{9,8},{10,11... | collective-permute-start | bytes 835592 | tf_op jit(solution)/shard_map/ppermute | solution.py:420
  129.9 13.1 %collective-permute-start.8 = (bf16[4,136,256]{2,1,0:T(8,128)(2,1)S(1)}, bf16[4,136,256]{2,1,0:T(8,128)(2,1)S(1)}, u32[]{:S(2)}, u32[]{:S(2)}) collective-permute-start(bf16[4,136,256]{2,1,0:T(8,128)(2,1)S(1)} %collective-permute-done.7.rest_6_), channel_id=1, source_target_pairs={{0,1},{1,0},{2,3},{3,2},{4,5},{5,4},{6,7},{7,6},{8,9},{9,8},{10,11... | collective-permute-start | bytes 835592 | tf_op jit(solution)/shard_map/ppermute | solution.py:420
  130.5 12.6 %collective-permute-start.10 = (bf16[4,136,256]{2,1,0:T(8,128)(2,1)S(1)}, bf16[4,136,256]{2,1,0:T(8,128)(2,1)S(1)}, u32[]{:S(2)}, u32[]{:S(2)}) collective-permute-start(bf16[4,136,256]{2,1,0:T(8,128)(2,1)S(1)} %collective-permute-done.9.rest_8_), channel_id=1, source_target_pairs={{0,1},{1,0},{2,3},{3,2},{4,5},{5,4},{6,7},{7,6},{8,9},{9,8},{10,11... | collective-permute-start | bytes 835592 | tf_op jit(solution)/shard_map/ppermute | solution.py:420
  130.6 12.9 %collective-permute-start.12 = (bf16[4,136,256]{2,1,0:T(8,128)(2,1)S(1)}, bf16[4,136,256]{2,1,0:T(8,128)(2,1)S(1)}, u32[]{:S(2)}, u32[]{:S(2)}) collective-permute-start(bf16[4,136,256]{2,1,0:T(8,128)(2,1)S(1)} %collective-permute-done.11.rest_10_), channel_id=1, source_target_pairs={{0,1},{1,0},{2,3},{3,2},{4,5},{5,4},{6,7},{7,6},{8,9},{9,8},{10,11... | collective-permute-start | bytes 835592 | tf_op jit(solution)/shard_map/ppermute | solution.py:420
  142.4 1.6 collective-permute-start.14
  142.6 1.8 collective-permute-start.24
  143.0 1.8 collective-permute-start.26
  143.1 2.1 collective-permute-start.28
  143.5 2.1 collective-permute-start.29
  185.2 1.3 collective-permute-start.31
  (7 other events, 67.7 us)

commit v2 on v1

--- a/solution.py
+++ b/solution.py
@@ -37,26 +37,32 @@
     return first + list(range(1, top)) + far[top // 2 :]
 
 
+def fact_place(j, half, camps, pieces, width):
+    across = width // camps
+    return pl.ds(half * camps + j // across * pieces, pieces), pl.ds(j % across * camps, camps)
+
+
 def gather_kernel(half, shifts, where_ref, asked_ref, camp_ref, fact_ref, *rest):
     outs, (stage, sem) = rest[:-2], rest[-2:]
     me, rep = where_ref[0], where_ref[1]
-    camps = camp_ref.shape[1]
+    _, camps, width = camp_ref.shape
     arriving, leaving = [], []
     for n, (shift, out) in enumerate(zip(shifts, outs)):
         for j in range(half):
-            at = n * half + j
             block = asked_ref[me ^ shift, rep * half + j]
-            for part, source, rows in (
-                (0, camp_ref, pl.ds(0, camps)),
-                (1, fact_ref, pl.ds(camps, fact_ref.shape[1])),
+            rows, lanes = fact_place(j, half, camps, fact_ref.shape[1], width)
+            for copy in (
+                pltpu.make_async_copy(
+                    camp_ref.at[block], stage.at[n, pl.ds(j * camps, camps)], sem.at[0, n * half + j]
+                ),
+                pltpu.make_async_copy(fact_ref.at[block], stage.at[n, rows, lanes], sem.at[1, n * half + j]),
             ):
-                copy = pltpu.make_async_copy(source.at[block], stage.at[at, rows], sem.at[part, at])
                 copy.start()
                 arriving.append(copy)
-            leaving.append(pltpu.make_async_copy(stage.at[at], out.at[j], sem.at[2, at]))
-    for at, copy in enumerate(leaving):
-        arriving[2 * at].wait()
-        arriving[2 * at + 1].wait()
+        leaving.append(pltpu.make_async_copy(stage.at[n], out, sem.at[2, n]))
+    for n, copy in enumerate(leaving):
+        for part in arriving[2 * half * n : 2 * half * (n + 1)]:
+            part.wait()
         copy.start()
     for copy in leaving:
         copy.wait()
@@ -116,7 +122,7 @@
                 item_landed(k * fanout + e, item_ref, item_sem)
 
     def multiply(k, dots):
-        blocks = item_ref[pl.ds(pl.multiple_of(k * fanout, fanout), fanout), :camps].reshape(fanout * camps, width)
+        blocks = item_ref[pl.ds(pl.multiple_of(k * fanout, fanout), fanout)].reshape(fanout * camps, width)
         dots[...] = lax.dot_general(
             user_ref[k], blocks, (((1,), (1,)), ((), ())), preferred_element_type=jnp.float32
         )
@@ -185,24 +191,35 @@
     theirs_ref[...] = spend_scr[pl.ds(pl.multiple_of((1 - rep) * count, count), count), :]
 
 
-def item_facts(item_ref, item_sem, dual_ref, limit_ref, live_ref, item_scale_ref):
+def item_facts(fact_ref, item_ref, item_sem, fact_sem, dual_ref, limit_ref, live_ref, item_scale_ref):
     items, camps = dual_ref.shape
     width = item_ref.shape[2]
     eye = lax.broadcasted_iota(jnp.int32, (camps, camps), 0) == lax.broadcasted_iota(jnp.int32, (camps, camps), 1)
 
-    def one(item, carry):
+    def wait(item, carry):
         item_landed(item, item_ref, item_sem)
-        facts = item_ref[item, camps:, :camps].astype(jnp.float32)
-        dual_ref[pl.ds(item, 1), :] = facts[0:1] + facts[1:2] + facts[2:3]
-        limit_ref[pl.ds(item, 1), :] = facts[3:4] + facts[4:5] + facts[5:6]
-        live_ref[pl.ds(item, 1), :] = facts[6:7]
-        rows = item_ref[item, :camps].astype(jnp.float32)
-        total = jnp.broadcast_to(jnp.sum(rows * rows, axis=1, keepdims=True), (camps, camps))
-        total = jnp.sum(jnp.where(eye, total, 0.0), axis=0, keepdims=True)
-        item_scale_ref[pl.ds(item, 1), :] = lax.rsqrt(total * (1.0 / width) + epsilon)
+        pltpu.make_async_copy(fact_ref.at[item], fact_ref.at[item], fact_sem.at[item]).wait()
         return carry
 
-    lax.fori_loop(0, items, one, 0, unroll=4)
+    lax.fori_loop(0, items, wait, 0, unroll=8)
+    group = 8
+
+    def some(n, carry):
+        first = pl.multiple_of(n * group, group)
+        facts = fact_ref[pl.ds(first, group)].astype(jnp.float32)
+        dual_ref[pl.ds(first, group), :] = facts[:, 0] + facts[:, 1] + facts[:, 2]
+        limit_ref[pl.ds(first, group), :] = facts[:, 3] + facts[:, 4] + facts[:, 5]
+        live_ref[pl.ds(first, group), :] = facts[:, 6]
+        totals_here = []
+        for e in range(group):
+            rows = item_ref[first + e].astype(jnp.float32)
+            total = jnp.broadcast_to(jnp.sum(rows * rows, axis=1, keepdims=True), (camps, camps))
+            totals_here.append(jnp.sum(jnp.where(eye, total, 0.0), axis=0, keepdims=True))
+        mean = jnp.concatenate(totals_here, axis=0) * (1.0 / width)
+        item_scale_ref[pl.ds(first, group), :] = lax.rsqrt(mean + epsilon)
+        return carry
+
+    lax.fori_loop(0, items // group, some, 0)
 
 
 def first_kernel(
@@ -210,35 +227,31 @@
 ):
     received, outs = rest[: 2 * (shards - 1)], rest[2 * (shards - 1) :][:7]
     mine_ref, theirs_ref, duals_ref, limit_ref, live_ref, item_scale_ref, item_out = outs
-    user_ref, scale_ref, item_ref, row_sem, item_sem, dots_a, dots_b, dual_scr, spend_scr, out_sem = rest[-10:]
+    user_ref, scale_ref, item_ref, row_sem, item_sem, dots_a, dots_b, dual_scr, spend_scr = rest[-12:-3]
+    landed_ref, fact_sem, out_sem = rest[-3:]
     cap = 2 * half
     rep = where_ref[1]
     users = user_ref.shape[1]
-    camps = camp_ref.shape[1]
-
-    def fetch(slot, pairs):
+    _, camps, width = camp_ref.shape
+    pieces = fact_ref.shape[1]
+
+    def fetch(slot, block, facts):
         item = item_at_ref[slot]
 
         @pl.when(item >= 0)
         def _():
-            for source, rows in pairs:
-                pltpu.make_async_copy(source, item_ref.at[item, rows], item_sem.at[item]).start()
-
-    everything = pl.ds(0, item_ref.shape[1])
+            pltpu.make_async_copy(block, item_ref.at[item], item_sem.at[item]).start()
+            pltpu.make_async_copy(facts, landed_ref.at[item], fact_sem.at[item]).start()
+
     for j in range(cap):
-        fetch(
-            j,
-            [
-                (camp_ref.at[own_ref[j]], pl.ds(0, camps)),
-                (fact_ref.at[own_ref[j]], pl.ds(camps, fact_ref.shape[1])),
-            ],
-        )
+        fetch(j, camp_ref.at[own_ref[j]], fact_ref.at[own_ref[j]])
     for n in range(shards - 1):
         for j in range(half):
-            fetch((n + 1) * cap + rep * half + j, [(received[2 * n].at[j], everything)])
-            fetch((n + 1) * cap + (1 - rep) * half + j, [(received[2 * n + 1].at[j], everything)])
+            for side, message in ((rep, received[2 * n]), (1 - rep, received[2 * n + 1])):
+                rows, lanes = fact_place(j, half, camps, pieces, width)
+                fetch((n + 1) * cap + side * half + j, message.at[pl.ds(j * camps, camps)], message.at[rows, lanes])
     start_rows(user_hbm, scale_hbm, user_ref, scale_ref, row_sem)
-    item_facts(item_ref, item_sem, duals_ref, limit_ref, live_ref, item_scale_ref)
+    item_facts(landed_ref, item_ref, item_sem, fact_sem, duals_ref, limit_ref, live_ref, item_scale_ref)
     keep = pltpu.make_async_copy(item_ref, item_out, out_sem)
     keep.start()
     dual_scr[...] = jnp.where(live_ref[...] > 0.5, duals_ref[...] * gain, masked)
@@ -354,8 +367,7 @@
     live = (jnp.arange(camps, dtype=jnp.int32)[None, :] < camp_count[:, None]).astype(f32)
     rows = pieces(dual_init) + pieces(spend_limit) + [live, jnp.zeros_like(live)]
     facts = jnp.stack(rows, axis=1).astype(camp_emb.dtype)
-    facts = jnp.concatenate([facts, jnp.zeros_like(facts)], axis=2)
-    fact_rows = len(rows)
+    message = half * camps + -(-half * camps // width) * len(rows)
     camp_rows, facts = in_hbm(camp_emb), in_hbm(facts)
 
     order = send_order(shards)
@@ -363,11 +375,11 @@
     for shifts in (order[:4], order[4:]):
         outs = pl.pallas_call(
             functools.partial(gather_kernel, half, shifts),
-            out_shape=[pltpu.HBM((half, camps + fact_rows, width), camp_emb.dtype)] * len(shifts),
+            out_shape=[pltpu.HBM((message, width), camp_emb.dtype)] * len(shifts),
             in_specs=[SMEM, SMEM, HBM, HBM],
             out_specs=[HBM] * len(shifts),
             scratch_shapes=[
-                pltpu.VMEM((len(shifts) * half, camps + fact_rows, width), camp_emb.dtype),
+                pltpu.VMEM((len(shifts), message, width), camp_emb.dtype),
                 pltpu.SemaphoreType.DMA((3, len(shifts) * half)),
             ],
             compiler_params=pltpu.CompilerParams(vmem_limit_bytes=8 * 2**20),
@@ -431,7 +443,7 @@
     work = [
         pltpu.VMEM((clusters, users, width), user_emb.dtype),
         pltpu.VMEM((clusters, users, camps), f32),
-        pltpu.VMEM((items, camps + fact_rows, width), camp_emb.dtype),
+        pltpu.VMEM((items, camps, width), camp_emb.dtype),
         pltpu.SemaphoreType.DMA((2, clusters)),
         pltpu.SemaphoreType.DMA((items,)),
         pltpu.VMEM((users, fanout * camps), f32),
@@ -445,10 +457,16 @@
         functools.partial(first_kernel, shards, half, fanout),
         out_shape=spend_out
         + [jax.ShapeDtypeStruct((items, camps), f32)] * 4
-        + [pltpu.HBM((items, camps + fact_rows, width), camp_emb.dtype)],
+        + [pltpu.HBM((items, camps, width), camp_emb.dtype)],
         in_specs=[SMEM] * 4 + [HBM] * 4 + [ANY] * len(received),
         out_specs=[VMEM] * 6 + [HBM],
-        scratch_shapes=work + spend_work + [pltpu.SemaphoreType.DMA],
+        scratch_shapes=work
+        + spend_work
+        + [
+            pltpu.VMEM((items, len(rows), camps), camp_emb.dtype),
+            pltpu.SemaphoreType.DMA((items,)),
+            pltpu.SemaphoreType.DMA,
+        ],
         compiler_params=limits,
     )(where, cluster_size, item_of_slot, own_wanted, user_rows, user_scale, camp_rows, facts, *received)
     item_emb = in_hbm(item_emb)

time: 221 us -> 213 us (0.964)
  Pallas kernels: 59.7 us -> 54.9 us
  waiting for transfers between devices: 82 us -> 79.1 us
    pallas_call x1, Pallas kernels: 20.9 us -> 16.7 us  [program(): pl.pallas_call(functools.partial(first_kernel, shards, half, fanout), out...]
    ppermute x15, waiting for transfers between devices: 72.4 us -> 69.3 us  [program(): lax.ppermute(sent[shift], 'shard', [(i, i ^ shift) for i in range(shards)])]
where the time goes in v2:
time: 213 us; the launch traced here: 212 us
  waiting for transfers between devices  79.1 us (37%)
  Pallas kernels  54.9 us (26%)
  starting transfers between devices  39.1 us (18%)
  blocking collectives  27.8 us (13%)
  local copies, waits for them, and re-layouts  6.7 us (3%)
  other arithmetic  3.34 us (2%)
    ppermute x15, waiting for transfers between devices, program(): lax.ppermute(sent[shift], 'shard', [(i, i ^ shift) for i in range(shards)])  69.3 us
    all_to_all x2, blocking collectives, exchange(): lax.all_to_all(spread, 'shard', split_axis=0, concat_axis=0, tiled=True)  27.8 us
    ppermute x15, starting transfers between devices, program(): lax.ppermute(sent[shift], 'shard', [(i, i ^ shift) for i in range(shards)])  27.6 us
    pallas_call x1, Pallas kernels, program(): pl.pallas_call(functools.partial(first_kernel, shards, half, fanout), out...  16.7 us
    pallas_call x1, Pallas kernels, program(): pl.pallas_call(functools.partial(second_kernel, fanout), out_shape=spend_...  10.2 us
    pallas_call x1, Pallas kernels, program(): pl.pallas_call(functools.partial(third_kernel, fanout), out_shape=[jax.Sh...  9.9 us
    pallas_call x1, Pallas kernels, program(): pl.pallas_call(user_kernel, out_shape=jax.ShapeDtypeStruct((clusters, use...  9.19 us
    pallas_call x2, Pallas kernels, program(): pl.pallas_call(functools.partial(gather_kernel, half, shifts), out_shape=...  8.85 us
  transfers between devices with their start and end apart: 35, of which 21 were waited for; matrix products, arithmetic and copies ran while one was open for 2% of the time, Pallas kernels for 7%

profile of v2, /device:TPU:0, one launch (start us, length us, event | category | flops | bytes accessed | tf_op | source)
XLA Modules:
  0.0 211.8 jit_solution(16406725023440246424)
XLA Ops:
  3.6 8.3 %all-to-all-start = ((s32[16,1,72]{2,1,0:T(1,128)}), s32[16,1,72]{2,1,0:T(1,128)S(1)}, u32[]{:S(2)}, u32[]{:S(2)}) async-start(s32[16,1,72]{2,1,0:T(1,128)} %bitcast.2), calls=%async_computation | async-start | bytes 16384 | tf_op jit(solution)/shard_map/all_to_all | solution.py:356
  14.9 1.5 stack.63.fact_ref
  16.4 2.8 %all-to-all-done = s32[16,1,72]{2,1,0:T(1,128)S(1)} async-done(((s32[16,1,72]{2,1,0:T(1,128)}), s32[16,1,72]{2,1,0:T(1,128)S(1)}, u32[]{:S(2)}, u32[]{:S(2)}) %all-to-all-start) | async-done | bytes 4640 | tf_op jit(solution)/shard_map/all_to_all | solution.py:356
  19.2 3.2 %shard_map.97 = (bf16[528,256]{1,0:T(8,128)(2,1)}, bf16[528,256]{1,0:T(8,128)(2,1)}, bf16[528,256]{1,0:T(8,128)(2,1)}, bf16[528,256]{1,0:T(8,128)(2,1)}) custom-call(s32[2]{0:T(128)S(1)} %pad_add_fusion.1.where_ref, s32[16,72]{1,0:T(8,128)S(1)} %bitcast.26, bf16[128,128,256]{2,1,0:T(8,128)(2,1)} %camp_ref.5, bf16[128,8,128]{2,1,0:T(8,128)(2,1)} %stack.63.fact_ref), custom_call_target="tpu_custom_call" | custom-call | bytes 2097152 | tf_op jit(solution)/shard_map/pallas_call | solution.py:376
  23.0 2.7 %collective-permute-start.17 = (bf16[528,256]{1,0:T(8,128)(2,1)}, bf16[528,256]{1,0:T(8,128)(2,1)S(1)}, u32[]{:S(2)}, u32[]{:S(2)}) collective-permute-start(bf16[528,256]{1,0:T(8,128)(2,1)} %get-tuple-element.49), channel_id=1, source_target_pairs={{0,18},{2,16},{4,22},{6,20},{8,26},{10,24},{12,30},{14,28},{16,2},... | collective-permute-start | bytes 811016 | tf_op jit(solution)/shard_map/ppermute | solution.py:392
  25.7 1.8 collective-permute-start.19
  27.5 2.6 %collective-permute-start.21 = (bf16[528,256]{1,0:T(8,128)(2,1)}, bf16[528,256]{1,0:T(8,128)(2,1)S(1)}, u32[]{:S(2)}, u32[]{:S(2)}) collective-permute-start(bf16[528,256]{1,0:T(8,128)(2,1)} %get-tuple-element.51), channel_id=1, source_target_pairs={{0,22},{2,20},{4,18},{6,16},{8,30},{10,28},{12,26},{14,24},{16,6},... | collective-permute-start | bytes 811016 | tf_op jit(solution)/shard_map/ppermute | solution.py:392
  30.1 5.6 %shard_map.95 = (bf16[528,256]{1,0:T(8,128)(2,1)}, bf16[528,256]{1,0:T(8,128)(2,1)}, bf16[528,256]{1,0:T(8,128)(2,1)}, bf16[528,256]{1,0:T(8,128)(2,1)}, bf16[52...) custom-call(s32[2]{0:T(128)S(1)} %pad_add_fusion.1.where_ref, ...), custom_call_target="tpu_custom_call" | custom-call | bytes 5767168 | tf_op jit(solution)/shard_map/pallas_call | solution.py:376
  35.7 2.2 %collective-permute-start = (bf16[528,256]{1,0:T(8,128)(2,1)}, bf16[528,256]{1,0:T(8,128)(2,1)S(1)}, u32[]{:S(2)}, u32[]{:S(2)}) collective-permute-start(bf16[528,256]{1,0:T(8,128)(2,1)} %get-tuple-element.35), channel_id=1, source_target_pairs={{0,30},{2,28},{4,26},{6,24},{8,22},{10,20},{12,18},{14,16},{16,14}... | collective-permute-start | bytes 811016 | tf_op jit(solution)/shard_map/ppermute | solution.py:392
  37.9 22.2 %collective-permute-done.15.rest_14_ = bf16[528,256]{1,0:T(8,128)(2,1)S(1)} collective-permute-done((bf16[528,256]{1,0:T(8,128)(2,1)}, bf16[528,256]{1,0:T(8,128)(2,1)S(1)}, u32[]{:S(2)}, u32[]{:S(2)}) %collective-permute-start.15) | collective-permute-done | bytes 270368 | tf_op jit(solution)/shard_map/ppermute | solution.py:392
  60.6 5.3 %collective-permute-done.17.rest_16_ = bf16[528,256]{1,0:T(8,128)(2,1)S(1)} collective-permute-done((bf16[528,256]{1,0:T(8,128)(2,1)}, bf16[528,256]{1,0:T(8,128)(2,1)S(1)}, u32[]{:S(2)}, u32[]{:S(2)}) %collective-permute-start.17) | collective-permute-done | bytes 270368 | tf_op jit(solution)/shard_map/ppermute | solution.py:392
  65.9 1.6 collective-permute-start.3
  67.5 4.5 %collective-permute-done.19.rest_18_ = bf16[528,256]{1,0:T(8,128)(2,1)S(1)} collective-permute-done((bf16[528,256]{1,0:T(8,128)(2,1)}, bf16[528,256]{1,0:T(8,128)(2,1)S(1)}, u32[]{:S(2)}, u32[]{:S(2)}) %collective-permute-start.19) | collective-permute-done | bytes 270368 | tf_op jit(solution)/shard_map/ppermute | solution.py:392
  73.2 5.3 %collective-permute-done.21.rest_20_ = bf16[528,256]{1,0:T(8,128)(2,1)S(1)} collective-permute-done((bf16[528,256]{1,0:T(8,128)(2,1)}, bf16[528,256]{1,0:T(8,128)(2,1)S(1)}, u32[]{:S(2)}, u32[]{:S(2)}) %collective-permute-start.21) | collective-permute-done | bytes 270368 | tf_op jit(solution)/shard_map/ppermute | solution.py:392
  78.5 5.6 %collective-permute-start.9 = (bf16[528,256]{1,0:T(8,128)(2,1)}, bf16[528,256]{1,0:T(8,128)(2,1)S(1)}, u32[]{:S(2)}, u32[]{:S(2)}) collective-permute-start(bf16[528,256]{1,0:T(8,128)(2,1)} %get-tuple-element.45), channel_id=1, source_target_pairs={{0,10},{2,8},{4,14},{6,12},{8,2},{10,0},{12,6},{14,4},{16,26},{18,... | collective-permute-start | bytes 811016 | tf_op jit(solution)/shard_map/ppermute | solution.py:392
  84.9 3.4 %collective-permute-done.3.rest_2_ = bf16[528,256]{1,0:T(8,128)(2,1)S(1)} collective-permute-done((bf16[528,256]{1,0:T(8,128)(2,1)}, bf16[528,256]{1,0:T(8,128)(2,1)S(1)}, u32[]{:S(2)}, u32[]{:S(2)}) %collective-permute-start.3) | collective-permute-done | bytes 270368 | tf_op jit(solution)/shard_map/ppermute | solution.py:392
  88.3 3.3 %collective-permute-start.23 = (bf16[528,256]{1,0:T(8,128)(2,1)}, bf16[528,256]{1,0:T(8,128)(2,1)S(1)}, u32[]{:S(2)}, u32[]{:S(2)}) collective-permute-start(bf16[528,256]{1,0:T(8,128)(2,1)} %get-tuple-element.52), channel_id=1, source_target_pairs={{0,24},{2,26},{4,28},{6,30},{8,16},{10,18},{12,20},{14,22},{16,8},... | collective-permute-start | bytes 811016 | tf_op jit(solution)/shard_map/ppermute | solution.py:392
  91.6 1.6 collective-permute-start.25
  93.2 3.3 %collective-permute-start.27 = (bf16[528,256]{1,0:T(8,128)(2,1)}, bf16[528,256]{1,0:T(8,128)(2,1)}, u32[]{:S(2)}, u32[]{:S(2)}) collective-permute-start(bf16[528,256]{1,0:T(8,128)(2,1)} %get-tuple-element.54), channel_id=1, source_target_pairs={{0,28},{2,30},{4,24},{6,26},{8,20},{10,22},{12,16},{14,18},{16,12}... | collective-permute-start | bytes 811016 | tf_op jit(solution)/shard_map/ppermute | solution.py:392
  96.6 3.0 %collective-permute-done.11.rest_10_ = bf16[528,256]{1,0:T(8,128)(2,1)S(1)} collective-permute-done((bf16[528,256]{1,0:T(8,128)(2,1)}, bf16[528,256]{1,0:T(8,128)(2,1)S(1)}, u32[]{:S(2)}, u32[]{:S(2)}) %collective-permute-start.11) | collective-permute-done | bytes 270368 | tf_op jit(solution)/shard_map/ppermute | solution.py:392
  99.6 5.6 %collective-permute-done.13.rest_12_ = bf16[528,256]{1,0:T(8,128)(2,1)S(1)} collective-permute-done((bf16[528,256]{1,0:T(8,128)(2,1)}, bf16[528,256]{1,0:T(8,128)(2,1)S(1)}, u32[]{:S(2)}, u32[]{:S(2)}) %collective-permute-start.13) | collective-permute-done | bytes 270368 | tf_op jit(solution)/shard_map/ppermute | solution.py:392
  105.3 8.9 %collective-permute-done.23.rest_22_ = bf16[528,256]{1,0:T(8,128)(2,1)S(1)} collective-permute-done((bf16[528,256]{1,0:T(8,128)(2,1)}, bf16[528,256]{1,0:T(8,128)(2,1)S(1)}, u32[]{:S(2)}, u32[]{:S(2)}) %collective-permute-start.23) | collective-permute-done | bytes 270368 | tf_op jit(solution)/shard_map/ppermute | solution.py:392
  114.2 7.9 %collective-permute-done.25.rest_24_ = bf16[528,256]{1,0:T(8,128)(2,1)} collective-permute-done((bf16[528,256]{1,0:T(8,128)(2,1)}, bf16[528,256]{1,0:T(8,128)(2,1)}, u32[]{:S(2)}, u32[]{:S(2)}) %collective-permute-start.25) | collective-permute-done | bytes 270368 | tf_op jit(solution)/shard_map/ppermute | solution.py:392
  122.0 3.2 %collective-permute-done.27.rest_26_ = bf16[528,256]{1,0:T(8,128)(2,1)} collective-permute-done((bf16[528,256]{1,0:T(8,128)(2,1)}, bf16[528,256]{1,0:T(8,128)(2,1)}, u32[]{:S(2)}, u32[]{:S(2)}) %collective-permute-start.27) | collective-permute-done | bytes 270368 | tf_op jit(solution)/shard_map/ppermute | solution.py:392
  127.5 9.2 %shard_map.96.scale_hbm = f32[16,512,128]{2,1,0:T(8,128)S(1)} custom-call(bf16[16,512,256]{2,1,0:T(8,128)(2,1)} %user_hbm.5), custom_call_target="tpu_custom_call" | custom-call | flops 8388608 | bytes 8388608 | tf_op jit(solution)/shard_map/pallas_call | solution.py:408
  136.7 2.0 copy-done
  141.9 16.7 %shard_map.98 = (f32[32,128]{1,0:T(8,128)S(1)}, f32[32,128]{1,0:T(8,128)S(1)}, f32[64,128]{1,0:T(8,128)S(1)}, f32[64,128]{1,0:T(8,128)S(1)}, f32[64,128]{1,0:T(8...) custom-call(s32[2]{0:T(128)S(1)} %pad_add_fusion.1.where_ref, s32[16]{0:T(128)S(1)} %copy-done.3, ...), custom_call_target="tpu_custom_call" | custom-call | tf_op jit(solution)/shard_map/pallas_call | solution.py:456
  159.9 17.0 %all_to_all.21 = bf16[16,32,128]{2,1,0:T(8,128)(2,1)S(1)} all-to-all(bf16[16,32,128]{2,1,0:T(8,128)(2,1)S(1)} %broadcast_in_dim.31), channel_id=1, replica_groups=mesh['shard'=16,'rep'=2] {'shard'}, dimensions={0} | all-to-all | bytes 262144 | tf_op jit(solution)/shard_map/all_to_all | solution.py:438
  177.0 1.3 collective-permute-done.31.other_ref.other_one_ref
  178.3 10.2 %shard_map.99 = (f32[32,128]{1,0:T(8,128)S(1)}, f32[32,128]{1,0:T(8,128)S(1)}, f32[64,128]{1,0:T(8,128)S(1)}) custom-call(s32[2]{0:T(128)S(1)} %pad_add_fusion.1.where_ref, s32[16]{0:T(128)S(1)} %copy-done.3, f32[64,128]{1,0:T(8,128)S(1)} %get-tuple-element.56.duals_ref, f32[64,128]{1,0:T(8,128)S(1)} %get-tuple-element.57.live_ref, ...), custom_call_target="tpu_custom_call" | custom-call | tf_op jit(solution)/shard_map/pallas_call | solution.py:475
  189.8 10.7 %all_to_all.22 = bf16[16,32,128]{2,1,0:T(8,128)(2,1)S(1)} all-to-all(bf16[16,32,128]{2,1,0:T(8,128)(2,1)S(1)} %broadcast_in_dim.56), channel_id=1, replica_groups=mesh['shard'=16,'rep'=2] {'shard'}, dimensions={0} | all-to-all | bytes 262144 | tf_op jit(solution)/shard_map/all_to_all | solution.py:438
  201.9 9.9 %shard_map.100 = (f32[16,512]{1,0:T(8,128)}, f32[128,128]{1,0:T(8,128)}) custom-call(s32[2]{0:T(128)S(1)} %pad_add_fusion.1.where_ref, s32[16]{0:T(128)S(1)} %copy-done.3, f32[64,128]{1,0:T(8,128)S(1)} %get-tuple-element.64.duals_ref, f32[64,128]{1,0:T(8,128)S(1)} %get-tuple-element.57.live_ref, f32[64,128]{1,0:T(8,128)S(1)} %get-tuple-element.58.item_scale_ref, ...), custom_call_target="tpu_custom_call" | custom-call | tf_op jit(solution)/shard_map/pallas_call | solution.py:486
  (95 shorter events, 18.3 us)
Async XLA Ops:
  3.6 15.6 %all-to-all-start = ((s32[16,1,72]{2,1,0:T(1,128)}), s32[16,1,72]{2,1,0:T(1,128)S(1)}, u32[]{:S(2)}, u32[]{:S(2)}) async-start(s32[16,1,72]{2,1,0:T(1,128)} %bitcast.2), calls=%async_computation | async-start | bytes 16384 | tf_op jit(solution)/shard_map/all_to_all | solution.py:356
  22.4 37.7 %collective-permute-start.15 = (bf16[528,256]{1,0:T(8,128)(2,1)}, bf16[528,256]{1,0:T(8,128)(2,1)S(1)}, u32[]{:S(2)}, u32[]{:S(2)}) collective-permute-start(bf16[528,256]{1,0:T(8,128)(2,1)} %get-tuple-element.48), channel_id=1, source_target_pairs={{0,16},{2,18},{4,20},{6,22},{8,24},{10,26},{12,28},{14,30},{16,0},... | collective-permute-start | bytes 811016 | tf_op jit(solution)/shard_map/ppermute | solution.py:392
  23.0 42.9 %collective-permute-start.17 = (bf16[528,256]{1,0:T(8,128)(2,1)}, bf16[528,256]{1,0:T(8,128)(2,1)S(1)}, u32[]{:S(2)}, u32[]{:S(2)}) collective-permute-start(bf16[528,256]{1,0:T(8,128)(2,1)} %get-tuple-element.49), channel_id=1, source_target_pairs={{0,18},{2,16},{4,22},{6,20},{8,26},{10,24},{12,30},{14,28},{16,2},... | collective-permute-start | bytes 811016 | tf_op jit(solution)/shard_map/ppermute | solution.py:392
  25.7 46.4 %collective-permute-start.19 = (bf16[528,256]{1,0:T(8,128)(2,1)}, bf16[528,256]{1,0:T(8,128)(2,1)S(1)}, u32[]{:S(2)}, u32[]{:S(2)}) collective-permute-start(bf16[528,256]{1,0:T(8,128)(2,1)} %get-tuple-element.50), channel_id=1, source_target_pairs={{0,20},{2,22},{4,16},{6,18},{8,28},{10,30},{12,24},{14,26},{16,4},... | collective-permute-start | bytes 811016 | tf_op jit(solution)/shard_map/ppermute | solution.py:392
  27.5 51.0 %collective-permute-start.21 = (bf16[528,256]{1,0:T(8,128)(2,1)}, bf16[528,256]{1,0:T(8,128)(2,1)S(1)}, u32[]{:S(2)}, u32[]{:S(2)}) collective-permute-start(bf16[528,256]{1,0:T(8,128)(2,1)} %get-tuple-element.51), channel_id=1, source_target_pairs={{0,22},{2,20},{4,18},{6,16},{8,30},{10,28},{12,26},{14,24},{16,6},... | collective-permute-start | bytes 811016 | tf_op jit(solution)/shard_map/ppermute | solution.py:392
  35.7 42.8 %collective-permute-start = (bf16[528,256]{1,0:T(8,128)(2,1)}, bf16[528,256]{1,0:T(8,128)(2,1)S(1)}, u32[]{:S(2)}, u32[]{:S(2)}) collective-permute-start(bf16[528,256]{1,0:T(8,128)(2,1)} %get-tuple-element.35), channel_id=1, source_target_pairs={{0,30},{2,28},{4,26},{6,24},{8,22},{10,20},{12,18},{14,16},{16,14}... | collective-permute-start | bytes 811016 | tf_op jit(solution)/shard_map/ppermute | solution.py:392
  60.1 24.2 %collective-permute-start.1 = (bf16[528,256]{1,0:T(8,128)(2,1)}, bf16[528,256]{1,0:T(8,128)(2,1)S(1)}, u32[]{:S(2)}, u32[]{:S(2)}) collective-permute-start(bf16[528,256]{1,0:T(8,128)(2,1)} %get-tuple-element.36), channel_id=1, source_target_pairs={{0,2},{2,0},{4,6},{6,4},{8,10},{10,8},{12,14},{14,12},{16,18},{18,... | collective-permute-start | bytes 811016 | tf_op jit(solution)/shard_map/ppermute | solution.py:392
  65.9 22.4 %collective-permute-start.3 = (bf16[528,256]{1,0:T(8,128)(2,1)}, bf16[528,256]{1,0:T(8,128)(2,1)S(1)}, u32[]{:S(2)}, u32[]{:S(2)}) collective-permute-start(bf16[528,256]{1,0:T(8,128)(2,1)} %get-tuple-element.42), channel_id=1, source_target_pairs={{0,4},{2,6},{4,0},{6,2},{8,12},{10,14},{12,8},{14,10},{16,20},{18,... | collective-permute-start | bytes 811016 | tf_op jit(solution)/shard_map/ppermute | solution.py:392
  72.0 16.2 %collective-permute-start.5 = (bf16[528,256]{1,0:T(8,128)(2,1)}, bf16[528,256]{1,0:T(8,128)(2,1)S(1)}, u32[]{:S(2)}, u32[]{:S(2)}) collective-permute-start(bf16[528,256]{1,0:T(8,128)(2,1)} %get-tuple-element.43), channel_id=1, source_target_pairs={{0,6},{2,4},{4,2},{6,0},{8,14},{10,12},{12,10},{14,8},{16,22},{18,... | collective-permute-start | bytes 811016 | tf_op jit(solution)/shard_map/ppermute | solution.py:392
  78.5 13.1 %collective-permute-start.7 = (bf16[528,256]{1,0:T(8,128)(2,1)}, bf16[528,256]{1,0:T(8,128)(2,1)S(1)}, u32[]{:S(2)}, u32[]{:S(2)}) collective-permute-start(bf16[528,256]{1,0:T(8,128)(2,1)} %get-tuple-element.44), channel_id=1, source_target_pairs={{0,8},{2,10},{4,12},{6,14},{8,0},{10,2},{12,4},{14,6},{16,24},{18,... | collective-permute-start | bytes 811016 | tf_op jit(solution)/shard_map/ppermute | solution.py:392
  78.5 14.7 %collective-permute-start.9 = (bf16[528,256]{1,0:T(8,128)(2,1)}, bf16[528,256]{1,0:T(8,128)(2,1)S(1)}, u32[]{:S(2)}, u32[]{:S(2)}) collective-permute-start(bf16[528,256]{1,0:T(8,128)(2,1)} %get-tuple-element.45), channel_id=1, source_target_pairs={{0,10},{2,8},{4,14},{6,12},{8,2},{10,0},{12,6},{14,4},{16,26},{18,... | collective-permute-start | bytes 811016 | tf_op jit(solution)/shard_map/ppermute | solution.py:392
  84.3 15.3 %collective-permute-start.11 = (bf16[528,256]{1,0:T(8,128)(2,1)}, bf16[528,256]{1,0:T(8,128)(2,1)S(1)}, u32[]{:S(2)}, u32[]{:S(2)}) collective-permute-start(bf16[528,256]{1,0:T(8,128)(2,1)} %get-tuple-element.46), channel_id=1, source_target_pairs={{0,12},{2,14},{4,8},{6,10},{8,4},{10,6},{12,0},{14,2},{16,28},{18,... | collective-permute-start | bytes 811016 | tf_op jit(solution)/shard_map/ppermute | solution.py:392
  88.3 17.0 %collective-permute-start.13 = (bf16[528,256]{1,0:T(8,128)(2,1)}, bf16[528,256]{1,0:T(8,128)(2,1)S(1)}, u32[]{:S(2)}, u32[]{:S(2)}) collective-permute-start(bf16[528,256]{1,0:T(8,128)(2,1)} %get-tuple-element.47), channel_id=1, source_target_pairs={{0,14},{2,12},{4,10},{6,8},{8,6},{10,4},{12,2},{14,0},{16,30},{18,... | collective-permute-start | bytes 811016 | tf_op jit(solution)/shard_map/ppermute | solution.py:392
  88.3 25.9 %collective-permute-start.23 = (bf16[528,256]{1,0:T(8,128)(2,1)}, bf16[528,256]{1,0:T(8,128)(2,1)S(1)}, u32[]{:S(2)}, u32[]{:S(2)}) collective-permute-start(bf16[528,256]{1,0:T(8,128)(2,1)} %get-tuple-element.52), channel_id=1, source_target_pairs={{0,24},{2,26},{4,28},{6,30},{8,16},{10,18},{12,20},{14,22},{16,8},... | collective-permute-start | bytes 811016 | tf_op jit(solution)/shard_map/ppermute | solution.py:392
  91.6 30.5 %collective-permute-start.25 = (bf16[528,256]{1,0:T(8,128)(2,1)}, bf16[528,256]{1,0:T(8,128)(2,1)}, u32[]{:S(2)}, u32[]{:S(2)}) collective-permute-start(bf16[528,256]{1,0:T(8,128)(2,1)} %get-tuple-element.53), channel_id=1, source_target_pairs={{0,26},{2,24},{4,30},{6,28},{8,18},{10,16},{12,22},{14,20},{16,10}... | collective-permute-start | bytes 811016 | tf_op jit(solution)/shard_map/ppermute | solution.py:392
  93.2 32.0 %collective-permute-start.27 = (bf16[528,256]{1,0:T(8,128)(2,1)}, bf16[528,256]{1,0:T(8,128)(2,1)}, u32[]{:S(2)}, u32[]{:S(2)}) collective-permute-start(bf16[528,256]{1,0:T(8,128)(2,1)} %get-tuple-element.54), channel_id=1, source_target_pairs={{0,28},{2,30},{4,24},{6,26},{8,20},{10,22},{12,16},{14,18},{16,12}... | collective-permute-start | bytes 811016 | tf_op jit(solution)/shard_map/ppermute | solution.py:392
  99.6 27.4 %collective-permute-start.2 = (bf16[528,256]{1,0:T(8,128)(2,1)S(1)}, bf16[528,256]{1,0:T(8,128)(2,1)}, u32[]{:S(2)}, u32[]{:S(2)}) collective-permute-start(bf16[528,256]{1,0:T(8,128)(2,1)S(1)} %collective-permute-done.1.rest_0_), channel_id=1, source_target_pairs={{0,1},{1,0},{2,3},{3,2},{4,5},{5,4},{6,7},{7,6},{8,9},{9,8},{10,11... | collective-permute-start | bytes 811016 | tf_op jit(solution)/shard_map/ppermute | solution.py:432
  105.2 20.3 %collective-permute-start.16 = (bf16[528,256]{1,0:T(8,128)(2,1)S(1)}, bf16[528,256]{1,0:T(8,128)(2,1)}, u32[]{:S(2)}, u32[]{:S(2)}) collective-permute-start(bf16[528,256]{1,0:T(8,128)(2,1)S(1)} %collective-permute-done.15.rest_14_), channel_id=1, source_target_pairs={{0,1},{1,0},{2,3},{3,2},{4,5},{5,4},{6,7},{7,6},{8,9},{9,8},{10,11... | collective-permute-start | bytes 811016 | tf_op jit(solution)/shard_map/ppermute | solution.py:432
  114.2 12.0 %collective-permute-start.18 = (bf16[528,256]{1,0:T(8,128)(2,1)S(1)}, bf16[528,256]{1,0:T(8,128)(2,1)}, u32[]{:S(2)}, u32[]{:S(2)}) collective-permute-start(bf16[528,256]{1,0:T(8,128)(2,1)S(1)} %collective-permute-done.17.rest_16_), channel_id=1, source_target_pairs={{0,1},{1,0},{2,3},{3,2},{4,5},{5,4},{6,7},{7,6},{8,9},{9,8},{10,11... | collective-permute-start | bytes 811016 | tf_op jit(solution)/shard_map/ppermute | solution.py:432
  122.0 4.2 %collective-permute-start.20 = (bf16[528,256]{1,0:T(8,128)(2,1)S(1)}, bf16[528,256]{1,0:T(8,128)(2,1)}, u32[]{:S(2)}, u32[]{:S(2)}) collective-permute-start(bf16[528,256]{1,0:T(8,128)(2,1)S(1)} %collective-permute-done.19.rest_18_), channel_id=1, source_target_pairs={{0,1},{1,0},{2,3},{3,2},{4,5},{5,4},{6,7},{7,6},{8,9},{9,8},{10,11... | collective-permute-start | bytes 811016 | tf_op jit(solution)/shard_map/ppermute | solution.py:432
  125.2 1.7 collective-permute-start.22
  125.6 13.1 %collective-permute-start.4 = (bf16[528,256]{1,0:T(8,128)(2,1)S(1)}, bf16[528,256]{1,0:T(8,128)(2,1)S(1)}, u32[]{:S(2)}, u32[]{:S(2)}) collective-permute-start(bf16[528,256]{1,0:T(8,128)(2,1)S(1)} %collective-permute-done.3.rest_2_), channel_id=1, source_target_pairs={{0,1},{1,0},{2,3},{3,2},{4,5},{5,4},{6,7},{7,6},{8,9},{9,8},{10,11... | collective-permute-start | bytes 811016 | tf_op jit(solution)/shard_map/ppermute | solution.py:432
  126.2 12.8 %collective-permute-start.6 = (bf16[528,256]{1,0:T(8,128)(2,1)S(1)}, bf16[528,256]{1,0:T(8,128)(2,1)S(1)}, u32[]{:S(2)}, u32[]{:S(2)}) collective-permute-start(bf16[528,256]{1,0:T(8,128)(2,1)S(1)} %collective-permute-done.5.rest_4_), channel_id=1, source_target_pairs={{0,1},{1,0},{2,3},{3,2},{4,5},{5,4},{6,7},{7,6},{8,9},{9,8},{10,11... | collective-permute-start | bytes 811016 | tf_op jit(solution)/shard_map/ppermute | solution.py:432
  126.3 13.1 %collective-permute-start.8 = (bf16[528,256]{1,0:T(8,128)(2,1)S(1)}, bf16[528,256]{1,0:T(8,128)(2,1)S(1)}, u32[]{:S(2)}, u32[]{:S(2)}) collective-permute-start(bf16[528,256]{1,0:T(8,128)(2,1)S(1)} %collective-permute-done.7.rest_6_), channel_id=1, source_target_pairs={{0,1},{1,0},{2,3},{3,2},{4,5},{5,4},{6,7},{7,6},{8,9},{9,8},{10,11... | collective-permute-start | bytes 811016 | tf_op jit(solution)/shard_map/ppermute | solution.py:432
  126.9 12.6 %collective-permute-start.10 = (bf16[528,256]{1,0:T(8,128)(2,1)S(1)}, bf16[528,256]{1,0:T(8,128)(2,1)S(1)}, u32[]{:S(2)}, u32[]{:S(2)}) collective-permute-start(bf16[528,256]{1,0:T(8,128)(2,1)S(1)} %collective-permute-done.9.rest_8_), channel_id=1, source_target_pairs={{0,1},{1,0},{2,3},{3,2},{4,5},{5,4},{6,7},{7,6},{8,9},{9,8},{10,11... | collective-permute-start | bytes 811016 | tf_op jit(solution)/shard_map/ppermute | solution.py:432
  127.0 12.8 %collective-permute-start.12 = (bf16[528,256]{1,0:T(8,128)(2,1)S(1)}, bf16[528,256]{1,0:T(8,128)(2,1)S(1)}, u32[]{:S(2)}, u32[]{:S(2)}) collective-permute-start(bf16[528,256]{1,0:T(8,128)(2,1)S(1)} %collective-permute-done.11.rest_10_), channel_id=1, source_target_pairs={{0,1},{1,0},{2,3},{3,2},{4,5},{5,4},{6,7},{7,6},{8,9},{9,8},{10,11... | collective-permute-start | bytes 811016 | tf_op jit(solution)/shard_map/ppermute | solution.py:432
  138.7 1.6 collective-permute-start.14
  139.0 1.8 collective-permute-start.24
  139.3 1.8 collective-permute-start.26
  139.5 2.0 collective-permute-start.28
  139.9 2.1 collective-permute-start.29
  177.0 1.3 collective-permute-start.31
  (7 other events, 67.4 us)

commit v3 on v2

--- a/solution.py
+++ b/solution.py
@@ -423,9 +423,9 @@
     match = jnp.stack([(names[:, None] == side).astype(jnp.bfloat16) for side in sides])
     own_match = jnp.stack([(own_names[:, None] == side).astype(jnp.bfloat16) for side in sides])
 
-    last = order[-1]
-    got_blocks[last], item_of_slot, own_wanted, user_scale, match, own_match = lax.optimization_barrier(
-        (got_blocks[last], item_of_slot, own_wanted, user_scale, match, own_match)
+    gate = 2
+    got_blocks[gate], item_of_slot, own_wanted, user_scale, match, own_match = lax.optimization_barrier(
+        (got_blocks[gate], item_of_slot, own_wanted, user_scale, match, own_match)
     )
     received = []
     for shift in range(1, shards):

time: 213 us -> 212 us (level)
  blocking collectives: 27.8 us -> 31.3 us
  starting transfers between devices: 39.1 us -> 36.5 us
  waiting for transfers between devices: 79.1 us -> 76.8 us
    all_to_all x2, blocking collectives: 27.8 us -> 31.3 us  [exchange(): lax.all_to_all(spread, 'shard', split_axis=0, concat_axis=0, tiled=True)]
    ppermute x15, starting transfers between devices: 27.6 us -> 25 us  [program(): lax.ppermute(sent[shift], 'shard', [(i, i ^ shift) for i in range(shards)])]
    ppermute x15, waiting for transfers between devices: 69.3 us -> 67 us  [program(): lax.ppermute(sent[shift], 'shard', [(i, i ^ shift) for i in range(shards)])]
  transfers between devices with their start and end apart: 35 -> 35, of which waited for: 21 -> 23; matrix products, arithmetic and copies ran while one was open for 2% -> 2% of each run, Pallas kernels for 7% -> 7%
where the time goes in v3:
time: 212 us; the launch traced here: 211 us
  waiting for transfers between devices  76.8 us (36%)
  Pallas kernels  55.4 us (26%)
  starting transfers between devices  36.5 us (17%)
  blocking collectives  31.3 us (15%)
  local copies, waits for them, and re-layouts  6.7 us (3%)
  other arithmetic  3.34 us (2%)
    ppermute x15, waiting for transfers between devices, program(): lax.ppermute(sent[shift], 'shard', [(i, i ^ shift) for i in range(shards)])  67 us
    all_to_all x2, blocking collectives, exchange(): lax.all_to_all(spread, 'shard', split_axis=0, concat_axis=0, tiled=True)  31.3 us
    ppermute x15, starting transfers between devices, program(): lax.ppermute(sent[shift], 'shard', [(i, i ^ shift) for i in range(shards)])  25 us
    pallas_call x1, Pallas kernels, program(): pl.pallas_call(functools.partial(first_kernel, shards, half, fanout), out...  17.2 us
    pallas_call x1, Pallas kernels, program(): pl.pallas_call(functools.partial(second_kernel, fanout), out_shape=spend_...  10.2 us
    pallas_call x1, Pallas kernels, program(): pl.pallas_call(functools.partial(third_kernel, fanout), out_shape=[jax.Sh...  9.9 us
    pallas_call x1, Pallas kernels, program(): pl.pallas_call(user_kernel, out_shape=jax.ShapeDtypeStruct((clusters, use...  9.19 us
    pallas_call x2, Pallas kernels, program(): pl.pallas_call(functools.partial(gather_kernel, half, shifts), out_shape=...  8.85 us
  transfers between devices with their start and end apart: 35, of which 23 were waited for; matrix products, arithmetic and copies ran while one was open for 2% of the time, Pallas kernels for 7%

profile of v3, /device:TPU:0, one launch (start us, length us, event | category | flops | bytes accessed | tf_op | source)
XLA Modules:
  0.0 210.9 jit_solution(8541444534331332488)
XLA Ops:
  3.6 8.3 %all-to-all-start = ((s32[16,1,72]{2,1,0:T(1,128)}), s32[16,1,72]{2,1,0:T(1,128)S(1)}, u32[]{:S(2)}, u32[]{:S(2)}) async-start(s32[16,1,72]{2,1,0:T(1,128)} %bitcast.2), calls=%async_computation | async-start | bytes 16384 | tf_op jit(solution)/shard_map/all_to_all | solution.py:356
  14.9 1.5 stack.63.fact_ref
  16.4 2.8 %all-to-all-done = s32[16,1,72]{2,1,0:T(1,128)S(1)} async-done(((s32[16,1,72]{2,1,0:T(1,128)}), s32[16,1,72]{2,1,0:T(1,128)S(1)}, u32[]{:S(2)}, u32[]{:S(2)}) %all-to-all-start) | async-done | bytes 4640 | tf_op jit(solution)/shard_map/all_to_all | solution.py:356
  19.2 3.2 %shard_map.97 = (bf16[528,256]{1,0:T(8,128)(2,1)}, bf16[528,256]{1,0:T(8,128)(2,1)}, bf16[528,256]{1,0:T(8,128)(2,1)}, bf16[528,256]{1,0:T(8,128)(2,1)}) custom-call(s32[2]{0:T(128)S(1)} %pad_add_fusion.1.where_ref, s32[16,72]{1,0:T(8,128)S(1)} %bitcast.26, bf16[128,128,256]{2,1,0:T(8,128)(2,1)} %camp_ref.5, bf16[128,8,128]{2,1,0:T(8,128)(2,1)} %stack.63.fact_ref), custom_call_target="tpu_custom_call" | custom-call | bytes 2097152 | tf_op jit(solution)/shard_map/pallas_call | solution.py:376
  23.0 2.7 %collective-permute-start.16 = (bf16[528,256]{1,0:T(8,128)(2,1)}, bf16[528,256]{1,0:T(8,128)(2,1)S(1)}, u32[]{:S(2)}, u32[]{:S(2)}) collective-permute-start(bf16[528,256]{1,0:T(8,128)(2,1)} %get-tuple-element.49), channel_id=1, source_target_pairs={{0,18},{2,16},{4,22},{6,20},{8,26},{10,24},{12,30},{14,28},{16,2},... | collective-permute-start | bytes 811016 | tf_op jit(solution)/shard_map/ppermute | solution.py:392
  25.7 1.8 collective-permute-start.18
  27.5 2.6 %collective-permute-start.20 = (bf16[528,256]{1,0:T(8,128)(2,1)}, bf16[528,256]{1,0:T(8,128)(2,1)S(1)}, u32[]{:S(2)}, u32[]{:S(2)}) collective-permute-start(bf16[528,256]{1,0:T(8,128)(2,1)} %get-tuple-element.51), channel_id=1, source_target_pairs={{0,22},{2,20},{4,18},{6,16},{8,30},{10,28},{12,26},{14,24},{16,6},... | collective-permute-start | bytes 811016 | tf_op jit(solution)/shard_map/ppermute | solution.py:392
  30.1 5.6 %shard_map.95 = (bf16[528,256]{1,0:T(8,128)(2,1)}, bf16[528,256]{1,0:T(8,128)(2,1)}, bf16[528,256]{1,0:T(8,128)(2,1)}, bf16[528,256]{1,0:T(8,128)(2,1)}, bf16[52...) custom-call(s32[2]{0:T(128)S(1)} %pad_add_fusion.1.where_ref, ...), custom_call_target="tpu_custom_call" | custom-call | bytes 5767168 | tf_op jit(solution)/shard_map/pallas_call | solution.py:376
  35.8 18.5 %collective-permute-done.14.rest_14_ = bf16[528,256]{1,0:T(8,128)(2,1)S(1)} collective-permute-done((bf16[528,256]{1,0:T(8,128)(2,1)}, bf16[528,256]{1,0:T(8,128)(2,1)S(1)}, u32[]{:S(2)}, u32[]{:S(2)}) %collective-permute-start.14) | collective-permute-done | bytes 270368 | tf_op jit(solution)/shard_map/ppermute | solution.py:392
  54.8 5.3 %collective-permute-done.16.rest_16_ = bf16[528,256]{1,0:T(8,128)(2,1)S(1)} collective-permute-done((bf16[528,256]{1,0:T(8,128)(2,1)}, bf16[528,256]{1,0:T(8,128)(2,1)S(1)}, u32[]{:S(2)}, u32[]{:S(2)}) %collective-permute-start.16) | collective-permute-done | bytes 270368 | tf_op jit(solution)/shard_map/ppermute | solution.py:392
  60.1 1.8 collective-permute-start.4
  61.9 4.3 %collective-permute-done.18.rest_18_ = bf16[528,256]{1,0:T(8,128)(2,1)S(1)} collective-permute-done((bf16[528,256]{1,0:T(8,128)(2,1)}, bf16[528,256]{1,0:T(8,128)(2,1)S(1)}, u32[]{:S(2)}, u32[]{:S(2)}) %collective-permute-start.18) | collective-permute-done | bytes 270368 | tf_op jit(solution)/shard_map/ppermute | solution.py:392
  66.2 5.9 %collective-permute-done.20.rest_20_ = bf16[528,256]{1,0:T(8,128)(2,1)S(1)} collective-permute-done((bf16[528,256]{1,0:T(8,128)(2,1)}, bf16[528,256]{1,0:T(8,128)(2,1)S(1)}, u32[]{:S(2)}, u32[]{:S(2)}) %collective-permute-start.20) | collective-permute-done | bytes 270368 | tf_op jit(solution)/shard_map/ppermute | solution.py:392
  72.1 3.4 %collective-permute-start.10 = (bf16[528,256]{1,0:T(8,128)(2,1)}, bf16[528,256]{1,0:T(8,128)(2,1)S(1)}, u32[]{:S(2)}, u32[]{:S(2)}) collective-permute-start(bf16[528,256]{1,0:T(8,128)(2,1)} %get-tuple-element.46), channel_id=1, source_target_pairs={{0,12},{2,14},{4,8},{6,10},{8,4},{10,6},{12,0},{14,2},{16,28},{18,... | collective-permute-start | bytes 811016 | tf_op jit(solution)/shard_map/ppermute | solution.py:392
  75.8 1.9 collective-permute-done.4.rest_4_
  77.7 3.3 %collective-permute-start.22 = (bf16[528,256]{1,0:T(8,128)(2,1)}, bf16[528,256]{1,0:T(8,128)(2,1)S(1)}, u32[]{:S(2)}, u32[]{:S(2)}) collective-permute-start(bf16[528,256]{1,0:T(8,128)(2,1)} %get-tuple-element.52), channel_id=1, source_target_pairs={{0,24},{2,26},{4,28},{6,30},{8,16},{10,18},{12,20},{14,22},{16,8},... | collective-permute-start | bytes 811016 | tf_op jit(solution)/shard_map/ppermute | solution.py:392
  81.6 1.7 collective-permute-done.8.rest_8_
  83.3 3.7 %collective-permute-start.26 = (bf16[528,256]{1,0:T(8,128)(2,1)}, bf16[528,256]{1,0:T(8,128)(2,1)}, u32[]{:S(2)}, u32[]{:S(2)}) collective-permute-start(bf16[528,256]{1,0:T(8,128)(2,1)} %get-tuple-element.54), channel_id=1, source_target_pairs={{0,28},{2,30},{4,24},{6,26},{8,20},{10,22},{12,16},{14,18},{16,12}... | collective-permute-start | bytes 811016 | tf_op jit(solution)/shard_map/ppermute | solution.py:392
  87.0 1.9 collective-permute-done.10.rest_10_
  88.9 3.8 %collective-permute-start.28 = (bf16[528,256]{1,0:T(8,128)(2,1)}, bf16[528,256]{1,0:T(8,128)(2,1)}, u32[]{:S(2)}, u32[]{:S(2)}) collective-permute-start(bf16[528,256]{1,0:T(8,128)(2,1)} %get-tuple-element.55), channel_id=1, source_target_pairs={{0,30},{2,28},{4,26},{6,24},{8,22},{10,20},{12,18},{14,16},{16,14}... | collective-permute-start | bytes 811016 | tf_op jit(solution)/shard_map/ppermute | solution.py:392
  92.7 2.5 %collective-permute-done.12.rest_12_ = bf16[528,256]{1,0:T(8,128)(2,1)S(1)} collective-permute-done((bf16[528,256]{1,0:T(8,128)(2,1)}, bf16[528,256]{1,0:T(8,128)(2,1)S(1)}, u32[]{:S(2)}, u32[]{:S(2)}) %collective-permute-start.12) | collective-permute-done | bytes 270368 | tf_op jit(solution)/shard_map/ppermute | solution.py:392
  95.2 8.0 %collective-permute-done.22.rest_22_ = bf16[528,256]{1,0:T(8,128)(2,1)S(1)} collective-permute-done((bf16[528,256]{1,0:T(8,128)(2,1)}, bf16[528,256]{1,0:T(8,128)(2,1)S(1)}, u32[]{:S(2)}, u32[]{:S(2)}) %collective-permute-start.22) | collective-permute-done | bytes 270368 | tf_op jit(solution)/shard_map/ppermute | solution.py:392
  103.2 5.7 %collective-permute-done.24.rest_24_ = bf16[528,256]{1,0:T(8,128)(2,1)S(1)} collective-permute-done((bf16[528,256]{1,0:T(8,128)(2,1)}, bf16[528,256]{1,0:T(8,128)(2,1)S(1)}, u32[]{:S(2)}, u32[]{:S(2)}) %collective-permute-start.24) | collective-permute-done | bytes 270368 | tf_op jit(solution)/shard_map/ppermute | solution.py:392
  109.0 6.0 %collective-permute-done.26.rest_26_ = bf16[528,256]{1,0:T(8,128)(2,1)} collective-permute-done((bf16[528,256]{1,0:T(8,128)(2,1)}, bf16[528,256]{1,0:T(8,128)(2,1)}, u32[]{:S(2)}, u32[]{:S(2)}) %collective-permute-start.26) | collective-permute-done | bytes 270368 | tf_op jit(solution)/shard_map/ppermute | solution.py:392
  115.0 5.2 %collective-permute-done.28.rest_28_ = bf16[528,256]{1,0:T(8,128)(2,1)} collective-permute-done((bf16[528,256]{1,0:T(8,128)(2,1)}, bf16[528,256]{1,0:T(8,128)(2,1)}, u32[]{:S(2)}, u32[]{:S(2)}) %collective-permute-start.28) | collective-permute-done | bytes 270368 | tf_op jit(solution)/shard_map/ppermute | solution.py:392
  122.5 9.2 %shard_map.96.scale_hbm = f32[16,512,128]{2,1,0:T(8,128)S(1)} custom-call(bf16[16,512,256]{2,1,0:T(8,128)(2,1)} %user_hbm.5), custom_call_target="tpu_custom_call" | custom-call | flops 8388608 | bytes 8388608 | tf_op jit(solution)/shard_map/pallas_call | solution.py:408
  131.8 2.0 copy-done
  136.9 17.2 %shard_map.98 = (f32[32,128]{1,0:T(8,128)S(1)}, f32[32,128]{1,0:T(8,128)S(1)}, f32[64,128]{1,0:T(8,128)S(1)}, f32[64,128]{1,0:T(8,128)S(1)}, f32[64,128]{1,0:T(8...) custom-call(s32[2]{0:T(128)S(1)} %pad_add_fusion.1.where_ref, s32[16]{0:T(128)S(1)} %copy-done.3, ...), custom_call_target="tpu_custom_call" | custom-call | tf_op jit(solution)/shard_map/pallas_call | solution.py:456
  155.5 20.6 %all_to_all.21 = bf16[16,32,128]{2,1,0:T(8,128)(2,1)S(1)} all-to-all(bf16[16,32,128]{2,1,0:T(8,128)(2,1)S(1)} %broadcast_in_dim.31), channel_id=1, replica_groups=mesh['shard'=16,'rep'=2] {'shard'}, dimensions={0} | all-to-all | bytes 262144 | tf_op jit(solution)/shard_map/all_to_all | solution.py:438
  177.4 10.2 %shard_map.99 = (f32[32,128]{1,0:T(8,128)S(1)}, f32[32,128]{1,0:T(8,128)S(1)}, f32[64,128]{1,0:T(8,128)S(1)}) custom-call(s32[2]{0:T(128)S(1)} %pad_add_fusion.1.where_ref, s32[16]{0:T(128)S(1)} %copy-done.3, f32[64,128]{1,0:T(8,128)S(1)} %get-tuple-element.56.duals_ref, f32[64,128]{1,0:T(8,128)S(1)} %get-tuple-element.57.live_ref, ...), custom_call_target="tpu_custom_call" | custom-call | tf_op jit(solution)/shard_map/pallas_call | solution.py:475
  188.9 10.7 %all_to_all.22 = bf16[16,32,128]{2,1,0:T(8,128)(2,1)S(1)} all-to-all(bf16[16,32,128]{2,1,0:T(8,128)(2,1)S(1)} %broadcast_in_dim.56), channel_id=1, replica_groups=mesh['shard'=16,'rep'=2] {'shard'}, dimensions={0} | all-to-all | bytes 262144 | tf_op jit(solution)/shard_map/all_to_all | solution.py:438
  201.0 9.9 %shard_map.100 = (f32[16,512]{1,0:T(8,128)}, f32[128,128]{1,0:T(8,128)}) custom-call(s32[2]{0:T(128)S(1)} %pad_add_fusion.1.where_ref, s32[16]{0:T(128)S(1)} %copy-done.3, f32[64,128]{1,0:T(8,128)S(1)} %get-tuple-element.64.duals_ref, f32[64,128]{1,0:T(8,128)S(1)} %get-tuple-element.57.live_ref, f32[64,128]{1,0:T(8,128)S(1)} %get-tuple-element.58.item_scale_ref, ...), custom_call_target="tpu_custom_call" | custom-call | tf_op jit(solution)/shard_map/pallas_call | solution.py:486
  (95 shorter events, 18.7 us)
Async XLA Ops:
  3.6 15.6 %all-to-all-start = ((s32[16,1,72]{2,1,0:T(1,128)}), s32[16,1,72]{2,1,0:T(1,128)S(1)}, u32[]{:S(2)}, u32[]{:S(2)}) async-start(s32[16,1,72]{2,1,0:T(1,128)} %bitcast.2), calls=%async_computation | async-start | bytes 16384 | tf_op jit(solution)/shard_map/all_to_all | solution.py:356
  22.4 31.9 %collective-permute-start.14 = (bf16[528,256]{1,0:T(8,128)(2,1)}, bf16[528,256]{1,0:T(8,128)(2,1)S(1)}, u32[]{:S(2)}, u32[]{:S(2)}) collective-permute-start(bf16[528,256]{1,0:T(8,128)(2,1)} %get-tuple-element.48), channel_id=1, source_target_pairs={{0,16},{2,18},{4,20},{6,22},{8,24},{10,26},{12,28},{14,30},{16,0},... | collective-permute-start | bytes 811016 | tf_op jit(solution)/shard_map/ppermute | solution.py:392
  23.0 37.1 %collective-permute-start.16 = (bf16[528,256]{1,0:T(8,128)(2,1)}, bf16[528,256]{1,0:T(8,128)(2,1)S(1)}, u32[]{:S(2)}, u32[]{:S(2)}) collective-permute-start(bf16[528,256]{1,0:T(8,128)(2,1)} %get-tuple-element.49), channel_id=1, source_target_pairs={{0,18},{2,16},{4,22},{6,20},{8,26},{10,24},{12,30},{14,28},{16,2},... | collective-permute-start | bytes 811016 | tf_op jit(solution)/shard_map/ppermute | solution.py:392
  25.7 40.6 %collective-permute-start.18 = (bf16[528,256]{1,0:T(8,128)(2,1)}, bf16[528,256]{1,0:T(8,128)(2,1)S(1)}, u32[]{:S(2)}, u32[]{:S(2)}) collective-permute-start(bf16[528,256]{1,0:T(8,128)(2,1)} %get-tuple-element.50), channel_id=1, source_target_pairs={{0,20},{2,22},{4,16},{6,18},{8,28},{10,30},{12,24},{14,26},{16,4},... | collective-permute-start | bytes 811016 | tf_op jit(solution)/shard_map/ppermute | solution.py:392
  27.5 44.6 %collective-permute-start.20 = (bf16[528,256]{1,0:T(8,128)(2,1)}, bf16[528,256]{1,0:T(8,128)(2,1)S(1)}, u32[]{:S(2)}, u32[]{:S(2)}) collective-permute-start(bf16[528,256]{1,0:T(8,128)(2,1)} %get-tuple-element.51), channel_id=1, source_target_pairs={{0,22},{2,20},{4,18},{6,16},{8,30},{10,28},{12,26},{14,24},{16,6},... | collective-permute-start | bytes 811016 | tf_op jit(solution)/shard_map/ppermute | solution.py:392
  35.7 36.4 %collective-permute-start = (bf16[528,256]{1,0:T(8,128)(2,1)}, bf16[528,256]{1,0:T(8,128)(2,1)S(1)}, u32[]{:S(2)}, u32[]{:S(2)}) collective-permute-start(bf16[528,256]{1,0:T(8,128)(2,1)} %get-tuple-element.35), channel_id=1, source_target_pairs={{0,4},{2,6},{4,0},{6,2},{8,12},{10,14},{12,8},{14,10},{16,20},{18,... | collective-permute-start | bytes 811016 | tf_op jit(solution)/shard_map/ppermute | solution.py:392
  54.3 21.3 %collective-permute-start.1 = (bf16[528,256]{1,0:T(8,128)(2,1)}, bf16[528,256]{1,0:T(8,128)(2,1)S(1)}, u32[]{:S(2)}, u32[]{:S(2)}) collective-permute-start(bf16[528,256]{1,0:T(8,128)(2,1)} %get-tuple-element.36), channel_id=1, source_target_pairs={{0,2},{2,0},{4,6},{6,4},{8,10},{10,8},{12,14},{14,12},{16,18},{18,... | collective-permute-start | bytes 811016 | tf_op jit(solution)/shard_map/ppermute | solution.py:392
  60.1 17.6 %collective-permute-start.4 = (bf16[528,256]{1,0:T(8,128)(2,1)}, bf16[528,256]{1,0:T(8,128)(2,1)S(1)}, u32[]{:S(2)}, u32[]{:S(2)}) collective-permute-start(bf16[528,256]{1,0:T(8,128)(2,1)} %get-tuple-element.43), channel_id=1, source_target_pairs={{0,6},{2,4},{4,2},{6,0},{8,14},{10,12},{12,10},{14,8},{16,22},{18,... | collective-permute-start | bytes 811016 | tf_op jit(solution)/shard_map/ppermute | solution.py:392
  66.2 14.8 %collective-permute-start.6 = (bf16[528,256]{1,0:T(8,128)(2,1)}, bf16[528,256]{1,0:T(8,128)(2,1)S(1)}, u32[]{:S(2)}, u32[]{:S(2)}) collective-permute-start(bf16[528,256]{1,0:T(8,128)(2,1)} %get-tuple-element.44), channel_id=1, source_target_pairs={{0,8},{2,10},{4,12},{6,14},{8,0},{10,2},{12,4},{14,6},{16,24},{18,... | collective-permute-start | bytes 811016 | tf_op jit(solution)/shard_map/ppermute | solution.py:392
  72.1 11.2 %collective-permute-start.8 = (bf16[528,256]{1,0:T(8,128)(2,1)}, bf16[528,256]{1,0:T(8,128)(2,1)S(1)}, u32[]{:S(2)}, u32[]{:S(2)}) collective-permute-start(bf16[528,256]{1,0:T(8,128)(2,1)} %get-tuple-element.45), channel_id=1, source_target_pairs={{0,10},{2,8},{4,14},{6,12},{8,2},{10,0},{12,6},{14,4},{16,26},{18,... | collective-permute-start | bytes 811016 | tf_op jit(solution)/shard_map/ppermute | solution.py:392
  72.1 16.7 %collective-permute-start.10 = (bf16[528,256]{1,0:T(8,128)(2,1)}, bf16[528,256]{1,0:T(8,128)(2,1)S(1)}, u32[]{:S(2)}, u32[]{:S(2)}) collective-permute-start(bf16[528,256]{1,0:T(8,128)(2,1)} %get-tuple-element.46), channel_id=1, source_target_pairs={{0,12},{2,14},{4,8},{6,10},{8,4},{10,6},{12,0},{14,2},{16,28},{18,... | collective-permute-start | bytes 811016 | tf_op jit(solution)/shard_map/ppermute | solution.py:392
  75.6 19.6 %collective-permute-start.12 = (bf16[528,256]{1,0:T(8,128)(2,1)}, bf16[528,256]{1,0:T(8,128)(2,1)S(1)}, u32[]{:S(2)}, u32[]{:S(2)}) collective-permute-start(bf16[528,256]{1,0:T(8,128)(2,1)} %get-tuple-element.47), channel_id=1, source_target_pairs={{0,14},{2,12},{4,10},{6,8},{8,6},{10,4},{12,2},{14,0},{16,30},{18,... | collective-permute-start | bytes 811016 | tf_op jit(solution)/shard_map/ppermute | solution.py:392
  77.7 25.5 %collective-permute-start.22 = (bf16[528,256]{1,0:T(8,128)(2,1)}, bf16[528,256]{1,0:T(8,128)(2,1)S(1)}, u32[]{:S(2)}, u32[]{:S(2)}) collective-permute-start(bf16[528,256]{1,0:T(8,128)(2,1)} %get-tuple-element.52), channel_id=1, source_target_pairs={{0,24},{2,26},{4,28},{6,30},{8,16},{10,18},{12,20},{14,22},{16,8},... | collective-permute-start | bytes 811016 | tf_op jit(solution)/shard_map/ppermute | solution.py:392
  81.0 28.0 %collective-permute-start.24 = (bf16[528,256]{1,0:T(8,128)(2,1)}, bf16[528,256]{1,0:T(8,128)(2,1)S(1)}, u32[]{:S(2)}, u32[]{:S(2)}) collective-permute-start(bf16[528,256]{1,0:T(8,128)(2,1)} %get-tuple-element.53), channel_id=1, source_target_pairs={{0,26},{2,24},{4,30},{6,28},{8,18},{10,16},{12,22},{14,20},{16,10}... | collective-permute-start | bytes 811016 | tf_op jit(solution)/shard_map/ppermute | solution.py:392
  83.3 31.7 %collective-permute-start.26 = (bf16[528,256]{1,0:T(8,128)(2,1)}, bf16[528,256]{1,0:T(8,128)(2,1)}, u32[]{:S(2)}, u32[]{:S(2)}) collective-permute-start(bf16[528,256]{1,0:T(8,128)(2,1)} %get-tuple-element.54), channel_id=1, source_target_pairs={{0,28},{2,30},{4,24},{6,26},{8,20},{10,22},{12,16},{14,18},{16,12}... | collective-permute-start | bytes 811016 | tf_op jit(solution)/shard_map/ppermute | solution.py:392
  88.9 31.4 %collective-permute-start.28 = (bf16[528,256]{1,0:T(8,128)(2,1)}, bf16[528,256]{1,0:T(8,128)(2,1)}, u32[]{:S(2)}, u32[]{:S(2)}) collective-permute-start(bf16[528,256]{1,0:T(8,128)(2,1)} %get-tuple-element.55), channel_id=1, source_target_pairs={{0,30},{2,28},{4,26},{6,24},{8,22},{10,20},{12,18},{14,16},{16,14}... | collective-permute-start | bytes 811016 | tf_op jit(solution)/shard_map/ppermute | solution.py:392
  95.2 26.9 %collective-permute-start.2 = (bf16[528,256]{1,0:T(8,128)(2,1)S(1)}, bf16[528,256]{1,0:T(8,128)(2,1)}, u32[]{:S(2)}, u32[]{:S(2)}) collective-permute-start(bf16[528,256]{1,0:T(8,128)(2,1)S(1)} %collective-permute-done.1.rest_0_), channel_id=1, source_target_pairs={{0,1},{1,0},{2,3},{3,2},{4,5},{5,4},{6,7},{7,6},{8,9},{9,8},{10,11... | collective-permute-start | bytes 811016 | tf_op jit(solution)/shard_map/ppermute | solution.py:432
  103.2 17.4 %collective-permute-start.15 = (bf16[528,256]{1,0:T(8,128)(2,1)S(1)}, bf16[528,256]{1,0:T(8,128)(2,1)}, u32[]{:S(2)}, u32[]{:S(2)}) collective-permute-start(bf16[528,256]{1,0:T(8,128)(2,1)S(1)} %collective-permute-done.14.rest_14_), channel_id=1, source_target_pairs={{0,1},{1,0},{2,3},{3,2},{4,5},{5,4},{6,7},{7,6},{8,9},{9,8},{10,11... | collective-permute-start | bytes 811016 | tf_op jit(solution)/shard_map/ppermute | solution.py:432
  109.0 12.2 %collective-permute-start.17 = (bf16[528,256]{1,0:T(8,128)(2,1)S(1)}, bf16[528,256]{1,0:T(8,128)(2,1)}, u32[]{:S(2)}, u32[]{:S(2)}) collective-permute-start(bf16[528,256]{1,0:T(8,128)(2,1)S(1)} %collective-permute-done.16.rest_16_), channel_id=1, source_target_pairs={{0,1},{1,0},{2,3},{3,2},{4,5},{5,4},{6,7},{7,6},{8,9},{9,8},{10,11... | collective-permute-start | bytes 811016 | tf_op jit(solution)/shard_map/ppermute | solution.py:432
  115.0 6.3 %collective-permute-start.19 = (bf16[528,256]{1,0:T(8,128)(2,1)S(1)}, bf16[528,256]{1,0:T(8,128)(2,1)}, u32[]{:S(2)}, u32[]{:S(2)}) collective-permute-start(bf16[528,256]{1,0:T(8,128)(2,1)S(1)} %collective-permute-done.18.rest_18_), channel_id=1, source_target_pairs={{0,1},{1,0},{2,3},{3,2},{4,5},{5,4},{6,7},{7,6},{8,9},{9,8},{10,11... | collective-permute-start | bytes 811016 | tf_op jit(solution)/shard_map/ppermute | solution.py:432
  120.2 1.7 collective-permute-start.21
  120.6 13.1 %collective-permute-start.5 = (bf16[528,256]{1,0:T(8,128)(2,1)S(1)}, bf16[528,256]{1,0:T(8,128)(2,1)S(1)}, u32[]{:S(2)}, u32[]{:S(2)}) collective-permute-start(bf16[528,256]{1,0:T(8,128)(2,1)S(1)} %collective-permute-done.4.rest_4_), channel_id=1, source_target_pairs={{0,1},{1,0},{2,3},{3,2},{4,5},{5,4},{6,7},{7,6},{8,9},{9,8},{10,11... | collective-permute-start | bytes 811016 | tf_op jit(solution)/shard_map/ppermute | solution.py:432
  121.2 12.8 %collective-permute-start.7 = (bf16[528,256]{1,0:T(8,128)(2,1)S(1)}, bf16[528,256]{1,0:T(8,128)(2,1)S(1)}, u32[]{:S(2)}, u32[]{:S(2)}) collective-permute-start(bf16[528,256]{1,0:T(8,128)(2,1)S(1)} %collective-permute-done.6.rest_6_), channel_id=1, source_target_pairs={{0,1},{1,0},{2,3},{3,2},{4,5},{5,4},{6,7},{7,6},{8,9},{9,8},{10,11... | collective-permute-start | bytes 811016 | tf_op jit(solution)/shard_map/ppermute | solution.py:432
  121.3 13.1 %collective-permute-start.9 = (bf16[528,256]{1,0:T(8,128)(2,1)S(1)}, bf16[528,256]{1,0:T(8,128)(2,1)S(1)}, u32[]{:S(2)}, u32[]{:S(2)}) collective-permute-start(bf16[528,256]{1,0:T(8,128)(2,1)S(1)} %collective-permute-done.8.rest_8_), channel_id=1, source_target_pairs={{0,1},{1,0},{2,3},{3,2},{4,5},{5,4},{6,7},{7,6},{8,9},{9,8},{10,11... | collective-permute-start | bytes 811016 | tf_op jit(solution)/shard_map/ppermute | solution.py:432
  121.9 12.6 %collective-permute-start.11 = (bf16[528,256]{1,0:T(8,128)(2,1)S(1)}, bf16[528,256]{1,0:T(8,128)(2,1)S(1)}, u32[]{:S(2)}, u32[]{:S(2)}) collective-permute-start(bf16[528,256]{1,0:T(8,128)(2,1)S(1)} %collective-permute-done.10.rest_10_), channel_id=1, source_target_pairs={{0,1},{1,0},{2,3},{3,2},{4,5},{5,4},{6,7},{7,6},{8,9},{9,8},{10,11... | collective-permute-start | bytes 811016 | tf_op jit(solution)/shard_map/ppermute | solution.py:432
  122.1 12.8 %collective-permute-start.13 = (bf16[528,256]{1,0:T(8,128)(2,1)S(1)}, bf16[528,256]{1,0:T(8,128)(2,1)S(1)}, u32[]{:S(2)}, u32[]{:S(2)}) collective-permute-start(bf16[528,256]{1,0:T(8,128)(2,1)S(1)} %collective-permute-done.12.rest_12_), channel_id=1, source_target_pairs={{0,1},{1,0},{2,3},{3,2},{4,5},{5,4},{6,7},{7,6},{8,9},{9,8},{10,11... | collective-permute-start | bytes 811016 | tf_op jit(solution)/shard_map/ppermute | solution.py:432
  133.8 1.6 collective-permute-start.23
  134.0 1.8 collective-permute-start.25
  134.4 1.8 collective-permute-start.27
  134.5 2.0 collective-permute-start.29
  134.9 2.1 collective-permute-start.3
  176.0 1.3 collective-permute-start.31
  (7 other events, 67.4 us)

commit v4 on v3

--- a/solution.py
+++ b/solution.py
@@ -42,15 +42,16 @@
     return pl.ds(half * camps + j // across * pieces, pieces), pl.ds(j % across * camps, camps)
 
 
-def gather_kernel(half, shifts, where_ref, asked_ref, camp_ref, fact_ref, *rest):
+def gather_kernel(half, sends, where_ref, asked_ref, camp_ref, fact_ref, *rest):
     outs, (stage, sem) = rest[:-2], rest[-2:]
     me, rep = where_ref[0], where_ref[1]
     _, camps, width = camp_ref.shape
+    pieces = fact_ref.shape[1]
     arriving, leaving = [], []
-    for n, (shift, out) in enumerate(zip(shifts, outs)):
+    for n, ((shift, other), out) in enumerate(zip(sends, outs)):
         for j in range(half):
-            block = asked_ref[me ^ shift, rep * half + j]
-            rows, lanes = fact_place(j, half, camps, fact_ref.shape[1], width)
+            block = asked_ref[me ^ shift, (1 - rep if other else rep) * half + j]
+            rows, lanes = fact_place(j, half, camps, pieces, width)
             for copy in (
                 pltpu.make_async_copy(
                     camp_ref.at[block], stage.at[n, pl.ds(j * camps, camps)], sem.at[0, n * half + j]
@@ -60,9 +61,26 @@
                 copy.start()
                 arriving.append(copy)
         leaving.append(pltpu.make_async_copy(stage.at[n], out, sem.at[2, n]))
-    for n, copy in enumerate(leaving):
-        for part in arriving[2 * half * n : 2 * half * (n + 1)]:
-            part.wait()
+    for copy in arriving:
+        copy.wait()
+    eye = lax.broadcasted_iota(jnp.int32, (camps, camps), 0) == lax.broadcasted_iota(jnp.int32, (camps, camps), 1)
+    piece = lax.broadcasted_iota(jnp.int32, (pieces, camps), 0)
+
+    def scales(n, carry):
+        for j in range(half):
+            block = stage[n, j * camps : (j + 1) * camps].astype(jnp.float32)
+            total = jnp.broadcast_to(jnp.sum(block * block, axis=1, keepdims=True), (camps, camps))
+            total = jnp.sum(jnp.where(eye, total, 0.0), axis=0, keepdims=True)
+            rows, lanes = fact_place(j, half, camps, pieces, width)
+            facts = stage[n, rows, lanes].astype(jnp.float32)
+            scale = lax.rsqrt(total * (1.0 / width) + epsilon) * facts[pieces - 2 : pieces - 1]
+            high = scale.astype(jnp.bfloat16).astype(jnp.float32)
+            facts = jnp.where(piece == pieces - 2, high, jnp.where(piece == pieces - 1, scale - high, facts))
+            stage[n, rows, lanes] = facts.astype(stage.dtype)
+        return carry
+
+    lax.fori_loop(0, len(sends), scales, 0, unroll=3 if len(sends) % 3 == 0 else 2 if len(sends) % 2 == 0 else 1)
+    for copy in leaving:
         copy.start()
     for copy in leaving:
         copy.wait()
@@ -170,8 +188,8 @@
             for e in range(fanout):
                 spend_scr[pl.ds(k * fanout + e, 1), :] = jnp.sum(sums[e], axis=0, keepdims=True)
             return 0
-        place = where_ref[1] * users + start + lax.broadcasted_iota(jnp.int32, (rows, 1), 0)
-        share = jnp.where(place < size_ref[k], 1.0 / den, 0.0)
+        left = size_ref[k] - where_ref[1] * users - start
+        share = jnp.where(lax.broadcasted_iota(jnp.int32, (rows, 1), 0) < left, 1.0 / den, 0.0)
         out = []
         for e in range(fanout):
             part = weights[e] * share
@@ -192,9 +210,7 @@
 
 
 def item_facts(fact_ref, item_ref, item_sem, fact_sem, dual_ref, limit_ref, live_ref, item_scale_ref):
-    items, camps = dual_ref.shape
-    width = item_ref.shape[2]
-    eye = lax.broadcasted_iota(jnp.int32, (camps, camps), 0) == lax.broadcasted_iota(jnp.int32, (camps, camps), 1)
+    items = dual_ref.shape[0]
 
     def wait(item, carry):
         item_landed(item, item_ref, item_sem)
@@ -203,37 +219,26 @@
 
     lax.fori_loop(0, items, wait, 0, unroll=8)
     group = 8
-
-    def some(n, carry):
-        first = pl.multiple_of(n * group, group)
-        facts = fact_ref[pl.ds(first, group)].astype(jnp.float32)
-        dual_ref[pl.ds(first, group), :] = facts[:, 0] + facts[:, 1] + facts[:, 2]
-        limit_ref[pl.ds(first, group), :] = facts[:, 3] + facts[:, 4] + facts[:, 5]
-        live_ref[pl.ds(first, group), :] = facts[:, 6]
-        totals_here = []
-        for e in range(group):
-            rows = item_ref[first + e].astype(jnp.float32)
-            total = jnp.broadcast_to(jnp.sum(rows * rows, axis=1, keepdims=True), (camps, camps))
-            totals_here.append(jnp.sum(jnp.where(eye, total, 0.0), axis=0, keepdims=True))
-        mean = jnp.concatenate(totals_here, axis=0) * (1.0 / width)
-        item_scale_ref[pl.ds(first, group), :] = lax.rsqrt(mean + epsilon)
-        return carry
-
-    lax.fori_loop(0, items // group, some, 0)
+    for first in range(0, items, group):
+        facts = fact_ref[first : first + group].astype(jnp.float32)
+        here = slice(first, first + group)
+        dual_ref[here, :] = facts[:, 0] + facts[:, 1] + facts[:, 2]
+        limit_ref[here, :] = facts[:, 3] + facts[:, 4] + facts[:, 5]
+        live_ref[here, :] = facts[:, 6]
+        item_scale_ref[here, :] = facts[:, 6] + facts[:, 7]
 
 
 def first_kernel(
-    shards, half, fanout, where_ref, size_ref, item_at_ref, own_ref, user_hbm, scale_hbm, camp_ref, fact_ref, *rest
+    shards, half, fanout, camps, pieces, where_ref, size_ref, item_at_ref, user_hbm, scale_hbm, *rest
 ):
-    received, outs = rest[: 2 * (shards - 1)], rest[2 * (shards - 1) :][:7]
+    received, outs = rest[: 2 * shards], rest[2 * shards :][:7]
     mine_ref, theirs_ref, duals_ref, limit_ref, live_ref, item_scale_ref, item_out = outs
     user_ref, scale_ref, item_ref, row_sem, item_sem, dots_a, dots_b, dual_scr, spend_scr = rest[-12:-3]
     landed_ref, fact_sem, out_sem = rest[-3:]
     cap = 2 * half
     rep = where_ref[1]
     users = user_ref.shape[1]
-    _, camps, width = camp_ref.shape
-    pieces = fact_ref.shape[1]
+    width = item_ref.shape[2]
 
     def fetch(slot, block, facts):
         item = item_at_ref[slot]
@@ -243,18 +248,16 @@
             pltpu.make_async_copy(block, item_ref.at[item], item_sem.at[item]).start()
             pltpu.make_async_copy(facts, landed_ref.at[item], fact_sem.at[item]).start()
 
-    for j in range(cap):
-        fetch(j, camp_ref.at[own_ref[j]], fact_ref.at[own_ref[j]])
-    for n in range(shards - 1):
+    for n in range(shards):
         for j in range(half):
             for side, message in ((rep, received[2 * n]), (1 - rep, received[2 * n + 1])):
                 rows, lanes = fact_place(j, half, camps, pieces, width)
-                fetch((n + 1) * cap + side * half + j, message.at[pl.ds(j * camps, camps)], message.at[rows, lanes])
+                fetch(n * cap + side * half + j, message.at[pl.ds(j * camps, camps)], message.at[rows, lanes])
     start_rows(user_hbm, scale_hbm, user_ref, scale_ref, row_sem)
     item_facts(landed_ref, item_ref, item_sem, fact_sem, duals_ref, limit_ref, live_ref, item_scale_ref)
     keep = pltpu.make_async_copy(item_ref, item_out, out_sem)
     keep.start()
-    dual_scr[...] = jnp.where(live_ref[...] > 0.5, duals_ref[...] * gain, masked)
+    dual_scr[...] = jnp.where(live_ref[...] > 0.0, duals_ref[...] * gain, masked)
     finish = spend_finish(where_ref, size_ref, users, fanout, spend_scr)
     sweep_users(
         user_hbm, scale_hbm, user_ref, scale_ref, item_ref, row_sem, None, item_scale_ref,
@@ -273,7 +276,7 @@
     start_rows(user_hbm, scale_hbm, user_ref, scale_ref, row_sem)
     duals = updated(duals_ref[...], totals(match_ref, got_ref, other_ref), limit_ref[...])
     next_ref[...] = duals
-    dual_scr[...] = jnp.where(live_ref[...] > 0.5, duals * gain, masked)
+    dual_scr[...] = jnp.where(live_ref[...] > 0.0, duals * gain, masked)
     finish = spend_finish(where_ref, size_ref, user_ref.shape[1], fanout, spend_scr)
     sweep_users(
         user_hbm, scale_hbm, user_ref, scale_ref, item_ref, row_sem, item_sem, item_scale_ref,
@@ -290,7 +293,7 @@
     start_items(item_hbm, item_ref, item_sem)
     start_rows(user_hbm, scale_hbm, user_ref, scale_ref, row_sem)
     duals = updated(duals_ref[...], totals(match_ref, got_ref, other_ref), limit_ref[...])
-    dual_scr[...] = jnp.where(live_ref[...] > 0.5, duals * gain, masked)
+    dual_scr[...] = jnp.where(live_ref[...] > 0.0, duals * gain, masked)
     own = updated(own_dual_ref[...], totals(own_match_ref, got_one_ref, other_one_ref), own_limit_ref[...])
     own_out_ref[...] = updated(own, totals(own_match_ref, got_ref, other_ref), own_limit_ref[...])
     users = user_ref.shape[1]
@@ -343,8 +346,10 @@
     swap = [(0, 1), (1, 0)]
     f32 = jnp.float32
 
-    owners = elig_owner.reshape(-1)
-    locals_ = elig_local.reshape(-1)
+    owners = elig_owner.T.reshape(-1)
+    locals_ = elig_local.T.reshape(-1)
+    asked = jnp.arange(items, dtype=jnp.int32)
+    item_ids = asked % clusters * fanout + asked // clusters
     shard_ids = jnp.arange(shards, dtype=jnp.int32)
     hot = (owners[:, None] == shard_ids[None, :]).astype(jnp.int32)
     rank = jnp.sum((jnp.cumsum(hot, axis=0) - hot) * hot, axis=1)
@@ -372,39 +377,40 @@
 
     order = send_order(shards)
     sent = {}
-    for shifts in (order[:4], order[4:]):
+    sends = [(shift, False) for shift in order] + [(0, False), (0, True)]
+    for some in (sends[:2], sends[2:]):
         outs = pl.pallas_call(
-            functools.partial(gather_kernel, half, shifts),
-            out_shape=[pltpu.HBM((message, width), camp_emb.dtype)] * len(shifts),
+            functools.partial(gather_kernel, half, some),
+            out_shape=[pltpu.HBM((message, width), camp_emb.dtype)] * len(some),
             in_specs=[SMEM, SMEM, HBM, HBM],
-            out_specs=[HBM] * len(shifts),
+            out_specs=[HBM] * len(some),
             scratch_shapes=[
-                pltpu.VMEM((len(shifts), message, width), camp_emb.dtype),
-                pltpu.SemaphoreType.DMA((3, len(shifts) * half)),
+                pltpu.VMEM((len(some), message, width), camp_emb.dtype),
+                pltpu.SemaphoreType.DMA((3, len(some) * half)),
             ],
-            compiler_params=pltpu.CompilerParams(vmem_limit_bytes=8 * 2**20),
-            cost_estimate=pl.CostEstimate(flops=0, bytes_accessed=len(shifts) * 2**19, transcendentals=0),
+            compiler_params=pltpu.CompilerParams(vmem_limit_bytes=12 * 2**20),
+            cost_estimate=pl.CostEstimate(flops=0, bytes_accessed=len(some) * 2**19, transcendentals=0),
         )(where, heard, camp_rows, facts)
-        sent.update(zip(shifts, outs))
+        sent.update(zip(some, outs))
 
     got_blocks = {}
     for shift in order:
-        got_blocks[shift] = lax.ppermute(sent[shift], "shard", [(i, i ^ shift) for i in range(shards)])
+        got_blocks[shift] = lax.ppermute(sent[shift, False], "shard", [(i, i ^ shift) for i in range(shards)])
 
     heard, user_late, _ = lax.optimization_barrier((heard, user_emb, got_blocks[1]))
-    all_names = heard[:, cap:]
+    all_names = heard[:, cap:].reshape(shards, fanout, clusters).transpose(0, 2, 1).reshape(shards, items)
+    names = names.reshape(fanout, clusters).T.reshape(-1)
     item_of_slot = (
         jnp.sum(
             jnp.where(
                 ((owners ^ me) * cap + rank)[:, None] == jnp.arange(shards * cap, dtype=jnp.int32)[None, :],
-                jnp.arange(1, items + 1, dtype=jnp.int32)[:, None],
+                (item_ids + 1)[:, None],
                 0,
             ),
             axis=0,
         )
         - 1
     )
-    own_wanted = lax.dynamic_slice_in_dim(wanted, me, 1, 0).reshape(cap)
     user_scale = pl.pallas_call(
         user_kernel,
         out_shape=jax.ShapeDtypeStruct((clusters, users, camps), f32),
@@ -424,10 +430,10 @@
     own_match = jnp.stack([(own_names[:, None] == side).astype(jnp.bfloat16) for side in sides])
 
     gate = 2
-    got_blocks[gate], item_of_slot, own_wanted, user_scale, match, own_match = lax.optimization_barrier(
-        (got_blocks[gate], item_of_slot, own_wanted, user_scale, match, own_match)
+    got_blocks[gate], item_of_slot, user_scale, match, own_match = lax.optimization_barrier(
+        (got_blocks[gate], item_of_slot, user_scale, match, own_match)
     )
-    received = []
+    received = [sent[0, False], sent[0, True]]
     for shift in range(1, shards):
         received += [got_blocks[shift], lax.ppermute(got_blocks[shift], "rep", swap)]
     user_rows, user_scale = in_hbm(user_emb), in_hbm(user_scale)
@@ -454,11 +460,11 @@
     limits = pltpu.CompilerParams(vmem_limit_bytes=24 * 2**20)
 
     mine, theirs, item_dual, item_limit, item_live, item_scale, item_emb = pl.pallas_call(
-        functools.partial(first_kernel, shards, half, fanout),
+        functools.partial(first_kernel, shards, half, fanout, camps, len(rows)),
         out_shape=spend_out
         + [jax.ShapeDtypeStruct((items, camps), f32)] * 4
         + [pltpu.HBM((items, camps, width), camp_emb.dtype)],
-        in_specs=[SMEM] * 4 + [HBM] * 4 + [ANY] * len(received),
+        in_specs=[SMEM] * 3 + [HBM] * 2 + [ANY] * len(received),
         out_specs=[VMEM] * 6 + [HBM],
         scratch_shapes=work
         + spend_work
@@ -468,7 +474,7 @@
             pltpu.SemaphoreType.DMA,
         ],
         compiler_params=limits,
-    )(where, cluster_size, item_of_slot, own_wanted, user_rows, user_scale, camp_rows, facts, *received)
+    )(where, cluster_size, item_of_slot, user_rows, user_scale, *received)
     item_emb = in_hbm(item_emb)
     got_one, other_one = exchange(mine, theirs)
 

time: 212 us -> 220 us (1.038)
  blocking collectives: 31.3 us -> 43.9 us
  waiting for transfers between devices: 76.8 us -> 65 us
  local copies, waits for them, and re-layouts: 6.7 us -> 11 us
    all_to_all x2, blocking collectives: 31.3 us -> 43.9 us  [exchange(): lax.all_to_all(spread, 'shard', split_axis=0, concat_axis=0, tiled=True)]
    ppermute x15, waiting for transfers between devices: 67 us -> 55.4 us  [program(): lax.ppermute(sent[shift, False], 'shard', [(i, i ^ shift) for i in range(...]
    reshape x2 -> x3, local copies, waits for them, and re-layouts: 0.09 us -> 2.91 us  [the longest x2 2.15 us: program(): heard[:, cap:].reshape(shards, fanout, clusters).transpose(0, 2, 1)]
  transfers between devices with their start and end apart: 35 -> 35, of which waited for: 23 -> 17; matrix products, arithmetic and copies ran while one was open for 2% -> 5% of each run, Pallas kernels for 7% -> 8%
where the time goes in v4:
time: 220 us; the launch traced here: 219 us
  waiting for transfers between devices  65 us (30%)
  Pallas kernels  56.4 us (26%)
  blocking collectives  43.9 us (20%)
  starting transfers between devices  37.2 us (17%)
  local copies, waits for them, and re-layouts  11 us (5%)
  other arithmetic  4.48 us (2%)
    ppermute x15, waiting for transfers between devices, program(): lax.ppermute(sent[shift, False], 'shard', [(i, i ^ shift) for i in range(...  55.4 us
    all_to_all x2, blocking collectives, exchange(): lax.all_to_all(spread, 'shard', split_axis=0, concat_axis=0, tiled=True)  43.9 us
    ppermute x15, starting transfers between devices, program(): lax.ppermute(sent[shift, False], 'shard', [(i, i ^ shift) for i in range(...  24.7 us
    pallas_call x1, Pallas kernels, program(): pl.pallas_call(functools.partial(first_kernel, shards, half, fanout, camp...  15.6 us
    pallas_call x2, Pallas kernels, program(): pl.pallas_call(functools.partial(gather_kernel, half, some), out_shape=[p...  11.8 us
    pallas_call x1, Pallas kernels, program(): pl.pallas_call(functools.partial(second_kernel, fanout), out_shape=spend_...  9.96 us
    pallas_call x1, Pallas kernels, program(): pl.pallas_call(functools.partial(third_kernel, fanout), out_shape=[jax.Sh...  9.77 us
    pallas_call x1, Pallas kernels, program(): pl.pallas_call(user_kernel, out_shape=jax.ShapeDtypeStruct((clusters, use...  9.25 us
  transfers between devices with their start and end apart: 35, of which 17 were waited for; matrix products, arithmetic and copies ran while one was open for 5% of the time, Pallas kernels for 8%

profile of v4, /device:TPU:0, one launch (start us, length us, event | category | flops | bytes accessed | tf_op | source)
XLA Modules:
  0.0 218.9 jit_solution(12280282491164771307)
XLA Ops:
  3.4 8.3 %all-to-all-start = ((s32[16,1,72]{2,1,0:T(1,128)}), s32[16,1,72]{2,1,0:T(1,128)S(1)}, u32[]{:S(2)}, u32[]{:S(2)}) async-start(s32[16,1,72]{2,1,0:T(1,128)} %bitcast.4), calls=%async_computation | async-start | bytes 16384 | tf_op jit(solution)/shard_map/all_to_all | solution.py:361
  14.8 1.5 stack.63.fact_ref
  16.2 2.7 %all-to-all-done = s32[16,1,72]{2,1,0:T(1,128)S(1)} async-done(((s32[16,1,72]{2,1,0:T(1,128)}), s32[16,1,72]{2,1,0:T(1,128)S(1)}, u32[]{:S(2)}, u32[]{:S(2)}) %all-to-all-start) | async-done | bytes 4640 | tf_op jit(solution)/shard_map/all_to_all | solution.py:361
  19.0 3.0 %shard_map.97 = (bf16[528,256]{1,0:T(8,128)(2,1)}, bf16[528,256]{1,0:T(8,128)(2,1)}) custom-call(s32[2]{0:T(128)S(1)} %pad_add_fusion.1.where_ref, s32[16,72]{1,0:T(8,128)S(1)} %bitcast.29, bf16[128,128,256]{2,1,0:T(8,128)(2,1)} %camp_ref.3, bf16[128,8,128]{2,1,0:T(8,128)(2,1)} %stack.63.fact_ref), custom_call_target="tpu_custom_call" | custom-call | bytes 1048576 | tf_op jit(solution)/shard_map/pallas_call | solution.py:382
  22.7 2.4 %collective-permute-start.16 = (bf16[528,256]{1,0:T(8,128)(2,1)}, bf16[528,256]{1,0:T(8,128)(2,1)S(1)}, u32[]{:S(2)}, u32[]{:S(2)}) collective-permute-start(bf16[528,256]{1,0:T(8,128)(2,1)} %get-tuple-element.51), channel_id=1, source_target_pairs={{0,18},{2,16},{4,22},{6,20},{8,26},{10,24},{12,30},{14,28},{16,2},... | collective-permute-start | bytes 811016 | tf_op jit(solution)/shard_map/ppermute | solution.py:398
  25.1 8.8 %shard_map.95 = (bf16[528,256]{1,0:T(8,128)(2,1)}, bf16[528,256]{1,0:T(8,128)(2,1)}, bf16[528,256]{1,0:T(8,128)(2,1)}, bf16[528,256]{1,0:T(8,128)(2,1)}, bf16[52...) custom-call(s32[2]{0:T(128)S(1)} %pad_add_fusion.1.where_ref, ...), custom_call_target="tpu_custom_call" | custom-call | bytes 7864320 | tf_op jit(solution)/shard_map/pallas_call | solution.py:382
  34.0 2.2 %collective-permute-start.1 = (bf16[528,256]{1,0:T(8,128)(2,1)}, bf16[528,256]{1,0:T(8,128)(2,1)S(1)}, u32[]{:S(2)}, u32[]{:S(2)}) collective-permute-start(bf16[528,256]{1,0:T(8,128)(2,1)} %get-tuple-element.37), channel_id=1, source_target_pairs={{0,2},{2,0},{4,6},{6,4},{8,10},{10,8},{12,14},{14,12},{16,18},{18,... | collective-permute-start | bytes 811016 | tf_op jit(solution)/shard_map/ppermute | solution.py:398
  36.2 1.2 collective-permute-start.4
  37.4 4.4 %collective-permute-done.14.rest_16_ = bf16[528,256]{1,0:T(8,128)(2,1)S(1)} collective-permute-done((bf16[528,256]{1,0:T(8,128)(2,1)}, bf16[528,256]{1,0:T(8,128)(2,1)S(1)}, u32[]{:S(2)}, u32[]{:S(2)}) %collective-permute-start.14) | collective-permute-done | bytes 270368 | tf_op jit(solution)/shard_map/ppermute | solution.py:398
  41.8 5.9 %collective-permute-done.16.rest_18_ = bf16[528,256]{1,0:T(8,128)(2,1)S(1)} collective-permute-done((bf16[528,256]{1,0:T(8,128)(2,1)}, bf16[528,256]{1,0:T(8,128)(2,1)S(1)}, u32[]{:S(2)}, u32[]{:S(2)}) %collective-permute-start.16) | collective-permute-done | bytes 270368 | tf_op jit(solution)/shard_map/ppermute | solution.py:398
  47.7 2.8 %collective-permute-start.10 = (bf16[528,256]{1,0:T(8,128)(2,1)}, bf16[528,256]{1,0:T(8,128)(2,1)S(1)}, u32[]{:S(2)}, u32[]{:S(2)}) collective-permute-start(bf16[528,256]{1,0:T(8,128)(2,1)} %get-tuple-element.48), channel_id=1, source_target_pairs={{0,12},{2,14},{4,8},{6,10},{8,4},{10,6},{12,0},{14,2},{16,28},{18,... | collective-permute-start | bytes 811016 | tf_op jit(solution)/shard_map/ppermute | solution.py:398
  51.5 10.2 %collective-permute-done.4.rest_6_ = bf16[528,256]{1,0:T(8,128)(2,1)S(1)} collective-permute-done((bf16[528,256]{1,0:T(8,128)(2,1)}, bf16[528,256]{1,0:T(8,128)(2,1)S(1)}, u32[]{:S(2)}, u32[]{:S(2)}) %collective-permute-start.4) | collective-permute-done | bytes 270368 | tf_op jit(solution)/shard_map/ppermute | solution.py:398
  61.8 5.3 %collective-permute-start.20 = (bf16[528,256]{1,0:T(8,128)(2,1)}, bf16[528,256]{1,0:T(8,128)(2,1)S(1)}, u32[]{:S(2)}, u32[]{:S(2)}) collective-permute-start(bf16[528,256]{1,0:T(8,128)(2,1)} %get-tuple-element.53), channel_id=1, source_target_pairs={{0,22},{2,20},{4,18},{6,16},{8,30},{10,28},{12,26},{14,24},{16,6},... | collective-permute-start | bytes 811016 | tf_op jit(solution)/shard_map/ppermute | solution.py:398
  67.9 5.2 %collective-permute-done.10.rest_12_ = bf16[528,256]{1,0:T(8,128)(2,1)S(1)} collective-permute-done((bf16[528,256]{1,0:T(8,128)(2,1)}, bf16[528,256]{1,0:T(8,128)(2,1)S(1)}, u32[]{:S(2)}, u32[]{:S(2)}) %collective-permute-start.10) | collective-permute-done | bytes 270368 | tf_op jit(solution)/shard_map/ppermute | solution.py:398
  73.1 4.1 %collective-permute-start.24 = (bf16[528,256]{1,0:T(8,128)(2,1)}, bf16[528,256]{1,0:T(8,128)(2,1)S(1)}, u32[]{:S(2)}, u32[]{:S(2)}) collective-permute-start(bf16[528,256]{1,0:T(8,128)(2,1)} %get-tuple-element.55), channel_id=1, source_target_pairs={{0,26},{2,24},{4,30},{6,28},{8,18},{10,16},{12,22},{14,20},{16,10}... | collective-permute-start | bytes 811016 | tf_op jit(solution)/shard_map/ppermute | solution.py:398
  77.3 1.7 collective-permute-done.12.rest_14_
  79.0 25.6 %collective-permute-done.18.rest_20_ = bf16[528,256]{1,0:T(8,128)(2,1)S(1)} collective-permute-done((bf16[528,256]{1,0:T(8,128)(2,1)}, bf16[528,256]{1,0:T(8,128)(2,1)S(1)}, u32[]{:S(2)}, u32[]{:S(2)}) %collective-permute-start.18) | collective-permute-done | bytes 270368 | tf_op jit(solution)/shard_map/ppermute | solution.py:398
  104.6 4.2 %collective-permute-start.28 = (bf16[528,256]{1,0:T(8,128)(2,1)}, bf16[528,256]{1,0:T(8,128)(2,1)}, u32[]{:S(2)}, u32[]{:S(2)}) collective-permute-start(bf16[528,256]{1,0:T(8,128)(2,1)} %get-tuple-element.57), channel_id=1, source_target_pairs={{0,30},{2,28},{4,26},{6,24},{8,22},{10,20},{12,18},{14,16},{16,14}... | collective-permute-start | bytes 811016 | tf_op jit(solution)/shard_map/ppermute | solution.py:398
  110.3 1.4 copy.67
  112.8 2.3 %collective-permute-done.28.rest_30_ = bf16[528,256]{1,0:T(8,128)(2,1)} collective-permute-done((bf16[528,256]{1,0:T(8,128)(2,1)}, bf16[528,256]{1,0:T(8,128)(2,1)}, u32[]{:S(2)}, u32[]{:S(2)}) %collective-permute-start.28) | collective-permute-done | bytes 270368 | tf_op jit(solution)/shard_map/ppermute | solution.py:398
  115.1 1.3 constant_dynamic-slice_fusion.1
  120.0 9.2 %shard_map.96.scale_hbm = f32[16,512,128]{2,1,0:T(8,128)S(1)} custom-call(bf16[16,512,256]{2,1,0:T(8,128)(2,1)} %user_hbm.5), custom_call_target="tpu_custom_call" | custom-call | flops 8388608 | bytes 8388608 | tf_op jit(solution)/shard_map/pallas_call | solution.py:414
  129.2 2.0 copy-done
  134.5 15.6 %shard_map.98 = (f32[32,128]{1,0:T(8,128)S(1)}, f32[32,128]{1,0:T(8,128)S(1)}, f32[64,128]{1,0:T(8,128)S(1)}, f32[64,128]{1,0:T(8,128)S(1)}, f32[64,128]{1,0:T(8...) custom-call(s32[2]{0:T(128)S(1)} %pad_add_fusion.1.where_ref, s32[16]{0:T(128)S(1)} %copy-done.5, ...), custom_call_target="tpu_custom_call" | custom-call | tf_op jit(solution)/shard_map/pallas_call | solution.py:462
  150.1 1.2 collective-permute-done.30
  151.3 33.2 %all_to_all.21 = bf16[16,32,128]{2,1,0:T(8,128)(2,1)S(1)} all-to-all(bf16[16,32,128]{2,1,0:T(8,128)(2,1)S(1)} %broadcast_in_dim.53), channel_id=1, replica_groups=mesh['shard'=16,'rep'=2] {'shard'}, dimensions={0} | all-to-all | bytes 262144 | tf_op jit(solution)/shard_map/all_to_all | solution.py:444
  184.5 1.3 collective-permute-done.31.other_ref.other_one_ref
  185.8 10.0 %shard_map.99 = (f32[32,128]{1,0:T(8,128)S(1)}, f32[32,128]{1,0:T(8,128)S(1)}, f32[64,128]{1,0:T(8,128)S(1)}) custom-call(s32[2]{0:T(128)S(1)} %pad_add_fusion.1.where_ref, s32[16]{0:T(128)S(1)} %copy-done.5, f32[64,128]{1,0:T(8,128)S(1)} %get-tuple-element.58.duals_ref, f32[64,128]{1,0:T(8,128)S(1)} %get-tuple-element.59.live_ref, ...), custom_call_target="tpu_custom_call" | custom-call | tf_op jit(solution)/shard_map/pallas_call | solution.py:481
  196.0 1.0 collective-permute-done.32
  197.1 10.7 %all_to_all.22 = bf16[16,32,128]{2,1,0:T(8,128)(2,1)S(1)} all-to-all(bf16[16,32,128]{2,1,0:T(8,128)(2,1)S(1)} %broadcast_in_dim.54), channel_id=1, replica_groups=mesh['shard'=16,'rep'=2] {'shard'}, dimensions={0} | all-to-all | bytes 262144 | tf_op jit(solution)/shard_map/all_to_all | solution.py:444
  207.8 1.3 collective-permute-done.33.other_ref
  209.2 9.8 %shard_map.100 = (f32[16,512]{1,0:T(8,128)}, f32[128,128]{1,0:T(8,128)}) custom-call(s32[2]{0:T(128)S(1)} %pad_add_fusion.1.where_ref, s32[16]{0:T(128)S(1)} %copy-done.5, f32[64,128]{1,0:T(8,128)S(1)} %get-tuple-element.66.duals_ref, f32[64,128]{1,0:T(8,128)S(1)} %get-tuple-element.59.live_ref, f32[64,128]{1,0:T(8,128)S(1)} %get-tuple-element.60.item_scale_ref, ...), custom_call_target="tpu_custom_call" | custom-call | tf_op jit(solution)/shard_map/pallas_call | solution.py:492
  (107 shorter events, 17.9 us)
Async XLA Ops:
  3.4 15.6 %all-to-all-start = ((s32[16,1,72]{2,1,0:T(1,128)}), s32[16,1,72]{2,1,0:T(1,128)S(1)}, u32[]{:S(2)}, u32[]{:S(2)}) async-start(s32[16,1,72]{2,1,0:T(1,128)} %bitcast.4), calls=%async_computation | async-start | bytes 16384 | tf_op jit(solution)/shard_map/all_to_all | solution.py:361
  22.0 19.8 %collective-permute-start.14 = (bf16[528,256]{1,0:T(8,128)(2,1)}, bf16[528,256]{1,0:T(8,128)(2,1)S(1)}, u32[]{:S(2)}, u32[]{:S(2)}) collective-permute-start(bf16[528,256]{1,0:T(8,128)(2,1)} %get-tuple-element.50), channel_id=1, source_target_pairs={{0,16},{2,18},{4,20},{6,22},{8,24},{10,26},{12,28},{14,30},{16,0},... | collective-permute-start | bytes 811016 | tf_op jit(solution)/shard_map/ppermute | solution.py:398
  22.7 25.0 %collective-permute-start.16 = (bf16[528,256]{1,0:T(8,128)(2,1)}, bf16[528,256]{1,0:T(8,128)(2,1)S(1)}, u32[]{:S(2)}, u32[]{:S(2)}) collective-permute-start(bf16[528,256]{1,0:T(8,128)(2,1)} %get-tuple-element.51), channel_id=1, source_target_pairs={{0,18},{2,16},{4,22},{6,20},{8,26},{10,24},{12,30},{14,28},{16,2},... | collective-permute-start | bytes 811016 | tf_op jit(solution)/shard_map/ppermute | solution.py:398
  33.9 13.8 %collective-permute-start = (bf16[528,256]{1,0:T(8,128)(2,1)}, bf16[528,256]{1,0:T(8,128)(2,1)S(1)}, u32[]{:S(2)}, u32[]{:S(2)}) collective-permute-start(bf16[528,256]{1,0:T(8,128)(2,1)} %get-tuple-element.36), channel_id=1, source_target_pairs={{0,4},{2,6},{4,0},{6,2},{8,12},{10,14},{12,8},{14,10},{16,20},{18,... | collective-permute-start | bytes 811016 | tf_op jit(solution)/shard_map/ppermute | solution.py:398
  34.0 16.5 %collective-permute-start.1 = (bf16[528,256]{1,0:T(8,128)(2,1)}, bf16[528,256]{1,0:T(8,128)(2,1)S(1)}, u32[]{:S(2)}, u32[]{:S(2)}) collective-permute-start(bf16[528,256]{1,0:T(8,128)(2,1)} %get-tuple-element.37), channel_id=1, source_target_pairs={{0,2},{2,0},{4,6},{6,4},{8,10},{10,8},{12,14},{14,12},{16,18},{18,... | collective-permute-start | bytes 811016 | tf_op jit(solution)/shard_map/ppermute | solution.py:398
  36.2 25.5 %collective-permute-start.4 = (bf16[528,256]{1,0:T(8,128)(2,1)}, bf16[528,256]{1,0:T(8,128)(2,1)S(1)}, u32[]{:S(2)}, u32[]{:S(2)}) collective-permute-start(bf16[528,256]{1,0:T(8,128)(2,1)} %get-tuple-element.45), channel_id=1, source_target_pairs={{0,6},{2,4},{4,2},{6,0},{8,14},{10,12},{12,10},{14,8},{16,22},{18,... | collective-permute-start | bytes 811016 | tf_op jit(solution)/shard_map/ppermute | solution.py:398
  41.8 20.0 %collective-permute-start.6 = (bf16[528,256]{1,0:T(8,128)(2,1)}, bf16[528,256]{1,0:T(8,128)(2,1)S(1)}, u32[]{:S(2)}, u32[]{:S(2)}) collective-permute-start(bf16[528,256]{1,0:T(8,128)(2,1)} %get-tuple-element.46), channel_id=1, source_target_pairs={{0,8},{2,10},{4,12},{6,14},{8,0},{10,2},{12,4},{14,6},{16,24},{18,... | collective-permute-start | bytes 811016 | tf_op jit(solution)/shard_map/ppermute | solution.py:398
  47.7 19.4 %collective-permute-start.8 = (bf16[528,256]{1,0:T(8,128)(2,1)}, bf16[528,256]{1,0:T(8,128)(2,1)S(1)}, u32[]{:S(2)}, u32[]{:S(2)}) collective-permute-start(bf16[528,256]{1,0:T(8,128)(2,1)} %get-tuple-element.47), channel_id=1, source_target_pairs={{0,10},{2,8},{4,14},{6,12},{8,2},{10,0},{12,6},{14,4},{16,26},{18,... | collective-permute-start | bytes 811016 | tf_op jit(solution)/shard_map/ppermute | solution.py:398
  47.7 25.4 %collective-permute-start.10 = (bf16[528,256]{1,0:T(8,128)(2,1)}, bf16[528,256]{1,0:T(8,128)(2,1)S(1)}, u32[]{:S(2)}, u32[]{:S(2)}) collective-permute-start(bf16[528,256]{1,0:T(8,128)(2,1)} %get-tuple-element.48), channel_id=1, source_target_pairs={{0,12},{2,14},{4,8},{6,10},{8,4},{10,6},{12,0},{14,2},{16,28},{18,... | collective-permute-start | bytes 811016 | tf_op jit(solution)/shard_map/ppermute | solution.py:398
  50.5 28.5 %collective-permute-start.12 = (bf16[528,256]{1,0:T(8,128)(2,1)}, bf16[528,256]{1,0:T(8,128)(2,1)S(1)}, u32[]{:S(2)}, u32[]{:S(2)}) collective-permute-start(bf16[528,256]{1,0:T(8,128)(2,1)} %get-tuple-element.49), channel_id=1, source_target_pairs={{0,14},{2,12},{4,10},{6,8},{8,6},{10,4},{12,2},{14,0},{16,30},{18,... | collective-permute-start | bytes 811016 | tf_op jit(solution)/shard_map/ppermute | solution.py:398
  61.7 42.9 %collective-permute-start.18 = (bf16[528,256]{1,0:T(8,128)(2,1)}, bf16[528,256]{1,0:T(8,128)(2,1)S(1)}, u32[]{:S(2)}, u32[]{:S(2)}) collective-permute-start(bf16[528,256]{1,0:T(8,128)(2,1)} %get-tuple-element.52), channel_id=1, source_target_pairs={{0,20},{2,22},{4,16},{6,18},{8,28},{10,30},{12,24},{14,26},{16,4},... | collective-permute-start | bytes 811016 | tf_op jit(solution)/shard_map/ppermute | solution.py:398
  61.8 49.9 %collective-permute-start.20 = (bf16[528,256]{1,0:T(8,128)(2,1)}, bf16[528,256]{1,0:T(8,128)(2,1)S(1)}, u32[]{:S(2)}, u32[]{:S(2)}) collective-permute-start(bf16[528,256]{1,0:T(8,128)(2,1)} %get-tuple-element.53), channel_id=1, source_target_pairs={{0,22},{2,20},{4,18},{6,16},{8,30},{10,28},{12,26},{14,24},{16,6},... | collective-permute-start | bytes 811016 | tf_op jit(solution)/shard_map/ppermute | solution.py:398
  67.1 44.6 %collective-permute-start.22 = (bf16[528,256]{1,0:T(8,128)(2,1)}, bf16[528,256]{1,0:T(8,128)(2,1)S(1)}, u32[]{:S(2)}, u32[]{:S(2)}) collective-permute-start(bf16[528,256]{1,0:T(8,128)(2,1)} %get-tuple-element.54), channel_id=1, source_target_pairs={{0,24},{2,26},{4,28},{6,30},{8,16},{10,18},{12,20},{14,22},{16,8},... | collective-permute-start | bytes 811016 | tf_op jit(solution)/shard_map/ppermute | solution.py:398
  73.1 39.1 %collective-permute-start.24 = (bf16[528,256]{1,0:T(8,128)(2,1)}, bf16[528,256]{1,0:T(8,128)(2,1)S(1)}, u32[]{:S(2)}, u32[]{:S(2)}) collective-permute-start(bf16[528,256]{1,0:T(8,128)(2,1)} %get-tuple-element.55), channel_id=1, source_target_pairs={{0,26},{2,24},{4,30},{6,28},{8,18},{10,16},{12,22},{14,20},{16,10}... | collective-permute-start | bytes 811016 | tf_op jit(solution)/shard_map/ppermute | solution.py:398
  79.0 33.3 %collective-permute-start.26 = (bf16[528,256]{1,0:T(8,128)(2,1)}, bf16[528,256]{1,0:T(8,128)(2,1)}, u32[]{:S(2)}, u32[]{:S(2)}) collective-permute-start(bf16[528,256]{1,0:T(8,128)(2,1)} %get-tuple-element.56), channel_id=1, source_target_pairs={{0,28},{2,30},{4,24},{6,26},{8,20},{10,22},{12,16},{14,18},{16,12}... | collective-permute-start | bytes 811016 | tf_op jit(solution)/shard_map/ppermute | solution.py:398
  104.6 10.5 %collective-permute-start.28 = (bf16[528,256]{1,0:T(8,128)(2,1)}, bf16[528,256]{1,0:T(8,128)(2,1)}, u32[]{:S(2)}, u32[]{:S(2)}) collective-permute-start(bf16[528,256]{1,0:T(8,128)(2,1)} %get-tuple-element.57), channel_id=1, source_target_pairs={{0,30},{2,28},{4,26},{6,24},{8,22},{10,20},{12,18},{14,16},{16,14}... | collective-permute-start | bytes 811016 | tf_op jit(solution)/shard_map/ppermute | solution.py:398
  111.7 7.2 %collective-permute-start.2 = (bf16[528,256]{1,0:T(8,128)(2,1)S(1)}, bf16[528,256]{1,0:T(8,128)(2,1)}, u32[]{:S(2)}, u32[]{:S(2)}) collective-permute-start(bf16[528,256]{1,0:T(8,128)(2,1)S(1)} %collective-permute-done.1.rest_2_), channel_id=1, source_target_pairs={{0,1},{1,0},{2,3},{3,2},{4,5},{5,4},{6,7},{7,6},{8,9},{9,8},{10,11... | collective-permute-start | bytes 811016 | tf_op jit(solution)/shard_map/ppermute | solution.py:438
  111.7 6.5 %collective-permute-start.15 = (bf16[528,256]{1,0:T(8,128)(2,1)S(1)}, bf16[528,256]{1,0:T(8,128)(2,1)}, u32[]{:S(2)}, u32[]{:S(2)}) collective-permute-start(bf16[528,256]{1,0:T(8,128)(2,1)S(1)} %collective-permute-done.14.rest_16_), channel_id=1, source_target_pairs={{0,1},{1,0},{2,3},{3,2},{4,5},{5,4},{6,7},{7,6},{8,9},{9,8},{10,11... | collective-permute-start | bytes 811016 | tf_op jit(solution)/shard_map/ppermute | solution.py:438
  112.2 6.6 %collective-permute-start.17 = (bf16[528,256]{1,0:T(8,128)(2,1)S(1)}, bf16[528,256]{1,0:T(8,128)(2,1)}, u32[]{:S(2)}, u32[]{:S(2)}) collective-permute-start(bf16[528,256]{1,0:T(8,128)(2,1)S(1)} %collective-permute-done.16.rest_18_), channel_id=1, source_target_pairs={{0,1},{1,0},{2,3},{3,2},{4,5},{5,4},{6,7},{7,6},{8,9},{9,8},{10,11... | collective-permute-start | bytes 811016 | tf_op jit(solution)/shard_map/ppermute | solution.py:438
  112.3 7.0 %collective-permute-start.5 = (bf16[528,256]{1,0:T(8,128)(2,1)S(1)}, bf16[528,256]{1,0:T(8,128)(2,1)}, u32[]{:S(2)}, u32[]{:S(2)}) collective-permute-start(bf16[528,256]{1,0:T(8,128)(2,1)S(1)} %collective-permute-done.4.rest_6_), channel_id=1, source_target_pairs={{0,1},{1,0},{2,3},{3,2},{4,5},{5,4},{6,7},{7,6},{8,9},{9,8},{10,11... | collective-permute-start | bytes 811016 | tf_op jit(solution)/shard_map/ppermute | solution.py:438
  115.1 4.3 %collective-permute-start.7 = (bf16[528,256]{1,0:T(8,128)(2,1)S(1)}, bf16[528,256]{1,0:T(8,128)(2,1)}, u32[]{:S(2)}, u32[]{:S(2)}) collective-permute-start(bf16[528,256]{1,0:T(8,128)(2,1)S(1)} %collective-permute-done.6.rest_8_), channel_id=1, source_target_pairs={{0,1},{1,0},{2,3},{3,2},{4,5},{5,4},{6,7},{7,6},{8,9},{9,8},{10,11... | collective-permute-start | bytes 811016 | tf_op jit(solution)/shard_map/ppermute | solution.py:438
  118.2 13.0 %collective-permute-start.9 = (bf16[528,256]{1,0:T(8,128)(2,1)S(1)}, bf16[528,256]{1,0:T(8,128)(2,1)S(1)}, u32[]{:S(2)}, u32[]{:S(2)}) collective-permute-start(bf16[528,256]{1,0:T(8,128)(2,1)S(1)} %collective-permute-done.8.rest_10_), channel_id=1, source_target_pairs={{0,1},{1,0},{2,3},{3,2},{4,5},{5,4},{6,7},{7,6},{8,9},{9,8},{10,11... | collective-permute-start | bytes 811016 | tf_op jit(solution)/shard_map/ppermute | solution.py:438
  118.8 12.6 %collective-permute-start.11 = (bf16[528,256]{1,0:T(8,128)(2,1)S(1)}, bf16[528,256]{1,0:T(8,128)(2,1)S(1)}, u32[]{:S(2)}, u32[]{:S(2)}) collective-permute-start(bf16[528,256]{1,0:T(8,128)(2,1)S(1)} %collective-permute-done.10.rest_12_), channel_id=1, source_target_pairs={{0,1},{1,0},{2,3},{3,2},{4,5},{5,4},{6,7},{7,6},{8,9},{9,8},{10,11... | collective-permute-start | bytes 811016 | tf_op jit(solution)/shard_map/ppermute | solution.py:438
  118.9 13.0 %collective-permute-start.13 = (bf16[528,256]{1,0:T(8,128)(2,1)S(1)}, bf16[528,256]{1,0:T(8,128)(2,1)S(1)}, u32[]{:S(2)}, u32[]{:S(2)}) collective-permute-start(bf16[528,256]{1,0:T(8,128)(2,1)S(1)} %collective-permute-done.12.rest_14_), channel_id=1, source_target_pairs={{0,1},{1,0},{2,3},{3,2},{4,5},{5,4},{6,7},{7,6},{8,9},{9,8},{10,11... | collective-permute-start | bytes 811016 | tf_op jit(solution)/shard_map/ppermute | solution.py:438
  119.3 12.6 %collective-permute-start.19 = (bf16[528,256]{1,0:T(8,128)(2,1)S(1)}, bf16[528,256]{1,0:T(8,128)(2,1)S(1)}, u32[]{:S(2)}, u32[]{:S(2)}) collective-permute-start(bf16[528,256]{1,0:T(8,128)(2,1)S(1)} %collective-permute-done.18.rest_20_), channel_id=1, source_target_pairs={{0,1},{1,0},{2,3},{3,2},{4,5},{5,4},{6,7},{7,6},{8,9},{9,8},{10,11... | collective-permute-start | bytes 811016 | tf_op jit(solution)/shard_map/ppermute | solution.py:438
  119.4 13.0 %collective-permute-start.21 = (bf16[528,256]{1,0:T(8,128)(2,1)S(1)}, bf16[528,256]{1,0:T(8,128)(2,1)S(1)}, u32[]{:S(2)}, u32[]{:S(2)}) collective-permute-start(bf16[528,256]{1,0:T(8,128)(2,1)S(1)} %collective-permute-done.20.rest_22_), channel_id=1, source_target_pairs={{0,1},{1,0},{2,3},{3,2},{4,5},{5,4},{6,7},{7,6},{8,9},{9,8},{10,11... | collective-permute-start | bytes 811016 | tf_op jit(solution)/shard_map/ppermute | solution.py:438
  131.3 1.6 collective-permute-start.23
  131.4 1.8 collective-permute-start.25
  131.9 1.8 collective-permute-start.27
  132.0 2.1 collective-permute-start.29
  132.4 2.1 collective-permute-start.3
  184.5 1.3 collective-permute-start.31
  (11 other events, 174.2 us)

commit v5 on v4

--- a/solution.py
+++ b/solution.py
@@ -125,7 +125,7 @@
 
 def sweep_users(
     user_hbm, scale_hbm, user_ref, scale_ref, item_ref, row_sem, item_sem, item_scale_ref, dual_scr,
-    dots_a, dots_b, finish, fanout
+    dots_a, dots_b, finish, fanout, keep=None
 ):
     clusters, users, _ = user_ref.shape
     camps = item_scale_ref.shape[1]
@@ -135,9 +135,10 @@
     def landed(k):
         pltpu.make_async_copy(user_hbm.at[k], user_ref.at[k], row_sem.at[0, k]).wait()
         pltpu.make_async_copy(scale_hbm.at[k], scale_ref.at[k], row_sem.at[1, k]).wait()
-        if item_sem is not None:
-            for e in range(fanout):
-                item_landed(k * fanout + e, item_ref, item_sem)
+        for e in range(fanout):
+            item_landed(k * fanout + e, item_ref, item_sem)
+        if keep is not None:
+            keep(k).start()
 
     def multiply(k, dots):
         blocks = item_ref[pl.ds(pl.multiple_of(k * fanout, fanout), fanout)].reshape(fanout * camps, width)
@@ -209,11 +210,10 @@
     theirs_ref[...] = spend_scr[pl.ds(pl.multiple_of((1 - rep) * count, count), count), :]
 
 
-def item_facts(fact_ref, item_ref, item_sem, fact_sem, dual_ref, limit_ref, live_ref, item_scale_ref):
+def item_facts(fact_ref, fact_sem, dual_ref, limit_ref, live_ref, item_scale_ref):
     items = dual_ref.shape[0]
 
     def wait(item, carry):
-        item_landed(item, item_ref, item_sem)
         pltpu.make_async_copy(fact_ref.at[item], fact_ref.at[item], fact_sem.at[item]).wait()
         return carry
 
@@ -254,17 +254,25 @@
                 rows, lanes = fact_place(j, half, camps, pieces, width)
                 fetch(n * cap + side * half + j, message.at[pl.ds(j * camps, camps)], message.at[rows, lanes])
     start_rows(user_hbm, scale_hbm, user_ref, scale_ref, row_sem)
-    item_facts(landed_ref, item_ref, item_sem, fact_sem, duals_ref, limit_ref, live_ref, item_scale_ref)
-    keep = pltpu.make_async_copy(item_ref, item_out, out_sem)
-    keep.start()
+    item_facts(landed_ref, fact_sem, duals_ref, limit_ref, live_ref, item_scale_ref)
+
+    def keep(k):
+        rows = pl.ds(pl.multiple_of(k * fanout, fanout), fanout)
+        return pltpu.make_async_copy(item_ref.at[rows], item_out.at[rows], out_sem.at[k])
+
     dual_scr[...] = jnp.where(live_ref[...] > 0.0, duals_ref[...] * gain, masked)
     finish = spend_finish(where_ref, size_ref, users, fanout, spend_scr)
     sweep_users(
-        user_hbm, scale_hbm, user_ref, scale_ref, item_ref, row_sem, None, item_scale_ref,
-        dual_scr, dots_a, dots_b, finish, fanout
+        user_hbm, scale_hbm, user_ref, scale_ref, item_ref, row_sem, item_sem, item_scale_ref,
+        dual_scr, dots_a, dots_b, finish, fanout, keep
     )
     halves(where_ref, spend_scr, mine_ref, theirs_ref)
-    keep.wait()
+
+    def kept(k, carry):
+        keep(k).wait()
+        return carry
+
+    lax.fori_loop(0, user_ref.shape[0], kept, 0)
 
 
 def second_kernel(
@@ -378,7 +386,7 @@
     order = send_order(shards)
     sent = {}
     sends = [(shift, False) for shift in order] + [(0, False), (0, True)]
-    for some in (sends[:2], sends[2:]):
+    for some in (sends[:4], sends[4:]):
         outs = pl.pallas_call(
             functools.partial(gather_kernel, half, some),
             out_shape=[pltpu.HBM((message, width), camp_emb.dtype)] * len(some),
@@ -471,7 +479,7 @@
         + [
             pltpu.VMEM((items, len(rows), camps), camp_emb.dtype),
             pltpu.SemaphoreType.DMA((items,)),
-            pltpu.SemaphoreType.DMA,
+            pltpu.SemaphoreType.DMA((clusters,)),
         ],
         compiler_params=limits,
     )(where, cluster_size, item_of_slot, user_rows, user_scale, *received)

time: 220 us -> 213 us (0.968)
  blocking collectives: 43.9 us -> 31.1 us
  waiting for transfers between devices: 65 us -> 70.5 us
    all_to_all x2, blocking collectives: 43.9 us -> 31.1 us  [exchange(): lax.all_to_all(spread, 'shard', split_axis=0, concat_axis=0, tiled=True)]
    ppermute x15, waiting for transfers between devices: 55.4 us -> 60.8 us  [program(): lax.ppermute(sent[shift, False], 'shard', [(i, i ^ shift) for i in range(...]
  transfers between devices with their start and end apart: 35 -> 35, of which waited for: 17 -> 21; matrix products, arithmetic and copies ran while one was open for 5% -> 5% of each run, Pallas kernels for 8% -> 9%
where the time goes in v5:
time: 213 us; the launch traced here: 212 us
  waiting for transfers between devices  70.5 us (33%)
  Pallas kernels  57.5 us (27%)
  starting transfers between devices  36.4 us (17%)
  blocking collectives  31.1 us (15%)
  local copies, waits for them, and re-layouts  11 us (5%)
  other arithmetic  4.47 us (2%)
    ppermute x15, waiting for transfers between devices, program(): lax.ppermute(sent[shift, False], 'shard', [(i, i ^ shift) for i in range(...  60.8 us
    all_to_all x2, blocking collectives, exchange(): lax.all_to_all(spread, 'shard', split_axis=0, concat_axis=0, tiled=True)  31.1 us
    ppermute x15, starting transfers between devices, program(): lax.ppermute(sent[shift, False], 'shard', [(i, i ^ shift) for i in range(...  24.9 us
    pallas_call x1, Pallas kernels, program(): pl.pallas_call(functools.partial(first_kernel, shards, half, fanout, camp...  15.9 us
    pallas_call x2, Pallas kernels, program(): pl.pallas_call(functools.partial(gather_kernel, half, some), out_shape=[p...  12.7 us
    pallas_call x1, Pallas kernels, program(): pl.pallas_call(functools.partial(second_kernel, fanout), out_shape=spend_...  9.96 us
    pallas_call x1, Pallas kernels, program(): pl.pallas_call(functools.partial(third_kernel, fanout), out_shape=[jax.Sh...  9.77 us
    pallas_call x1, Pallas kernels, program(): pl.pallas_call(user_kernel, out_shape=jax.ShapeDtypeStruct((clusters, use...  9.25 us
  transfers between devices with their start and end apart: 35, of which 21 were waited for; matrix products, arithmetic and copies ran while one was open for 5% of the time, Pallas kernels for 9%

profile of v5, /device:TPU:0, one launch (start us, length us, event | category | flops | bytes accessed | tf_op | source)
XLA Modules:
  0.0 211.9 jit_solution(50036803456063449)
XLA Ops:
  3.4 8.3 %all-to-all-start = ((s32[16,1,72]{2,1,0:T(1,128)}), s32[16,1,72]{2,1,0:T(1,128)S(1)}, u32[]{:S(2)}, u32[]{:S(2)}) async-start(s32[16,1,72]{2,1,0:T(1,128)} %bitcast.4), calls=%async_computation | async-start | bytes 16384 | tf_op jit(solution)/shard_map/all_to_all | solution.py:369
  14.8 1.5 stack.63.fact_ref
  16.2 2.7 %all-to-all-done = s32[16,1,72]{2,1,0:T(1,128)S(1)} async-done(((s32[16,1,72]{2,1,0:T(1,128)}), s32[16,1,72]{2,1,0:T(1,128)S(1)}, u32[]{:S(2)}, u32[]{:S(2)}) %all-to-all-start) | async-done | bytes 4640 | tf_op jit(solution)/shard_map/all_to_all | solution.py:369
  19.0 3.9 %shard_map.97 = (bf16[528,256]{1,0:T(8,128)(2,1)}, bf16[528,256]{1,0:T(8,128)(2,1)}, bf16[528,256]{1,0:T(8,128)(2,1)}, bf16[528,256]{1,0:T(8,128)(2,1)}) custom-call(s32[2]{0:T(128)S(1)} %pad_add_fusion.1.where_ref, s32[16,72]{1,0:T(8,128)S(1)} %bitcast.29, bf16[128,128,256]{2,1,0:T(8,128)(2,1)} %camp_ref.3, bf16[128,8,128]{2,1,0:T(8,128)(2,1)} %stack.63.fact_ref), custom_call_target="tpu_custom_call" | custom-call | bytes 2097152 | tf_op jit(solution)/shard_map/pallas_call | solution.py:390
  23.6 2.5 %collective-permute-start.16 = (bf16[528,256]{1,0:T(8,128)(2,1)}, bf16[528,256]{1,0:T(8,128)(2,1)S(1)}, u32[]{:S(2)}, u32[]{:S(2)}) collective-permute-start(bf16[528,256]{1,0:T(8,128)(2,1)} %get-tuple-element.51), channel_id=1, source_target_pairs={{0,18},{2,16},{4,22},{6,20},{8,26},{10,24},{12,30},{14,28},{16,2},... | collective-permute-start | bytes 811016 | tf_op jit(solution)/shard_map/ppermute | solution.py:406
  26.0 1.8 collective-permute-start.18
  27.9 2.7 %collective-permute-start.20 = (bf16[528,256]{1,0:T(8,128)(2,1)}, bf16[528,256]{1,0:T(8,128)(2,1)S(1)}, u32[]{:S(2)}, u32[]{:S(2)}) collective-permute-start(bf16[528,256]{1,0:T(8,128)(2,1)} %get-tuple-element.53), channel_id=1, source_target_pairs={{0,22},{2,20},{4,18},{6,16},{8,30},{10,28},{12,26},{14,24},{16,6},... | collective-permute-start | bytes 811016 | tf_op jit(solution)/shard_map/ppermute | solution.py:406
  30.6 8.8 %shard_map.95 = (bf16[528,256]{1,0:T(8,128)(2,1)}, bf16[528,256]{1,0:T(8,128)(2,1)}, bf16[528,256]{1,0:T(8,128)(2,1)}, bf16[528,256]{1,0:T(8,128)(2,1)}, bf16[52...) custom-call(s32[2]{0:T(128)S(1)} %pad_add_fusion.1.where_ref, ...), custom_call_target="tpu_custom_call" | custom-call | bytes 6815744 | tf_op jit(solution)/shard_map/pallas_call | solution.py:390
  39.5 15.1 %collective-permute-done.14.rest_16_ = bf16[528,256]{1,0:T(8,128)(2,1)S(1)} collective-permute-done((bf16[528,256]{1,0:T(8,128)(2,1)}, bf16[528,256]{1,0:T(8,128)(2,1)S(1)}, u32[]{:S(2)}, u32[]{:S(2)}) %collective-permute-start.14) | collective-permute-done | bytes 270368 | tf_op jit(solution)/shard_map/ppermute | solution.py:406
  55.2 5.3 %collective-permute-done.16.rest_18_ = bf16[528,256]{1,0:T(8,128)(2,1)S(1)} collective-permute-done((bf16[528,256]{1,0:T(8,128)(2,1)}, bf16[528,256]{1,0:T(8,128)(2,1)S(1)}, u32[]{:S(2)}, u32[]{:S(2)}) %collective-permute-start.16) | collective-permute-done | bytes 270368 | tf_op jit(solution)/shard_map/ppermute | solution.py:406
  60.4 1.9 collective-permute-start.4
  62.3 4.3 %collective-permute-done.18.rest_20_ = bf16[528,256]{1,0:T(8,128)(2,1)S(1)} collective-permute-done((bf16[528,256]{1,0:T(8,128)(2,1)}, bf16[528,256]{1,0:T(8,128)(2,1)S(1)}, u32[]{:S(2)}, u32[]{:S(2)}) %collective-permute-start.18) | collective-permute-done | bytes 270368 | tf_op jit(solution)/shard_map/ppermute | solution.py:406
  66.7 5.8 %collective-permute-done.20.rest_22_ = bf16[528,256]{1,0:T(8,128)(2,1)S(1)} collective-permute-done((bf16[528,256]{1,0:T(8,128)(2,1)}, bf16[528,256]{1,0:T(8,128)(2,1)S(1)}, u32[]{:S(2)}, u32[]{:S(2)}) %collective-permute-start.20) | collective-permute-done | bytes 270368 | tf_op jit(solution)/shard_map/ppermute | solution.py:406
  72.5 3.4 %collective-permute-start.10 = (bf16[528,256]{1,0:T(8,128)(2,1)}, bf16[528,256]{1,0:T(8,128)(2,1)S(1)}, u32[]{:S(2)}, u32[]{:S(2)}) collective-permute-start(bf16[528,256]{1,0:T(8,128)(2,1)} %get-tuple-element.48), channel_id=1, source_target_pairs={{0,12},{2,14},{4,8},{6,10},{8,4},{10,6},{12,0},{14,2},{16,28},{18,... | collective-permute-start | bytes 811016 | tf_op jit(solution)/shard_map/ppermute | solution.py:406
  76.2 1.9 collective-permute-done.4.rest_6_
  78.1 3.3 %collective-permute-start.22 = (bf16[528,256]{1,0:T(8,128)(2,1)}, bf16[528,256]{1,0:T(8,128)(2,1)S(1)}, u32[]{:S(2)}, u32[]{:S(2)}) collective-permute-start(bf16[528,256]{1,0:T(8,128)(2,1)} %get-tuple-element.54), channel_id=1, source_target_pairs={{0,24},{2,26},{4,28},{6,30},{8,16},{10,18},{12,20},{14,22},{16,8},... | collective-permute-start | bytes 811016 | tf_op jit(solution)/shard_map/ppermute | solution.py:406
  82.0 1.7 collective-permute-done.8.rest_10_
  83.7 3.7 %collective-permute-start.26 = (bf16[528,256]{1,0:T(8,128)(2,1)}, bf16[528,256]{1,0:T(8,128)(2,1)}, u32[]{:S(2)}, u32[]{:S(2)}) collective-permute-start(bf16[528,256]{1,0:T(8,128)(2,1)} %get-tuple-element.56), channel_id=1, source_target_pairs={{0,28},{2,30},{4,24},{6,26},{8,20},{10,22},{12,16},{14,18},{16,12}... | collective-permute-start | bytes 811016 | tf_op jit(solution)/shard_map/ppermute | solution.py:406
  87.3 1.9 collective-permute-done.10.rest_12_
  89.3 3.7 %collective-permute-start.28 = (bf16[528,256]{1,0:T(8,128)(2,1)}, bf16[528,256]{1,0:T(8,128)(2,1)}, u32[]{:S(2)}, u32[]{:S(2)}) collective-permute-start(bf16[528,256]{1,0:T(8,128)(2,1)} %get-tuple-element.57), channel_id=1, source_target_pairs={{0,30},{2,28},{4,26},{6,24},{8,22},{10,20},{12,18},{14,16},{16,14}... | collective-permute-start | bytes 811016 | tf_op jit(solution)/shard_map/ppermute | solution.py:406
  94.5 1.4 copy.67
  95.9 7.7 %collective-permute-done.22.rest_24_ = bf16[528,256]{1,0:T(8,128)(2,1)S(1)} collective-permute-done((bf16[528,256]{1,0:T(8,128)(2,1)}, bf16[528,256]{1,0:T(8,128)(2,1)S(1)}, u32[]{:S(2)}, u32[]{:S(2)}) %collective-permute-start.22) | collective-permute-done | bytes 270368 | tf_op jit(solution)/shard_map/ppermute | solution.py:406
  103.6 5.7 %collective-permute-done.24.rest_26_ = bf16[528,256]{1,0:T(8,128)(2,1)S(1)} collective-permute-done((bf16[528,256]{1,0:T(8,128)(2,1)}, bf16[528,256]{1,0:T(8,128)(2,1)S(1)}, u32[]{:S(2)}, u32[]{:S(2)}) %collective-permute-start.24) | collective-permute-done | bytes 270368 | tf_op jit(solution)/shard_map/ppermute | solution.py:406
  109.3 6.0 %collective-permute-done.26.rest_28_ = bf16[528,256]{1,0:T(8,128)(2,1)} collective-permute-done((bf16[528,256]{1,0:T(8,128)(2,1)}, bf16[528,256]{1,0:T(8,128)(2,1)}, u32[]{:S(2)}, u32[]{:S(2)}) %collective-permute-start.26) | collective-permute-done | bytes 270368 | tf_op jit(solution)/shard_map/ppermute | solution.py:406
  115.3 5.3 %collective-permute-done.28.rest_30_ = bf16[528,256]{1,0:T(8,128)(2,1)} collective-permute-done((bf16[528,256]{1,0:T(8,128)(2,1)}, bf16[528,256]{1,0:T(8,128)(2,1)}, u32[]{:S(2)}, u32[]{:S(2)}) %collective-permute-start.28) | collective-permute-done | bytes 270368 | tf_op jit(solution)/shard_map/ppermute | solution.py:406
  125.5 9.2 %shard_map.96.scale_hbm = f32[16,512,128]{2,1,0:T(8,128)S(1)} custom-call(bf16[16,512,256]{2,1,0:T(8,128)(2,1)} %user_hbm.5), custom_call_target="tpu_custom_call" | custom-call | flops 8388608 | bytes 8388608 | tf_op jit(solution)/shard_map/pallas_call | solution.py:422
  134.7 2.0 copy-done
  139.9 15.9 %shard_map.98 = (f32[32,128]{1,0:T(8,128)S(1)}, f32[32,128]{1,0:T(8,128)S(1)}, f32[64,128]{1,0:T(8,128)S(1)}, f32[64,128]{1,0:T(8,128)S(1)}, f32[64,128]{1,0:T(8...) custom-call(s32[2]{0:T(128)S(1)} %pad_add_fusion.1.where_ref, s32[16]{0:T(128)S(1)} %copy-done.5, ...), custom_call_target="tpu_custom_call" | custom-call | tf_op jit(solution)/shard_map/pallas_call | solution.py:470
  157.1 20.4 %all_to_all.21 = bf16[16,32,128]{2,1,0:T(8,128)(2,1)S(1)} all-to-all(bf16[16,32,128]{2,1,0:T(8,128)(2,1)S(1)} %broadcast_in_dim.53), channel_id=1, replica_groups=mesh['shard'=16,'rep'=2] {'shard'}, dimensions={0} | all-to-all | bytes 262144 | tf_op jit(solution)/shard_map/all_to_all | solution.py:452
  178.8 10.0 %shard_map.99 = (f32[32,128]{1,0:T(8,128)S(1)}, f32[32,128]{1,0:T(8,128)S(1)}, f32[64,128]{1,0:T(8,128)S(1)}) custom-call(s32[2]{0:T(128)S(1)} %pad_add_fusion.1.where_ref, s32[16]{0:T(128)S(1)} %copy-done.5, f32[64,128]{1,0:T(8,128)S(1)} %get-tuple-element.58.duals_ref, f32[64,128]{1,0:T(8,128)S(1)} %get-tuple-element.59.live_ref, ...), custom_call_target="tpu_custom_call" | custom-call | tf_op jit(solution)/shard_map/pallas_call | solution.py:489
  190.0 10.7 %all_to_all.22 = bf16[16,32,128]{2,1,0:T(8,128)(2,1)S(1)} all-to-all(bf16[16,32,128]{2,1,0:T(8,128)(2,1)S(1)} %broadcast_in_dim.54), channel_id=1, replica_groups=mesh['shard'=16,'rep'=2] {'shard'}, dimensions={0} | all-to-all | bytes 262144 | tf_op jit(solution)/shard_map/all_to_all | solution.py:452
  202.1 9.8 %shard_map.100 = (f32[16,512]{1,0:T(8,128)}, f32[128,128]{1,0:T(8,128)}) custom-call(s32[2]{0:T(128)S(1)} %pad_add_fusion.1.where_ref, s32[16]{0:T(128)S(1)} %copy-done.5, f32[64,128]{1,0:T(8,128)S(1)} %get-tuple-element.66.duals_ref, f32[64,128]{1,0:T(8,128)S(1)} %get-tuple-element.59.live_ref, f32[64,128]{1,0:T(8,128)S(1)} %get-tuple-element.60.item_scale_ref, ...), custom_call_target="tpu_custom_call" | custom-call | tf_op jit(solution)/shard_map/pallas_call | solution.py:500
  (107 shorter events, 22.5 us)
Async XLA Ops:
  3.4 15.6 %all-to-all-start = ((s32[16,1,72]{2,1,0:T(1,128)}), s32[16,1,72]{2,1,0:T(1,128)S(1)}, u32[]{:S(2)}, u32[]{:S(2)}) async-start(s32[16,1,72]{2,1,0:T(1,128)} %bitcast.4), calls=%async_computation | async-start | bytes 16384 | tf_op jit(solution)/shard_map/all_to_all | solution.py:369
  22.9 31.8 %collective-permute-start.14 = (bf16[528,256]{1,0:T(8,128)(2,1)}, bf16[528,256]{1,0:T(8,128)(2,1)S(1)}, u32[]{:S(2)}, u32[]{:S(2)}) collective-permute-start(bf16[528,256]{1,0:T(8,128)(2,1)} %get-tuple-element.50), channel_id=1, source_target_pairs={{0,16},{2,18},{4,20},{6,22},{8,24},{10,26},{12,28},{14,30},{16,0},... | collective-permute-start | bytes 811016 | tf_op jit(solution)/shard_map/ppermute | solution.py:406
  23.6 36.9 %collective-permute-start.16 = (bf16[528,256]{1,0:T(8,128)(2,1)}, bf16[528,256]{1,0:T(8,128)(2,1)S(1)}, u32[]{:S(2)}, u32[]{:S(2)}) collective-permute-start(bf16[528,256]{1,0:T(8,128)(2,1)} %get-tuple-element.51), channel_id=1, source_target_pairs={{0,18},{2,16},{4,22},{6,20},{8,26},{10,24},{12,30},{14,28},{16,2},... | collective-permute-start | bytes 811016 | tf_op jit(solution)/shard_map/ppermute | solution.py:406
  26.0 40.6 %collective-permute-start.18 = (bf16[528,256]{1,0:T(8,128)(2,1)}, bf16[528,256]{1,0:T(8,128)(2,1)S(1)}, u32[]{:S(2)}, u32[]{:S(2)}) collective-permute-start(bf16[528,256]{1,0:T(8,128)(2,1)} %get-tuple-element.52), channel_id=1, source_target_pairs={{0,20},{2,22},{4,16},{6,18},{8,28},{10,30},{12,24},{14,26},{16,4},... | collective-permute-start | bytes 811016 | tf_op jit(solution)/shard_map/ppermute | solution.py:406
  27.9 44.6 %collective-permute-start.20 = (bf16[528,256]{1,0:T(8,128)(2,1)}, bf16[528,256]{1,0:T(8,128)(2,1)S(1)}, u32[]{:S(2)}, u32[]{:S(2)}) collective-permute-start(bf16[528,256]{1,0:T(8,128)(2,1)} %get-tuple-element.53), channel_id=1, source_target_pairs={{0,22},{2,20},{4,18},{6,16},{8,30},{10,28},{12,26},{14,24},{16,6},... | collective-permute-start | bytes 811016 | tf_op jit(solution)/shard_map/ppermute | solution.py:406
  39.4 33.1 %collective-permute-start = (bf16[528,256]{1,0:T(8,128)(2,1)}, bf16[528,256]{1,0:T(8,128)(2,1)S(1)}, u32[]{:S(2)}, u32[]{:S(2)}) collective-permute-start(bf16[528,256]{1,0:T(8,128)(2,1)} %get-tuple-element.36), channel_id=1, source_target_pairs={{0,4},{2,6},{4,0},{6,2},{8,12},{10,14},{12,8},{14,10},{16,20},{18,... | collective-permute-start | bytes 811016 | tf_op jit(solution)/shard_map/ppermute | solution.py:406
  54.7 21.4 %collective-permute-start.1 = (bf16[528,256]{1,0:T(8,128)(2,1)}, bf16[528,256]{1,0:T(8,128)(2,1)S(1)}, u32[]{:S(2)}, u32[]{:S(2)}) collective-permute-start(bf16[528,256]{1,0:T(8,128)(2,1)} %get-tuple-element.37), channel_id=1, source_target_pairs={{0,2},{2,0},{4,6},{6,4},{8,10},{10,8},{12,14},{14,12},{16,18},{18,... | collective-permute-start | bytes 811016 | tf_op jit(solution)/shard_map/ppermute | solution.py:406
  60.4 17.7 %collective-permute-start.4 = (bf16[528,256]{1,0:T(8,128)(2,1)}, bf16[528,256]{1,0:T(8,128)(2,1)S(1)}, u32[]{:S(2)}, u32[]{:S(2)}) collective-permute-start(bf16[528,256]{1,0:T(8,128)(2,1)} %get-tuple-element.45), channel_id=1, source_target_pairs={{0,6},{2,4},{4,2},{6,0},{8,14},{10,12},{12,10},{14,8},{16,22},{18,... | collective-permute-start | bytes 811016 | tf_op jit(solution)/shard_map/ppermute | solution.py:406
  66.7 14.7 %collective-permute-start.6 = (bf16[528,256]{1,0:T(8,128)(2,1)}, bf16[528,256]{1,0:T(8,128)(2,1)S(1)}, u32[]{:S(2)}, u32[]{:S(2)}) collective-permute-start(bf16[528,256]{1,0:T(8,128)(2,1)} %get-tuple-element.46), channel_id=1, source_target_pairs={{0,8},{2,10},{4,12},{6,14},{8,0},{10,2},{12,4},{14,6},{16,24},{18,... | collective-permute-start | bytes 811016 | tf_op jit(solution)/shard_map/ppermute | solution.py:406
  72.5 11.2 %collective-permute-start.8 = (bf16[528,256]{1,0:T(8,128)(2,1)}, bf16[528,256]{1,0:T(8,128)(2,1)S(1)}, u32[]{:S(2)}, u32[]{:S(2)}) collective-permute-start(bf16[528,256]{1,0:T(8,128)(2,1)} %get-tuple-element.47), channel_id=1, source_target_pairs={{0,10},{2,8},{4,14},{6,12},{8,2},{10,0},{12,6},{14,4},{16,26},{18,... | collective-permute-start | bytes 811016 | tf_op jit(solution)/shard_map/ppermute | solution.py:406
  72.5 16.8 %collective-permute-start.10 = (bf16[528,256]{1,0:T(8,128)(2,1)}, bf16[528,256]{1,0:T(8,128)(2,1)S(1)}, u32[]{:S(2)}, u32[]{:S(2)}) collective-permute-start(bf16[528,256]{1,0:T(8,128)(2,1)} %get-tuple-element.48), channel_id=1, source_target_pairs={{0,12},{2,14},{4,8},{6,10},{8,4},{10,6},{12,0},{14,2},{16,28},{18,... | collective-permute-start | bytes 811016 | tf_op jit(solution)/shard_map/ppermute | solution.py:406
  76.1 19.8 %collective-permute-start.12 = (bf16[528,256]{1,0:T(8,128)(2,1)}, bf16[528,256]{1,0:T(8,128)(2,1)S(1)}, u32[]{:S(2)}, u32[]{:S(2)}) collective-permute-start(bf16[528,256]{1,0:T(8,128)(2,1)} %get-tuple-element.49), channel_id=1, source_target_pairs={{0,14},{2,12},{4,10},{6,8},{8,6},{10,4},{12,2},{14,0},{16,30},{18,... | collective-permute-start | bytes 811016 | tf_op jit(solution)/shard_map/ppermute | solution.py:406
  78.1 25.5 %collective-permute-start.22 = (bf16[528,256]{1,0:T(8,128)(2,1)}, bf16[528,256]{1,0:T(8,128)(2,1)S(1)}, u32[]{:S(2)}, u32[]{:S(2)}) collective-permute-start(bf16[528,256]{1,0:T(8,128)(2,1)} %get-tuple-element.54), channel_id=1, source_target_pairs={{0,24},{2,26},{4,28},{6,30},{8,16},{10,18},{12,20},{14,22},{16,8},... | collective-permute-start | bytes 811016 | tf_op jit(solution)/shard_map/ppermute | solution.py:406
  81.4 27.9 %collective-permute-start.24 = (bf16[528,256]{1,0:T(8,128)(2,1)}, bf16[528,256]{1,0:T(8,128)(2,1)S(1)}, u32[]{:S(2)}, u32[]{:S(2)}) collective-permute-start(bf16[528,256]{1,0:T(8,128)(2,1)} %get-tuple-element.55), channel_id=1, source_target_pairs={{0,26},{2,24},{4,30},{6,28},{8,18},{10,16},{12,22},{14,20},{16,10}... | collective-permute-start | bytes 811016 | tf_op jit(solution)/shard_map/ppermute | solution.py:406
  83.7 31.6 %collective-permute-start.26 = (bf16[528,256]{1,0:T(8,128)(2,1)}, bf16[528,256]{1,0:T(8,128)(2,1)}, u32[]{:S(2)}, u32[]{:S(2)}) collective-permute-start(bf16[528,256]{1,0:T(8,128)(2,1)} %get-tuple-element.56), channel_id=1, source_target_pairs={{0,28},{2,30},{4,24},{6,26},{8,20},{10,22},{12,16},{14,18},{16,12}... | collective-permute-start | bytes 811016 | tf_op jit(solution)/shard_map/ppermute | solution.py:406
  89.3 31.3 %collective-permute-start.28 = (bf16[528,256]{1,0:T(8,128)(2,1)}, bf16[528,256]{1,0:T(8,128)(2,1)}, u32[]{:S(2)}, u32[]{:S(2)}) collective-permute-start(bf16[528,256]{1,0:T(8,128)(2,1)} %get-tuple-element.57), channel_id=1, source_target_pairs={{0,30},{2,28},{4,26},{6,24},{8,22},{10,20},{12,18},{14,16},{16,14}... | collective-permute-start | bytes 811016 | tf_op jit(solution)/shard_map/ppermute | solution.py:406
  95.9 29.0 %collective-permute-start.2 = (bf16[528,256]{1,0:T(8,128)(2,1)S(1)}, bf16[528,256]{1,0:T(8,128)(2,1)}, u32[]{:S(2)}, u32[]{:S(2)}) collective-permute-start(bf16[528,256]{1,0:T(8,128)(2,1)S(1)} %collective-permute-done.1.rest_2_), channel_id=1, source_target_pairs={{0,1},{1,0},{2,3},{3,2},{4,5},{5,4},{6,7},{7,6},{8,9},{9,8},{10,11... | collective-permute-start | bytes 811016 | tf_op jit(solution)/shard_map/ppermute | solution.py:446
  103.6 20.1 %collective-permute-start.15 = (bf16[528,256]{1,0:T(8,128)(2,1)S(1)}, bf16[528,256]{1,0:T(8,128)(2,1)}, u32[]{:S(2)}, u32[]{:S(2)}) collective-permute-start(bf16[528,256]{1,0:T(8,128)(2,1)S(1)} %collective-permute-done.14.rest_16_), channel_id=1, source_target_pairs={{0,1},{1,0},{2,3},{3,2},{4,5},{5,4},{6,7},{7,6},{8,9},{9,8},{10,11... | collective-permute-start | bytes 811016 | tf_op jit(solution)/shard_map/ppermute | solution.py:446
  109.3 15.0 %collective-permute-start.17 = (bf16[528,256]{1,0:T(8,128)(2,1)S(1)}, bf16[528,256]{1,0:T(8,128)(2,1)}, u32[]{:S(2)}, u32[]{:S(2)}) collective-permute-start(bf16[528,256]{1,0:T(8,128)(2,1)S(1)} %collective-permute-done.16.rest_18_), channel_id=1, source_target_pairs={{0,1},{1,0},{2,3},{3,2},{4,5},{5,4},{6,7},{7,6},{8,9},{9,8},{10,11... | collective-permute-start | bytes 811016 | tf_op jit(solution)/shard_map/ppermute | solution.py:446
  115.3 9.1 %collective-permute-start.19 = (bf16[528,256]{1,0:T(8,128)(2,1)S(1)}, bf16[528,256]{1,0:T(8,128)(2,1)}, u32[]{:S(2)}, u32[]{:S(2)}) collective-permute-start(bf16[528,256]{1,0:T(8,128)(2,1)S(1)} %collective-permute-done.18.rest_20_), channel_id=1, source_target_pairs={{0,1},{1,0},{2,3},{3,2},{4,5},{5,4},{6,7},{7,6},{8,9},{9,8},{10,11... | collective-permute-start | bytes 811016 | tf_op jit(solution)/shard_map/ppermute | solution.py:446
  120.6 4.2 %collective-permute-start.21 = (bf16[528,256]{1,0:T(8,128)(2,1)S(1)}, bf16[528,256]{1,0:T(8,128)(2,1)}, u32[]{:S(2)}, u32[]{:S(2)}) collective-permute-start(bf16[528,256]{1,0:T(8,128)(2,1)S(1)} %collective-permute-done.20.rest_22_), channel_id=1, source_target_pairs={{0,1},{1,0},{2,3},{3,2},{4,5},{5,4},{6,7},{7,6},{8,9},{9,8},{10,11... | collective-permute-start | bytes 811016 | tf_op jit(solution)/shard_map/ppermute | solution.py:446
  123.7 13.0 %collective-permute-start.5 = (bf16[528,256]{1,0:T(8,128)(2,1)S(1)}, bf16[528,256]{1,0:T(8,128)(2,1)S(1)}, u32[]{:S(2)}, u32[]{:S(2)}) collective-permute-start(bf16[528,256]{1,0:T(8,128)(2,1)S(1)} %collective-permute-done.4.rest_6_), channel_id=1, source_target_pairs={{0,1},{1,0},{2,3},{3,2},{4,5},{5,4},{6,7},{7,6},{8,9},{9,8},{10,11... | collective-permute-start | bytes 811016 | tf_op jit(solution)/shard_map/ppermute | solution.py:446
  124.3 12.6 %collective-permute-start.7 = (bf16[528,256]{1,0:T(8,128)(2,1)S(1)}, bf16[528,256]{1,0:T(8,128)(2,1)S(1)}, u32[]{:S(2)}, u32[]{:S(2)}) collective-permute-start(bf16[528,256]{1,0:T(8,128)(2,1)S(1)} %collective-permute-done.6.rest_8_), channel_id=1, source_target_pairs={{0,1},{1,0},{2,3},{3,2},{4,5},{5,4},{6,7},{7,6},{8,9},{9,8},{10,11... | collective-permute-start | bytes 811016 | tf_op jit(solution)/shard_map/ppermute | solution.py:446
  124.4 13.0 %collective-permute-start.9 = (bf16[528,256]{1,0:T(8,128)(2,1)S(1)}, bf16[528,256]{1,0:T(8,128)(2,1)S(1)}, u32[]{:S(2)}, u32[]{:S(2)}) collective-permute-start(bf16[528,256]{1,0:T(8,128)(2,1)S(1)} %collective-permute-done.8.rest_10_), channel_id=1, source_target_pairs={{0,1},{1,0},{2,3},{3,2},{4,5},{5,4},{6,7},{7,6},{8,9},{9,8},{10,11... | collective-permute-start | bytes 811016 | tf_op jit(solution)/shard_map/ppermute | solution.py:446
  124.8 12.6 %collective-permute-start.11 = (bf16[528,256]{1,0:T(8,128)(2,1)S(1)}, bf16[528,256]{1,0:T(8,128)(2,1)S(1)}, u32[]{:S(2)}, u32[]{:S(2)}) collective-permute-start(bf16[528,256]{1,0:T(8,128)(2,1)S(1)} %collective-permute-done.10.rest_12_), channel_id=1, source_target_pairs={{0,1},{1,0},{2,3},{3,2},{4,5},{5,4},{6,7},{7,6},{8,9},{9,8},{10,11... | collective-permute-start | bytes 811016 | tf_op jit(solution)/shard_map/ppermute | solution.py:446
  124.9 13.0 %collective-permute-start.13 = (bf16[528,256]{1,0:T(8,128)(2,1)S(1)}, bf16[528,256]{1,0:T(8,128)(2,1)S(1)}, u32[]{:S(2)}, u32[]{:S(2)}) collective-permute-start(bf16[528,256]{1,0:T(8,128)(2,1)S(1)} %collective-permute-done.12.rest_14_), channel_id=1, source_target_pairs={{0,1},{1,0},{2,3},{3,2},{4,5},{5,4},{6,7},{7,6},{8,9},{9,8},{10,11... | collective-permute-start | bytes 811016 | tf_op jit(solution)/shard_map/ppermute | solution.py:446
  136.8 1.6 collective-permute-start.23
  136.9 1.8 collective-permute-start.25
  137.4 1.8 collective-permute-start.27
  137.4 2.1 collective-permute-start.29
  137.9 2.1 collective-permute-start.3
  177.4 1.3 collective-permute-start.31
  (11 other events, 192.3 us)

commit v6 on v5

--- a/solution.py
+++ b/solution.py
@@ -111,21 +111,13 @@
     lax.fori_loop(0, user_ref.shape[0], start, 0)
 
 
-def start_items(item_hbm, item_ref, sem):
-    def start(k, carry):
-        pltpu.make_async_copy(item_hbm.at[k], item_ref.at[k], sem.at[k]).start()
-        return carry
-
-    lax.fori_loop(0, item_ref.shape[0], start, 0)
-
-
 def item_landed(item, item_ref, item_sem):
     pltpu.make_async_copy(item_ref.at[item], item_ref.at[item], item_sem.at[item]).wait()
 
 
 def sweep_users(
     user_hbm, scale_hbm, user_ref, scale_ref, item_ref, row_sem, item_sem, item_scale_ref, dual_scr,
-    dots_a, dots_b, finish, fanout, keep=None
+    dots_a, dots_b, finish, fanout, keep
 ):
     clusters, users, _ = user_ref.shape
     camps = item_scale_ref.shape[1]
@@ -137,8 +129,6 @@
         pltpu.make_async_copy(scale_hbm.at[k], scale_ref.at[k], row_sem.at[1, k]).wait()
         for e in range(fanout):
             item_landed(k * fanout + e, item_ref, item_sem)
-        if keep is not None:
-            keep(k).start()
 
     def multiply(k, dots):
         blocks = item_ref[pl.ds(pl.multiple_of(k * fanout, fanout), fanout)].reshape(fanout * camps, width)
@@ -178,13 +168,19 @@
         cluster(k, dots_a)
         multiply(jnp.minimum(k + 2, clusters - 1), dots_a)
         cluster(k + 1, dots_b)
+        keep(k).start()
+        keep(k + 1).start()
         return carry
 
     lax.fori_loop(0, clusters // 2, two, 0)
 
 
-def spend_finish(where_ref, size_ref, users, fanout, spend_scr):
+def spend_finish(where_ref, size_ref, users, fanout, spend_scr, kept_ref=None):
     def finish(k, start, rows, weights, den, sums):
+        if start is not None and kept_ref is not None:
+            camps = weights[0].shape[1]
+            for e in range(fanout):
+                kept_ref[k, start : start + rows, e * camps : (e + 1) * camps] = weights[e].astype(kept_ref.dtype)
         if start is None:
             for e in range(fanout):
                 spend_scr[pl.ds(k * fanout + e, 1), :] = jnp.sum(sums[e], axis=0, keepdims=True)
@@ -232,9 +228,9 @@
     shards, half, fanout, camps, pieces, where_ref, size_ref, item_at_ref, user_hbm, scale_hbm, *rest
 ):
     received, outs = rest[: 2 * shards], rest[2 * shards :][:7]
-    mine_ref, theirs_ref, duals_ref, limit_ref, live_ref, item_scale_ref, item_out = outs
-    user_ref, scale_ref, item_ref, row_sem, item_sem, dots_a, dots_b, dual_scr, spend_scr = rest[-12:-3]
-    landed_ref, fact_sem, out_sem = rest[-3:]
+    mine_ref, theirs_ref, duals_ref, limit_ref, live_ref, item_scale_ref, kept_out = outs
+    user_ref, scale_ref, item_ref, row_sem, item_sem, dots_a, dots_b, dual_scr, spend_scr = rest[-13:-4]
+    landed_ref, fact_sem, kept_ref, out_sem = rest[-4:]
     cap = 2 * half
     rep = where_ref[1]
     users = user_ref.shape[1]
@@ -257,11 +253,10 @@
     item_facts(landed_ref, fact_sem, duals_ref, limit_ref, live_ref, item_scale_ref)
 
     def keep(k):
-        rows = pl.ds(pl.multiple_of(k * fanout, fanout), fanout)
-        return pltpu.make_async_copy(item_ref.at[rows], item_out.at[rows], out_sem.at[k])
+        return pltpu.make_async_copy(kept_ref.at[k], kept_out.at[k], out_sem.at[k])
 
     dual_scr[...] = jnp.where(live_ref[...] > 0.0, duals_ref[...] * gain, masked)
-    finish = spend_finish(where_ref, size_ref, users, fanout, spend_scr)
+    finish = spend_finish(where_ref, size_ref, users, fanout, spend_scr, kept_ref)
     sweep_users(
         user_hbm, scale_hbm, user_ref, scale_ref, item_ref, row_sem, item_sem, item_scale_ref,
         dual_scr, dots_a, dots_b, finish, fanout, keep
@@ -275,36 +270,68 @@
     lax.fori_loop(0, user_ref.shape[0], kept, 0)
 
 
+def start_kept(kept_hbm, kept_ref, sem):
+    def start(k, carry):
+        pltpu.make_async_copy(kept_hbm.at[k], kept_ref.at[k], sem.at[k]).start()
+        return carry
+
+    lax.fori_loop(0, kept_ref.shape[0], start, 0)
+
+
+def reweigh(kept_hbm, kept_ref, sem, ratio_scr, finish, fanout):
+    clusters, users, wide = kept_ref.shape
+    camps = wide // fanout
+    rows = 64
+
+    def cluster(k):
+        ratio = ratio_scr[pl.ds(pl.multiple_of(k * fanout, fanout), fanout), :]
+        ratios = [jnp.broadcast_to(ratio[e : e + 1], (rows, camps)) for e in range(fanout)]
+        sums = [jnp.zeros((8, camps), jnp.float32) for _ in range(fanout)]
+        for start in range(0, users, rows):
+            kept = [
+                kept_ref[k, start : start + rows, e * camps : (e + 1) * camps].astype(jnp.float32)
+                for e in range(fanout)
+            ]
+            weights = [one * by for one, by in zip(kept, ratios)]
+            den = 1.0 + jnp.sum(functools.reduce(jnp.add, weights), axis=1, keepdims=True)
+            sums = finish(k, start, rows, kept, den, sums)
+        finish(k, None, rows, None, None, sums)
+
+    def two(n, carry):
+        for k in (2 * n, 2 * n + 1):
+            pltpu.make_async_copy(kept_hbm.at[k], kept_ref.at[k], sem.at[k]).wait()
+        cluster(2 * n)
+        cluster(2 * n + 1)
+        return carry
+
+    lax.fori_loop(0, clusters // 2, two, 0)
+
+
 def second_kernel(
-    fanout, where_ref, size_ref, duals_ref, live_ref, item_scale_ref, limit_ref, match_ref, got_ref, other_ref,
-    user_hbm, scale_hbm, item_hbm, mine_ref, theirs_ref, next_ref, user_ref, scale_ref, item_ref, row_sem, item_sem,
-    dots_a, dots_b, dual_scr, spend_scr
+    fanout, where_ref, size_ref, duals_ref, limit_ref, match_ref, got_ref, other_ref, kept_hbm, mine_ref, theirs_ref,
+    next_ref, kept_ref, sem, ratio_scr, spend_scr
 ):
-    start_items(item_hbm, item_ref, item_sem)
-    start_rows(user_hbm, scale_hbm, user_ref, scale_ref, row_sem)
+    start_kept(kept_hbm, kept_ref, sem)
     duals = updated(duals_ref[...], totals(match_ref, got_ref, other_ref), limit_ref[...])
     next_ref[...] = duals
-    dual_scr[...] = jnp.where(live_ref[...] > 0.0, duals * gain, masked)
-    finish = spend_finish(where_ref, size_ref, user_ref.shape[1], fanout, spend_scr)
-    sweep_users(
-        user_hbm, scale_hbm, user_ref, scale_ref, item_ref, row_sem, item_sem, item_scale_ref,
-        dual_scr, dots_a, dots_b, finish, fanout
-    )
+    ratio_scr[...] = jnp.exp2((duals_ref[...] - duals) * gain)
+    finish = spend_finish(where_ref, size_ref, kept_ref.shape[1], fanout, spend_scr)
+    reweigh(kept_hbm, kept_ref, sem, ratio_scr, finish, fanout)
+    spend_scr[...] = spend_scr[...] * ratio_scr[...]
     halves(where_ref, spend_scr, mine_ref, theirs_ref)
 
 
 def third_kernel(
-    fanout, where_ref, size_ref, duals_ref, live_ref, item_scale_ref, limit_ref, match_ref, got_ref, other_ref,
-    own_match_ref, got_one_ref, other_one_ref, own_dual_ref, own_limit_ref, user_hbm, scale_hbm, item_hbm,
-    user_dual_ref, own_out_ref, user_ref, scale_ref, item_ref, row_sem, item_sem, dots_a, dots_b, dual_scr, row_scr
+    fanout, where_ref, size_ref, start_ref, duals_ref, limit_ref, match_ref, got_ref, other_ref, own_match_ref,
+    got_one_ref, other_one_ref, own_dual_ref, own_limit_ref, kept_hbm, user_dual_ref, own_out_ref, kept_ref, sem,
+    ratio_scr, row_scr
 ):
-    start_items(item_hbm, item_ref, item_sem)
-    start_rows(user_hbm, scale_hbm, user_ref, scale_ref, row_sem)
+    start_kept(kept_hbm, kept_ref, sem)
     duals = updated(duals_ref[...], totals(match_ref, got_ref, other_ref), limit_ref[...])
-    dual_scr[...] = jnp.where(live_ref[...] > 0.0, duals * gain, masked)
+    ratio_scr[...] = jnp.exp2((start_ref[...] - duals) * gain)
     own = updated(own_dual_ref[...], totals(own_match_ref, got_one_ref, other_one_ref), own_limit_ref[...])
     own_out_ref[...] = updated(own, totals(own_match_ref, got_ref, other_ref), own_limit_ref[...])
-    users = user_ref.shape[1]
+    users = kept_ref.shape[1]
     partial = []
 
     def finish(k, start, rows, weights, den, sums):
@@ -329,10 +356,7 @@
         )
         return sums
 
-    sweep_users(
-        user_hbm, scale_hbm, user_ref, scale_ref, item_ref, row_sem, item_sem, item_scale_ref,
-        dual_scr, dots_a, dots_b, finish, fanout
-    )
+    reweigh(kept_hbm, kept_ref, sem, ratio_scr, finish, fanout)
     for n in range(row_scr.shape[1]):
         user_dual_ref[:, n * 128 : (n + 1) * 128] = row_scr[:, n, :]
 
@@ -465,13 +489,13 @@
         pltpu.VMEM((items, camps), f32),
     ]
     spend_work = [pltpu.VMEM((items, camps), f32)]
-    limits = pltpu.CompilerParams(vmem_limit_bytes=24 * 2**20)
-
-    mine, theirs, item_dual, item_limit, item_live, item_scale, item_emb = pl.pallas_call(
+    limits = pltpu.CompilerParams(vmem_limit_bytes=32 * 2**20)
+
+    mine, theirs, item_dual, item_limit, _, _, kept = pl.pallas_call(
         functools.partial(first_kernel, shards, half, fanout, camps, len(rows)),
         out_shape=spend_out
         + [jax.ShapeDtypeStruct((items, camps), f32)] * 4
-        + [pltpu.HBM((items, camps, width), camp_emb.dtype)],
+        + [pltpu.HBM((clusters, users, fanout * camps), jnp.bfloat16)],
         in_specs=[SMEM] * 3 + [HBM] * 2 + [ANY] * len(received),
         out_specs=[VMEM] * 6 + [HBM],
         scratch_shapes=work
@@ -479,22 +503,27 @@
         + [
             pltpu.VMEM((items, len(rows), camps), camp_emb.dtype),
             pltpu.SemaphoreType.DMA((items,)),
+            pltpu.VMEM((clusters, users, fanout * camps), jnp.bfloat16),
             pltpu.SemaphoreType.DMA((clusters,)),
         ],
         compiler_params=limits,
     )(where, cluster_size, item_of_slot, user_rows, user_scale, *received)
-    item_emb = in_hbm(item_emb)
+    kept = in_hbm(kept)
     got_one, other_one = exchange(mine, theirs)
+    again = [
+        pltpu.VMEM((clusters, users, fanout * camps), jnp.bfloat16),
+        pltpu.SemaphoreType.DMA((clusters,)),
+        pltpu.VMEM((items, camps), f32),
+    ]
 
     mine, theirs, next_dual = pl.pallas_call(
         functools.partial(second_kernel, fanout),
         out_shape=spend_out + [jax.ShapeDtypeStruct((items, camps), f32)],
-        in_specs=[SMEM] * 2 + [VMEM] * 7 + [HBM] * 3,
+        in_specs=[SMEM] * 2 + [VMEM] * 5 + [HBM],
         out_specs=[VMEM] * 3,
-        scratch_shapes=work + spend_work,
+        scratch_shapes=again + spend_work,
         compiler_params=limits,
-    )(where, cluster_size, item_dual, item_live, item_scale, item_limit, match, got_one, other_one, user_rows,
-      user_scale, item_emb)
+    )(where, cluster_size, item_dual, item_limit, match, got_one, other_one, kept)
     got_two, other_two = exchange(mine, theirs)
 
     user_dual, own_dual = pl.pallas_call(
@@ -503,12 +532,12 @@
             jax.ShapeDtypeStruct((clusters, users), f32),
             jax.ShapeDtypeStruct((blocks, camps), f32),
         ],
-        in_specs=[SMEM] * 2 + [VMEM] * 12 + [HBM] * 3,
+        in_specs=[SMEM] * 2 + [VMEM] * 11 + [HBM],
         out_specs=[VMEM] * 2,
-        scratch_shapes=work + [pltpu.VMEM((clusters, users // 128, 128), f32)],
+        scratch_shapes=again + [pltpu.VMEM((clusters, users // 128, 128), f32)],
         compiler_params=limits,
-    )(where, cluster_size, next_dual, item_live, item_scale, item_limit, match, got_two, other_two, own_match,
-      got_one, other_one, dual_init, spend_limit, user_rows, user_scale, item_emb)
+    )(where, cluster_size, item_dual, next_dual, item_limit, match, got_two, other_two, own_match, got_one, other_one,
+      dual_init, spend_limit, kept)
     return (user_dual, own_dual)
 
 

time: 213 us -> 205 us (0.962)
  Pallas kernels: 57.5 us -> 49.2 us
    pallas_call x1, Pallas kernels: 9.96 us -> 5.27 us  [program(): pl.pallas_call(functools.partial(second_kernel, fanout), out_shape=spend_...]
    pallas_call x1, Pallas kernels: 9.77 us -> 5.08 us  [program(): pl.pallas_call(functools.partial(third_kernel, fanout), out_shape=[jax.Sh...]
  transfers between devices with their start and end apart: 35 -> 35, of which waited for: 21 -> 21; matrix products, arithmetic and copies ran while one was open for 5% -> 6% of each run, Pallas kernels for 9% -> 9%
where the time goes in v6:
time: 205 us; the launch traced here: 204 us
  waiting for transfers between devices  70.1 us (34%)
  Pallas kernels  49.2 us (24%)
  starting transfers between devices  36.5 us (18%)
  blocking collectives  31 us (15%)
  local copies, waits for them, and re-layouts  11.6 us (6%)
  other arithmetic  5.18 us (3%)
    ppermute x15, waiting for transfers between devices, program(): lax.ppermute(sent[shift, False], 'shard', [(i, i ^ shift) for i in range(...  60.2 us
    all_to_all x2, blocking collectives, exchange(): lax.all_to_all(spread, 'shard', split_axis=0, concat_axis=0, tiled=True)  31 us
    ppermute x15, starting transfers between devices, program(): lax.ppermute(sent[shift, False], 'shard', [(i, i ^ shift) for i in range(...  25.1 us
    pallas_call x1, Pallas kernels, program(): pl.pallas_call(functools.partial(first_kernel, shards, half, fanout, camp...  17.1 us
    pallas_call x2, Pallas kernels, program(): pl.pallas_call(functools.partial(gather_kernel, half, some), out_shape=[p...  12.6 us
    pallas_call x1, Pallas kernels, program(): pl.pallas_call(user_kernel, out_shape=jax.ShapeDtypeStruct((clusters, use...  9.19 us
    all_to_all x1, starting transfers between devices, program(): lax.all_to_all(ask, 'shard', split_axis=0, concat_axis=0, tiled=True)  8.34 us
    pallas_call x1, Pallas kernels, program(): pl.pallas_call(functools.partial(second_kernel, fanout), out_shape=spend_...  5.27 us
  transfers between devices with their start and end apart: 35, of which 21 were waited for; matrix products, arithmetic and copies ran while one was open for 6% of the time, Pallas kernels for 9%

profile of v6, /device:TPU:0, one launch (start us, length us, event | category | flops | bytes accessed | tf_op | source)
XLA Modules:
  0.0 204.4 jit_solution(15982901502486564978)
XLA Ops:
  3.4 8.3 %all-to-all-start = ((s32[16,1,72]{2,1,0:T(1,128)}), s32[16,1,72]{2,1,0:T(1,128)S(1)}, u32[]{:S(2)}, u32[]{:S(2)}) async-start(s32[16,1,72]{2,1,0:T(1,128)} %bitcast.4), calls=%async_computation | async-start | bytes 16384 | tf_op jit(solution)/shard_map/all_to_all | solution.py:393
  14.8 1.5 stack.63.fact_ref
  16.2 2.8 %all-to-all-done = s32[16,1,72]{2,1,0:T(1,128)S(1)} async-done(((s32[16,1,72]{2,1,0:T(1,128)}), s32[16,1,72]{2,1,0:T(1,128)S(1)}, u32[]{:S(2)}, u32[]{:S(2)}) %all-to-all-start) | async-done | bytes 4640 | tf_op jit(solution)/shard_map/all_to_all | solution.py:393
  19.0 3.9 %shard_map.97 = (bf16[528,256]{1,0:T(8,128)(2,1)}, bf16[528,256]{1,0:T(8,128)(2,1)}, bf16[528,256]{1,0:T(8,128)(2,1)}, bf16[528,256]{1,0:T(8,128)(2,1)}) custom-call(s32[2]{0:T(128)S(1)} %pad_add_fusion.1.where_ref, s32[16,72]{1,0:T(8,128)S(1)} %bitcast.29, bf16[128,128,256]{2,1,0:T(8,128)(2,1)} %camp_ref.3, bf16[128,8,128]{2,1,0:T(8,128)(2,1)} %stack.63.fact_ref), custom_call_target="tpu_custom_call" | custom-call | bytes 2097152 | tf_op jit(solution)/shard_map/pallas_call | solution.py:414
  23.5 2.4 %collective-permute-start.16 = (bf16[528,256]{1,0:T(8,128)(2,1)}, bf16[528,256]{1,0:T(8,128)(2,1)S(1)}, u32[]{:S(2)}, u32[]{:S(2)}) collective-permute-start(bf16[528,256]{1,0:T(8,128)(2,1)} %get-tuple-element.49), channel_id=1, source_target_pairs={{0,18},{2,16},{4,22},{6,20},{8,26},{10,24},{12,30},{14,28},{16,2},... | collective-permute-start | bytes 811016 | tf_op jit(solution)/shard_map/ppermute | solution.py:430
  26.0 1.9 collective-permute-start.18
  27.8 2.7 %collective-permute-start.20 = (bf16[528,256]{1,0:T(8,128)(2,1)}, bf16[528,256]{1,0:T(8,128)(2,1)S(1)}, u32[]{:S(2)}, u32[]{:S(2)}) collective-permute-start(bf16[528,256]{1,0:T(8,128)(2,1)} %get-tuple-element.51), channel_id=1, source_target_pairs={{0,22},{2,20},{4,18},{6,16},{8,30},{10,28},{12,26},{14,24},{16,6},... | collective-permute-start | bytes 811016 | tf_op jit(solution)/shard_map/ppermute | solution.py:430
  30.6 8.7 %shard_map.95 = (bf16[528,256]{1,0:T(8,128)(2,1)}, bf16[528,256]{1,0:T(8,128)(2,1)}, bf16[528,256]{1,0:T(8,128)(2,1)}, bf16[528,256]{1,0:T(8,128)(2,1)}, bf16[52...) custom-call(s32[2]{0:T(128)S(1)} %pad_add_fusion.1.where_ref, ...), custom_call_target="tpu_custom_call" | custom-call | bytes 6815744 | tf_op jit(solution)/shard_map/pallas_call | solution.py:414
  39.5 15.1 %collective-permute-done.14.rest_16_ = bf16[528,256]{1,0:T(8,128)(2,1)S(1)} collective-permute-done((bf16[528,256]{1,0:T(8,128)(2,1)}, bf16[528,256]{1,0:T(8,128)(2,1)S(1)}, u32[]{:S(2)}, u32[]{:S(2)}) %collective-permute-start.14) | collective-permute-done | bytes 270368 | tf_op jit(solution)/shard_map/ppermute | solution.py:430
  55.1 5.3 %collective-permute-done.16.rest_18_ = bf16[528,256]{1,0:T(8,128)(2,1)S(1)} collective-permute-done((bf16[528,256]{1,0:T(8,128)(2,1)}, bf16[528,256]{1,0:T(8,128)(2,1)S(1)}, u32[]{:S(2)}, u32[]{:S(2)}) %collective-permute-start.16) | collective-permute-done | bytes 270368 | tf_op jit(solution)/shard_map/ppermute | solution.py:430
  60.4 1.8 collective-permute-start.4
  62.2 4.3 %collective-permute-done.18.rest_20_ = bf16[528,256]{1,0:T(8,128)(2,1)S(1)} collective-permute-done((bf16[528,256]{1,0:T(8,128)(2,1)}, bf16[528,256]{1,0:T(8,128)(2,1)S(1)}, u32[]{:S(2)}, u32[]{:S(2)}) %collective-permute-start.18) | collective-permute-done | bytes 270368 | tf_op jit(solution)/shard_map/ppermute | solution.py:430
  66.6 5.9 %collective-permute-done.20.rest_22_ = bf16[528,256]{1,0:T(8,128)(2,1)S(1)} collective-permute-done((bf16[528,256]{1,0:T(8,128)(2,1)}, bf16[528,256]{1,0:T(8,128)(2,1)S(1)}, u32[]{:S(2)}, u32[]{:S(2)}) %collective-permute-start.20) | collective-permute-done | bytes 270368 | tf_op jit(solution)/shard_map/ppermute | solution.py:430
  72.5 3.4 %collective-permute-start.10 = (bf16[528,256]{1,0:T(8,128)(2,1)}, bf16[528,256]{1,0:T(8,128)(2,1)S(1)}, u32[]{:S(2)}, u32[]{:S(2)}) collective-permute-start(bf16[528,256]{1,0:T(8,128)(2,1)} %get-tuple-element.46), channel_id=1, source_target_pairs={{0,12},{2,14},{4,8},{6,10},{8,4},{10,6},{12,0},{14,2},{16,28},{18,... | collective-permute-start | bytes 811016 | tf_op jit(solution)/shard_map/ppermute | solution.py:430
  76.2 1.9 collective-permute-done.4.rest_6_
  78.1 3.3 %collective-permute-start.22 = (bf16[528,256]{1,0:T(8,128)(2,1)}, bf16[528,256]{1,0:T(8,128)(2,1)}, u32[]{:S(2)}, u32[]{:S(2)}) collective-permute-start(bf16[528,256]{1,0:T(8,128)(2,1)} %get-tuple-element.52), channel_id=1, source_target_pairs={{0,24},{2,26},{4,28},{6,30},{8,16},{10,18},{12,20},{14,22},{16,8},... | collective-permute-start | bytes 811016 | tf_op jit(solution)/shard_map/ppermute | solution.py:430
  81.9 1.7 collective-permute-done.8.rest_10_
  83.6 3.7 %collective-permute-start.26 = (bf16[528,256]{1,0:T(8,128)(2,1)}, bf16[528,256]{1,0:T(8,128)(2,1)}, u32[]{:S(2)}, u32[]{:S(2)}) collective-permute-start(bf16[528,256]{1,0:T(8,128)(2,1)} %get-tuple-element.54), channel_id=1, source_target_pairs={{0,28},{2,30},{4,24},{6,26},{8,20},{10,22},{12,16},{14,18},{16,12}... | collective-permute-start | bytes 811016 | tf_op jit(solution)/shard_map/ppermute | solution.py:430
  87.3 1.9 collective-permute-done.10.rest_12_
  89.2 3.7 %collective-permute-start.28 = (bf16[528,256]{1,0:T(8,128)(2,1)}, bf16[528,256]{1,0:T(8,128)(2,1)}, u32[]{:S(2)}, u32[]{:S(2)}) collective-permute-start(bf16[528,256]{1,0:T(8,128)(2,1)} %get-tuple-element.55), channel_id=1, source_target_pairs={{0,30},{2,28},{4,26},{6,24},{8,22},{10,20},{12,18},{14,16},{16,14}... | collective-permute-start | bytes 811016 | tf_op jit(solution)/shard_map/ppermute | solution.py:430
  95.0 1.4 copy.67
  96.4 7.2 %collective-permute-done.22.rest_24_ = bf16[528,256]{1,0:T(8,128)(2,1)} collective-permute-done((bf16[528,256]{1,0:T(8,128)(2,1)}, bf16[528,256]{1,0:T(8,128)(2,1)}, u32[]{:S(2)}, u32[]{:S(2)}) %collective-permute-start.22) | collective-permute-done | bytes 270368 | tf_op jit(solution)/shard_map/ppermute | solution.py:430
  103.6 5.7 %collective-permute-done.24.rest_26_ = bf16[528,256]{1,0:T(8,128)(2,1)} collective-permute-done((bf16[528,256]{1,0:T(8,128)(2,1)}, bf16[528,256]{1,0:T(8,128)(2,1)}, u32[]{:S(2)}, u32[]{:S(2)}) %collective-permute-start.24) | collective-permute-done | bytes 270368 | tf_op jit(solution)/shard_map/ppermute | solution.py:430
  109.3 5.9 %collective-permute-done.26.rest_28_ = bf16[528,256]{1,0:T(8,128)(2,1)} collective-permute-done((bf16[528,256]{1,0:T(8,128)(2,1)}, bf16[528,256]{1,0:T(8,128)(2,1)}, u32[]{:S(2)}, u32[]{:S(2)}) %collective-permute-start.26) | collective-permute-done | bytes 270368 | tf_op jit(solution)/shard_map/ppermute | solution.py:430
  115.2 5.3 %collective-permute-done.28.rest_30_ = bf16[528,256]{1,0:T(8,128)(2,1)} collective-permute-done((bf16[528,256]{1,0:T(8,128)(2,1)}, bf16[528,256]{1,0:T(8,128)(2,1)}, u32[]{:S(2)}, u32[]{:S(2)}) %collective-permute-start.28) | collective-permute-done | bytes 270368 | tf_op jit(solution)/shard_map/ppermute | solution.py:430
  126.0 9.2 %shard_map.96.scale_hbm = f32[16,512,128]{2,1,0:T(8,128)S(1)} custom-call(bf16[16,512,256]{2,1,0:T(8,128)(2,1)} %user_hbm.1), custom_call_target="tpu_custom_call" | custom-call | flops 8388608 | bytes 8388608 | tf_op jit(solution)/shard_map/pallas_call | solution.py:446
  135.2 2.0 copy-done
  140.7 17.1 %shard_map.98 = (f32[32,128]{1,0:T(8,128)S(1)}, f32[32,128]{1,0:T(8,128)S(1)}, f32[64,128]{1,0:T(8,128)S(1)}, f32[64,128]{1,0:T(8,128)S(1)}, f32[64,128]{1,0:T(8...) custom-call(s32[2]{0:T(128)S(1)} %pad_add_fusion.1.where_ref, s32[16]{0:T(128)S(1)} %copy-done.5, ...), custom_call_target="tpu_custom_call" | custom-call | tf_op jit(solution)/shard_map/pallas_call | solution.py:494
  159.0 20.3 %all_to_all.21 = bf16[16,32,128]{2,1,0:T(8,128)(2,1)S(1)} all-to-all(bf16[16,32,128]{2,1,0:T(8,128)(2,1)S(1)} %broadcast_in_dim.53), channel_id=1, replica_groups=mesh['shard'=16,'rep'=2] {'shard'}, dimensions={0} | all-to-all | bytes 262144 | tf_op jit(solution)/shard_map/all_to_all | solution.py:476
  180.6 5.3 %shard_map.99 = (f32[32,128]{1,0:T(8,128)S(1)}, f32[32,128]{1,0:T(8,128)S(1)}, f32[64,128]{1,0:T(8,128)S(1)}) custom-call(s32[2]{0:T(128)S(1)} %pad_add_fusion.1.where_ref, s32[16]{0:T(128)S(1)} %copy-done.5, f32[64,128]{1,0:T(8,128)S(1)} %get-tuple-element.56.duals_ref.start_ref, f32[64,128]{1,0:T(8,128)S(1)} %get-tuple-element.57.limit_ref, ...), custom_call_target="tpu_custom_call" | custom-call | tf_op jit(solution)/shard_map/pallas_call | solution.py:519
  187.2 10.7 %all_to_all.22 = bf16[16,32,128]{2,1,0:T(8,128)(2,1)S(1)} all-to-all(bf16[16,32,128]{2,1,0:T(8,128)(2,1)S(1)} %broadcast_in_dim.54), channel_id=1, replica_groups=mesh['shard'=16,'rep'=2] {'shard'}, dimensions={0} | all-to-all | bytes 262144 | tf_op jit(solution)/shard_map/all_to_all | solution.py:476
  199.3 5.1 %shard_map.100 = (f32[16,512]{1,0:T(8,128)}, f32[128,128]{1,0:T(8,128)}) custom-call(s32[2]{0:T(128)S(1)} %pad_add_fusion.1.where_ref, s32[16]{0:T(128)S(1)} %copy-done.5, f32[64,128]{1,0:T(8,128)S(1)} %get-tuple-element.56.duals_ref.start_ref, f32[64,128]{1,0:T(8,128)S(1)} %get-tuple-element.62.duals_ref, f32[64,128]{1,0:T(8,128)S(1)} %get-tuple-element.57.limit_ref, ...), custom_call_target="tpu_custom_call" | custom-call | tf_op jit(solution)/shard_map/pallas_call | solution.py:529
  (107 shorter events, 24.1 us)
Async XLA Ops:
  3.4 15.6 %all-to-all-start = ((s32[16,1,72]{2,1,0:T(1,128)}), s32[16,1,72]{2,1,0:T(1,128)S(1)}, u32[]{:S(2)}, u32[]{:S(2)}) async-start(s32[16,1,72]{2,1,0:T(1,128)} %bitcast.4), calls=%async_computation | async-start | bytes 16384 | tf_op jit(solution)/shard_map/all_to_all | solution.py:393
  22.9 31.8 %collective-permute-start.14 = (bf16[528,256]{1,0:T(8,128)(2,1)}, bf16[528,256]{1,0:T(8,128)(2,1)S(1)}, u32[]{:S(2)}, u32[]{:S(2)}) collective-permute-start(bf16[528,256]{1,0:T(8,128)(2,1)} %get-tuple-element.48), channel_id=1, source_target_pairs={{0,16},{2,18},{4,20},{6,22},{8,24},{10,26},{12,28},{14,30},{16,0},... | collective-permute-start | bytes 811016 | tf_op jit(solution)/shard_map/ppermute | solution.py:430
  23.5 36.9 %collective-permute-start.16 = (bf16[528,256]{1,0:T(8,128)(2,1)}, bf16[528,256]{1,0:T(8,128)(2,1)S(1)}, u32[]{:S(2)}, u32[]{:S(2)}) collective-permute-start(bf16[528,256]{1,0:T(8,128)(2,1)} %get-tuple-element.49), channel_id=1, source_target_pairs={{0,18},{2,16},{4,22},{6,20},{8,26},{10,24},{12,30},{14,28},{16,2},... | collective-permute-start | bytes 811016 | tf_op jit(solution)/shard_map/ppermute | solution.py:430
  26.0 40.6 %collective-permute-start.18 = (bf16[528,256]{1,0:T(8,128)(2,1)}, bf16[528,256]{1,0:T(8,128)(2,1)S(1)}, u32[]{:S(2)}, u32[]{:S(2)}) collective-permute-start(bf16[528,256]{1,0:T(8,128)(2,1)} %get-tuple-element.50), channel_id=1, source_target_pairs={{0,20},{2,22},{4,16},{6,18},{8,28},{10,30},{12,24},{14,26},{16,4},... | collective-permute-start | bytes 811016 | tf_op jit(solution)/shard_map/ppermute | solution.py:430
  27.8 44.6 %collective-permute-start.20 = (bf16[528,256]{1,0:T(8,128)(2,1)}, bf16[528,256]{1,0:T(8,128)(2,1)S(1)}, u32[]{:S(2)}, u32[]{:S(2)}) collective-permute-start(bf16[528,256]{1,0:T(8,128)(2,1)} %get-tuple-element.51), channel_id=1, source_target_pairs={{0,22},{2,20},{4,18},{6,16},{8,30},{10,28},{12,26},{14,24},{16,6},... | collective-permute-start | bytes 811016 | tf_op jit(solution)/shard_map/ppermute | solution.py:430
  39.3 33.2 %collective-permute-start = (bf16[528,256]{1,0:T(8,128)(2,1)}, bf16[528,256]{1,0:T(8,128)(2,1)S(1)}, u32[]{:S(2)}, u32[]{:S(2)}) collective-permute-start(bf16[528,256]{1,0:T(8,128)(2,1)} %get-tuple-element.34), channel_id=1, source_target_pairs={{0,4},{2,6},{4,0},{6,2},{8,12},{10,14},{12,8},{14,10},{16,20},{18,... | collective-permute-start | bytes 811016 | tf_op jit(solution)/shard_map/ppermute | solution.py:430
  54.6 21.4 %collective-permute-start.1 = (bf16[528,256]{1,0:T(8,128)(2,1)}, bf16[528,256]{1,0:T(8,128)(2,1)S(1)}, u32[]{:S(2)}, u32[]{:S(2)}) collective-permute-start(bf16[528,256]{1,0:T(8,128)(2,1)} %get-tuple-element.35), channel_id=1, source_target_pairs={{0,2},{2,0},{4,6},{6,4},{8,10},{10,8},{12,14},{14,12},{16,18},{18,... | collective-permute-start | bytes 811016 | tf_op jit(solution)/shard_map/ppermute | solution.py:430
  60.4 17.7 %collective-permute-start.4 = (bf16[528,256]{1,0:T(8,128)(2,1)}, bf16[528,256]{1,0:T(8,128)(2,1)S(1)}, u32[]{:S(2)}, u32[]{:S(2)}) collective-permute-start(bf16[528,256]{1,0:T(8,128)(2,1)} %get-tuple-element.43), channel_id=1, source_target_pairs={{0,6},{2,4},{4,2},{6,0},{8,14},{10,12},{12,10},{14,8},{16,22},{18,... | collective-permute-start | bytes 811016 | tf_op jit(solution)/shard_map/ppermute | solution.py:430
  66.6 14.8 %collective-permute-start.6 = (bf16[528,256]{1,0:T(8,128)(2,1)}, bf16[528,256]{1,0:T(8,128)(2,1)S(1)}, u32[]{:S(2)}, u32[]{:S(2)}) collective-permute-start(bf16[528,256]{1,0:T(8,128)(2,1)} %get-tuple-element.44), channel_id=1, source_target_pairs={{0,8},{2,10},{4,12},{6,14},{8,0},{10,2},{12,4},{14,6},{16,24},{18,... | collective-permute-start | bytes 811016 | tf_op jit(solution)/shard_map/ppermute | solution.py:430
  72.5 11.2 %collective-permute-start.8 = (bf16[528,256]{1,0:T(8,128)(2,1)}, bf16[528,256]{1,0:T(8,128)(2,1)S(1)}, u32[]{:S(2)}, u32[]{:S(2)}) collective-permute-start(bf16[528,256]{1,0:T(8,128)(2,1)} %get-tuple-element.45), channel_id=1, source_target_pairs={{0,10},{2,8},{4,14},{6,12},{8,2},{10,0},{12,6},{14,4},{16,26},{18,... | collective-permute-start | bytes 811016 | tf_op jit(solution)/shard_map/ppermute | solution.py:430
  72.5 16.8 %collective-permute-start.10 = (bf16[528,256]{1,0:T(8,128)(2,1)}, bf16[528,256]{1,0:T(8,128)(2,1)S(1)}, u32[]{:S(2)}, u32[]{:S(2)}) collective-permute-start(bf16[528,256]{1,0:T(8,128)(2,1)} %get-tuple-element.46), channel_id=1, source_target_pairs={{0,12},{2,14},{4,8},{6,10},{8,4},{10,6},{12,0},{14,2},{16,28},{18,... | collective-permute-start | bytes 811016 | tf_op jit(solution)/shard_map/ppermute | solution.py:430
  76.0 20.4 %collective-permute-start.12 = (bf16[528,256]{1,0:T(8,128)(2,1)}, bf16[528,256]{1,0:T(8,128)(2,1)S(1)}, u32[]{:S(2)}, u32[]{:S(2)}) collective-permute-start(bf16[528,256]{1,0:T(8,128)(2,1)} %get-tuple-element.47), channel_id=1, source_target_pairs={{0,14},{2,12},{4,10},{6,8},{8,6},{10,4},{12,2},{14,0},{16,30},{18,... | collective-permute-start | bytes 811016 | tf_op jit(solution)/shard_map/ppermute | solution.py:430
  78.1 25.6 %collective-permute-start.22 = (bf16[528,256]{1,0:T(8,128)(2,1)}, bf16[528,256]{1,0:T(8,128)(2,1)}, u32[]{:S(2)}, u32[]{:S(2)}) collective-permute-start(bf16[528,256]{1,0:T(8,128)(2,1)} %get-tuple-element.52), channel_id=1, source_target_pairs={{0,24},{2,26},{4,28},{6,30},{8,16},{10,18},{12,20},{14,22},{16,8},... | collective-permute-start | bytes 811016 | tf_op jit(solution)/shard_map/ppermute | solution.py:430
  81.3 28.0 %collective-permute-start.24 = (bf16[528,256]{1,0:T(8,128)(2,1)}, bf16[528,256]{1,0:T(8,128)(2,1)}, u32[]{:S(2)}, u32[]{:S(2)}) collective-permute-start(bf16[528,256]{1,0:T(8,128)(2,1)} %get-tuple-element.53), channel_id=1, source_target_pairs={{0,26},{2,24},{4,30},{6,28},{8,18},{10,16},{12,22},{14,20},{16,10}... | collective-permute-start | bytes 811016 | tf_op jit(solution)/shard_map/ppermute | solution.py:430
  83.6 31.5 %collective-permute-start.26 = (bf16[528,256]{1,0:T(8,128)(2,1)}, bf16[528,256]{1,0:T(8,128)(2,1)}, u32[]{:S(2)}, u32[]{:S(2)}) collective-permute-start(bf16[528,256]{1,0:T(8,128)(2,1)} %get-tuple-element.54), channel_id=1, source_target_pairs={{0,28},{2,30},{4,24},{6,26},{8,20},{10,22},{12,16},{14,18},{16,12}... | collective-permute-start | bytes 811016 | tf_op jit(solution)/shard_map/ppermute | solution.py:430
  89.2 31.3 %collective-permute-start.28 = (bf16[528,256]{1,0:T(8,128)(2,1)}, bf16[528,256]{1,0:T(8,128)(2,1)}, u32[]{:S(2)}, u32[]{:S(2)}) collective-permute-start(bf16[528,256]{1,0:T(8,128)(2,1)} %get-tuple-element.55), channel_id=1, source_target_pairs={{0,30},{2,28},{4,26},{6,24},{8,22},{10,20},{12,18},{14,16},{16,14}... | collective-permute-start | bytes 811016 | tf_op jit(solution)/shard_map/ppermute | solution.py:430
  96.4 28.4 %collective-permute-start.2 = (bf16[528,256]{1,0:T(8,128)(2,1)S(1)}, bf16[528,256]{1,0:T(8,128)(2,1)}, u32[]{:S(2)}, u32[]{:S(2)}) collective-permute-start(bf16[528,256]{1,0:T(8,128)(2,1)S(1)} %collective-permute-done.1.rest_2_), channel_id=1, source_target_pairs={{0,1},{1,0},{2,3},{3,2},{4,5},{5,4},{6,7},{7,6},{8,9},{9,8},{10,11... | collective-permute-start | bytes 811016 | tf_op jit(solution)/shard_map/ppermute | solution.py:470
  103.6 20.0 %collective-permute-start.15 = (bf16[528,256]{1,0:T(8,128)(2,1)S(1)}, bf16[528,256]{1,0:T(8,128)(2,1)}, u32[]{:S(2)}, u32[]{:S(2)}) collective-permute-start(bf16[528,256]{1,0:T(8,128)(2,1)S(1)} %collective-permute-done.14.rest_16_), channel_id=1, source_target_pairs={{0,1},{1,0},{2,3},{3,2},{4,5},{5,4},{6,7},{7,6},{8,9},{9,8},{10,11... | collective-permute-start | bytes 811016 | tf_op jit(solution)/shard_map/ppermute | solution.py:470
  109.3 14.9 %collective-permute-start.17 = (bf16[528,256]{1,0:T(8,128)(2,1)S(1)}, bf16[528,256]{1,0:T(8,128)(2,1)}, u32[]{:S(2)}, u32[]{:S(2)}) collective-permute-start(bf16[528,256]{1,0:T(8,128)(2,1)S(1)} %collective-permute-done.16.rest_18_), channel_id=1, source_target_pairs={{0,1},{1,0},{2,3},{3,2},{4,5},{5,4},{6,7},{7,6},{8,9},{9,8},{10,11... | collective-permute-start | bytes 811016 | tf_op jit(solution)/shard_map/ppermute | solution.py:470
  115.2 9.2 %collective-permute-start.19 = (bf16[528,256]{1,0:T(8,128)(2,1)S(1)}, bf16[528,256]{1,0:T(8,128)(2,1)}, u32[]{:S(2)}, u32[]{:S(2)}) collective-permute-start(bf16[528,256]{1,0:T(8,128)(2,1)S(1)} %collective-permute-done.18.rest_20_), channel_id=1, source_target_pairs={{0,1},{1,0},{2,3},{3,2},{4,5},{5,4},{6,7},{7,6},{8,9},{9,8},{10,11... | collective-permute-start | bytes 811016 | tf_op jit(solution)/shard_map/ppermute | solution.py:470
  120.5 4.3 %collective-permute-start.21 = (bf16[528,256]{1,0:T(8,128)(2,1)S(1)}, bf16[528,256]{1,0:T(8,128)(2,1)}, u32[]{:S(2)}, u32[]{:S(2)}) collective-permute-start(bf16[528,256]{1,0:T(8,128)(2,1)S(1)} %collective-permute-done.20.rest_22_), channel_id=1, source_target_pairs={{0,1},{1,0},{2,3},{3,2},{4,5},{5,4},{6,7},{7,6},{8,9},{9,8},{10,11... | collective-permute-start | bytes 811016 | tf_op jit(solution)/shard_map/ppermute | solution.py:470
  123.7 13.6 %collective-permute-start.5 = (bf16[528,256]{1,0:T(8,128)(2,1)S(1)}, bf16[528,256]{1,0:T(8,128)(2,1)S(1)}, u32[]{:S(2)}, u32[]{:S(2)}) collective-permute-start(bf16[528,256]{1,0:T(8,128)(2,1)S(1)} %collective-permute-done.4.rest_6_), channel_id=1, source_target_pairs={{0,1},{1,0},{2,3},{3,2},{4,5},{5,4},{6,7},{7,6},{8,9},{9,8},{10,11... | collective-permute-start | bytes 811016 | tf_op jit(solution)/shard_map/ppermute | solution.py:470
  124.3 13.2 %collective-permute-start.7 = (bf16[528,256]{1,0:T(8,128)(2,1)S(1)}, bf16[528,256]{1,0:T(8,128)(2,1)S(1)}, u32[]{:S(2)}, u32[]{:S(2)}) collective-permute-start(bf16[528,256]{1,0:T(8,128)(2,1)S(1)} %collective-permute-done.6.rest_8_), channel_id=1, source_target_pairs={{0,1},{1,0},{2,3},{3,2},{4,5},{5,4},{6,7},{7,6},{8,9},{9,8},{10,11... | collective-permute-start | bytes 811016 | tf_op jit(solution)/shard_map/ppermute | solution.py:470
  124.3 13.5 %collective-permute-start.9 = (bf16[528,256]{1,0:T(8,128)(2,1)S(1)}, bf16[528,256]{1,0:T(8,128)(2,1)S(1)}, u32[]{:S(2)}, u32[]{:S(2)}) collective-permute-start(bf16[528,256]{1,0:T(8,128)(2,1)S(1)} %collective-permute-done.8.rest_10_), channel_id=1, source_target_pairs={{0,1},{1,0},{2,3},{3,2},{4,5},{5,4},{6,7},{7,6},{8,9},{9,8},{10,11... | collective-permute-start | bytes 811016 | tf_op jit(solution)/shard_map/ppermute | solution.py:470
  124.8 13.2 %collective-permute-start.11 = (bf16[528,256]{1,0:T(8,128)(2,1)S(1)}, bf16[528,256]{1,0:T(8,128)(2,1)S(1)}, u32[]{:S(2)}, u32[]{:S(2)}) collective-permute-start(bf16[528,256]{1,0:T(8,128)(2,1)S(1)} %collective-permute-done.10.rest_12_), channel_id=1, source_target_pairs={{0,1},{1,0},{2,3},{3,2},{4,5},{5,4},{6,7},{7,6},{8,9},{9,8},{10,11... | collective-permute-start | bytes 811016 | tf_op jit(solution)/shard_map/ppermute | solution.py:470
  124.9 13.5 %collective-permute-start.13 = (bf16[528,256]{1,0:T(8,128)(2,1)S(1)}, bf16[528,256]{1,0:T(8,128)(2,1)S(1)}, u32[]{:S(2)}, u32[]{:S(2)}) collective-permute-start(bf16[528,256]{1,0:T(8,128)(2,1)S(1)} %collective-permute-done.12.rest_14_), channel_id=1, source_target_pairs={{0,1},{1,0},{2,3},{3,2},{4,5},{5,4},{6,7},{7,6},{8,9},{9,8},{10,11... | collective-permute-start | bytes 811016 | tf_op jit(solution)/shard_map/ppermute | solution.py:470
  137.3 1.8 collective-permute-start.23
  137.4 2.1 %collective-permute-start.25 = (bf16[528,256]{1,0:T(8,128)(2,1)}, bf16[528,256]{1,0:T(8,128)(2,1)S(1)}, u32[]{:S(2)}, u32[]{:S(2)}) collective-permute-start(bf16[528,256]{1,0:T(8,128)(2,1)} %collective-permute-done.24.rest_26_), channel_id=1, source_target_pairs={{0,1},{1,0},{2,3},{3,2},{4,5},{5,4},{6,7},{7,6},{8,9},{9,8},{10,11... | collective-permute-start | bytes 811016 | tf_op jit(solution)/shard_map/ppermute | solution.py:470
  137.9 2.0 collective-permute-start.27
  138.0 2.3 %collective-permute-start.29 = (bf16[528,256]{1,0:T(8,128)(2,1)}, bf16[528,256]{1,0:T(8,128)(2,1)S(1)}, u32[]{:S(2)}, u32[]{:S(2)}) collective-permute-start(bf16[528,256]{1,0:T(8,128)(2,1)} %collective-permute-done.28.rest_30_), channel_id=1, source_target_pairs={{0,1},{1,0},{2,3},{3,2},{4,5},{5,4},{6,7},{7,6},{8,9},{9,8},{10,11... | collective-permute-start | bytes 811016 | tf_op jit(solution)/shard_map/ppermute | solution.py:470
  138.4 2.3 %collective-permute-start.3 = (bf16[528,256]{1,0:T(8,128)(2,1)S(1)}, bf16[528,256]{1,0:T(8,128)(2,1)S(1)}, u32[]{:S(2)}, u32[]{:S(2)}) collective-permute-start(bf16[528,256]{1,0:T(8,128)(2,1)S(1)} %collective-permute-done.rest_4_), channel_id=1, source_target_pairs={{0,1},{1,0},{2,3},{3,2},{4,5},{5,4},{6,7},{7,6},{8,9},{9,8},{10,11... | collective-permute-start | bytes 811016 | tf_op jit(solution)/shard_map/ppermute | solution.py:470
  179.3 1.3 collective-permute-start.31
  (11 other events, 518.6 us)

commit v7 on v6

--- a/solution.py
+++ b/solution.py
@@ -117,7 +117,7 @@
 
 def sweep_users(
     user_hbm, scale_hbm, user_ref, scale_ref, item_ref, row_sem, item_sem, item_scale_ref, dual_scr,
-    dots_a, dots_b, finish, fanout, keep
+    dots_a, dots_b, finish, fanout
 ):
     clusters, users, _ = user_ref.shape
     camps = item_scale_ref.shape[1]
@@ -168,8 +168,6 @@
         cluster(k, dots_a)
         multiply(jnp.minimum(k + 2, clusters - 1), dots_a)
         cluster(k + 1, dots_b)
-        keep(k).start()
-        keep(k + 1).start()
         return carry
 
     lax.fori_loop(0, clusters // 2, two, 0)
@@ -228,9 +226,9 @@
     shards, half, fanout, camps, pieces, where_ref, size_ref, item_at_ref, user_hbm, scale_hbm, *rest
 ):
     received, outs = rest[: 2 * shards], rest[2 * shards :][:7]
-    mine_ref, theirs_ref, duals_ref, limit_ref, live_ref, item_scale_ref, kept_out = outs
-    user_ref, scale_ref, item_ref, row_sem, item_sem, dots_a, dots_b, dual_scr, spend_scr = rest[-13:-4]
-    landed_ref, fact_sem, kept_ref, out_sem = rest[-4:]
+    mine_ref, theirs_ref, duals_ref, limit_ref, live_ref, item_scale_ref, kept_ref = outs
+    user_ref, scale_ref, item_ref, row_sem, item_sem, dots_a, dots_b, dual_scr, spend_scr = rest[-11:-2]
+    landed_ref, fact_sem = rest[-2:]
     cap = 2 * half
     rep = where_ref[1]
     users = user_ref.shape[1]
@@ -251,34 +249,16 @@
                 fetch(n * cap + side * half + j, message.at[pl.ds(j * camps, camps)], message.at[rows, lanes])
     start_rows(user_hbm, scale_hbm, user_ref, scale_ref, row_sem)
     item_facts(landed_ref, fact_sem, duals_ref, limit_ref, live_ref, item_scale_ref)
-
-    def keep(k):
-        return pltpu.make_async_copy(kept_ref.at[k], kept_out.at[k], out_sem.at[k])
-
     dual_scr[...] = jnp.where(live_ref[...] > 0.0, duals_ref[...] * gain, masked)
     finish = spend_finish(where_ref, size_ref, users, fanout, spend_scr, kept_ref)
     sweep_users(
         user_hbm, scale_hbm, user_ref, scale_ref, item_ref, row_sem, item_sem, item_scale_ref,
-        dual_scr, dots_a, dots_b, finish, fanout, keep
+        dual_scr, dots_a, dots_b, finish, fanout
     )
     halves(where_ref, spend_scr, mine_ref, theirs_ref)
 
-    def kept(k, carry):
-        keep(k).wait()
-        return carry
-
-    lax.fori_loop(0, user_ref.shape[0], kept, 0)
-
-
-def start_kept(kept_hbm, kept_ref, sem):
-    def start(k, carry):
-        pltpu.make_async_copy(kept_hbm.at[k], kept_ref.at[k], sem.at[k]).start()
-        return carry
-
-    lax.fori_loop(0, kept_ref.shape[0], start, 0)
-
-
-def reweigh(kept_hbm, kept_ref, sem, ratio_scr, finish, fanout):
+
+def reweigh(kept_ref, ratio_scr, finish, fanout):
     clusters, users, wide = kept_ref.shape
     camps = wide // fanout
     rows = 64
@@ -298,8 +278,6 @@
         finish(k, None, rows, None, None, sums)
 
     def two(n, carry):
-        for k in (2 * n, 2 * n + 1):
-            pltpu.make_async_copy(kept_hbm.at[k], kept_ref.at[k], sem.at[k]).wait()
         cluster(2 * n)
         cluster(2 * n + 1)
         return carry
@@ -308,25 +286,23 @@
 
 
 def second_kernel(
-    fanout, where_ref, size_ref, duals_ref, limit_ref, match_ref, got_ref, other_ref, kept_hbm, mine_ref, theirs_ref,
-    next_ref, kept_ref, sem, ratio_scr, spend_scr
+    fanout, where_ref, size_ref, duals_ref, limit_ref, match_ref, got_ref, other_ref, kept_ref, mine_ref, theirs_ref,
+    next_ref, ratio_scr, spend_scr
 ):
-    start_kept(kept_hbm, kept_ref, sem)
     duals = updated(duals_ref[...], totals(match_ref, got_ref, other_ref), limit_ref[...])
     next_ref[...] = duals
     ratio_scr[...] = jnp.exp2((duals_ref[...] - duals) * gain)
     finish = spend_finish(where_ref, size_ref, kept_ref.shape[1], fanout, spend_scr)
-    reweigh(kept_hbm, kept_ref, sem, ratio_scr, finish, fanout)
+    reweigh(kept_ref, ratio_scr, finish, fanout)
     spend_scr[...] = spend_scr[...] * ratio_scr[...]
     halves(where_ref, spend_scr, mine_ref, theirs_ref)
 
 
 def third_kernel(
     fanout, where_ref, size_ref, start_ref, duals_ref, limit_ref, match_ref, got_ref, other_ref, own_match_ref,
-    got_one_ref, other_one_ref, own_dual_ref, own_limit_ref, kept_hbm, user_dual_ref, own_out_ref, kept_ref, sem,
+    got_one_ref, other_one_ref, own_dual_ref, own_limit_ref, kept_ref, user_dual_ref, own_out_ref,
     ratio_scr, row_scr
 ):
-    start_kept(kept_hbm, kept_ref, sem)
     duals = updated(duals_ref[...], totals(match_ref, got_ref, other_ref), limit_ref[...])
     ratio_scr[...] = jnp.exp2((start_ref[...] - duals) * gain)
     own = updated(own_dual_ref[...], totals(own_match_ref, got_one_ref, other_one_ref), own_limit_ref[...])
@@ -356,7 +332,7 @@
         )
         return sums
 
-    reweigh(kept_hbm, kept_ref, sem, ratio_scr, finish, fanout)
+    reweigh(kept_ref, ratio_scr, finish, fanout)
     for n in range(row_scr.shape[1]):
         user_dual_ref[:, n * 128 : (n + 1) * 128] = row_scr[:, n, :]
 
@@ -495,31 +471,25 @@
         functools.partial(first_kernel, shards, half, fanout, camps, len(rows)),
         out_shape=spend_out
         + [jax.ShapeDtypeStruct((items, camps), f32)] * 4
-        + [pltpu.HBM((clusters, users, fanout * camps), jnp.bfloat16)],
+        + [pltpu.VMEM((clusters, users, fanout * camps), jnp.bfloat16)],
         in_specs=[SMEM] * 3 + [HBM] * 2 + [ANY] * len(received),
-        out_specs=[VMEM] * 6 + [HBM],
+        out_specs=[VMEM] * 7,
         scratch_shapes=work
         + spend_work
         + [
             pltpu.VMEM((items, len(rows), camps), camp_emb.dtype),
             pltpu.SemaphoreType.DMA((items,)),
-            pltpu.VMEM((clusters, users, fanout * camps), jnp.bfloat16),
-            pltpu.SemaphoreType.DMA((clusters,)),
         ],
         compiler_params=limits,
     )(where, cluster_size, item_of_slot, user_rows, user_scale, *received)
-    kept = in_hbm(kept)
+    kept = in_vmem(kept)
     got_one, other_one = exchange(mine, theirs)
-    again = [
-        pltpu.VMEM((clusters, users, fanout * camps), jnp.bfloat16),
-        pltpu.SemaphoreType.DMA((clusters,)),
-        pltpu.VMEM((items, camps), f32),
-    ]
+    again = [pltpu.VMEM((items, camps), f32)]
 
     mine, theirs, next_dual = pl.pallas_call(
         functools.partial(second_kernel, fanout),
         out_shape=spend_out + [jax.ShapeDtypeStruct((items, camps), f32)],
-        in_specs=[SMEM] * 2 + [VMEM] * 5 + [HBM],
+        in_specs=[SMEM] * 2 + [VMEM] * 6,
         out_specs=[VMEM] * 3,
         scratch_shapes=again + spend_work,
         compiler_params=limits,
@@ -532,7 +502,7 @@
             jax.ShapeDtypeStruct((clusters, users), f32),
             jax.ShapeDtypeStruct((blocks, camps), f32),
         ],
-        in_specs=[SMEM] * 2 + [VMEM] * 11 + [HBM],
+        in_specs=[SMEM] * 2 + [VMEM] * 12,
         out_specs=[VMEM] * 2,
         scratch_shapes=again + [pltpu.VMEM((clusters, users // 128, 128), f32)],
         compiler_params=limits,

time: 205 us -> 202 us (0.985)
  Pallas kernels: 49.2 us -> 46.5 us
where the time goes in v7:
time: 202 us
  waiting for transfers between devices  70.1 us (35%)
  Pallas kernels  46.5 us (23%)
  starting transfers between devices  36.4 us (18%)
  blocking collectives  31 us (15%)
  local copies, waits for them, and re-layouts  11.5 us (6%)
  other arithmetic  5.13 us (3%)
    ppermute x15, waiting for transfers between devices, program(): lax.ppermute(sent[shift, False], 'shard', [(i, i ^ shift) for i in range(...  60.3 us
    all_to_all x2, blocking collectives, exchange(): lax.all_to_all(spread, 'shard', split_axis=0, concat_axis=0, tiled=True)  31 us
    ppermute x15, starting transfers between devices, program(): lax.ppermute(sent[shift, False], 'shard', [(i, i ^ shift) for i in range(...  24.9 us
    pallas_call x1, Pallas kernels, program(): pl.pallas_call(functools.partial(first_kernel, shards, half, fanout, camp...  15.8 us
    pallas_call x2, Pallas kernels, program(): pl.pallas_call(functools.partial(gather_kernel, half, some), out_shape=[p...  12.7 us
    pallas_call x1, Pallas kernels, program(): pl.pallas_call(user_kernel, out_shape=jax.ShapeDtypeStruct((clusters, use...  9.19 us
    all_to_all x1, starting transfers between devices, program(): lax.all_to_all(ask, 'shard', split_axis=0, concat_axis=0, tiled=True)  8.34 us
    pallas_call x1, Pallas kernels, program(): pl.pallas_call(functools.partial(second_kernel, fanout), out_shape=spend_...  4.65 us
  transfers between devices with their start and end apart: 35, of which 21 were waited for; matrix products, arithmetic and copies ran while one was open for 6% of the time, Pallas kernels for 9%

profile of v7, /device:TPU:0, one launch (start us, length us, event | category | flops | bytes accessed | tf_op | source)
XLA Modules:
  0.0 201.6 jit_solution(15349054887179824764)
XLA Ops:
  3.4 8.3 %all-to-all-start = ((s32[16,1,72]{2,1,0:T(1,128)}), s32[16,1,72]{2,1,0:T(1,128)S(1)}, u32[]{:S(2)}, u32[]{:S(2)}) async-start(s32[16,1,72]{2,1,0:T(1,128)} %bitcast.4), calls=%async_computation | async-start | bytes 16384 | tf_op jit(solution)/shard_map/all_to_all | solution.py:369
  14.8 1.5 stack.63.fact_ref
  16.2 2.7 %all-to-all-done = s32[16,1,72]{2,1,0:T(1,128)S(1)} async-done(((s32[16,1,72]{2,1,0:T(1,128)}), s32[16,1,72]{2,1,0:T(1,128)S(1)}, u32[]{:S(2)}, u32[]{:S(2)}) %all-to-all-start) | async-done | bytes 4640 | tf_op jit(solution)/shard_map/all_to_all | solution.py:369
  19.0 3.9 %shard_map.97 = (bf16[528,256]{1,0:T(8,128)(2,1)}, bf16[528,256]{1,0:T(8,128)(2,1)}, bf16[528,256]{1,0:T(8,128)(2,1)}, bf16[528,256]{1,0:T(8,128)(2,1)}) custom-call(s32[2]{0:T(128)S(1)} %pad_add_fusion.1.where_ref, s32[16,72]{1,0:T(8,128)S(1)} %bitcast.29, bf16[128,128,256]{2,1,0:T(8,128)(2,1)} %camp_ref.3, bf16[128,8,128]{2,1,0:T(8,128)(2,1)} %stack.63.fact_ref), custom_call_target="tpu_custom_call" | custom-call | bytes 2097152 | tf_op jit(solution)/shard_map/pallas_call | solution.py:390
  23.6 2.5 %collective-permute-start.16 = (bf16[528,256]{1,0:T(8,128)(2,1)}, bf16[528,256]{1,0:T(8,128)(2,1)S(1)}, u32[]{:S(2)}, u32[]{:S(2)}) collective-permute-start(bf16[528,256]{1,0:T(8,128)(2,1)} %get-tuple-element.49), channel_id=1, source_target_pairs={{0,18},{2,16},{4,22},{6,20},{8,26},{10,24},{12,30},{14,28},{16,2},... | collective-permute-start | bytes 811016 | tf_op jit(solution)/shard_map/ppermute | solution.py:406
  26.0 1.8 collective-permute-start.18
  27.9 2.7 %collective-permute-start.20 = (bf16[528,256]{1,0:T(8,128)(2,1)}, bf16[528,256]{1,0:T(8,128)(2,1)S(1)}, u32[]{:S(2)}, u32[]{:S(2)}) collective-permute-start(bf16[528,256]{1,0:T(8,128)(2,1)} %get-tuple-element.51), channel_id=1, source_target_pairs={{0,22},{2,20},{4,18},{6,16},{8,30},{10,28},{12,26},{14,24},{16,6},... | collective-permute-start | bytes 811016 | tf_op jit(solution)/shard_map/ppermute | solution.py:406
  30.6 8.8 %shard_map.95 = (bf16[528,256]{1,0:T(8,128)(2,1)}, bf16[528,256]{1,0:T(8,128)(2,1)}, bf16[528,256]{1,0:T(8,128)(2,1)}, bf16[528,256]{1,0:T(8,128)(2,1)}, bf16[52...) custom-call(s32[2]{0:T(128)S(1)} %pad_add_fusion.1.where_ref, ...), custom_call_target="tpu_custom_call" | custom-call | bytes 6815744 | tf_op jit(solution)/shard_map/pallas_call | solution.py:390
  39.6 15.1 %collective-permute-done.14.rest_16_ = bf16[528,256]{1,0:T(8,128)(2,1)S(1)} collective-permute-done((bf16[528,256]{1,0:T(8,128)(2,1)}, bf16[528,256]{1,0:T(8,128)(2,1)S(1)}, u32[]{:S(2)}, u32[]{:S(2)}) %collective-permute-start.14) | collective-permute-done | bytes 270368 | tf_op jit(solution)/shard_map/ppermute | solution.py:406
  55.2 5.3 %collective-permute-done.16.rest_18_ = bf16[528,256]{1,0:T(8,128)(2,1)S(1)} collective-permute-done((bf16[528,256]{1,0:T(8,128)(2,1)}, bf16[528,256]{1,0:T(8,128)(2,1)S(1)}, u32[]{:S(2)}, u32[]{:S(2)}) %collective-permute-start.16) | collective-permute-done | bytes 270368 | tf_op jit(solution)/shard_map/ppermute | solution.py:406
  60.4 1.9 collective-permute-start.4
  62.3 4.3 %collective-permute-done.18.rest_20_ = bf16[528,256]{1,0:T(8,128)(2,1)S(1)} collective-permute-done((bf16[528,256]{1,0:T(8,128)(2,1)}, bf16[528,256]{1,0:T(8,128)(2,1)S(1)}, u32[]{:S(2)}, u32[]{:S(2)}) %collective-permute-start.18) | collective-permute-done | bytes 270368 | tf_op jit(solution)/shard_map/ppermute | solution.py:406
  66.7 5.8 %collective-permute-done.20.rest_22_ = bf16[528,256]{1,0:T(8,128)(2,1)S(1)} collective-permute-done((bf16[528,256]{1,0:T(8,128)(2,1)}, bf16[528,256]{1,0:T(8,128)(2,1)S(1)}, u32[]{:S(2)}, u32[]{:S(2)}) %collective-permute-start.20) | collective-permute-done | bytes 270368 | tf_op jit(solution)/shard_map/ppermute | solution.py:406
  72.5 3.4 %collective-permute-start.10 = (bf16[528,256]{1,0:T(8,128)(2,1)}, bf16[528,256]{1,0:T(8,128)(2,1)S(1)}, u32[]{:S(2)}, u32[]{:S(2)}) collective-permute-start(bf16[528,256]{1,0:T(8,128)(2,1)} %get-tuple-element.46), channel_id=1, source_target_pairs={{0,12},{2,14},{4,8},{6,10},{8,4},{10,6},{12,0},{14,2},{16,28},{18,... | collective-permute-start | bytes 811016 | tf_op jit(solution)/shard_map/ppermute | solution.py:406
  76.2 1.9 collective-permute-done.4.rest_6_
  78.1 3.3 %collective-permute-start.22 = (bf16[528,256]{1,0:T(8,128)(2,1)}, bf16[528,256]{1,0:T(8,128)(2,1)}, u32[]{:S(2)}, u32[]{:S(2)}) collective-permute-start(bf16[528,256]{1,0:T(8,128)(2,1)} %get-tuple-element.52), channel_id=1, source_target_pairs={{0,24},{2,26},{4,28},{6,30},{8,16},{10,18},{12,20},{14,22},{16,8},... | collective-permute-start | bytes 811016 | tf_op jit(solution)/shard_map/ppermute | solution.py:406
  82.0 1.7 collective-permute-done.8.rest_10_
  83.7 3.7 %collective-permute-start.26 = (bf16[528,256]{1,0:T(8,128)(2,1)}, bf16[528,256]{1,0:T(8,128)(2,1)}, u32[]{:S(2)}, u32[]{:S(2)}) collective-permute-start(bf16[528,256]{1,0:T(8,128)(2,1)} %get-tuple-element.54), channel_id=1, source_target_pairs={{0,28},{2,30},{4,24},{6,26},{8,20},{10,22},{12,16},{14,18},{16,12}... | collective-permute-start | bytes 811016 | tf_op jit(solution)/shard_map/ppermute | solution.py:406
  87.3 1.9 collective-permute-done.10.rest_12_
  89.3 3.7 %collective-permute-start.28 = (bf16[528,256]{1,0:T(8,128)(2,1)}, bf16[528,256]{1,0:T(8,128)(2,1)}, u32[]{:S(2)}, u32[]{:S(2)}) collective-permute-start(bf16[528,256]{1,0:T(8,128)(2,1)} %get-tuple-element.55), channel_id=1, source_target_pairs={{0,30},{2,28},{4,26},{6,24},{8,22},{10,20},{12,18},{14,16},{16,14}... | collective-permute-start | bytes 811016 | tf_op jit(solution)/shard_map/ppermute | solution.py:406
  95.0 1.4 copy.67
  96.5 7.2 %collective-permute-done.22.rest_24_ = bf16[528,256]{1,0:T(8,128)(2,1)} collective-permute-done((bf16[528,256]{1,0:T(8,128)(2,1)}, bf16[528,256]{1,0:T(8,128)(2,1)}, u32[]{:S(2)}, u32[]{:S(2)}) %collective-permute-start.22) | collective-permute-done | bytes 270368 | tf_op jit(solution)/shard_map/ppermute | solution.py:406
  103.7 5.7 %collective-permute-done.24.rest_26_ = bf16[528,256]{1,0:T(8,128)(2,1)} collective-permute-done((bf16[528,256]{1,0:T(8,128)(2,1)}, bf16[528,256]{1,0:T(8,128)(2,1)}, u32[]{:S(2)}, u32[]{:S(2)}) %collective-permute-start.24) | collective-permute-done | bytes 270368 | tf_op jit(solution)/shard_map/ppermute | solution.py:406
  109.4 5.8 %collective-permute-done.26.rest_28_ = bf16[528,256]{1,0:T(8,128)(2,1)} collective-permute-done((bf16[528,256]{1,0:T(8,128)(2,1)}, bf16[528,256]{1,0:T(8,128)(2,1)}, u32[]{:S(2)}, u32[]{:S(2)}) %collective-permute-start.26) | collective-permute-done | bytes 270368 | tf_op jit(solution)/shard_map/ppermute | solution.py:406
  115.3 5.3 %collective-permute-done.28.rest_30_ = bf16[528,256]{1,0:T(8,128)(2,1)} collective-permute-done((bf16[528,256]{1,0:T(8,128)(2,1)}, bf16[528,256]{1,0:T(8,128)(2,1)}, u32[]{:S(2)}, u32[]{:S(2)}) %collective-permute-start.28) | collective-permute-done | bytes 270368 | tf_op jit(solution)/shard_map/ppermute | solution.py:406
  126.1 9.2 %shard_map.96.scale_hbm = f32[16,512,128]{2,1,0:T(8,128)S(1)} custom-call(bf16[16,512,256]{2,1,0:T(8,128)(2,1)} %user_hbm.1), custom_call_target="tpu_custom_call" | custom-call | flops 8388608 | bytes 8388608 | tf_op jit(solution)/shard_map/pallas_call | solution.py:422
  135.3 2.0 copy-done
  140.7 15.8 %shard_map.98 = (f32[32,128]{1,0:T(8,128)S(1)}, f32[32,128]{1,0:T(8,128)S(1)}, f32[64,128]{1,0:T(8,128)S(1)}, f32[64,128]{1,0:T(8,128)S(1)}, f32[64,128]{1,0:T(8...) custom-call(s32[2]{0:T(128)S(1)} %pad_add_fusion.1.where_ref, s32[16]{0:T(128)S(1)} %copy-done.5, ...), custom_call_target="tpu_custom_call" | custom-call | tf_op jit(solution)/shard_map/pallas_call | solution.py:470
  157.8 20.3 %all_to_all.21 = bf16[16,32,128]{2,1,0:T(8,128)(2,1)S(1)} all-to-all(bf16[16,32,128]{2,1,0:T(8,128)(2,1)S(1)} %broadcast_in_dim.53), channel_id=1, replica_groups=mesh['shard'=16,'rep'=2] {'shard'}, dimensions={0} | all-to-all | bytes 262144 | tf_op jit(solution)/shard_map/all_to_all | solution.py:452
  179.5 4.7 %shard_map.99 = (f32[32,128]{1,0:T(8,128)S(1)}, f32[32,128]{1,0:T(8,128)S(1)}, f32[64,128]{1,0:T(8,128)S(1)}) custom-call(s32[2]{0:T(128)S(1)} %pad_add_fusion.1.where_ref, s32[16]{0:T(128)S(1)} %copy-done.5, f32[64,128]{1,0:T(8,128)S(1)} %get-tuple-element.56.duals_ref.start_ref, f32[64,128]{1,0:T(8,128)S(1)} %get-tuple-element.57.limit_ref, ...), custom_call_target="tpu_custom_call" | custom-call | tf_op jit(solution)/shard_map/pallas_call | solution.py:489
  185.4 10.7 %all_to_all.22 = bf16[16,32,128]{2,1,0:T(8,128)(2,1)S(1)} all-to-all(bf16[16,32,128]{2,1,0:T(8,128)(2,1)S(1)} %broadcast_in_dim.54), channel_id=1, replica_groups=mesh['shard'=16,'rep'=2] {'shard'}, dimensions={0} | all-to-all | bytes 262144 | tf_op jit(solution)/shard_map/all_to_all | solution.py:452
  197.5 4.1 %shard_map.100 = (f32[16,512]{1,0:T(8,128)}, f32[128,128]{1,0:T(8,128)}) custom-call(s32[2]{0:T(128)S(1)} %pad_add_fusion.1.where_ref, s32[16]{0:T(128)S(1)} %copy-done.5, f32[64,128]{1,0:T(8,128)S(1)} %get-tuple-element.56.duals_ref.start_ref, f32[64,128]{1,0:T(8,128)S(1)} %get-tuple-element.62.duals_ref, f32[64,128]{1,0:T(8,128)S(1)} %get-tuple-element.57.limit_ref, ...), custom_call_target="tpu_custom_call" | custom-call | tf_op jit(solution)/shard_map/pallas_call | solution.py:499
  (107 shorter events, 23.9 us)
Async XLA Ops:
  3.4 15.6 %all-to-all-start = ((s32[16,1,72]{2,1,0:T(1,128)}), s32[16,1,72]{2,1,0:T(1,128)S(1)}, u32[]{:S(2)}, u32[]{:S(2)}) async-start(s32[16,1,72]{2,1,0:T(1,128)} %bitcast.4), calls=%async_computation | async-start | bytes 16384 | tf_op jit(solution)/shard_map/all_to_all | solution.py:369
  22.9 31.8 %collective-permute-start.14 = (bf16[528,256]{1,0:T(8,128)(2,1)}, bf16[528,256]{1,0:T(8,128)(2,1)S(1)}, u32[]{:S(2)}, u32[]{:S(2)}) collective-permute-start(bf16[528,256]{1,0:T(8,128)(2,1)} %get-tuple-element.48), channel_id=1, source_target_pairs={{0,16},{2,18},{4,20},{6,22},{8,24},{10,26},{12,28},{14,30},{16,0},... | collective-permute-start | bytes 811016 | tf_op jit(solution)/shard_map/ppermute | solution.py:406
  23.6 36.9 %collective-permute-start.16 = (bf16[528,256]{1,0:T(8,128)(2,1)}, bf16[528,256]{1,0:T(8,128)(2,1)S(1)}, u32[]{:S(2)}, u32[]{:S(2)}) collective-permute-start(bf16[528,256]{1,0:T(8,128)(2,1)} %get-tuple-element.49), channel_id=1, source_target_pairs={{0,18},{2,16},{4,22},{6,20},{8,26},{10,24},{12,30},{14,28},{16,2},... | collective-permute-start | bytes 811016 | tf_op jit(solution)/shard_map/ppermute | solution.py:406
  26.0 40.6 %collective-permute-start.18 = (bf16[528,256]{1,0:T(8,128)(2,1)}, bf16[528,256]{1,0:T(8,128)(2,1)S(1)}, u32[]{:S(2)}, u32[]{:S(2)}) collective-permute-start(bf16[528,256]{1,0:T(8,128)(2,1)} %get-tuple-element.50), channel_id=1, source_target_pairs={{0,20},{2,22},{4,16},{6,18},{8,28},{10,30},{12,24},{14,26},{16,4},... | collective-permute-start | bytes 811016 | tf_op jit(solution)/shard_map/ppermute | solution.py:406
  27.9 44.6 %collective-permute-start.20 = (bf16[528,256]{1,0:T(8,128)(2,1)}, bf16[528,256]{1,0:T(8,128)(2,1)S(1)}, u32[]{:S(2)}, u32[]{:S(2)}) collective-permute-start(bf16[528,256]{1,0:T(8,128)(2,1)} %get-tuple-element.51), channel_id=1, source_target_pairs={{0,22},{2,20},{4,18},{6,16},{8,30},{10,28},{12,26},{14,24},{16,6},... | collective-permute-start | bytes 811016 | tf_op jit(solution)/shard_map/ppermute | solution.py:406
  39.5 33.0 %collective-permute-start = (bf16[528,256]{1,0:T(8,128)(2,1)}, bf16[528,256]{1,0:T(8,128)(2,1)S(1)}, u32[]{:S(2)}, u32[]{:S(2)}) collective-permute-start(bf16[528,256]{1,0:T(8,128)(2,1)} %get-tuple-element.34), channel_id=1, source_target_pairs={{0,4},{2,6},{4,0},{6,2},{8,12},{10,14},{12,8},{14,10},{16,20},{18,... | collective-permute-start | bytes 811016 | tf_op jit(solution)/shard_map/ppermute | solution.py:406
  54.7 21.4 %collective-permute-start.1 = (bf16[528,256]{1,0:T(8,128)(2,1)}, bf16[528,256]{1,0:T(8,128)(2,1)S(1)}, u32[]{:S(2)}, u32[]{:S(2)}) collective-permute-start(bf16[528,256]{1,0:T(8,128)(2,1)} %get-tuple-element.35), channel_id=1, source_target_pairs={{0,2},{2,0},{4,6},{6,4},{8,10},{10,8},{12,14},{14,12},{16,18},{18,... | collective-permute-start | bytes 811016 | tf_op jit(solution)/shard_map/ppermute | solution.py:406
  60.4 17.7 %collective-permute-start.4 = (bf16[528,256]{1,0:T(8,128)(2,1)}, bf16[528,256]{1,0:T(8,128)(2,1)S(1)}, u32[]{:S(2)}, u32[]{:S(2)}) collective-permute-start(bf16[528,256]{1,0:T(8,128)(2,1)} %get-tuple-element.43), channel_id=1, source_target_pairs={{0,6},{2,4},{4,2},{6,0},{8,14},{10,12},{12,10},{14,8},{16,22},{18,... | collective-permute-start | bytes 811016 | tf_op jit(solution)/shard_map/ppermute | solution.py:406
  66.7 14.7 %collective-permute-start.6 = (bf16[528,256]{1,0:T(8,128)(2,1)}, bf16[528,256]{1,0:T(8,128)(2,1)S(1)}, u32[]{:S(2)}, u32[]{:S(2)}) collective-permute-start(bf16[528,256]{1,0:T(8,128)(2,1)} %get-tuple-element.44), channel_id=1, source_target_pairs={{0,8},{2,10},{4,12},{6,14},{8,0},{10,2},{12,4},{14,6},{16,24},{18,... | collective-permute-start | bytes 811016 | tf_op jit(solution)/shard_map/ppermute | solution.py:406
  72.5 11.2 %collective-permute-start.8 = (bf16[528,256]{1,0:T(8,128)(2,1)}, bf16[528,256]{1,0:T(8,128)(2,1)S(1)}, u32[]{:S(2)}, u32[]{:S(2)}) collective-permute-start(bf16[528,256]{1,0:T(8,128)(2,1)} %get-tuple-element.45), channel_id=1, source_target_pairs={{0,10},{2,8},{4,14},{6,12},{8,2},{10,0},{12,6},{14,4},{16,26},{18,... | collective-permute-start | bytes 811016 | tf_op jit(solution)/shard_map/ppermute | solution.py:406
  72.5 16.8 %collective-permute-start.10 = (bf16[528,256]{1,0:T(8,128)(2,1)}, bf16[528,256]{1,0:T(8,128)(2,1)S(1)}, u32[]{:S(2)}, u32[]{:S(2)}) collective-permute-start(bf16[528,256]{1,0:T(8,128)(2,1)} %get-tuple-element.46), channel_id=1, source_target_pairs={{0,12},{2,14},{4,8},{6,10},{8,4},{10,6},{12,0},{14,2},{16,28},{18,... | collective-permute-start | bytes 811016 | tf_op jit(solution)/shard_map/ppermute | solution.py:406
  76.1 20.4 %collective-permute-start.12 = (bf16[528,256]{1,0:T(8,128)(2,1)}, bf16[528,256]{1,0:T(8,128)(2,1)S(1)}, u32[]{:S(2)}, u32[]{:S(2)}) collective-permute-start(bf16[528,256]{1,0:T(8,128)(2,1)} %get-tuple-element.47), channel_id=1, source_target_pairs={{0,14},{2,12},{4,10},{6,8},{8,6},{10,4},{12,2},{14,0},{16,30},{18,... | collective-permute-start | bytes 811016 | tf_op jit(solution)/shard_map/ppermute | solution.py:406
  78.1 25.6 %collective-permute-start.22 = (bf16[528,256]{1,0:T(8,128)(2,1)}, bf16[528,256]{1,0:T(8,128)(2,1)}, u32[]{:S(2)}, u32[]{:S(2)}) collective-permute-start(bf16[528,256]{1,0:T(8,128)(2,1)} %get-tuple-element.52), channel_id=1, source_target_pairs={{0,24},{2,26},{4,28},{6,30},{8,16},{10,18},{12,20},{14,22},{16,8},... | collective-permute-start | bytes 811016 | tf_op jit(solution)/shard_map/ppermute | solution.py:406
  81.4 28.0 %collective-permute-start.24 = (bf16[528,256]{1,0:T(8,128)(2,1)}, bf16[528,256]{1,0:T(8,128)(2,1)}, u32[]{:S(2)}, u32[]{:S(2)}) collective-permute-start(bf16[528,256]{1,0:T(8,128)(2,1)} %get-tuple-element.53), channel_id=1, source_target_pairs={{0,26},{2,24},{4,30},{6,28},{8,18},{10,16},{12,22},{14,20},{16,10}... | collective-permute-start | bytes 811016 | tf_op jit(solution)/shard_map/ppermute | solution.py:406
  83.7 31.6 %collective-permute-start.26 = (bf16[528,256]{1,0:T(8,128)(2,1)}, bf16[528,256]{1,0:T(8,128)(2,1)}, u32[]{:S(2)}, u32[]{:S(2)}) collective-permute-start(bf16[528,256]{1,0:T(8,128)(2,1)} %get-tuple-element.54), channel_id=1, source_target_pairs={{0,28},{2,30},{4,24},{6,26},{8,20},{10,22},{12,16},{14,18},{16,12}... | collective-permute-start | bytes 811016 | tf_op jit(solution)/shard_map/ppermute | solution.py:406
  89.3 31.3 %collective-permute-start.28 = (bf16[528,256]{1,0:T(8,128)(2,1)}, bf16[528,256]{1,0:T(8,128)(2,1)}, u32[]{:S(2)}, u32[]{:S(2)}) collective-permute-start(bf16[528,256]{1,0:T(8,128)(2,1)} %get-tuple-element.55), channel_id=1, source_target_pairs={{0,30},{2,28},{4,26},{6,24},{8,22},{10,20},{12,18},{14,16},{16,14}... | collective-permute-start | bytes 811016 | tf_op jit(solution)/shard_map/ppermute | solution.py:406
  96.5 28.5 %collective-permute-start.2 = (bf16[528,256]{1,0:T(8,128)(2,1)S(1)}, bf16[528,256]{1,0:T(8,128)(2,1)}, u32[]{:S(2)}, u32[]{:S(2)}) collective-permute-start(bf16[528,256]{1,0:T(8,128)(2,1)S(1)} %collective-permute-done.1.rest_2_), channel_id=1, source_target_pairs={{0,1},{1,0},{2,3},{3,2},{4,5},{5,4},{6,7},{7,6},{8,9},{9,8},{10,11... | collective-permute-start | bytes 811016 | tf_op jit(solution)/shard_map/ppermute | solution.py:446
  103.7 20.0 %collective-permute-start.15 = (bf16[528,256]{1,0:T(8,128)(2,1)S(1)}, bf16[528,256]{1,0:T(8,128)(2,1)}, u32[]{:S(2)}, u32[]{:S(2)}) collective-permute-start(bf16[528,256]{1,0:T(8,128)(2,1)S(1)} %collective-permute-done.14.rest_16_), channel_id=1, source_target_pairs={{0,1},{1,0},{2,3},{3,2},{4,5},{5,4},{6,7},{7,6},{8,9},{9,8},{10,11... | collective-permute-start | bytes 811016 | tf_op jit(solution)/shard_map/ppermute | solution.py:446
  109.4 14.9 %collective-permute-start.17 = (bf16[528,256]{1,0:T(8,128)(2,1)S(1)}, bf16[528,256]{1,0:T(8,128)(2,1)}, u32[]{:S(2)}, u32[]{:S(2)}) collective-permute-start(bf16[528,256]{1,0:T(8,128)(2,1)S(1)} %collective-permute-done.16.rest_18_), channel_id=1, source_target_pairs={{0,1},{1,0},{2,3},{3,2},{4,5},{5,4},{6,7},{7,6},{8,9},{9,8},{10,11... | collective-permute-start | bytes 811016 | tf_op jit(solution)/shard_map/ppermute | solution.py:446
  115.3 9.2 %collective-permute-start.19 = (bf16[528,256]{1,0:T(8,128)(2,1)S(1)}, bf16[528,256]{1,0:T(8,128)(2,1)}, u32[]{:S(2)}, u32[]{:S(2)}) collective-permute-start(bf16[528,256]{1,0:T(8,128)(2,1)S(1)} %collective-permute-done.18.rest_20_), channel_id=1, source_target_pairs={{0,1},{1,0},{2,3},{3,2},{4,5},{5,4},{6,7},{7,6},{8,9},{9,8},{10,11... | collective-permute-start | bytes 811016 | tf_op jit(solution)/shard_map/ppermute | solution.py:446
  120.6 4.3 %collective-permute-start.21 = (bf16[528,256]{1,0:T(8,128)(2,1)S(1)}, bf16[528,256]{1,0:T(8,128)(2,1)}, u32[]{:S(2)}, u32[]{:S(2)}) collective-permute-start(bf16[528,256]{1,0:T(8,128)(2,1)S(1)} %collective-permute-done.20.rest_22_), channel_id=1, source_target_pairs={{0,1},{1,0},{2,3},{3,2},{4,5},{5,4},{6,7},{7,6},{8,9},{9,8},{10,11... | collective-permute-start | bytes 811016 | tf_op jit(solution)/shard_map/ppermute | solution.py:446
  123.8 13.6 %collective-permute-start.5 = (bf16[528,256]{1,0:T(8,128)(2,1)S(1)}, bf16[528,256]{1,0:T(8,128)(2,1)S(1)}, u32[]{:S(2)}, u32[]{:S(2)}) collective-permute-start(bf16[528,256]{1,0:T(8,128)(2,1)S(1)} %collective-permute-done.4.rest_6_), channel_id=1, source_target_pairs={{0,1},{1,0},{2,3},{3,2},{4,5},{5,4},{6,7},{7,6},{8,9},{9,8},{10,11... | collective-permute-start | bytes 811016 | tf_op jit(solution)/shard_map/ppermute | solution.py:446
  124.3 13.2 %collective-permute-start.7 = (bf16[528,256]{1,0:T(8,128)(2,1)S(1)}, bf16[528,256]{1,0:T(8,128)(2,1)S(1)}, u32[]{:S(2)}, u32[]{:S(2)}) collective-permute-start(bf16[528,256]{1,0:T(8,128)(2,1)S(1)} %collective-permute-done.6.rest_8_), channel_id=1, source_target_pairs={{0,1},{1,0},{2,3},{3,2},{4,5},{5,4},{6,7},{7,6},{8,9},{9,8},{10,11... | collective-permute-start | bytes 811016 | tf_op jit(solution)/shard_map/ppermute | solution.py:446
  124.4 13.5 %collective-permute-start.9 = (bf16[528,256]{1,0:T(8,128)(2,1)S(1)}, bf16[528,256]{1,0:T(8,128)(2,1)S(1)}, u32[]{:S(2)}, u32[]{:S(2)}) collective-permute-start(bf16[528,256]{1,0:T(8,128)(2,1)S(1)} %collective-permute-done.8.rest_10_), channel_id=1, source_target_pairs={{0,1},{1,0},{2,3},{3,2},{4,5},{5,4},{6,7},{7,6},{8,9},{9,8},{10,11... | collective-permute-start | bytes 811016 | tf_op jit(solution)/shard_map/ppermute | solution.py:446
  124.8 13.2 %collective-permute-start.11 = (bf16[528,256]{1,0:T(8,128)(2,1)S(1)}, bf16[528,256]{1,0:T(8,128)(2,1)S(1)}, u32[]{:S(2)}, u32[]{:S(2)}) collective-permute-start(bf16[528,256]{1,0:T(8,128)(2,1)S(1)} %collective-permute-done.10.rest_12_), channel_id=1, source_target_pairs={{0,1},{1,0},{2,3},{3,2},{4,5},{5,4},{6,7},{7,6},{8,9},{9,8},{10,11... | collective-permute-start | bytes 811016 | tf_op jit(solution)/shard_map/ppermute | solution.py:446
  124.9 13.5 %collective-permute-start.13 = (bf16[528,256]{1,0:T(8,128)(2,1)S(1)}, bf16[528,256]{1,0:T(8,128)(2,1)S(1)}, u32[]{:S(2)}, u32[]{:S(2)}) collective-permute-start(bf16[528,256]{1,0:T(8,128)(2,1)S(1)} %collective-permute-done.12.rest_14_), channel_id=1, source_target_pairs={{0,1},{1,0},{2,3},{3,2},{4,5},{5,4},{6,7},{7,6},{8,9},{9,8},{10,11... | collective-permute-start | bytes 811016 | tf_op jit(solution)/shard_map/ppermute | solution.py:446
  137.3 1.8 collective-permute-start.23
  137.5 2.1 %collective-permute-start.25 = (bf16[528,256]{1,0:T(8,128)(2,1)}, bf16[528,256]{1,0:T(8,128)(2,1)S(1)}, u32[]{:S(2)}, u32[]{:S(2)}) collective-permute-start(bf16[528,256]{1,0:T(8,128)(2,1)} %collective-permute-done.24.rest_26_), channel_id=1, source_target_pairs={{0,1},{1,0},{2,3},{3,2},{4,5},{5,4},{6,7},{7,6},{8,9},{9,8},{10,11... | collective-permute-start | bytes 811016 | tf_op jit(solution)/shard_map/ppermute | solution.py:446
  137.9 2.0 collective-permute-start.27
  138.0 2.3 %collective-permute-start.29 = (bf16[528,256]{1,0:T(8,128)(2,1)}, bf16[528,256]{1,0:T(8,128)(2,1)S(1)}, u32[]{:S(2)}, u32[]{:S(2)}) collective-permute-start(bf16[528,256]{1,0:T(8,128)(2,1)} %collective-permute-done.28.rest_30_), channel_id=1, source_target_pairs={{0,1},{1,0},{2,3},{3,2},{4,5},{5,4},{6,7},{7,6},{8,9},{9,8},{10,11... | collective-permute-start | bytes 811016 | tf_op jit(solution)/shard_map/ppermute | solution.py:446
  138.4 2.3 %collective-permute-start.3 = (bf16[528,256]{1,0:T(8,128)(2,1)S(1)}, bf16[528,256]{1,0:T(8,128)(2,1)S(1)}, u32[]{:S(2)}, u32[]{:S(2)}) collective-permute-start(bf16[528,256]{1,0:T(8,128)(2,1)S(1)} %collective-permute-done.rest_4_), channel_id=1, source_target_pairs={{0,1},{1,0},{2,3},{3,2},{4,5},{5,4},{6,7},{7,6},{8,9},{9,8},{10,11... | collective-permute-start | bytes 811016 | tf_op jit(solution)/shard_map/ppermute | solution.py:446
  178.1 1.3 collective-permute-start.31
  (11 other events, 517.2 us)

commit v8 on v7

--- a/solution.py
+++ b/solution.py
@@ -86,10 +86,25 @@
         copy.wait()
 
 
-def user_kernel(user_ref, scale_ref):
-    rows = user_ref[0].astype(jnp.float32)
-    scale = lax.rsqrt(jnp.sum(rows * rows, axis=1, keepdims=True) * (1.0 / rows.shape[1]) + epsilon)
-    scale_ref[0] = jnp.broadcast_to(scale * (sharpness / rows.shape[1] * gain), scale_ref.shape[1:])
+def user_kernel(user_ref, row_ref, scale_ref, sem):
+    clusters, _, width = row_ref.shape
+
+    def copy(k):
+        return pltpu.make_async_copy(user_ref.at[k], row_ref.at[k], sem.at[k])
+
+    def start(k, carry):
+        copy(k).start()
+        return carry
+
+    def cluster(k, carry):
+        copy(k).wait()
+        rows = row_ref[k].astype(jnp.float32)
+        scale = lax.rsqrt(jnp.sum(rows * rows, axis=1, keepdims=True) * (1.0 / width) + epsilon)
+        scale_ref[k] = jnp.broadcast_to(scale * (sharpness / width * gain), scale_ref.shape[1:])
+        return carry
+
+    lax.fori_loop(0, clusters, start, 0)
+    lax.fori_loop(0, clusters, cluster, 0)
 
 
 def updated(duals, spend, limit):
@@ -102,31 +117,17 @@
     ) + jnp.dot(match_ref[1], other_ref[...], preferred_element_type=jnp.float32)
 
 
-def start_rows(user_hbm, scale_hbm, user_ref, scale_ref, sem):
-    def start(k, carry):
-        pltpu.make_async_copy(user_hbm.at[k], user_ref.at[k], sem.at[0, k]).start()
-        pltpu.make_async_copy(scale_hbm.at[k], scale_ref.at[k], sem.at[1, k]).start()
-        return carry
-
-    lax.fori_loop(0, user_ref.shape[0], start, 0)
-
-
 def item_landed(item, item_ref, item_sem):
     pltpu.make_async_copy(item_ref.at[item], item_ref.at[item], item_sem.at[item]).wait()
 
 
-def sweep_users(
-    user_hbm, scale_hbm, user_ref, scale_ref, item_ref, row_sem, item_sem, item_scale_ref, dual_scr,
-    dots_a, dots_b, finish, fanout
-):
+def sweep_users(user_ref, scale_ref, item_ref, item_sem, item_scale_ref, dual_scr, dots_a, dots_b, finish, fanout):
     clusters, users, _ = user_ref.shape
     camps = item_scale_ref.shape[1]
     width = item_ref.shape[2]
     rows = 64
 
     def landed(k):
-        pltpu.make_async_copy(user_hbm.at[k], user_ref.at[k], row_sem.at[0, k]).wait()
-        pltpu.make_async_copy(scale_hbm.at[k], scale_ref.at[k], row_sem.at[1, k]).wait()
         for e in range(fanout):
             item_landed(k * fanout + e, item_ref, item_sem)
 
@@ -223,11 +224,11 @@
 
 
 def first_kernel(
-    shards, half, fanout, camps, pieces, where_ref, size_ref, item_at_ref, user_hbm, scale_hbm, *rest
+    shards, half, fanout, camps, pieces, where_ref, size_ref, item_at_ref, user_ref, scale_ref, *rest
 ):
     received, outs = rest[: 2 * shards], rest[2 * shards :][:7]
     mine_ref, theirs_ref, duals_ref, limit_ref, live_ref, item_scale_ref, kept_ref = outs
-    user_ref, scale_ref, item_ref, row_sem, item_sem, dots_a, dots_b, dual_scr, spend_scr = rest[-11:-2]
+    item_ref, item_sem, dots_a, dots_b, dual_scr, spend_scr = rest[-8:-2]
     landed_ref, fact_sem = rest[-2:]
     cap = 2 * half
     rep = where_ref[1]
@@ -247,14 +248,10 @@
             for side, message in ((rep, received[2 * n]), (1 - rep, received[2 * n + 1])):
                 rows, lanes = fact_place(j, half, camps, pieces, width)
                 fetch(n * cap + side * half + j, message.at[pl.ds(j * camps, camps)], message.at[rows, lanes])
-    start_rows(user_hbm, scale_hbm, user_ref, scale_ref, row_sem)
     item_facts(landed_ref, fact_sem, duals_ref, limit_ref, live_ref, item_scale_ref)
     dual_scr[...] = jnp.where(live_ref[...] > 0.0, duals_ref[...] * gain, masked)
     finish = spend_finish(where_ref, size_ref, users, fanout, spend_scr, kept_ref)
-    sweep_users(
-        user_hbm, scale_hbm, user_ref, scale_ref, item_ref, row_sem, item_sem, item_scale_ref,
-        dual_scr, dots_a, dots_b, finish, fanout
-    )
+    sweep_users(user_ref, scale_ref, item_ref, item_sem, item_scale_ref, dual_scr, dots_a, dots_b, finish, fanout)
     halves(where_ref, spend_scr, mine_ref, theirs_ref)
 
 
@@ -419,13 +416,16 @@
         )
         - 1
     )
-    user_scale = pl.pallas_call(
+    user_rows, user_scale = pl.pallas_call(
         user_kernel,
-        out_shape=jax.ShapeDtypeStruct((clusters, users, camps), f32),
-        grid=(clusters,),
-        in_specs=[pl.BlockSpec((1, users, width), lambda k: (k, 0, 0))],
-        out_specs=pl.BlockSpec((1, users, camps), lambda k: (k, 0, 0)),
-        compiler_params=pltpu.CompilerParams(vmem_limit_bytes=16 * 2**20),
+        out_shape=[
+            pltpu.VMEM((clusters, users, width), user_emb.dtype),
+            pltpu.VMEM((clusters, users, camps), f32),
+        ],
+        in_specs=[HBM],
+        out_specs=[VMEM] * 2,
+        scratch_shapes=[pltpu.SemaphoreType.DMA((clusters,))],
+        compiler_params=pltpu.CompilerParams(vmem_limit_bytes=12 * 2**20),
         cost_estimate=pl.CostEstimate(flops=8 * 2**20, bytes_accessed=8 * 2**20, transcendentals=0),
     )(in_hbm(user_late))
 
@@ -438,13 +438,13 @@
     own_match = jnp.stack([(own_names[:, None] == side).astype(jnp.bfloat16) for side in sides])
 
     gate = 2
-    got_blocks[gate], item_of_slot, user_scale, match, own_match = lax.optimization_barrier(
-        (got_blocks[gate], item_of_slot, user_scale, match, own_match)
+    got_blocks[gate], item_of_slot, user_rows, user_scale, match, own_match = lax.optimization_barrier(
+        (got_blocks[gate], item_of_slot, user_rows, user_scale, match, own_match)
     )
     received = [sent[0, False], sent[0, True]]
     for shift in range(1, shards):
         received += [got_blocks[shift], lax.ppermute(got_blocks[shift], "rep", swap)]
-    user_rows, user_scale = in_hbm(user_emb), in_hbm(user_scale)
+    user_rows, user_scale = in_vmem(user_rows), in_vmem(user_scale)
 
     def exchange(mine, theirs):
         total = mine + lax.ppermute(theirs, "rep", swap)
@@ -455,10 +455,7 @@
 
     spend_out = [jax.ShapeDtypeStruct((part, camps), f32)] * 2
     work = [
-        pltpu.VMEM((clusters, users, width), user_emb.dtype),
-        pltpu.VMEM((clusters, users, camps), f32),
         pltpu.VMEM((items, camps, width), camp_emb.dtype),
-        pltpu.SemaphoreType.DMA((2, clusters)),
         pltpu.SemaphoreType.DMA((items,)),
         pltpu.VMEM((users, fanout * camps), f32),
         pltpu.VMEM((users, fanout * camps), f32),
@@ -472,7 +469,7 @@
         out_shape=spend_out
         + [jax.ShapeDtypeStruct((items, camps), f32)] * 4
         + [pltpu.VMEM((clusters, users, fanout * camps), jnp.bfloat16)],
-        in_specs=[SMEM] * 3 + [HBM] * 2 + [ANY] * len(received),
+        in_specs=[SMEM] * 3 + [VMEM] * 2 + [ANY] * len(received),
         out_specs=[VMEM] * 7,
         scratch_shapes=work
         + spend_work

time: 202 us -> 196 us (0.970)
  Pallas kernels: 46.5 us -> 40.4 us
  starting transfers between devices: 36.4 us -> 38.9 us
  local copies, waits for them, and re-layouts: 11.5 us -> 9.27 us
    pallas_call x1, Pallas kernels: 9.19 us -> 3.57 us  [program(): pl.pallas_call(user_kernel, out_shape=[pltpu.VMEM((clusters, users, width...]
    ppermute x15, starting transfers between devices: 24.9 us -> 27.5 us  [program(): lax.ppermute(sent[shift, False], 'shard', [(i, i ^ shift) for i in range(...]
  transfers between devices with their start and end apart: 35 -> 35, of which waited for: 21 -> 20; matrix products, arithmetic and copies ran while one was open for 6% -> 5% of each run, Pallas kernels for 9% -> 7%
where the time goes in v8:
time: 196 us; the launch traced here: 195 us
  waiting for transfers between devices  68.9 us (35%)
  Pallas kernels  40.4 us (21%)
  starting transfers between devices  38.9 us (20%)
  blocking collectives  31.4 us (16%)
  local copies, waits for them, and re-layouts  9.27 us (5%)
  other arithmetic  5.26 us (3%)
    ppermute x15, waiting for transfers between devices, program(): lax.ppermute(sent[shift, False], 'shard', [(i, i ^ shift) for i in range(...  59.1 us
    all_to_all x2, blocking collectives, exchange(): lax.all_to_all(spread, 'shard', split_axis=0, concat_axis=0, tiled=True)  31.4 us
    ppermute x15, starting transfers between devices, program(): lax.ppermute(sent[shift, False], 'shard', [(i, i ^ shift) for i in range(...  27.5 us
    pallas_call x1, Pallas kernels, program(): pl.pallas_call(functools.partial(first_kernel, shards, half, fanout, camp...  15.1 us
    pallas_call x2, Pallas kernels, program(): pl.pallas_call(functools.partial(gather_kernel, half, some), out_shape=[p...  13 us
    all_to_all x1, starting transfers between devices, program(): lax.all_to_all(ask, 'shard', split_axis=0, concat_axis=0, tiled=True)  8.34 us
    pallas_call x1, Pallas kernels, program(): pl.pallas_call(functools.partial(second_kernel, fanout), out_shape=spend_...  4.67 us
    pallas_call x1, Pallas kernels, program(): pl.pallas_call(functools.partial(third_kernel, fanout), out_shape=[jax.Sh...  4.09 us
  transfers between devices with their start and end apart: 35, of which 20 were waited for; matrix products, arithmetic and copies ran while one was open for 5% of the time, Pallas kernels for 7%

profile of v8, /device:TPU:0, one launch (start us, length us, event | category | flops | bytes accessed | tf_op | source)
XLA Modules:
  0.0 195.1 jit_solution(13525213838684043526)
XLA Ops:
  3.4 8.3 %all-to-all-start = ((s32[16,1,72]{2,1,0:T(1,128)}), s32[16,1,72]{2,1,0:T(1,128)S(1)}, u32[]{:S(2)}, u32[]{:S(2)}) async-start(s32[16,1,72]{2,1,0:T(1,128)} %bitcast.4), calls=%async_computation | async-start | bytes 16384 | tf_op jit(solution)/shard_map/all_to_all | solution.py:366
  14.8 1.5 stack.63.fact_ref
  16.2 2.8 %all-to-all-done = s32[16,1,72]{2,1,0:T(1,128)S(1)} async-done(((s32[16,1,72]{2,1,0:T(1,128)}), s32[16,1,72]{2,1,0:T(1,128)S(1)}, u32[]{:S(2)}, u32[]{:S(2)}) %all-to-all-start) | async-done | bytes 4640 | tf_op jit(solution)/shard_map/all_to_all | solution.py:366
  19.0 3.9 %shard_map.97 = (bf16[528,256]{1,0:T(8,128)(2,1)}, bf16[528,256]{1,0:T(8,128)(2,1)}, bf16[528,256]{1,0:T(8,128)(2,1)}, bf16[528,256]{1,0:T(8,128)(2,1)}) custom-call(s32[2]{0:T(128)S(1)} %pad_add_fusion.1.where_ref, s32[16,72]{1,0:T(8,128)S(1)} %bitcast.29, bf16[128,128,256]{2,1,0:T(8,128)(2,1)} %camp_ref.3, bf16[128,8,128]{2,1,0:T(8,128)(2,1)} %stack.63.fact_ref), custom_call_target="tpu_custom_call" | custom-call | bytes 2097152 | tf_op jit(solution)/shard_map/pallas_call | solution.py:387
  23.5 2.6 %collective-permute-start.16 = (bf16[528,256]{1,0:T(8,128)(2,1)}, bf16[528,256]{1,0:T(8,128)(2,1)S(1)}, u32[]{:S(2)}, u32[]{:S(2)}) collective-permute-start(bf16[528,256]{1,0:T(8,128)(2,1)} %get-tuple-element.55), channel_id=1, source_target_pairs={{0,18},{2,16},{4,22},{6,20},{8,26},{10,24},{12,30},{14,28},{16,2},... | collective-permute-start | bytes 811016 | tf_op jit(solution)/shard_map/ppermute | solution.py:403
  26.1 1.9 collective-permute-start.18
  28.0 2.6 %collective-permute-start.20 = (bf16[528,256]{1,0:T(8,128)(2,1)}, bf16[528,256]{1,0:T(8,128)(2,1)S(1)}, u32[]{:S(2)}, u32[]{:S(2)}) collective-permute-start(bf16[528,256]{1,0:T(8,128)(2,1)} %get-tuple-element.57), channel_id=1, source_target_pairs={{0,22},{2,20},{4,18},{6,16},{8,30},{10,28},{12,26},{14,24},{16,6},... | collective-permute-start | bytes 811016 | tf_op jit(solution)/shard_map/ppermute | solution.py:403
  30.6 9.1 %shard_map.95 = (bf16[528,256]{1,0:T(8,128)(2,1)}, bf16[528,256]{1,0:T(8,128)(2,1)}, bf16[528,256]{1,0:T(8,128)(2,1)}, bf16[528,256]{1,0:T(8,128)(2,1)}, bf16[52...) custom-call(s32[2]{0:T(128)S(1)} %pad_add_fusion.1.where_ref, ...), custom_call_target="tpu_custom_call" | custom-call | bytes 6815744 | tf_op jit(solution)/shard_map/pallas_call | solution.py:387
  39.9 15.3 %collective-permute-done.14.rest_16_ = bf16[528,256]{1,0:T(8,128)(2,1)S(1)} collective-permute-done((bf16[528,256]{1,0:T(8,128)(2,1)}, bf16[528,256]{1,0:T(8,128)(2,1)S(1)}, u32[]{:S(2)}, u32[]{:S(2)}) %collective-permute-start.14) | collective-permute-done | bytes 270368 | tf_op jit(solution)/shard_map/ppermute | solution.py:403
  55.6 5.3 %collective-permute-done.16.rest_18_ = bf16[528,256]{1,0:T(8,128)(2,1)S(1)} collective-permute-done((bf16[528,256]{1,0:T(8,128)(2,1)}, bf16[528,256]{1,0:T(8,128)(2,1)S(1)}, u32[]{:S(2)}, u32[]{:S(2)}) %collective-permute-start.16) | collective-permute-done | bytes 270368 | tf_op jit(solution)/shard_map/ppermute | solution.py:403
  60.8 1.9 collective-permute-start.4
  62.7 4.3 %collective-permute-done.18.rest_20_ = bf16[528,256]{1,0:T(8,128)(2,1)S(1)} collective-permute-done((bf16[528,256]{1,0:T(8,128)(2,1)}, bf16[528,256]{1,0:T(8,128)(2,1)S(1)}, u32[]{:S(2)}, u32[]{:S(2)}) %collective-permute-start.18) | collective-permute-done | bytes 270368 | tf_op jit(solution)/shard_map/ppermute | solution.py:403
  67.1 5.9 %collective-permute-done.20.rest_22_ = bf16[528,256]{1,0:T(8,128)(2,1)S(1)} collective-permute-done((bf16[528,256]{1,0:T(8,128)(2,1)}, bf16[528,256]{1,0:T(8,128)(2,1)S(1)}, u32[]{:S(2)}, u32[]{:S(2)}) %collective-permute-start.20) | collective-permute-done | bytes 270368 | tf_op jit(solution)/shard_map/ppermute | solution.py:403
  73.7 3.4 %collective-permute-start.10 = (bf16[528,256]{1,0:T(8,128)(2,1)}, bf16[528,256]{1,0:T(8,128)(2,1)S(1)}, u32[]{:S(2)}, u32[]{:S(2)}) collective-permute-start(bf16[528,256]{1,0:T(8,128)(2,1)} %get-tuple-element.52), channel_id=1, source_target_pairs={{0,12},{2,14},{4,8},{6,10},{8,4},{10,6},{12,0},{14,2},{16,28},{18,... | collective-permute-start | bytes 811016 | tf_op jit(solution)/shard_map/ppermute | solution.py:403
  77.4 1.2 collective-permute-done.4.rest_6_
  78.6 3.3 %collective-permute-start.22 = (bf16[528,256]{1,0:T(8,128)(2,1)}, bf16[528,256]{1,0:T(8,128)(2,1)}, u32[]{:S(2)}, u32[]{:S(2)}) collective-permute-start(bf16[528,256]{1,0:T(8,128)(2,1)} %get-tuple-element.58), channel_id=1, source_target_pairs={{0,24},{2,26},{4,28},{6,30},{8,16},{10,18},{12,20},{14,22},{16,8},... | collective-permute-start | bytes 811016 | tf_op jit(solution)/shard_map/ppermute | solution.py:403
  81.9 5.7 %collective-permute-start.24 = (bf16[528,256]{1,0:T(8,128)(2,1)}, bf16[528,256]{1,0:T(8,128)(2,1)}, u32[]{:S(2)}, u32[]{:S(2)}) collective-permute-start(bf16[528,256]{1,0:T(8,128)(2,1)} %get-tuple-element.59), channel_id=1, source_target_pairs={{0,26},{2,24},{4,30},{6,28},{8,18},{10,16},{12,22},{14,20},{16,10}... | collective-permute-start | bytes 811016 | tf_op jit(solution)/shard_map/ppermute | solution.py:403
  88.2 2.2 %collective-permute-done.10.rest_12_ = bf16[528,256]{1,0:T(8,128)(2,1)S(1)} collective-permute-done((bf16[528,256]{1,0:T(8,128)(2,1)}, bf16[528,256]{1,0:T(8,128)(2,1)S(1)}, u32[]{:S(2)}, u32[]{:S(2)}) %collective-permute-start.10) | collective-permute-done | bytes 270368 | tf_op jit(solution)/shard_map/ppermute | solution.py:403
  90.5 4.3 %collective-permute-start.28 = (bf16[528,256]{1,0:T(8,128)(2,1)}, bf16[528,256]{1,0:T(8,128)(2,1)}, u32[]{:S(2)}, u32[]{:S(2)}) collective-permute-start(bf16[528,256]{1,0:T(8,128)(2,1)} %get-tuple-element.61), channel_id=1, source_target_pairs={{0,30},{2,28},{4,26},{6,24},{8,22},{10,20},{12,18},{14,16},{16,14}... | collective-permute-start | bytes 811016 | tf_op jit(solution)/shard_map/ppermute | solution.py:403
  96.9 8.3 %collective-permute-done.22.rest_24_ = bf16[528,256]{1,0:T(8,128)(2,1)} collective-permute-done((bf16[528,256]{1,0:T(8,128)(2,1)}, bf16[528,256]{1,0:T(8,128)(2,1)}, u32[]{:S(2)}, u32[]{:S(2)}) %collective-permute-start.22) | collective-permute-done | bytes 270368 | tf_op jit(solution)/shard_map/ppermute | solution.py:403
  105.3 4.7 %collective-permute-done.24.rest_26_ = bf16[528,256]{1,0:T(8,128)(2,1)} collective-permute-done((bf16[528,256]{1,0:T(8,128)(2,1)}, bf16[528,256]{1,0:T(8,128)(2,1)}, u32[]{:S(2)}, u32[]{:S(2)}) %collective-permute-start.24) | collective-permute-done | bytes 270368 | tf_op jit(solution)/shard_map/ppermute | solution.py:403
  110.0 6.1 %collective-permute-done.26.rest_28_ = bf16[528,256]{1,0:T(8,128)(2,1)} collective-permute-done((bf16[528,256]{1,0:T(8,128)(2,1)}, bf16[528,256]{1,0:T(8,128)(2,1)}, u32[]{:S(2)}, u32[]{:S(2)}) %collective-permute-start.26) | collective-permute-done | bytes 270368 | tf_op jit(solution)/shard_map/ppermute | solution.py:403
  116.1 5.6 %collective-permute-done.28.rest_30_ = bf16[528,256]{1,0:T(8,128)(2,1)} collective-permute-done((bf16[528,256]{1,0:T(8,128)(2,1)}, bf16[528,256]{1,0:T(8,128)(2,1)}, u32[]{:S(2)}, u32[]{:S(2)}) %collective-permute-start.28) | collective-permute-done | bytes 270368 | tf_op jit(solution)/shard_map/ppermute | solution.py:403
  121.7 1.3 constant_dynamic-slice_fusion.1
  127.3 3.6 %shard_map.96 = (bf16[16,512,256]{2,1,0:T(8,128)(2,1)S(1)}, f32[16,512,128]{2,1,0:T(8,128)S(1)}) custom-call(bf16[16,512,256]{2,1,0:T(8,128)(2,1)} %user_ref), custom_call_target="tpu_custom_call" | custom-call | flops 8388608 | bytes 8388608 | tf_op jit(solution)/shard_map/pallas_call | solution.py:419
  134.6 15.1 %shard_map.98 = (f32[32,128]{1,0:T(8,128)S(1)}, f32[32,128]{1,0:T(8,128)S(1)}, f32[64,128]{1,0:T(8,128)S(1)}, f32[64,128]{1,0:T(8,128)S(1)}, f32[64,128]{1,0:T(8...) custom-call(s32[2]{0:T(128)S(1)} %pad_add_fusion.1.where_ref, s32[16]{0:T(128)S(1)} %copy-done.4, ...), custom_call_target="tpu_custom_call" | custom-call | tf_op jit(solution)/shard_map/pallas_call | solution.py:467
  151.0 20.6 %all_to_all.21 = bf16[16,32,128]{2,1,0:T(8,128)(2,1)S(1)} all-to-all(bf16[16,32,128]{2,1,0:T(8,128)(2,1)S(1)} %broadcast_in_dim.53), channel_id=1, replica_groups=mesh['shard'=16,'rep'=2] {'shard'}, dimensions={0} | all-to-all | bytes 262144 | tf_op jit(solution)/shard_map/all_to_all | solution.py:452
  171.6 1.3 collective-permute-done.31.other_ref.other_one_ref
  172.9 4.7 %shard_map.99 = (f32[32,128]{1,0:T(8,128)S(1)}, f32[32,128]{1,0:T(8,128)S(1)}, f32[64,128]{1,0:T(8,128)S(1)}) custom-call(s32[2]{0:T(128)S(1)} %pad_add_fusion.1.where_ref, s32[16]{0:T(128)S(1)} %copy-done.4, f32[64,128]{1,0:T(8,128)S(1)} %get-tuple-element.62.duals_ref.start_ref, f32[64,128]{1,0:T(8,128)S(1)} %get-tuple-element.63.limit_ref, ...), custom_call_target="tpu_custom_call" | custom-call | tf_op jit(solution)/shard_map/pallas_call | solution.py:486
  178.9 10.7 %all_to_all.22 = bf16[16,32,128]{2,1,0:T(8,128)(2,1)S(1)} all-to-all(bf16[16,32,128]{2,1,0:T(8,128)(2,1)S(1)} %broadcast_in_dim.54), channel_id=1, replica_groups=mesh['shard'=16,'rep'=2] {'shard'}, dimensions={0} | all-to-all | bytes 262144 | tf_op jit(solution)/shard_map/all_to_all | solution.py:452
  189.6 1.3 collective-permute-done.33.other_ref
  191.0 4.1 %shard_map.100 = (f32[16,512]{1,0:T(8,128)}, f32[128,128]{1,0:T(8,128)}) custom-call(s32[2]{0:T(128)S(1)} %pad_add_fusion.1.where_ref, s32[16]{0:T(128)S(1)} %copy-done.4, f32[64,128]{1,0:T(8,128)S(1)} %get-tuple-element.62.duals_ref.start_ref, f32[64,128]{1,0:T(8,128)S(1)} %get-tuple-element.68.duals_ref, f32[64,128]{1,0:T(8,128)S(1)} %get-tuple-element.63.limit_ref, ...), custom_call_target="tpu_custom_call" | custom-call | tf_op jit(solution)/shard_map/pallas_call | solution.py:496
  (115 shorter events, 21.1 us)
Async XLA Ops:
  3.4 15.6 %all-to-all-start = ((s32[16,1,72]{2,1,0:T(1,128)}), s32[16,1,72]{2,1,0:T(1,128)S(1)}, u32[]{:S(2)}, u32[]{:S(2)}) async-start(s32[16,1,72]{2,1,0:T(1,128)} %bitcast.4), calls=%async_computation | async-start | bytes 16384 | tf_op jit(solution)/shard_map/all_to_all | solution.py:366
  22.9 32.3 %collective-permute-start.14 = (bf16[528,256]{1,0:T(8,128)(2,1)}, bf16[528,256]{1,0:T(8,128)(2,1)S(1)}, u32[]{:S(2)}, u32[]{:S(2)}) collective-permute-start(bf16[528,256]{1,0:T(8,128)(2,1)} %get-tuple-element.54), channel_id=1, source_target_pairs={{0,16},{2,18},{4,20},{6,22},{8,24},{10,26},{12,28},{14,30},{16,0},... | collective-permute-start | bytes 811016 | tf_op jit(solution)/shard_map/ppermute | solution.py:403
  23.5 37.3 %collective-permute-start.16 = (bf16[528,256]{1,0:T(8,128)(2,1)}, bf16[528,256]{1,0:T(8,128)(2,1)S(1)}, u32[]{:S(2)}, u32[]{:S(2)}) collective-permute-start(bf16[528,256]{1,0:T(8,128)(2,1)} %get-tuple-element.55), channel_id=1, source_target_pairs={{0,18},{2,16},{4,22},{6,20},{8,26},{10,24},{12,30},{14,28},{16,2},... | collective-permute-start | bytes 811016 | tf_op jit(solution)/shard_map/ppermute | solution.py:403
  26.1 40.9 %collective-permute-start.18 = (bf16[528,256]{1,0:T(8,128)(2,1)}, bf16[528,256]{1,0:T(8,128)(2,1)S(1)}, u32[]{:S(2)}, u32[]{:S(2)}) collective-permute-start(bf16[528,256]{1,0:T(8,128)(2,1)} %get-tuple-element.56), channel_id=1, source_target_pairs={{0,20},{2,22},{4,16},{6,18},{8,28},{10,30},{12,24},{14,26},{16,4},... | collective-permute-start | bytes 811016 | tf_op jit(solution)/shard_map/ppermute | solution.py:403
  28.0 45.0 %collective-permute-start.20 = (bf16[528,256]{1,0:T(8,128)(2,1)}, bf16[528,256]{1,0:T(8,128)(2,1)S(1)}, u32[]{:S(2)}, u32[]{:S(2)}) collective-permute-start(bf16[528,256]{1,0:T(8,128)(2,1)} %get-tuple-element.57), channel_id=1, source_target_pairs={{0,22},{2,20},{4,18},{6,16},{8,30},{10,28},{12,26},{14,24},{16,6},... | collective-permute-start | bytes 811016 | tf_op jit(solution)/shard_map/ppermute | solution.py:403
  39.8 34.0 %collective-permute-start = (bf16[528,256]{1,0:T(8,128)(2,1)}, bf16[528,256]{1,0:T(8,128)(2,1)S(1)}, u32[]{:S(2)}, u32[]{:S(2)}) collective-permute-start(bf16[528,256]{1,0:T(8,128)(2,1)} %get-tuple-element.37), channel_id=1, source_target_pairs={{0,4},{2,6},{4,0},{6,2},{8,12},{10,14},{12,8},{14,10},{16,20},{18,... | collective-permute-start | bytes 811016 | tf_op jit(solution)/shard_map/ppermute | solution.py:403
  55.2 22.1 %collective-permute-start.1 = (bf16[528,256]{1,0:T(8,128)(2,1)}, bf16[528,256]{1,0:T(8,128)(2,1)S(1)}, u32[]{:S(2)}, u32[]{:S(2)}) collective-permute-start(bf16[528,256]{1,0:T(8,128)(2,1)} %get-tuple-element.38), channel_id=1, source_target_pairs={{0,2},{2,0},{4,6},{6,4},{8,10},{10,8},{12,14},{14,12},{16,18},{18,... | collective-permute-start | bytes 811016 | tf_op jit(solution)/shard_map/ppermute | solution.py:403
  60.8 17.8 %collective-permute-start.4 = (bf16[528,256]{1,0:T(8,128)(2,1)}, bf16[528,256]{1,0:T(8,128)(2,1)S(1)}, u32[]{:S(2)}, u32[]{:S(2)}) collective-permute-start(bf16[528,256]{1,0:T(8,128)(2,1)} %get-tuple-element.49), channel_id=1, source_target_pairs={{0,6},{2,4},{4,2},{6,0},{8,14},{10,12},{12,10},{14,8},{16,22},{18,... | collective-permute-start | bytes 811016 | tf_op jit(solution)/shard_map/ppermute | solution.py:403
  67.1 14.8 %collective-permute-start.6 = (bf16[528,256]{1,0:T(8,128)(2,1)}, bf16[528,256]{1,0:T(8,128)(2,1)S(1)}, u32[]{:S(2)}, u32[]{:S(2)}) collective-permute-start(bf16[528,256]{1,0:T(8,128)(2,1)} %get-tuple-element.50), channel_id=1, source_target_pairs={{0,8},{2,10},{4,12},{6,14},{8,0},{10,2},{12,4},{14,6},{16,24},{18,... | collective-permute-start | bytes 811016 | tf_op jit(solution)/shard_map/ppermute | solution.py:403
  73.7 13.9 %collective-permute-start.8 = (bf16[528,256]{1,0:T(8,128)(2,1)}, bf16[528,256]{1,0:T(8,128)(2,1)S(1)}, u32[]{:S(2)}, u32[]{:S(2)}) collective-permute-start(bf16[528,256]{1,0:T(8,128)(2,1)} %get-tuple-element.51), channel_id=1, source_target_pairs={{0,10},{2,8},{4,14},{6,12},{8,2},{10,0},{12,6},{14,4},{16,26},{18,... | collective-permute-start | bytes 811016 | tf_op jit(solution)/shard_map/ppermute | solution.py:403
  73.7 16.7 %collective-permute-start.10 = (bf16[528,256]{1,0:T(8,128)(2,1)}, bf16[528,256]{1,0:T(8,128)(2,1)S(1)}, u32[]{:S(2)}, u32[]{:S(2)}) collective-permute-start(bf16[528,256]{1,0:T(8,128)(2,1)} %get-tuple-element.52), channel_id=1, source_target_pairs={{0,12},{2,14},{4,8},{6,10},{8,4},{10,6},{12,0},{14,2},{16,28},{18,... | collective-permute-start | bytes 811016 | tf_op jit(solution)/shard_map/ppermute | solution.py:403
  77.3 19.6 %collective-permute-start.12 = (bf16[528,256]{1,0:T(8,128)(2,1)}, bf16[528,256]{1,0:T(8,128)(2,1)S(1)}, u32[]{:S(2)}, u32[]{:S(2)}) collective-permute-start(bf16[528,256]{1,0:T(8,128)(2,1)} %get-tuple-element.53), channel_id=1, source_target_pairs={{0,14},{2,12},{4,10},{6,8},{8,6},{10,4},{12,2},{14,0},{16,30},{18,... | collective-permute-start | bytes 811016 | tf_op jit(solution)/shard_map/ppermute | solution.py:403
  78.6 26.6 %collective-permute-start.22 = (bf16[528,256]{1,0:T(8,128)(2,1)}, bf16[528,256]{1,0:T(8,128)(2,1)}, u32[]{:S(2)}, u32[]{:S(2)}) collective-permute-start(bf16[528,256]{1,0:T(8,128)(2,1)} %get-tuple-element.58), channel_id=1, source_target_pairs={{0,24},{2,26},{4,28},{6,30},{8,16},{10,18},{12,20},{14,22},{16,8},... | collective-permute-start | bytes 811016 | tf_op jit(solution)/shard_map/ppermute | solution.py:403
  81.9 28.1 %collective-permute-start.24 = (bf16[528,256]{1,0:T(8,128)(2,1)}, bf16[528,256]{1,0:T(8,128)(2,1)}, u32[]{:S(2)}, u32[]{:S(2)}) collective-permute-start(bf16[528,256]{1,0:T(8,128)(2,1)} %get-tuple-element.59), channel_id=1, source_target_pairs={{0,26},{2,24},{4,30},{6,28},{8,18},{10,16},{12,22},{14,20},{16,10}... | collective-permute-start | bytes 811016 | tf_op jit(solution)/shard_map/ppermute | solution.py:403
  87.6 28.5 %collective-permute-start.26 = (bf16[528,256]{1,0:T(8,128)(2,1)}, bf16[528,256]{1,0:T(8,128)(2,1)}, u32[]{:S(2)}, u32[]{:S(2)}) collective-permute-start(bf16[528,256]{1,0:T(8,128)(2,1)} %get-tuple-element.60), channel_id=1, source_target_pairs={{0,28},{2,30},{4,24},{6,26},{8,20},{10,22},{12,16},{14,18},{16,12}... | collective-permute-start | bytes 811016 | tf_op jit(solution)/shard_map/ppermute | solution.py:403
  90.5 31.2 %collective-permute-start.28 = (bf16[528,256]{1,0:T(8,128)(2,1)}, bf16[528,256]{1,0:T(8,128)(2,1)}, u32[]{:S(2)}, u32[]{:S(2)}) collective-permute-start(bf16[528,256]{1,0:T(8,128)(2,1)} %get-tuple-element.61), channel_id=1, source_target_pairs={{0,30},{2,28},{4,26},{6,24},{8,22},{10,20},{12,18},{14,16},{16,14}... | collective-permute-start | bytes 811016 | tf_op jit(solution)/shard_map/ppermute | solution.py:403
  96.9 29.2 %collective-permute-start.2 = (bf16[528,256]{1,0:T(8,128)(2,1)S(1)}, bf16[528,256]{1,0:T(8,128)(2,1)S(1)}, u32[]{:S(2)}, u32[]{:S(2)}) collective-permute-start(bf16[528,256]{1,0:T(8,128)(2,1)S(1)} %collective-permute-done.1.rest_2_), channel_id=1, source_target_pairs={{0,1},{1,0},{2,3},{3,2},{4,5},{5,4},{6,7},{7,6},{8,9},{9,8},{10,11... | collective-permute-start | bytes 811016 | tf_op jit(solution)/shard_map/ppermute | solution.py:446
  105.3 19.6 %collective-permute-start.15 = (bf16[528,256]{1,0:T(8,128)(2,1)S(1)}, bf16[528,256]{1,0:T(8,128)(2,1)}, u32[]{:S(2)}, u32[]{:S(2)}) collective-permute-start(bf16[528,256]{1,0:T(8,128)(2,1)S(1)} %collective-permute-done.14.rest_16_), channel_id=1, source_target_pairs={{0,1},{1,0},{2,3},{3,2},{4,5},{5,4},{6,7},{7,6},{8,9},{9,8},{10,11... | collective-permute-start | bytes 811016 | tf_op jit(solution)/shard_map/ppermute | solution.py:446
  110.0 15.5 %collective-permute-start.17 = (bf16[528,256]{1,0:T(8,128)(2,1)S(1)}, bf16[528,256]{1,0:T(8,128)(2,1)}, u32[]{:S(2)}, u32[]{:S(2)}) collective-permute-start(bf16[528,256]{1,0:T(8,128)(2,1)S(1)} %collective-permute-done.16.rest_18_), channel_id=1, source_target_pairs={{0,1},{1,0},{2,3},{3,2},{4,5},{5,4},{6,7},{7,6},{8,9},{9,8},{10,11... | collective-permute-start | bytes 811016 | tf_op jit(solution)/shard_map/ppermute | solution.py:446
  116.1 9.5 %collective-permute-start.19 = (bf16[528,256]{1,0:T(8,128)(2,1)S(1)}, bf16[528,256]{1,0:T(8,128)(2,1)}, u32[]{:S(2)}, u32[]{:S(2)}) collective-permute-start(bf16[528,256]{1,0:T(8,128)(2,1)S(1)} %collective-permute-done.18.rest_20_), channel_id=1, source_target_pairs={{0,1},{1,0},{2,3},{3,2},{4,5},{5,4},{6,7},{7,6},{8,9},{9,8},{10,11... | collective-permute-start | bytes 811016 | tf_op jit(solution)/shard_map/ppermute | solution.py:446
  121.7 4.3 %collective-permute-start.21 = (bf16[528,256]{1,0:T(8,128)(2,1)}, bf16[528,256]{1,0:T(8,128)(2,1)}, u32[]{:S(2)}, u32[]{:S(2)}) collective-permute-start(bf16[528,256]{1,0:T(8,128)(2,1)} %copy-done.5), channel_id=1, source_target_pairs={{0,1},{1,0},{2,3},{3,2},{4,5},{5,4},{6,7},{7,6},{8,9},{9,8},{10,11... | collective-permute-start | bytes 811016 | tf_op jit(solution)/shard_map/ppermute | solution.py:446
  124.9 6.0 %collective-permute-start.5 = (bf16[528,256]{1,0:T(8,128)(2,1)S(1)}, bf16[528,256]{1,0:T(8,128)(2,1)S(1)}, u32[]{:S(2)}, u32[]{:S(2)}) collective-permute-start(bf16[528,256]{1,0:T(8,128)(2,1)S(1)} %collective-permute-done.4.rest_6_), channel_id=1, source_target_pairs={{0,1},{1,0},{2,3},{3,2},{4,5},{5,4},{6,7},{7,6},{8,9},{9,8},{10,11... | collective-permute-start | bytes 811016 | tf_op jit(solution)/shard_map/ppermute | solution.py:446
  125.5 5.6 %collective-permute-start.7 = (bf16[528,256]{1,0:T(8,128)(2,1)S(1)}, bf16[528,256]{1,0:T(8,128)(2,1)S(1)}, u32[]{:S(2)}, u32[]{:S(2)}) collective-permute-start(bf16[528,256]{1,0:T(8,128)(2,1)S(1)} %collective-permute-done.6.rest_8_), channel_id=1, source_target_pairs={{0,1},{1,0},{2,3},{3,2},{4,5},{5,4},{6,7},{7,6},{8,9},{9,8},{10,11... | collective-permute-start | bytes 811016 | tf_op jit(solution)/shard_map/ppermute | solution.py:446
  125.6 5.9 %collective-permute-start.9 = (bf16[528,256]{1,0:T(8,128)(2,1)S(1)}, bf16[528,256]{1,0:T(8,128)(2,1)S(1)}, u32[]{:S(2)}, u32[]{:S(2)}) collective-permute-start(bf16[528,256]{1,0:T(8,128)(2,1)S(1)} %collective-permute-done.8.rest_10_), channel_id=1, source_target_pairs={{0,1},{1,0},{2,3},{3,2},{4,5},{5,4},{6,7},{7,6},{8,9},{9,8},{10,11... | collective-permute-start | bytes 811016 | tf_op jit(solution)/shard_map/ppermute | solution.py:446
  126.0 5.6 %collective-permute-start.11 = (bf16[528,256]{1,0:T(8,128)(2,1)S(1)}, bf16[528,256]{1,0:T(8,128)(2,1)S(1)}, u32[]{:S(2)}, u32[]{:S(2)}) collective-permute-start(bf16[528,256]{1,0:T(8,128)(2,1)S(1)} %collective-permute-done.10.rest_12_), channel_id=1, source_target_pairs={{0,1},{1,0},{2,3},{3,2},{4,5},{5,4},{6,7},{7,6},{8,9},{9,8},{10,11... | collective-permute-start | bytes 811016 | tf_op jit(solution)/shard_map/ppermute | solution.py:446
  126.1 5.9 %collective-permute-start.13 = (bf16[528,256]{1,0:T(8,128)(2,1)S(1)}, bf16[528,256]{1,0:T(8,128)(2,1)S(1)}, u32[]{:S(2)}, u32[]{:S(2)}) collective-permute-start(bf16[528,256]{1,0:T(8,128)(2,1)S(1)} %collective-permute-done.12.rest_14_), channel_id=1, source_target_pairs={{0,1},{1,0},{2,3},{3,2},{4,5},{5,4},{6,7},{7,6},{8,9},{9,8},{10,11... | collective-permute-start | bytes 811016 | tf_op jit(solution)/shard_map/ppermute | solution.py:446
  130.9 1.8 collective-permute-start.23
  131.1 2.1 %collective-permute-start.25 = (bf16[528,256]{1,0:T(8,128)(2,1)}, bf16[528,256]{1,0:T(8,128)(2,1)S(1)}, u32[]{:S(2)}, u32[]{:S(2)}) collective-permute-start(bf16[528,256]{1,0:T(8,128)(2,1)} %collective-permute-done.24.rest_26_), channel_id=1, source_target_pairs={{0,1},{1,0},{2,3},{3,2},{4,5},{5,4},{6,7},{7,6},{8,9},{9,8},{10,11... | collective-permute-start | bytes 811016 | tf_op jit(solution)/shard_map/ppermute | solution.py:446
  131.5 2.0 %collective-permute-start.27 = (bf16[528,256]{1,0:T(8,128)(2,1)}, bf16[528,256]{1,0:T(8,128)(2,1)S(1)}, u32[]{:S(2)}, u32[]{:S(2)}) collective-permute-start(bf16[528,256]{1,0:T(8,128)(2,1)} %collective-permute-done.26.rest_28_), channel_id=1, source_target_pairs={{0,1},{1,0},{2,3},{3,2},{4,5},{5,4},{6,7},{7,6},{8,9},{9,8},{10,11... | collective-permute-start | bytes 811016 | tf_op jit(solution)/shard_map/ppermute | solution.py:446
  131.6 2.3 %collective-permute-start.29 = (bf16[528,256]{1,0:T(8,128)(2,1)}, bf16[528,256]{1,0:T(8,128)(2,1)S(1)}, u32[]{:S(2)}, u32[]{:S(2)}) collective-permute-start(bf16[528,256]{1,0:T(8,128)(2,1)} %collective-permute-done.28.rest_30_), channel_id=1, source_target_pairs={{0,1},{1,0},{2,3},{3,2},{4,5},{5,4},{6,7},{7,6},{8,9},{9,8},{10,11... | collective-permute-start | bytes 811016 | tf_op jit(solution)/shard_map/ppermute | solution.py:446
  132.0 2.3 %collective-permute-start.3 = (bf16[528,256]{1,0:T(8,128)(2,1)S(1)}, bf16[528,256]{1,0:T(8,128)(2,1)S(1)}, u32[]{:S(2)}, u32[]{:S(2)}) collective-permute-start(bf16[528,256]{1,0:T(8,128)(2,1)S(1)} %collective-permute-done.rest_4_), channel_id=1, source_target_pairs={{0,1},{1,0},{2,3},{3,2},{4,5},{5,4},{6,7},{7,6},{8,9},{9,8},{10,11... | collective-permute-start | bytes 811016 | tf_op jit(solution)/shard_map/ppermute | solution.py:446
  189.6 1.3 collective-permute-start.33
  (15 other events, 427.9 us)

commit v9 on v8

--- a/solution.py
+++ b/solution.py
@@ -58,7 +58,7 @@
                 ),
                 pltpu.make_async_copy(fact_ref.at[block], stage.at[n, rows, lanes], sem.at[1, n * half + j]),
             ):
-                copy.start()
+                copy.start(priority=j % 2)
                 arriving.append(copy)
         leaving.append(pltpu.make_async_copy(stage.at[n], out, sem.at[2, n]))
     for copy in arriving:
@@ -80,8 +80,8 @@
         return carry
 
     lax.fori_loop(0, len(sends), scales, 0, unroll=3 if len(sends) % 3 == 0 else 2 if len(sends) % 2 == 0 else 1)
-    for copy in leaving:
-        copy.start()
+    for n, copy in enumerate(leaving):
+        copy.start(priority=n % 2)
     for copy in leaving:
         copy.wait()
 
@@ -235,19 +235,19 @@
     users = user_ref.shape[1]
     width = item_ref.shape[2]
 
-    def fetch(slot, block, facts):
+    def fetch(slot, queue, block, facts):
         item = item_at_ref[slot]
 
         @pl.when(item >= 0)
         def _():
-            pltpu.make_async_copy(block, item_ref.at[item], item_sem.at[item]).start()
-            pltpu.make_async_copy(facts, landed_ref.at[item], fact_sem.at[item]).start()
+            pltpu.make_async_copy(block, item_ref.at[item], item_sem.at[item]).start(priority=queue)
+            pltpu.make_async_copy(facts, landed_ref.at[item], fact_sem.at[item]).start(priority=1 - queue)
 
     for n in range(shards):
         for j in range(half):
             for side, message in ((rep, received[2 * n]), (1 - rep, received[2 * n + 1])):
                 rows, lanes = fact_place(j, half, camps, pieces, width)
-                fetch(n * cap + side * half + j, message.at[pl.ds(j * camps, camps)], message.at[rows, lanes])
+                fetch(n * cap + side * half + j, j % 2, message.at[pl.ds(j * camps, camps)], message.at[rows, lanes])
     item_facts(landed_ref, fact_sem, duals_ref, limit_ref, live_ref, item_scale_ref)
     dual_scr[...] = jnp.where(live_ref[...] > 0.0, duals_ref[...] * gain, masked)
     finish = spend_finish(where_ref, size_ref, users, fanout, spend_scr, kept_ref)

time: 196 us -> 196 us (level)
  no operation moved by 1% of the time
where the time goes in v9:
time: 196 us; the launch traced here: 195 us
  waiting for transfers between devices  68.9 us (35%)
  Pallas kernels  40.6 us (21%)
  starting transfers between devices  38.9 us (20%)
  blocking collectives  31.4 us (16%)
  local copies, waits for them, and re-layouts  9.27 us (5%)
  other arithmetic  5.26 us (3%)
    ppermute x15, waiting for transfers between devices, program(): lax.ppermute(sent[shift, False], 'shard', [(i, i ^ shift) for i in range(...  59 us
    all_to_all x2, blocking collectives, exchange(): lax.all_to_all(spread, 'shard', split_axis=0, concat_axis=0, tiled=True)  31.4 us
    ppermute x15, starting transfers between devices, program(): lax.ppermute(sent[shift, False], 'shard', [(i, i ^ shift) for i in range(...  27.5 us
    pallas_call x1, Pallas kernels, program(): pl.pallas_call(functools.partial(first_kernel, shards, half, fanout, camp...  15.1 us
    pallas_call x2, Pallas kernels, program(): pl.pallas_call(functools.partial(gather_kernel, half, some), out_shape=[p...  13.1 us
    all_to_all x1, starting transfers between devices, program(): lax.all_to_all(ask, 'shard', split_axis=0, concat_axis=0, tiled=True)  8.34 us
    pallas_call x1, Pallas kernels, program(): pl.pallas_call(functools.partial(second_kernel, fanout), out_shape=spend_...  4.67 us
    pallas_call x1, Pallas kernels, program(): pl.pallas_call(functools.partial(third_kernel, fanout), out_shape=[jax.Sh...  4.09 us
  transfers between devices with their start and end apart: 35, of which 20 were waited for; matrix products, arithmetic and copies ran while one was open for 5% of the time, Pallas kernels for 7%

profile of v9, /device:TPU:0, one launch (start us, length us, event | category | flops | bytes accessed | tf_op | source)
XLA Modules:
  0.0 195.2 jit_solution(10366199980068878810)
XLA Ops:
  3.4 8.3 %all-to-all-start = ((s32[16,1,72]{2,1,0:T(1,128)}), s32[16,1,72]{2,1,0:T(1,128)S(1)}, u32[]{:S(2)}, u32[]{:S(2)}) async-start(s32[16,1,72]{2,1,0:T(1,128)} %bitcast.4), calls=%async_computation | async-start | bytes 16384 | tf_op jit(solution)/shard_map/all_to_all | solution.py:366
  14.8 1.5 stack.63.fact_ref
  16.2 2.8 %all-to-all-done = s32[16,1,72]{2,1,0:T(1,128)S(1)} async-done(((s32[16,1,72]{2,1,0:T(1,128)}), s32[16,1,72]{2,1,0:T(1,128)S(1)}, u32[]{:S(2)}, u32[]{:S(2)}) %all-to-all-start) | async-done | bytes 4640 | tf_op jit(solution)/shard_map/all_to_all | solution.py:366
  19.0 3.9 %shard_map.97 = (bf16[528,256]{1,0:T(8,128)(2,1)}, bf16[528,256]{1,0:T(8,128)(2,1)}, bf16[528,256]{1,0:T(8,128)(2,1)}, bf16[528,256]{1,0:T(8,128)(2,1)}) custom-call(s32[2]{0:T(128)S(1)} %pad_add_fusion.1.where_ref, s32[16,72]{1,0:T(8,128)S(1)} %bitcast.29, bf16[128,128,256]{2,1,0:T(8,128)(2,1)} %camp_ref.3, bf16[128,8,128]{2,1,0:T(8,128)(2,1)} %stack.63.fact_ref), custom_call_target="tpu_custom_call" | custom-call | bytes 2097152 | tf_op jit(solution)/shard_map/pallas_call | solution.py:387
  23.6 2.6 %collective-permute-start.16 = (bf16[528,256]{1,0:T(8,128)(2,1)}, bf16[528,256]{1,0:T(8,128)(2,1)S(1)}, u32[]{:S(2)}, u32[]{:S(2)}) collective-permute-start(bf16[528,256]{1,0:T(8,128)(2,1)} %get-tuple-element.55), channel_id=1, source_target_pairs={{0,18},{2,16},{4,22},{6,20},{8,26},{10,24},{12,30},{14,28},{16,2},... | collective-permute-start | bytes 811016 | tf_op jit(solution)/shard_map/ppermute | solution.py:403
  26.1 1.9 collective-permute-start.18
  28.0 2.6 %collective-permute-start.20 = (bf16[528,256]{1,0:T(8,128)(2,1)}, bf16[528,256]{1,0:T(8,128)(2,1)S(1)}, u32[]{:S(2)}, u32[]{:S(2)}) collective-permute-start(bf16[528,256]{1,0:T(8,128)(2,1)} %get-tuple-element.57), channel_id=1, source_target_pairs={{0,22},{2,20},{4,18},{6,16},{8,30},{10,28},{12,26},{14,24},{16,6},... | collective-permute-start | bytes 811016 | tf_op jit(solution)/shard_map/ppermute | solution.py:403
  30.6 9.2 %shard_map.95 = (bf16[528,256]{1,0:T(8,128)(2,1)}, bf16[528,256]{1,0:T(8,128)(2,1)}, bf16[528,256]{1,0:T(8,128)(2,1)}, bf16[528,256]{1,0:T(8,128)(2,1)}, bf16[52...) custom-call(s32[2]{0:T(128)S(1)} %pad_add_fusion.1.where_ref, ...), custom_call_target="tpu_custom_call" | custom-call | bytes 6815744 | tf_op jit(solution)/shard_map/pallas_call | solution.py:387
  39.9 15.3 %collective-permute-done.14.rest_16_ = bf16[528,256]{1,0:T(8,128)(2,1)S(1)} collective-permute-done((bf16[528,256]{1,0:T(8,128)(2,1)}, bf16[528,256]{1,0:T(8,128)(2,1)S(1)}, u32[]{:S(2)}, u32[]{:S(2)}) %collective-permute-start.14) | collective-permute-done | bytes 270368 | tf_op jit(solution)/shard_map/ppermute | solution.py:403
  55.6 5.3 %collective-permute-done.16.rest_18_ = bf16[528,256]{1,0:T(8,128)(2,1)S(1)} collective-permute-done((bf16[528,256]{1,0:T(8,128)(2,1)}, bf16[528,256]{1,0:T(8,128)(2,1)S(1)}, u32[]{:S(2)}, u32[]{:S(2)}) %collective-permute-start.16) | collective-permute-done | bytes 270368 | tf_op jit(solution)/shard_map/ppermute | solution.py:403
  60.8 1.9 collective-permute-start.4
  62.8 4.3 %collective-permute-done.18.rest_20_ = bf16[528,256]{1,0:T(8,128)(2,1)S(1)} collective-permute-done((bf16[528,256]{1,0:T(8,128)(2,1)}, bf16[528,256]{1,0:T(8,128)(2,1)S(1)}, u32[]{:S(2)}, u32[]{:S(2)}) %collective-permute-start.18) | collective-permute-done | bytes 270368 | tf_op jit(solution)/shard_map/ppermute | solution.py:403
  67.1 5.9 %collective-permute-done.20.rest_22_ = bf16[528,256]{1,0:T(8,128)(2,1)S(1)} collective-permute-done((bf16[528,256]{1,0:T(8,128)(2,1)}, bf16[528,256]{1,0:T(8,128)(2,1)S(1)}, u32[]{:S(2)}, u32[]{:S(2)}) %collective-permute-start.20) | collective-permute-done | bytes 270368 | tf_op jit(solution)/shard_map/ppermute | solution.py:403
  73.8 3.4 %collective-permute-start.10 = (bf16[528,256]{1,0:T(8,128)(2,1)}, bf16[528,256]{1,0:T(8,128)(2,1)S(1)}, u32[]{:S(2)}, u32[]{:S(2)}) collective-permute-start(bf16[528,256]{1,0:T(8,128)(2,1)} %get-tuple-element.52), channel_id=1, source_target_pairs={{0,12},{2,14},{4,8},{6,10},{8,4},{10,6},{12,0},{14,2},{16,28},{18,... | collective-permute-start | bytes 811016 | tf_op jit(solution)/shard_map/ppermute | solution.py:403
  77.5 1.2 collective-permute-done.4.rest_6_
  78.7 3.3 %collective-permute-start.22 = (bf16[528,256]{1,0:T(8,128)(2,1)}, bf16[528,256]{1,0:T(8,128)(2,1)}, u32[]{:S(2)}, u32[]{:S(2)}) collective-permute-start(bf16[528,256]{1,0:T(8,128)(2,1)} %get-tuple-element.58), channel_id=1, source_target_pairs={{0,24},{2,26},{4,28},{6,30},{8,16},{10,18},{12,20},{14,22},{16,8},... | collective-permute-start | bytes 811016 | tf_op jit(solution)/shard_map/ppermute | solution.py:403
  81.9 5.7 %collective-permute-start.24 = (bf16[528,256]{1,0:T(8,128)(2,1)}, bf16[528,256]{1,0:T(8,128)(2,1)}, u32[]{:S(2)}, u32[]{:S(2)}) collective-permute-start(bf16[528,256]{1,0:T(8,128)(2,1)} %get-tuple-element.59), channel_id=1, source_target_pairs={{0,26},{2,24},{4,30},{6,28},{8,18},{10,16},{12,22},{14,20},{16,10}... | collective-permute-start | bytes 811016 | tf_op jit(solution)/shard_map/ppermute | solution.py:403
  88.3 2.2 %collective-permute-done.10.rest_12_ = bf16[528,256]{1,0:T(8,128)(2,1)S(1)} collective-permute-done((bf16[528,256]{1,0:T(8,128)(2,1)}, bf16[528,256]{1,0:T(8,128)(2,1)S(1)}, u32[]{:S(2)}, u32[]{:S(2)}) %collective-permute-start.10) | collective-permute-done | bytes 270368 | tf_op jit(solution)/shard_map/ppermute | solution.py:403
  90.5 4.3 %collective-permute-start.28 = (bf16[528,256]{1,0:T(8,128)(2,1)}, bf16[528,256]{1,0:T(8,128)(2,1)}, u32[]{:S(2)}, u32[]{:S(2)}) collective-permute-start(bf16[528,256]{1,0:T(8,128)(2,1)} %get-tuple-element.61), channel_id=1, source_target_pairs={{0,30},{2,28},{4,26},{6,24},{8,22},{10,20},{12,18},{14,16},{16,14}... | collective-permute-start | bytes 811016 | tf_op jit(solution)/shard_map/ppermute | solution.py:403
  97.0 8.3 %collective-permute-done.22.rest_24_ = bf16[528,256]{1,0:T(8,128)(2,1)} collective-permute-done((bf16[528,256]{1,0:T(8,128)(2,1)}, bf16[528,256]{1,0:T(8,128)(2,1)}, u32[]{:S(2)}, u32[]{:S(2)}) %collective-permute-start.22) | collective-permute-done | bytes 270368 | tf_op jit(solution)/shard_map/ppermute | solution.py:403
  105.3 4.7 %collective-permute-done.24.rest_26_ = bf16[528,256]{1,0:T(8,128)(2,1)} collective-permute-done((bf16[528,256]{1,0:T(8,128)(2,1)}, bf16[528,256]{1,0:T(8,128)(2,1)}, u32[]{:S(2)}, u32[]{:S(2)}) %collective-permute-start.24) | collective-permute-done | bytes 270368 | tf_op jit(solution)/shard_map/ppermute | solution.py:403
  110.0 6.1 %collective-permute-done.26.rest_28_ = bf16[528,256]{1,0:T(8,128)(2,1)} collective-permute-done((bf16[528,256]{1,0:T(8,128)(2,1)}, bf16[528,256]{1,0:T(8,128)(2,1)}, u32[]{:S(2)}, u32[]{:S(2)}) %collective-permute-start.26) | collective-permute-done | bytes 270368 | tf_op jit(solution)/shard_map/ppermute | solution.py:403
  116.1 5.6 %collective-permute-done.28.rest_30_ = bf16[528,256]{1,0:T(8,128)(2,1)} collective-permute-done((bf16[528,256]{1,0:T(8,128)(2,1)}, bf16[528,256]{1,0:T(8,128)(2,1)}, u32[]{:S(2)}, u32[]{:S(2)}) %collective-permute-start.28) | collective-permute-done | bytes 270368 | tf_op jit(solution)/shard_map/ppermute | solution.py:403
  121.7 1.3 constant_dynamic-slice_fusion.1
  127.3 3.6 %shard_map.96 = (bf16[16,512,256]{2,1,0:T(8,128)(2,1)S(1)}, f32[16,512,128]{2,1,0:T(8,128)S(1)}) custom-call(bf16[16,512,256]{2,1,0:T(8,128)(2,1)} %user_ref), custom_call_target="tpu_custom_call" | custom-call | flops 8388608 | bytes 8388608 | tf_op jit(solution)/shard_map/pallas_call | solution.py:419
  134.6 15.1 %shard_map.98 = (f32[32,128]{1,0:T(8,128)S(1)}, f32[32,128]{1,0:T(8,128)S(1)}, f32[64,128]{1,0:T(8,128)S(1)}, f32[64,128]{1,0:T(8,128)S(1)}, f32[64,128]{1,0:T(8...) custom-call(s32[2]{0:T(128)S(1)} %pad_add_fusion.1.where_ref, s32[16]{0:T(128)S(1)} %copy-done.4, ...), custom_call_target="tpu_custom_call" | custom-call | tf_op jit(solution)/shard_map/pallas_call | solution.py:467
  151.1 20.7 %all_to_all.21 = bf16[16,32,128]{2,1,0:T(8,128)(2,1)S(1)} all-to-all(bf16[16,32,128]{2,1,0:T(8,128)(2,1)S(1)} %broadcast_in_dim.53), channel_id=1, replica_groups=mesh['shard'=16,'rep'=2] {'shard'}, dimensions={0} | all-to-all | bytes 262144 | tf_op jit(solution)/shard_map/all_to_all | solution.py:452
  171.7 1.3 collective-permute-done.31.other_ref.other_one_ref
  173.1 4.7 %shard_map.99 = (f32[32,128]{1,0:T(8,128)S(1)}, f32[32,128]{1,0:T(8,128)S(1)}, f32[64,128]{1,0:T(8,128)S(1)}) custom-call(s32[2]{0:T(128)S(1)} %pad_add_fusion.1.where_ref, s32[16]{0:T(128)S(1)} %copy-done.4, f32[64,128]{1,0:T(8,128)S(1)} %get-tuple-element.62.duals_ref.start_ref, f32[64,128]{1,0:T(8,128)S(1)} %get-tuple-element.63.limit_ref, ...), custom_call_target="tpu_custom_call" | custom-call | tf_op jit(solution)/shard_map/pallas_call | solution.py:486
  179.0 10.7 %all_to_all.22 = bf16[16,32,128]{2,1,0:T(8,128)(2,1)S(1)} all-to-all(bf16[16,32,128]{2,1,0:T(8,128)(2,1)S(1)} %broadcast_in_dim.54), channel_id=1, replica_groups=mesh['shard'=16,'rep'=2] {'shard'}, dimensions={0} | all-to-all | bytes 262144 | tf_op jit(solution)/shard_map/all_to_all | solution.py:452
  189.7 1.3 collective-permute-done.33.other_ref
  191.1 4.1 %shard_map.100 = (f32[16,512]{1,0:T(8,128)}, f32[128,128]{1,0:T(8,128)}) custom-call(s32[2]{0:T(128)S(1)} %pad_add_fusion.1.where_ref, s32[16]{0:T(128)S(1)} %copy-done.4, f32[64,128]{1,0:T(8,128)S(1)} %get-tuple-element.62.duals_ref.start_ref, f32[64,128]{1,0:T(8,128)S(1)} %get-tuple-element.68.duals_ref, f32[64,128]{1,0:T(8,128)S(1)} %get-tuple-element.63.limit_ref, ...), custom_call_target="tpu_custom_call" | custom-call | tf_op jit(solution)/shard_map/pallas_call | solution.py:496
  (115 shorter events, 21.1 us)
Async XLA Ops:
  3.4 15.6 %all-to-all-start = ((s32[16,1,72]{2,1,0:T(1,128)}), s32[16,1,72]{2,1,0:T(1,128)S(1)}, u32[]{:S(2)}, u32[]{:S(2)}) async-start(s32[16,1,72]{2,1,0:T(1,128)} %bitcast.4), calls=%async_computation | async-start | bytes 16384 | tf_op jit(solution)/shard_map/all_to_all | solution.py:366
  22.9 32.3 %collective-permute-start.14 = (bf16[528,256]{1,0:T(8,128)(2,1)}, bf16[528,256]{1,0:T(8,128)(2,1)S(1)}, u32[]{:S(2)}, u32[]{:S(2)}) collective-permute-start(bf16[528,256]{1,0:T(8,128)(2,1)} %get-tuple-element.54), channel_id=1, source_target_pairs={{0,16},{2,18},{4,20},{6,22},{8,24},{10,26},{12,28},{14,30},{16,0},... | collective-permute-start | bytes 811016 | tf_op jit(solution)/shard_map/ppermute | solution.py:403
  23.6 37.3 %collective-permute-start.16 = (bf16[528,256]{1,0:T(8,128)(2,1)}, bf16[528,256]{1,0:T(8,128)(2,1)S(1)}, u32[]{:S(2)}, u32[]{:S(2)}) collective-permute-start(bf16[528,256]{1,0:T(8,128)(2,1)} %get-tuple-element.55), channel_id=1, source_target_pairs={{0,18},{2,16},{4,22},{6,20},{8,26},{10,24},{12,30},{14,28},{16,2},... | collective-permute-start | bytes 811016 | tf_op jit(solution)/shard_map/ppermute | solution.py:403
  26.1 40.9 %collective-permute-start.18 = (bf16[528,256]{1,0:T(8,128)(2,1)}, bf16[528,256]{1,0:T(8,128)(2,1)S(1)}, u32[]{:S(2)}, u32[]{:S(2)}) collective-permute-start(bf16[528,256]{1,0:T(8,128)(2,1)} %get-tuple-element.56), channel_id=1, source_target_pairs={{0,20},{2,22},{4,16},{6,18},{8,28},{10,30},{12,24},{14,26},{16,4},... | collective-permute-start | bytes 811016 | tf_op jit(solution)/shard_map/ppermute | solution.py:403
  28.0 45.0 %collective-permute-start.20 = (bf16[528,256]{1,0:T(8,128)(2,1)}, bf16[528,256]{1,0:T(8,128)(2,1)S(1)}, u32[]{:S(2)}, u32[]{:S(2)}) collective-permute-start(bf16[528,256]{1,0:T(8,128)(2,1)} %get-tuple-element.57), channel_id=1, source_target_pairs={{0,22},{2,20},{4,18},{6,16},{8,30},{10,28},{12,26},{14,24},{16,6},... | collective-permute-start | bytes 811016 | tf_op jit(solution)/shard_map/ppermute | solution.py:403
  39.8 33.9 %collective-permute-start = (bf16[528,256]{1,0:T(8,128)(2,1)}, bf16[528,256]{1,0:T(8,128)(2,1)S(1)}, u32[]{:S(2)}, u32[]{:S(2)}) collective-permute-start(bf16[528,256]{1,0:T(8,128)(2,1)} %get-tuple-element.37), channel_id=1, source_target_pairs={{0,4},{2,6},{4,0},{6,2},{8,12},{10,14},{12,8},{14,10},{16,20},{18,... | collective-permute-start | bytes 811016 | tf_op jit(solution)/shard_map/ppermute | solution.py:403
  55.2 22.1 %collective-permute-start.1 = (bf16[528,256]{1,0:T(8,128)(2,1)}, bf16[528,256]{1,0:T(8,128)(2,1)S(1)}, u32[]{:S(2)}, u32[]{:S(2)}) collective-permute-start(bf16[528,256]{1,0:T(8,128)(2,1)} %get-tuple-element.38), channel_id=1, source_target_pairs={{0,2},{2,0},{4,6},{6,4},{8,10},{10,8},{12,14},{14,12},{16,18},{18,... | collective-permute-start | bytes 811016 | tf_op jit(solution)/shard_map/ppermute | solution.py:403
  60.8 17.8 %collective-permute-start.4 = (bf16[528,256]{1,0:T(8,128)(2,1)}, bf16[528,256]{1,0:T(8,128)(2,1)S(1)}, u32[]{:S(2)}, u32[]{:S(2)}) collective-permute-start(bf16[528,256]{1,0:T(8,128)(2,1)} %get-tuple-element.49), channel_id=1, source_target_pairs={{0,6},{2,4},{4,2},{6,0},{8,14},{10,12},{12,10},{14,8},{16,22},{18,... | collective-permute-start | bytes 811016 | tf_op jit(solution)/shard_map/ppermute | solution.py:403
  67.1 14.8 %collective-permute-start.6 = (bf16[528,256]{1,0:T(8,128)(2,1)}, bf16[528,256]{1,0:T(8,128)(2,1)S(1)}, u32[]{:S(2)}, u32[]{:S(2)}) collective-permute-start(bf16[528,256]{1,0:T(8,128)(2,1)} %get-tuple-element.50), channel_id=1, source_target_pairs={{0,8},{2,10},{4,12},{6,14},{8,0},{10,2},{12,4},{14,6},{16,24},{18,... | collective-permute-start | bytes 811016 | tf_op jit(solution)/shard_map/ppermute | solution.py:403
  73.8 13.9 %collective-permute-start.8 = (bf16[528,256]{1,0:T(8,128)(2,1)}, bf16[528,256]{1,0:T(8,128)(2,1)S(1)}, u32[]{:S(2)}, u32[]{:S(2)}) collective-permute-start(bf16[528,256]{1,0:T(8,128)(2,1)} %get-tuple-element.51), channel_id=1, source_target_pairs={{0,10},{2,8},{4,14},{6,12},{8,2},{10,0},{12,6},{14,4},{16,26},{18,... | collective-permute-start | bytes 811016 | tf_op jit(solution)/shard_map/ppermute | solution.py:403
  73.8 16.7 %collective-permute-start.10 = (bf16[528,256]{1,0:T(8,128)(2,1)}, bf16[528,256]{1,0:T(8,128)(2,1)S(1)}, u32[]{:S(2)}, u32[]{:S(2)}) collective-permute-start(bf16[528,256]{1,0:T(8,128)(2,1)} %get-tuple-element.52), channel_id=1, source_target_pairs={{0,12},{2,14},{4,8},{6,10},{8,4},{10,6},{12,0},{14,2},{16,28},{18,... | collective-permute-start | bytes 811016 | tf_op jit(solution)/shard_map/ppermute | solution.py:403
  77.3 19.6 %collective-permute-start.12 = (bf16[528,256]{1,0:T(8,128)(2,1)}, bf16[528,256]{1,0:T(8,128)(2,1)S(1)}, u32[]{:S(2)}, u32[]{:S(2)}) collective-permute-start(bf16[528,256]{1,0:T(8,128)(2,1)} %get-tuple-element.53), channel_id=1, source_target_pairs={{0,14},{2,12},{4,10},{6,8},{8,6},{10,4},{12,2},{14,0},{16,30},{18,... | collective-permute-start | bytes 811016 | tf_op jit(solution)/shard_map/ppermute | solution.py:403
  78.7 26.6 %collective-permute-start.22 = (bf16[528,256]{1,0:T(8,128)(2,1)}, bf16[528,256]{1,0:T(8,128)(2,1)}, u32[]{:S(2)}, u32[]{:S(2)}) collective-permute-start(bf16[528,256]{1,0:T(8,128)(2,1)} %get-tuple-element.58), channel_id=1, source_target_pairs={{0,24},{2,26},{4,28},{6,30},{8,16},{10,18},{12,20},{14,22},{16,8},... | collective-permute-start | bytes 811016 | tf_op jit(solution)/shard_map/ppermute | solution.py:403
  81.9 28.1 %collective-permute-start.24 = (bf16[528,256]{1,0:T(8,128)(2,1)}, bf16[528,256]{1,0:T(8,128)(2,1)}, u32[]{:S(2)}, u32[]{:S(2)}) collective-permute-start(bf16[528,256]{1,0:T(8,128)(2,1)} %get-tuple-element.59), channel_id=1, source_target_pairs={{0,26},{2,24},{4,30},{6,28},{8,18},{10,16},{12,22},{14,20},{16,10}... | collective-permute-start | bytes 811016 | tf_op jit(solution)/shard_map/ppermute | solution.py:403
  87.6 28.5 %collective-permute-start.26 = (bf16[528,256]{1,0:T(8,128)(2,1)}, bf16[528,256]{1,0:T(8,128)(2,1)}, u32[]{:S(2)}, u32[]{:S(2)}) collective-permute-start(bf16[528,256]{1,0:T(8,128)(2,1)} %get-tuple-element.60), channel_id=1, source_target_pairs={{0,28},{2,30},{4,24},{6,26},{8,20},{10,22},{12,16},{14,18},{16,12}... | collective-permute-start | bytes 811016 | tf_op jit(solution)/shard_map/ppermute | solution.py:403
  90.5 31.2 %collective-permute-start.28 = (bf16[528,256]{1,0:T(8,128)(2,1)}, bf16[528,256]{1,0:T(8,128)(2,1)}, u32[]{:S(2)}, u32[]{:S(2)}) collective-permute-start(bf16[528,256]{1,0:T(8,128)(2,1)} %get-tuple-element.61), channel_id=1, source_target_pairs={{0,30},{2,28},{4,26},{6,24},{8,22},{10,20},{12,18},{14,16},{16,14}... | collective-permute-start | bytes 811016 | tf_op jit(solution)/shard_map/ppermute | solution.py:403
  97.0 29.2 %collective-permute-start.2 = (bf16[528,256]{1,0:T(8,128)(2,1)S(1)}, bf16[528,256]{1,0:T(8,128)(2,1)S(1)}, u32[]{:S(2)}, u32[]{:S(2)}) collective-permute-start(bf16[528,256]{1,0:T(8,128)(2,1)S(1)} %collective-permute-done.1.rest_2_), channel_id=1, source_target_pairs={{0,1},{1,0},{2,3},{3,2},{4,5},{5,4},{6,7},{7,6},{8,9},{9,8},{10,11... | collective-permute-start | bytes 811016 | tf_op jit(solution)/shard_map/ppermute | solution.py:446
  105.3 19.6 %collective-permute-start.15 = (bf16[528,256]{1,0:T(8,128)(2,1)S(1)}, bf16[528,256]{1,0:T(8,128)(2,1)}, u32[]{:S(2)}, u32[]{:S(2)}) collective-permute-start(bf16[528,256]{1,0:T(8,128)(2,1)S(1)} %collective-permute-done.14.rest_16_), channel_id=1, source_target_pairs={{0,1},{1,0},{2,3},{3,2},{4,5},{5,4},{6,7},{7,6},{8,9},{9,8},{10,11... | collective-permute-start | bytes 811016 | tf_op jit(solution)/shard_map/ppermute | solution.py:446
  110.0 15.5 %collective-permute-start.17 = (bf16[528,256]{1,0:T(8,128)(2,1)S(1)}, bf16[528,256]{1,0:T(8,128)(2,1)}, u32[]{:S(2)}, u32[]{:S(2)}) collective-permute-start(bf16[528,256]{1,0:T(8,128)(2,1)S(1)} %collective-permute-done.16.rest_18_), channel_id=1, source_target_pairs={{0,1},{1,0},{2,3},{3,2},{4,5},{5,4},{6,7},{7,6},{8,9},{9,8},{10,11... | collective-permute-start | bytes 811016 | tf_op jit(solution)/shard_map/ppermute | solution.py:446
  116.1 9.5 %collective-permute-start.19 = (bf16[528,256]{1,0:T(8,128)(2,1)S(1)}, bf16[528,256]{1,0:T(8,128)(2,1)}, u32[]{:S(2)}, u32[]{:S(2)}) collective-permute-start(bf16[528,256]{1,0:T(8,128)(2,1)S(1)} %collective-permute-done.18.rest_20_), channel_id=1, source_target_pairs={{0,1},{1,0},{2,3},{3,2},{4,5},{5,4},{6,7},{7,6},{8,9},{9,8},{10,11... | collective-permute-start | bytes 811016 | tf_op jit(solution)/shard_map/ppermute | solution.py:446
  121.7 4.3 %collective-permute-start.21 = (bf16[528,256]{1,0:T(8,128)(2,1)}, bf16[528,256]{1,0:T(8,128)(2,1)}, u32[]{:S(2)}, u32[]{:S(2)}) collective-permute-start(bf16[528,256]{1,0:T(8,128)(2,1)} %copy-done.5), channel_id=1, source_target_pairs={{0,1},{1,0},{2,3},{3,2},{4,5},{5,4},{6,7},{7,6},{8,9},{9,8},{10,11... | collective-permute-start | bytes 811016 | tf_op jit(solution)/shard_map/ppermute | solution.py:446
  124.9 6.0 %collective-permute-start.5 = (bf16[528,256]{1,0:T(8,128)(2,1)S(1)}, bf16[528,256]{1,0:T(8,128)(2,1)S(1)}, u32[]{:S(2)}, u32[]{:S(2)}) collective-permute-start(bf16[528,256]{1,0:T(8,128)(2,1)S(1)} %collective-permute-done.4.rest_6_), channel_id=1, source_target_pairs={{0,1},{1,0},{2,3},{3,2},{4,5},{5,4},{6,7},{7,6},{8,9},{9,8},{10,11... | collective-permute-start | bytes 811016 | tf_op jit(solution)/shard_map/ppermute | solution.py:446
  125.5 5.6 %collective-permute-start.7 = (bf16[528,256]{1,0:T(8,128)(2,1)S(1)}, bf16[528,256]{1,0:T(8,128)(2,1)S(1)}, u32[]{:S(2)}, u32[]{:S(2)}) collective-permute-start(bf16[528,256]{1,0:T(8,128)(2,1)S(1)} %collective-permute-done.6.rest_8_), channel_id=1, source_target_pairs={{0,1},{1,0},{2,3},{3,2},{4,5},{5,4},{6,7},{7,6},{8,9},{9,8},{10,11... | collective-permute-start | bytes 811016 | tf_op jit(solution)/shard_map/ppermute | solution.py:446
  125.6 5.9 %collective-permute-start.9 = (bf16[528,256]{1,0:T(8,128)(2,1)S(1)}, bf16[528,256]{1,0:T(8,128)(2,1)S(1)}, u32[]{:S(2)}, u32[]{:S(2)}) collective-permute-start(bf16[528,256]{1,0:T(8,128)(2,1)S(1)} %collective-permute-done.8.rest_10_), channel_id=1, source_target_pairs={{0,1},{1,0},{2,3},{3,2},{4,5},{5,4},{6,7},{7,6},{8,9},{9,8},{10,11... | collective-permute-start | bytes 811016 | tf_op jit(solution)/shard_map/ppermute | solution.py:446
  126.0 5.6 %collective-permute-start.11 = (bf16[528,256]{1,0:T(8,128)(2,1)S(1)}, bf16[528,256]{1,0:T(8,128)(2,1)S(1)}, u32[]{:S(2)}, u32[]{:S(2)}) collective-permute-start(bf16[528,256]{1,0:T(8,128)(2,1)S(1)} %collective-permute-done.10.rest_12_), channel_id=1, source_target_pairs={{0,1},{1,0},{2,3},{3,2},{4,5},{5,4},{6,7},{7,6},{8,9},{9,8},{10,11... | collective-permute-start | bytes 811016 | tf_op jit(solution)/shard_map/ppermute | solution.py:446
  126.1 5.9 %collective-permute-start.13 = (bf16[528,256]{1,0:T(8,128)(2,1)S(1)}, bf16[528,256]{1,0:T(8,128)(2,1)S(1)}, u32[]{:S(2)}, u32[]{:S(2)}) collective-permute-start(bf16[528,256]{1,0:T(8,128)(2,1)S(1)} %collective-permute-done.12.rest_14_), channel_id=1, source_target_pairs={{0,1},{1,0},{2,3},{3,2},{4,5},{5,4},{6,7},{7,6},{8,9},{9,8},{10,11... | collective-permute-start | bytes 811016 | tf_op jit(solution)/shard_map/ppermute | solution.py:446
  130.9 1.8 collective-permute-start.23
  131.1 2.1 %collective-permute-start.25 = (bf16[528,256]{1,0:T(8,128)(2,1)}, bf16[528,256]{1,0:T(8,128)(2,1)S(1)}, u32[]{:S(2)}, u32[]{:S(2)}) collective-permute-start(bf16[528,256]{1,0:T(8,128)(2,1)} %collective-permute-done.24.rest_26_), channel_id=1, source_target_pairs={{0,1},{1,0},{2,3},{3,2},{4,5},{5,4},{6,7},{7,6},{8,9},{9,8},{10,11... | collective-permute-start | bytes 811016 | tf_op jit(solution)/shard_map/ppermute | solution.py:446
  131.5 2.0 %collective-permute-start.27 = (bf16[528,256]{1,0:T(8,128)(2,1)}, bf16[528,256]{1,0:T(8,128)(2,1)S(1)}, u32[]{:S(2)}, u32[]{:S(2)}) collective-permute-start(bf16[528,256]{1,0:T(8,128)(2,1)} %collective-permute-done.26.rest_28_), channel_id=1, source_target_pairs={{0,1},{1,0},{2,3},{3,2},{4,5},{5,4},{6,7},{7,6},{8,9},{9,8},{10,11... | collective-permute-start | bytes 811016 | tf_op jit(solution)/shard_map/ppermute | solution.py:446
  131.6 2.3 %collective-permute-start.29 = (bf16[528,256]{1,0:T(8,128)(2,1)}, bf16[528,256]{1,0:T(8,128)(2,1)S(1)}, u32[]{:S(2)}, u32[]{:S(2)}) collective-permute-start(bf16[528,256]{1,0:T(8,128)(2,1)} %collective-permute-done.28.rest_30_), channel_id=1, source_target_pairs={{0,1},{1,0},{2,3},{3,2},{4,5},{5,4},{6,7},{7,6},{8,9},{9,8},{10,11... | collective-permute-start | bytes 811016 | tf_op jit(solution)/shard_map/ppermute | solution.py:446
  132.0 2.3 %collective-permute-start.3 = (bf16[528,256]{1,0:T(8,128)(2,1)S(1)}, bf16[528,256]{1,0:T(8,128)(2,1)S(1)}, u32[]{:S(2)}, u32[]{:S(2)}) collective-permute-start(bf16[528,256]{1,0:T(8,128)(2,1)S(1)} %collective-permute-done.rest_4_), channel_id=1, source_target_pairs={{0,1},{1,0},{2,3},{3,2},{4,5},{5,4},{6,7},{7,6},{8,9},{9,8},{10,11... | collective-permute-start | bytes 811016 | tf_op jit(solution)/shard_map/ppermute | solution.py:446
  171.7 1.3 collective-permute-start.31
  (15 other events, 427.8 us)
